TPU v7x, 32 devices: a whole 2x2x4 slice. The times are simulated.
32 devices in a mesh: ctx: 8 (over y, x, core), fsdp: 4 (over z).
Axes of the slice: x: 2, y: 2, z: 4, core: 2. Of those that a mesh axis runs over, the one named last changes fastest.
Arguments:
- inputs: bfloat16 [2048, 8, 1024], P('ctx', 'fsdp'), may hold values from -6 to 6
- w_query: bfloat16 [1024, 1024], P('fsdp'), may hold values from -0.25 to 0.25
- w_key: bfloat16 [1024, 1024], P('fsdp'), may hold values from -0.25 to 0.25
- w_value: bfloat16 [1024, 1024], P('fsdp'), may hold values from -0.1875 to 0.1875
- w_out: bfloat16 [1024, 1024], P('fsdp'), may hold values from -0.75 to 0.75
- w_gate: bfloat16 [1024, 4096], P('fsdp'), may hold values from -0.1875 to 0.1875
- w_up: bfloat16 [1024, 4096], P('fsdp'), may hold values from -0.1875 to 0.1875
- w_down: bfloat16 [4096, 1024], P('fsdp'), may hold values from -0.125 to 0.125
- gain_attn: bfloat16 [1024], P('fsdp'), may hold values from 0.25 to 1.75
- gain_ffn: bfloat16 [1024], P('fsdp'), may hold values from 0.25 to 1.75
- segments: int32 [2048, 8], P(None, 'fsdp'), may hold values from 0 to 2047
- deal_order: int32 [16], replicated, may hold values from 0 to 15, as said below
- cotangent: bfloat16 [2048, 8, 1024], P('ctx', 'fsdp'), may hold values from -6 to 6
Outputs:
- output: bfloat16 [2048, 8, 1024], P('ctx', 'fsdp')
- grad_inputs: bfloat16 [2048, 8, 1024], P('ctx', 'fsdp')
- grad_w_query: float32 [1024, 1024], P('fsdp')
- grad_w_key: float32 [1024, 1024], P('fsdp')
- grad_w_value: float32 [1024, 1024], P('fsdp')
- grad_w_out: float32 [1024, 1024], P('fsdp')
- grad_w_gate: float32 [1024, 4096], P('fsdp')
- grad_w_up: float32 [1024, 4096], P('fsdp')
- grad_w_down: float32 [4096, 1024], P('fsdp')
- grad_gain_attn: float32 [1024], P('fsdp')
- grad_gain_ffn: float32 [1024], P('fsdp')
Inputs may be any that keep to these rules, and one draw needn't show every extreme that they name: deal_order is a permutation of the 16 blocks in which entries 2c and 2c + 1 are some p and 15 - p.
All inputs are finite; a program needn't handle non-finite values.
Results may differ from a plain program's by a relative error of at most 0.023.
Values may be sent and summed in bfloat16 or wider, within the bound.
No kernel may reach another device: no remote copies, remote signals or barrier semaphores. Data moves between devices by JAX's collectives and lax.ppermute only.
A program may use at most 320 MiB of HBM per device.

v0:
```python
import math

import jax
import jax.numpy as jnp
from jax import lax
from jax.sharding import PartitionSpec as P

HEAD_DIM = 64


epsilon = 1e-05
masked_score = -1e30


def row_scale(values):
    return lax.rsqrt(jnp.mean(values * values, axis=-1, keepdims=True) + epsilon)


def dot_trans(left_op, right_op):
    return lax.dot_general(
        left_op, right_op, (((1,), (1,)), ((), ())), preferred_element_type=jnp.float32
    )


def trans_dot(left_op, right_op):
    return lax.dot_general(
        left_op, right_op, (((0,), (0,)), ((), ())), preferred_element_type=jnp.float32
    )


def masked_scores(queries, key_blk, q_pos, k_pos, q_seg, k_seg, factor):
    raw_scores = (
        jnp.einsum("qbhd,kbhd->bhqk", queries, key_blk, preferred_element_type=jnp.float32) * factor
    )
    allowed = (q_seg.T[:, :, None] == k_seg.T[:, None, :]) & (
        k_pos[None, None, :] <= q_pos[None, :, None]
    )
    allowed = allowed[:, None]
    return (jnp.where(allowed, raw_scores, masked_score), allowed)


def per_device(
    inputs,
    w_query,
    w_key,
    w_value,
    w_out,
    w_gate,
    w_up,
    w_down,
    gain_attn,
    gain_ffn,
    segments,
    deal_order,
    cotangent,
):
    row_count, seq_count, feat_width = inputs.shape
    groups = lax.axis_size("ctx")
    seq_len = row_count * groups
    half_rows = row_count // 2
    head_dim = HEAD_DIM
    head_count = feat_width // head_dim
    factor = head_dim ** (-0.5)
    tokens = row_count * seq_count
    key_block = math.gcd(seq_len, 512)
    block_count = seq_len // key_block
    my_index = lax.axis_index("ctx")
    offsets = jnp.arange(half_rows, dtype=jnp.int32)
    pos_all = (deal_order[:, None] * half_rows + offsets[None, :]).reshape(seq_len)
    pos_here = lax.dynamic_slice_in_dim(pos_all, my_index * row_count, row_count)
    seg_here = lax.dynamic_slice_in_dim(segments, my_index * row_count, row_count, 0)
    gathered = (
        lax.all_gather(w_query, "fsdp", axis=0, tiled=True),
        lax.all_gather(w_key, "fsdp", axis=0, tiled=True),
        lax.all_gather(w_value, "fsdp", axis=0, tiled=True),
        lax.all_gather(w_out, "fsdp", axis=0, tiled=True),
        lax.all_gather(w_gate, "fsdp", axis=0, tiled=True),
        lax.all_gather(w_up, "fsdp", axis=0, tiled=True),
        lax.all_gather(w_down, "fsdp", axis=0, tiled=True),
        lax.all_gather(gain_attn, "fsdp", axis=0, tiled=True),
        lax.all_gather(gain_ffn, "fsdp", axis=0, tiled=True),
    )
    (
        full_query,
        full_key,
        full_value,
        full_out,
        full_gate,
        full_up,
        full_down,
        gain_one,
        gain_two,
    ) = gathered
    flat_in = inputs.reshape(tokens, feat_width).astype(jnp.float32)
    scale_one = row_scale(flat_in)
    unit_one = flat_in * scale_one
    normed_in = (unit_one * gain_one.astype(jnp.float32)).astype(jnp.bfloat16)
    query_rows = jnp.dot(normed_in, full_query, preferred_element_type=jnp.float32).astype(
        jnp.bfloat16
    )
    key_here = jnp.dot(normed_in, full_key, preferred_element_type=jnp.float32).astype(jnp.bfloat16)
    value_here = jnp.dot(normed_in, full_value, preferred_element_type=jnp.float32).astype(
        jnp.bfloat16
    )
    key_all, value_all = (
        lax.all_gather(
            key_here.reshape(row_count, seq_count, feat_width), "ctx", axis=0, tiled=True
        ),
        lax.all_gather(
            value_here.reshape(row_count, seq_count, feat_width), "ctx", axis=0, tiled=True
        ),
    )
    query_heads = query_rows.reshape(row_count, seq_count, head_count, head_dim)
    key_heads = key_all.reshape(seq_len, seq_count, head_count, head_dim)
    value_heads = value_all.reshape(seq_len, seq_count, head_count, head_dim)

    def take_block(first_row, sub_rows):
        return (
            lax.dynamic_slice_in_dim(key_heads, first_row, sub_rows),
            lax.dynamic_slice_in_dim(value_heads, first_row, sub_rows),
            lax.dynamic_slice_in_dim(pos_all, first_row, sub_rows),
            lax.dynamic_slice_in_dim(segments, first_row, sub_rows),
        )

    def stats_step(carried, block_index):
        run_max, run_sum = carried
        key_blk, _, k_pos, k_seg = take_block(block_index * key_block, key_block)
        scores, allowed = masked_scores(
            query_heads, key_blk, pos_here, k_pos, seg_here, k_seg, factor
        )
        new_max = jnp.maximum(run_max, jnp.max(scores, axis=-1))
        expo = jnp.where(allowed, jnp.exp(scores - new_max[..., None]), 0.0)
        return ((new_max, run_sum * jnp.exp(run_max - new_max) + jnp.sum(expo, axis=-1)), None)

    stat_shape = (seq_count, head_count, row_count)
    (run_max, run_sum), _ = lax.scan(
        stats_step,
        (jnp.full(stat_shape, masked_score, jnp.float32), jnp.zeros(stat_shape, jnp.float32)),
        jnp.arange(block_count, dtype=jnp.int32),
    )
    log_total = run_max + jnp.log(run_sum)

    def prob_block(first_row, sub_rows):
        key_blk, value_blk, k_pos, k_seg = take_block(first_row, sub_rows)
        scores, allowed = masked_scores(
            query_heads, key_blk, pos_here, k_pos, seg_here, k_seg, factor
        )
        prob_f = jnp.where(allowed, jnp.exp(scores - log_total[..., None]), 0.0)
        return (key_blk, value_blk, prob_f)

    def output_step(carried, block_index):
        _, value_blk, prob_f = prob_block(block_index * key_block, key_block)
        prob_low = prob_f.astype(jnp.bfloat16)
        prob_rest = (prob_f - prob_low.astype(jnp.float32)).astype(jnp.bfloat16)
        stacked = jnp.concatenate([prob_low, prob_rest], axis=2)
        return (
            carried
            + jnp.einsum("bhqk,kbhd->qbhd", stacked, value_blk, preferred_element_type=jnp.float32),
            None,
        )

    sums_out, _ = lax.scan(
        output_step,
        jnp.zeros((2 * row_count, seq_count, head_count, head_dim), jnp.float32),
        jnp.arange(block_count, dtype=jnp.int32),
    )
    attended_f = sums_out[:row_count]
    fine_out = sums_out[:row_count] + sums_out[row_count:]
    attended = attended_f.astype(jnp.bfloat16).reshape(tokens, feat_width)
    middle = flat_in + jnp.dot(attended, full_out, preferred_element_type=jnp.float32)
    scale_two = row_scale(middle)
    unit_two = middle * scale_two
    normed_mid = (unit_two * gain_two.astype(jnp.float32)).astype(jnp.bfloat16)
    gate_pre = jnp.dot(normed_mid, full_gate, preferred_element_type=jnp.float32)
    up_pre = jnp.dot(normed_mid, full_up, preferred_element_type=jnp.float32)
    sigma = jax.nn.sigmoid(gate_pre)
    active = gate_pre * sigma
    hidden = (active * up_pre).astype(jnp.bfloat16)
    output = (middle + jnp.dot(hidden, full_down, preferred_element_type=jnp.float32)).astype(
        jnp.bfloat16
    )
    (
        back_query,
        back_key,
        back_value,
        back_out,
        back_gate,
        back_up,
        back_down,
        back_gain_one,
        back_gain_two,
    ) = gathered
    grad_out = cotangent.reshape(tokens, feat_width)
    grad_hidden = dot_trans(grad_out, back_down)
    grad_gate = (grad_hidden * up_pre * sigma * (1.0 + gate_pre * (1.0 - sigma))).astype(
        jnp.bfloat16
    )
    grad_up = (grad_hidden * active).astype(jnp.bfloat16)
    grad_normed_mid = dot_trans(grad_gate, back_gate) + dot_trans(grad_up, back_up)
    grad_gain_ffn = jnp.sum(grad_normed_mid * unit_two, axis=0)
    scaled_two = grad_normed_mid * back_gain_two.astype(jnp.float32)
    grad_middle = grad_out.astype(jnp.float32) + scale_two * (
        scaled_two - unit_two * jnp.mean(scaled_two * unit_two, axis=-1, keepdims=True)
    )
    grad_branch = grad_middle.astype(jnp.bfloat16)
    grad_attended = dot_trans(grad_branch, back_out).astype(jnp.bfloat16)
    grad_heads = grad_attended.reshape(row_count, seq_count, head_count, head_dim)
    delta = jnp.einsum("qbhd,qbhd->bhq", grad_heads.astype(jnp.float32), fine_out)

    def score_grads(value_blk, prob_f):
        grad_probs = jnp.einsum(
            "qbhd,kbhd->bhqk", grad_heads, value_blk, preferred_element_type=jnp.float32
        )
        return (prob_f * (grad_probs - delta[..., None])).astype(jnp.bfloat16)

    def query_step(carried, block_index):
        key_blk, value_blk, prob_f = prob_block(block_index * key_block, key_block)
        grad_scores = score_grads(value_blk, prob_f)
        return (
            carried
            + jnp.einsum(
                "bhqk,kbhd->qbhd", grad_scores, key_blk, preferred_element_type=jnp.float32
            ),
            None,
        )

    query_sums, _ = lax.scan(
        query_step,
        jnp.zeros((row_count, seq_count, head_count, head_dim), jnp.float32),
        jnp.arange(block_count, dtype=jnp.int32),
    )
    grad_query = (query_sums * factor).astype(jnp.bfloat16).reshape(tokens, feat_width)
    amount = row_count * lax.axis_size("ctx")
    sub_rows = math.gcd(amount, 512)

    def one_block(block_index):
        first_row = block_index * sub_rows
        _, value_blk, prob_f = prob_block(first_row, sub_rows)
        grad_scores = score_grads(value_blk, prob_f)
        grad_keys = (
            jnp.einsum(
                "bhqk,qbhd->kbhd", grad_scores, query_heads, preferred_element_type=jnp.float32
            )
            * factor
        )
        grad_values = jnp.einsum(
            "bhqk,qbhd->kbhd",
            prob_f.astype(jnp.bfloat16),
            grad_heads,
            preferred_element_type=jnp.float32,
        )
        return jnp.concatenate(
            [
                grad_keys.reshape(sub_rows, seq_count, feat_width),
                grad_values.reshape(sub_rows, seq_count, feat_width),
            ],
            axis=-1,
        )

    pieces = lax.map(one_block, jnp.arange(amount // sub_rows, dtype=jnp.int32))
    kv_sums = lax.psum_scatter(
        pieces.reshape(amount, seq_count, 2 * feat_width).astype(jnp.bfloat16),
        "ctx",
        scatter_dimension=0,
        tiled=True,
    ).astype(jnp.float32)
    grad_key = kv_sums[..., :feat_width].astype(jnp.bfloat16).reshape(tokens, feat_width)
    grad_value = kv_sums[..., feat_width:].astype(jnp.bfloat16).reshape(tokens, feat_width)
    grad_normed_in = (
        dot_trans(grad_query, back_query)
        + dot_trans(grad_key, back_key)
        + dot_trans(grad_value, back_value)
    )
    grad_gain_attn = jnp.sum(grad_normed_in * unit_one, axis=0)
    scaled_one = grad_normed_in * back_gain_one.astype(jnp.float32)
    grad_inputs = (
        grad_middle
        + scale_one
        * (scaled_one - unit_one * jnp.mean(scaled_one * unit_one, axis=-1, keepdims=True))
    ).astype(jnp.bfloat16)
    g_query = trans_dot(normed_in, grad_query)
    g_key = trans_dot(normed_in, grad_key)
    g_value = trans_dot(normed_in, grad_value)
    g_out = trans_dot(attended, grad_branch)
    g_gate = trans_dot(normed_mid, grad_gate)
    g_up = trans_dot(normed_mid, grad_up)
    g_down = trans_dot(hidden, grad_out)
    parted = (
        lax.psum_scatter(
            g_query.astype(jnp.bfloat16), "fsdp", scatter_dimension=0, tiled=True
        ).astype(jnp.float32),
        lax.psum_scatter(
            g_key.astype(jnp.bfloat16), "fsdp", scatter_dimension=0, tiled=True
        ).astype(jnp.float32),
        lax.psum_scatter(
            g_value.astype(jnp.bfloat16), "fsdp", scatter_dimension=0, tiled=True
        ).astype(jnp.float32),
        lax.psum_scatter(
            g_out.astype(jnp.bfloat16), "fsdp", scatter_dimension=0, tiled=True
        ).astype(jnp.float32),
        lax.psum_scatter(
            g_gate.astype(jnp.bfloat16), "fsdp", scatter_dimension=0, tiled=True
        ).astype(jnp.float32),
        lax.psum_scatter(g_up.astype(jnp.bfloat16), "fsdp", scatter_dimension=0, tiled=True).astype(
            jnp.float32
        ),
        lax.psum_scatter(
            g_down.astype(jnp.bfloat16), "fsdp", scatter_dimension=0, tiled=True
        ).astype(jnp.float32),
        lax.psum_scatter(
            grad_gain_attn.astype(jnp.bfloat16), "fsdp", scatter_dimension=0, tiled=True
        ).astype(jnp.float32),
        lax.psum_scatter(
            grad_gain_ffn.astype(jnp.bfloat16), "fsdp", scatter_dimension=0, tiled=True
        ).astype(jnp.float32),
    )
    s_query, s_key, s_value, s_out, s_gate, s_up, s_down, s_gain_one, s_gain_two = parted
    shares = (
        lax.psum(s_query.astype(jnp.bfloat16), "ctx").astype(jnp.float32),
        lax.psum(s_key.astype(jnp.bfloat16), "ctx").astype(jnp.float32),
        lax.psum(s_value.astype(jnp.bfloat16), "ctx").astype(jnp.float32),
        lax.psum(s_out.astype(jnp.bfloat16), "ctx").astype(jnp.float32),
        lax.psum(s_gate.astype(jnp.bfloat16), "ctx").astype(jnp.float32),
        lax.psum(s_up.astype(jnp.bfloat16), "ctx").astype(jnp.float32),
        lax.psum(s_down.astype(jnp.bfloat16), "ctx").astype(jnp.float32),
        lax.psum(s_gain_one.astype(jnp.bfloat16), "ctx").astype(jnp.float32),
        lax.psum(s_gain_two.astype(jnp.bfloat16), "ctx").astype(jnp.float32),
    )
    return (
        output.reshape(row_count, seq_count, feat_width),
        grad_inputs.reshape(row_count, seq_count, feat_width),
        shares[0],
        shares[1],
        shares[2],
        shares[3],
        shares[4],
        shares[5],
        shares[6],
        shares[7],
        shares[8],
    )


def solution(mesh):
    placed = (
        P("ctx", "fsdp", None),
        P("fsdp", None),
        P("fsdp", None),
        P("fsdp", None),
        P("fsdp", None),
        P("fsdp", None),
        P("fsdp", None),
        P("fsdp", None),
        P("fsdp"),
        P("fsdp"),
        P(None, "fsdp"),
        P(),
        P("ctx", "fsdp", None),
    )
    return jax.shard_map(
        per_device,
        mesh=mesh,
        in_specs=placed,
        out_specs=(
            P("ctx", "fsdp", None),
            P("ctx", "fsdp", None),
            P("fsdp", None),
            P("fsdp", None),
            P("fsdp", None),
            P("fsdp", None),
            P("fsdp", None),
            P("fsdp", None),
            P("fsdp", None),
            P("fsdp"),
            P("fsdp"),
        ),
        check_vma=False,
    )
```

profile of v0, /device:TPU:0, one launch (start us, length us, event | category | flops | bytes accessed | tf_op | source)
XLA Modules:
  0.0 1899.1 jit_solution(10013074849966342643)
XLA Ops:
  10.9 12.6 all-gather
  25.1 33.2 %all-gather.16.cloned.1.call-done = bf16[1024,1024]{1,0:T(8,128)(2,1)} async-done(((bf16[256,1024]{1,0:T(8,128)(2,1)}), bf16[1024,1024]{1,0:T(8,128)(2,1)}) %all-gather.16.cloned.1.call-update) | async-done | bytes 2097168 | tf_op jit(solution)/shard_map/all_gather | solution.py:74
  64.4 40.1 %all-gather.12.cloned.1.call-done = bf16[1024,1024]{1,0:T(8,128)(2,1)} async-done(((bf16[256,1024]{1,0:T(8,128)(2,1)}), bf16[1024,1024]{1,0:T(8,128)(2,1)}) %all-gather.12.cloned.1.call-update) | async-done | bytes 2097168 | tf_op jit(solution)/shard_map/all_gather | solution.py:75
  113.1 9.1 all-gather.1
  124.0 26.8 %all-gather.20.cloned.1.call-done = bf16[1024,1024]{1,0:T(8,128)(2,1)} async-done(((bf16[256,1024]{1,0:T(8,128)(2,1)}), bf16[1024,1024]{1,0:T(8,128)(2,1)}) %all-gather.20.cloned.1.call-update) | async-done | bytes 2097168 | tf_op jit(solution)/shard_map/all_gather | solution.py:73
  156.7 49.8 %all-gather.18.cloned.1.call-done = bf16[2048,2,1024]{2,1,0:T(2,128)(2,1)} async-done(((bf16[256,2,1024]{2,1,0:T(2,128)(2,1)}), bf16[2048,2,1024]{2,1,0:T(2,128)(2,1)}) %all-gather.18.cloned.1.call-update) | async-done | bytes 8388624 | tf_op jit(solution)/shard_map/all_gather | solution.py:106
  206.5 21.3 %copy.77 = bf16[2048,2,1024]{0,2,1:T(8,128)(2,1)} copy(bf16[2048,2,1024]{2,1,0:T(2,128)(2,1)} %all-gather.18.cloned.1.call-done) | data formatting | bytes 16777216 | tf_op jit(solution)/shard_map/all_gather | solution.py:106
  227.8 81.2 %while.46 = (s32[]{:T(128)}, f32[2,16,256]{2,1,0:T(8,128)S(1)}, f32[2,16,256]{2,1,0:T(8,128)S(1)}, s32[256,2]{0,1:T(2,128)S(1)}, s32[4]{0:T(128)S(1)}, /*index=5...) while((s32[]{:T(128)}, f32[2,16,256]{2,1,0:T(8,128)S(1)}, ...), condition=%wide.region_4.5_spmd.clone, body=%wide.region_1.4_spmd.clone.sunk | while | flops 571121664 | bytes 38196444 | solution.py:136
  229.6 11.2 fusion.172
  250.5 10.3 fusion.172
  260.8 8.4 select_reduce_fusion.2
  271.1 10.1 fusion.172
  291.0 10.1 fusion.172
  309.1 103.8 %while.47 = (s32[]{:T(128)}, f32[512,2,16,64]{0,3,2,1:T(8,128)}, s32[4]{0:T(128)S(1)}, bf16[2048,2,16,64]{0,3,2,1:T(8,128)(2,1)}, s32[256,2]{0,1:T(2,128)S(1)}, ...) while((s32[]{:T(128)}, f32[512,2,16,64]{0,3,2,1:T(8,128)}, ...), condition=%wide.region_6.7_spmd.clone, body=%wide.region_5.6_spmd.clone.sunk | while | flops 1680474112 | bytes 48026856 | solution.py:162
  311.1 11.6 fusion.177
  322.7 12.3 bitcast_add_fusion.4
  336.8 11.3 fusion.177
  348.0 13.0 bitcast_add_fusion.4
  362.8 11.3 fusion.177
  374.0 12.9 bitcast_add_fusion.4
  388.7 11.3 fusion.177
  400.0 12.9 bitcast_add_fusion.4
  429.3 32.8 %all-gather.24.cloned.1.call-done = bf16[1024,4096]{1,0:T(8,128)(2,1)} async-done(((bf16[256,4096]{1,0:T(8,128)(2,1)}), bf16[1024,4096]{1,0:T(8,128)(2,1)}) %all-gather.24.cloned.1.call-update) | async-done | bytes 8388624 | tf_op jit(solution)/shard_map/all_gather | solution.py:77
  462.2 10.1 fusion.84
  472.2 139.4 %all-gather.26.cloned.1.call-done = bf16[1024,4096]{1,0:T(8,128)(2,1)} async-done(((bf16[256,4096]{1,0:T(8,128)(2,1)}), bf16[1024,4096]{1,0:T(8,128)(2,1)}) %all-gather.26.cloned.1.call-update) | async-done | bytes 8388624 | tf_op jit(solution)/shard_map/all_gather | solution.py:78
  611.6 10.5 fusion.85
  622.1 139.0 %all-gather.28.cloned.1.call-done = bf16[4096,1024]{1,0:T(8,128)(2,1)} async-done(((bf16[1024,1024]{1,0:T(8,128)(2,1)}), bf16[4096,1024]{1,0:T(8,128)(2,1)}) %all-gather.28.cloned.1.call-update) | async-done | bytes 8388624 | tf_op jit(solution)/shard_map/all_gather | solution.py:79
  761.1 16.2 multiply_convert_fusion
  812.1 151.7 %while.45 = (s32[]{:T(128)}, bf16[4,512,2,2048]{1,3,2,0:T(8,128)(2,1)}, s32[256,2]{0,1:T(2,128)S(1)}, s32[4]{0:T(128)S(1)}, s32[2048,2]{0,1:T(2,128)S(1)}, /*ind...) while((s32[]{:T(128)}, ...), condition=%wide.region_12.13_spmd, body=%wide.region_11.12_spmd.sunk | while | flops 2208956416 | bytes 72471792 | solution.py:260
  813.3 9.7 fusion.168
  823.6 10.2 fusion.169
  833.8 12.4 broadcast_multiply_fusion.5
  851.2 9.7 fusion.168
  861.4 10.2 fusion.169
  871.7 12.4 broadcast_multiply_fusion.5
  889.1 9.8 fusion.168
  899.4 10.2 fusion.169
  909.6 12.4 broadcast_multiply_fusion.5
  927.1 9.7 fusion.168
  937.4 10.2 fusion.169
  947.6 12.4 broadcast_multiply_fusion.5
  963.7 21.6 %copy.86 = bf16[4,512,2,2048]{3,1,0,2:T(8,128)(2,1)} copy(bf16[4,512,2,2048]{1,3,2,0:T(8,128)(2,1)} %get-tuple-element.259) | data formatting | bytes 33554432 | tf_op jit(solution)/shard_map/convert_element_type | solution.py:262
  989.5 117.6 %while.48 = (s32[]{:T(128)}, f32[256,2,16,64]{0,3,2,1:T(8,128)}, s32[4]{0:T(128)S(1)}, bf16[2048,2,16,64]{0,3,2,1:T(8,128)(2,1)}, s32[256,2]{0,1:T(2,128)S(1)}, ...) while((s32[]{:T(128)}, f32[256,2,16,64]{0,3,2,1:T(8,128)}, ...), condition=%wide.region_10.11_spmd.clone, body=%wide.region_9.10_spmd.clone.sunk | while | flops 1641676800 | bytes 47012596 | solution.py:227
  990.7 13.5 fusion.184
  1004.7 17.7 bitcast_add_fusion.5
  1023.6 10.1 fusion.184
  1034.2 16.8 bitcast_add_fusion.5
  1052.2 9.9 fusion.184
  1062.6 16.3 bitcast_add_fusion.5
  1080.1 10.1 fusion.184
  1090.7 16.3 bitcast_add_fusion.5
  1124.6 10.8 convolution_convert_fusion.2
  1136.6 8.9 convolution_convert_fusion.1
  1146.7 9.0 convolution_convert_fusion
  1165.3 44.2 %reduce-scatter.17.cloned.1.call-done = bf16[256,1024]{1,0:T(8,128)(2,1)} async-done(((bf16[1024,1024]{1,0:T(8,128)(2,1)}), bf16[256,1024]{1,0:T(8,128)(2,1)}) %reduce-scatter.17.cloned.1.call-update) | async-done | bytes 524304 | tf_op jit(solution)/shard_map/reduce_scatter | solution.py:298
  1209.5 146.2 %reduce-scatter.19.cloned.1.call-done = bf16[256,4096]{1,0:T(8,128)(2,1)} async-done(((bf16[1024,4096]{1,0:T(8,128)(2,1)}), bf16[256,4096]{1,0:T(8,128)(2,1)}) %reduce-scatter.19.cloned.1.call-update) | async-done | bytes 2097168 | tf_op jit(solution)/shard_map/reduce_scatter | solution.py:301
  1355.7 147.4 %reduce-scatter.21.cloned.1.call-done = bf16[256,4096]{1,0:T(8,128)(2,1)} async-done(((bf16[1024,4096]{1,0:T(8,128)(2,1)}), bf16[256,4096]{1,0:T(8,128)(2,1)}) %reduce-scatter.21.cloned.1.call-update) | async-done | bytes 2097168 | tf_op jit(solution)/shard_map/reduce_scatter | solution.py:304
  1503.1 147.4 %reduce-scatter.23.cloned.1.call-done = bf16[1024,1024]{1,0:T(8,128)(2,1)} async-done(((bf16[4096,1024]{1,0:T(8,128)(2,1)}), bf16[1024,1024]{1,0:T(8,128)(2,1)}) %reduce-scatter.23.cloned.1.call-update) | async-done | bytes 2097168 | tf_op jit(solution)/shard_map/reduce_scatter | solution.py:307
  1650.6 47.4 %reduce-scatter.13.cloned.1.call-done = bf16[256,1024]{1,0:T(8,128)(2,1)} async-done(((bf16[1024,1024]{1,0:T(8,128)(2,1)}), bf16[256,1024]{1,0:T(8,128)(2,1)}) %reduce-scatter.13.cloned.1.call-update) | async-done | bytes 524304 | tf_op jit(solution)/shard_map/reduce_scatter | solution.py:292
  1697.9 46.0 %reduce-scatter.15.cloned.1.call-done = bf16[256,1024]{1,0:T(8,128)(2,1)} async-done(((bf16[1024,1024]{1,0:T(8,128)(2,1)}), bf16[256,1024]{1,0:T(8,128)(2,1)}) %reduce-scatter.15.cloned.1.call-update) | async-done | bytes 524304 | tf_op jit(solution)/shard_map/reduce_scatter | solution.py:295
  1745.9 10.2 add_convert_fusion.1
  1773.0 9.9 all-reduce.4
  1783.1 12.5 all-reduce.2
  1796.7 80.3 %all-reduce.7.cloned.1.call-done = (bf16[256,1024]{1,0:T(8,128)(2,1)}, bf16[256,1024]{1,0:T(8,128)(2,1)}, bf16[256,1024]{1,0:T(8,128)(2,1)}, bf16[256,1024]{1,0:...) async-done(((bf16[256,1024]{1,0:T(8,128)(2,1)}, bf16[256,1024]{1,0:T(8,128)(2,1)}, bf16[256,1024]{1,0:T(8,128)(2,1)}, ...) | async-done | bytes 8388624 | tf_op jit(solution)/shard_map/psum | solution.py:319
  (309 shorter events, 202.9 us)
Async XLA Ops:
  7.2 16.3 copy-start.3
  7.2 3.7 copy-start.40
  7.2 51.1 %all-gather.16.cloned.1.call-start = ((), (), s32[]{:S(2)}) async-start(), calls=%async_computation.10 | async-start | bytes 2621440 | tf_op jit(solution)/shard_map/all_gather | solution.py:74
  7.9 96.6 %all-gather.12.cloned.1.call-start = ((), (), s32[]{:S(2)}) async-start(), calls=%async_computation.8 | async-start | bytes 2621440 | tf_op jit(solution)/shard_map/all_gather | solution.py:75
  8.7 142.1 %all-gather.20.cloned.1.call-start = ((), (), s32[]{:S(2)}) async-start(), calls=%async_computation.12 | async-start | bytes 2621440 | tf_op jit(solution)/shard_map/all_gather | solution.py:73
  9.4 197.1 %all-gather.18.cloned.1.call-start = ((), (), s32[]{:S(2)}) async-start(), calls=%async_computation.11 | async-start | bytes 9437184 | tf_op jit(solution)/shard_map/all_gather | solution.py:106
  10.9 51.2 %copy-start = (f32[512,1024]{1,0:T(8,128)}, f32[512,1024]{1,0:T(8,128)S(1)}, u32[]{:S(2)}) copy-start(f32[512,1024]{1,0:T(8,128)S(1)} %reshape.322) | copy-start | bytes 6291460
  23.5 38.6 %copy-start.31 = (f32[4,1,256]{2,1,0:T(1,128)}, f32[4,1,256]{2,1,0:T(1,128)S(1)}, u32[]{:S(2)}) copy-start(f32[4,1,256]{2,1,0:T(1,128)S(1)} %convert_element_type.215) | copy-start | bytes 12292
  24.7 37.4 %copy-start.20 = (f32[256,2]{1,0:T(8,128)}, f32[256,2]{1,0:T(8,128)S(1)}, u32[]{:S(2)}) copy-start(f32[256,2]{1,0:T(8,128)S(1)} %add_rsqrt_fusion) | copy-start | bytes 6148
  24.8 37.3 %copy-start.35 = (f32[512]{0:T(512)}, f32[512]{0:T(512)S(1)}, u32[]{:S(2)}) copy-start(f32[512]{0:T(512)S(1)} %rsqrt.21) | copy-start | bytes 6148
  25.1 79.4 %copy-start.26 = (bf16[512,1024]{1,0:T(8,128)(2,1)}, bf16[512,1024]{1,0:T(8,128)(2,1)S(1)}, u32[]{:S(2)}) copy-start(bf16[512,1024]{1,0:T(8,128)(2,1)S(1)} %multiply_convert_fusion.6) | copy-start | bytes 3145732
  64.4 244.7 %all-gather.14.cloned.1.call-start = ((), (), s32[]{:S(2)}) async-start(), calls=%async_computation.9 | async-start | bytes 9437184 | tf_op jit(solution)/shard_map/all_gather | solution.py:109
  110.0 3.0 copy-start.41
  110.0 3.0 copy-start.30
  110.0 3.1 copy-start.42
  110.0 12.8 copy-start.23
  110.0 314.4 %all-gather.22.cloned.1.call-start = ((), (), s32[]{:S(2)}) async-start(), calls=%async_computation.13 | async-start | bytes 2621440 | tf_op jit(solution)/shard_map/all_gather | solution.py:76
  110.6 40.2 %copy-start.27 = (bf16[512,1024]{1,0:T(8,128)(2,1)S(1)}, bf16[512,1024]{1,0:T(8,128)(2,1)}, u32[]{:S(2)}) copy-start(bf16[512,1024]{1,0:T(8,128)(2,1)} %copy-done.26) | copy-start | bytes 3145732
  110.6 351.5 %all-gather.24.cloned.1.call-start = ((), (), s32[]{:S(2)}) async-start(), calls=%async_computation.14 | async-start | bytes 10485760 | tf_op jit(solution)/shard_map/all_gather | solution.py:77
  111.4 500.2 %all-gather.26.cloned.1.call-start = ((), (), s32[]{:S(2)}) async-start(), calls=%async_computation.15 | async-start | bytes 10485760 | tf_op jit(solution)/shard_map/all_gather | solution.py:78
  112.1 648.9 %all-gather.28.cloned.1.call-start = ((), (), s32[]{:S(2)}) async-start(), calls=%async_computation.16 | async-start | bytes 10485760 | tf_op jit(solution)/shard_map/all_gather | solution.py:79
  112.9 1045.4 %reduce-scatter.9.cloned.1.call-start = ((), (), s32[]{:S(2)}) async-start(), calls=%async_computation.17 | async-start | bytes 18874368 | tf_op jit(solution)/shard_map/reduce_scatter | solution.py:261
  412.9 11.6 copy-start.1
  424.5 4.6 copy-start.34
  427.8 1.3 copy-start.5
  429.3 182.3 %copy-start.24 = (bf16[512,1024]{1,0:T(8,128)(2,1)}, bf16[512,1024]{1,0:T(8,128)(2,1)S(1)}, u32[]{:S(2)}) copy-start(bf16[512,1024]{1,0:T(8,128)(2,1)S(1)} %multiply_convert_fusion.5) | copy-start | bytes 3145732
  472.2 288.9 %copy-start.11 = (bf16[512,1024]{1,0:T(8,128)(2,1)S(1)}, bf16[512,1024]{1,0:T(8,128)(2,1)}, u32[]{:S(2)}) copy-start(bf16[512,1024]{1,0:T(8,128)(2,1)} %reshape.316) | copy-start | bytes 3145732
  777.3 8.4 copy-start.6
  777.3 8.4 copy-start.38
  793.2 1.9 copy-start.39
  793.8 1.3 copy-start.8
  985.4 1.2 copy-start.4
  985.4 1.2 copy-start.21
  985.4 1.2 copy-start.32
  985.4 179.9 %reduce-scatter.11.cloned.1.call-start = ((), (), s32[]{:S(2)}) async-start(), calls=%async_computation.18 | async-start | bytes 2621440 | tf_op jit(solution)/shard_map/reduce_scatter | solution.py:289
  1116.2 4.4 copy-start.9
  1120.6 88.9 %reduce-scatter.17.cloned.1.call-start = ((), (), s32[]{:S(2)}) async-start(), calls=%async_computation.21 | async-start | bytes 2621440 | tf_op jit(solution)/shard_map/reduce_scatter | solution.py:298
  1124.5 231.1 %reduce-scatter.19.cloned.1.call-start = ((), (), s32[]{:S(2)}) async-start(), calls=%async_computation.22 | async-start | bytes 10485760 | tf_op jit(solution)/shard_map/reduce_scatter | solution.py:301
  1135.4 1.2 copy-start.25
  1135.4 367.7 %reduce-scatter.21.cloned.1.call-start = ((), (), s32[]{:S(2)}) async-start(), calls=%async_computation.23 | async-start | bytes 10485760 | tf_op jit(solution)/shard_map/reduce_scatter | solution.py:304
  1145.5 1.2 copy-start.12
  1145.5 505.0 %reduce-scatter.23.cloned.1.call-start = ((), (), s32[]{:S(2)}) async-start(), calls=%async_computation.24 | async-start | bytes 10485760 | tf_op jit(solution)/shard_map/reduce_scatter | solution.py:307
  1155.8 542.1 %reduce-scatter.13.cloned.1.call-start = ((), (), s32[]{:S(2)}) async-start(), calls=%async_computation.19 | async-start | bytes 2621440 | tf_op jit(solution)/shard_map/reduce_scatter | solution.py:292
  1158.2 4.3 copy-start.28
  1158.3 4.4 copy-start.16
  1162.5 581.4 %reduce-scatter.15.cloned.1.call-start = ((), (), s32[]{:S(2)}) async-start(), calls=%async_computation.20 | async-start | bytes 2621440 | tf_op jit(solution)/shard_map/reduce_scatter | solution.py:295
  1165.2 711.7 %all-reduce.7.cloned.1.call-start = ((), (), s32[]{:S(2)}) async-start(), calls=%async_computation.25 | async-start | bytes 16777216 | tf_op jit(solution)/shard_map/psum | solution.py:319
  1743.9 0.7 copy-start.43
  1743.9 1.9 copy-start.7
  1745.8 12.4 copy-start.22
  1758.3 4.4 copy-start.17
  1765.9 3.1 copy-start.2
  1765.9 3.1 copy-start.18
  1765.9 3.6 copy-start.19
  1765.9 3.6 copy-start.33
  1765.9 3.6 copy-start.36
  1769.5 1.7 copy-start.10
  1771.3 1.7 copy-start.37
  1877.0 6.5 copy-start.29
  1877.0 7.6 copy-start.15
  1883.5 3.6 copy-start.14
  1887.1 2.5 copy-start.13
Sparse Core Ops, SparseCore 0:
  9.6 48.6 all-gather.15
  59.8 44.6 all-gather.11
  106.1 44.6 all-gather.19
  153.1 53.3 all-gather.17
  208.8 55.9 all-gather.13
  266.2 45.9 all-gather.21
  313.8 148.3 all-gather.23
  463.7 147.8 all-gather.25
  613.2 147.8 all-gather.27
  985.5 114.1 reduce-scatter.8
  1120.7 43.2 reduce-scatter.10
  1166.3 43.1 reduce-scatter.16
  1211.8 143.7 reduce-scatter.18
  1357.9 145.1 reduce-scatter.20
  1505.3 145.1 reduce-scatter.22
  1653.3 44.5 reduce-scatter.12
  1700.7 43.1 reduce-scatter.14
  1748.6 128.3 all-reduce.6
where the time goes:
time: 1910 us; the launch traced here: 1900 us
  waiting for transfers between devices  1120 us (59%)
  matrix products  509 us (27%)
  local copies, waits for them, and re-layouts  110 us (6%)
  other arithmetic  83.8 us (4%)
  blocking collectives  44.1 us (2%)
    dot_general x16, matrix products, masked_scores(): jnp.einsum('qbhd,kbhd->bhqk', queries, key_blk, preferred_element_type=jn...  170 us
    reduce_scatter x1, waiting for transfers between devices, per_device(): lax.psum_scatter(g_up.astype(jnp.bfloat16), 'fsdp', scatter_dimension=0,...  147 us
    reduce_scatter x1, waiting for transfers between devices, per_device(): lax.psum_scatter(g_down.astype(jnp.bfloat16), 'fsdp', scatter_dimension=0...  147 us
    reduce_scatter x1, waiting for transfers between devices, per_device(): lax.psum_scatter(g_gate.astype(jnp.bfloat16), 'fsdp', scatter_dimension=0...  146 us
    all_gather x1, waiting for transfers between devices, per_device(): lax.all_gather(w_up, 'fsdp', axis=0, tiled=True)  139 us
    all_gather x1, waiting for transfers between devices, per_device(): lax.all_gather(w_down, 'fsdp', axis=0, tiled=True)  139 us
    psum x1, waiting for transfers between devices, per_device(): lax.psum(s_query.astype(jnp.bfloat16), 'ctx').astype(jnp.float32)  80.3 us
    dot_general x4, matrix products, query_step(): jnp.einsum('bhqk,kbhd->qbhd', grad_scores, key_blk, preferred_element_typ...  67.1 us
  transfers between devices with their start and end apart: 18, of which 14 were waited for; matrix products, arithmetic and copies ran while one was open for 24% of the time, Pallas kernels for 0%

commit v1 on v0

v1 whole, which is shorter than its diff:
```python
import functools

import jax
import jax.numpy as jnp
from jax import lax
from jax.experimental import pallas as pl
from jax.experimental.pallas import tpu as pltpu
from jax.sharding import Mesh, PartitionSpec as P

HEAD_DIM = 64
EPSILON = 1e-05
MASKED = -1e30
TILE = 256
PLANE = ("chip", "core")

bf16 = jnp.bfloat16
f32 = jnp.float32


def dot_nn(left_op, right_op):
    return lax.dot_general(left_op, right_op, (((1,), (0,)), ((), ())), preferred_element_type=f32)


def dot_nt(left_op, right_op):
    return lax.dot_general(left_op, right_op, (((1,), (1,)), ((), ())), preferred_element_type=f32)


def dot_tn(left_op, right_op):
    return lax.dot_general(left_op, right_op, (((0,), (0,)), ((), ())), preferred_element_type=f32)


def row_scale(values):
    return lax.rsqrt(jnp.mean(values * values, axis=-1, keepdims=True) + EPSILON)


def swap_core(value):
    return lax.ppermute(value, "core", [(0, 1), (1, 0)])


def swap_chip(value, mask):
    count = lax.axis_size("chip")
    return lax.ppermute(value, "chip", [(i, i ^ mask) for i in range(count)])


def plane_gather(value):
    count = lax.axis_size("chip")
    if count != 4:
        return jnp.stack([value] + [swap_chip(value, r) for r in range(1, count)])
    half = value.shape[0] // 2
    top, low = value[:half], value[half:]
    top_x = swap_chip(top, 1)
    low_y = swap_chip(low, 2)
    top_y = swap_chip(jnp.stack([top, top_x]), 2)
    low_x = swap_chip(jnp.stack([low, low_y]), 1)
    tops = jnp.stack([top, top_x, top_y[0], top_y[1]])
    lows = jnp.stack([low, low_x[0], low_y, low_x[1]])
    return jnp.concatenate([tops, lows], axis=1)


def gather_all(value):
    near = plane_gather(value)
    return near, swap_core(near)


def plane_reduce(own, other):
    count = lax.axis_size("chip")
    total = (own.astype(f32) + swap_core(other).astype(f32)).astype(bf16)
    if count != 4:
        result = total[0].astype(f32)
        for r in range(1, count):
            result = result + swap_chip(total[r], r).astype(f32)
        return result
    half = own.shape[1] // 2
    top, low = total[:, :half], total[:, half:]
    got_x = swap_chip(jnp.stack([top[1], top[3]]), 1)
    got_y = swap_chip(jnp.stack([low[2], low[3]]), 2)
    top_two = (top[2].astype(f32) + got_x[1].astype(f32)).astype(bf16)
    low_one = (low[1].astype(f32) + got_y[1].astype(f32)).astype(bf16)
    last_y = swap_chip(top_two, 2)
    last_x = swap_chip(low_one, 1)
    return jnp.concatenate(
        [
            top[0].astype(f32) + got_x[0].astype(f32) + last_y.astype(f32),
            low[0].astype(f32) + got_y[0].astype(f32) + last_x.astype(f32),
        ]
    )


def head_masks(rows, width):
    lanes = lax.broadcasted_iota(jnp.int32, (rows, width), 1) // HEAD_DIM
    return [lanes == h for h in range(width // HEAD_DIM)]


def stack_heads(values, masks):
    zero = jnp.zeros_like(values)
    return jnp.concatenate([jnp.where(mask, values, zero) for mask in masks], axis=0)


def merge_heads(stacked, masks, rows):
    merged = stacked[:rows]
    for h in range(1, len(masks)):
        merged = jnp.where(masks[h], stacked[h * rows : (h + 1) * rows], merged)
    return merged


def forward_kernel(
    rel, send, first, full, x_near, x_far, weight, gain, start,
    query, key, value, normed, attended, fine, logsum,
    scores, top, total,
):
    width = query.shape[1]
    seq_len = query.shape[0]
    heads = width // HEAD_DIM
    blk = TILE // 2
    tiles = x_near.shape[0] // TILE
    gain_row = gain[...].astype(f32)
    for s, source in ((0, x_near), (1, x_far)):

        def project(t, _, s=s, source=source):
            rows = pl.ds(pl.multiple_of(t * TILE, TILE), TILE)
            rows_in = source[rows, :].astype(f32)
            tile = (rows_in * row_scale(rows_in) * gain_row).astype(bf16)
            normed[s, rows, :] = tile
            mixed = dot_nn(tile, weight[...])
            for h in range(2):
                place = rel[(s * tiles + t) * 2 + h]
                where = pl.ds(pl.multiple_of(place * blk, blk), blk)
                part = mixed[h * blk : (h + 1) * blk]
                query[where, :] = (part[:, :width].astype(bf16) * 0.125).astype(bf16)
                key[where, :] = part[:, width : 2 * width].astype(bf16)
                value[where, :] = part[:, 2 * width :].astype(bf16)
            return 0

        lax.fori_loop(0, tiles, project, 0)

    masks = head_masks(TILE, width)
    big = heads * TILE

    def query_tile(qb, _):
        rows = pl.ds(pl.multiple_of(qb * TILE, TILE), TILE)
        stacked = stack_heads(query[rows, :], masks)
        top[...] = jnp.full_like(top, MASKED)
        begin = jnp.concatenate([start[rows, :]] * heads, axis=0)

        def score(kb, masked):
            keys = key[pl.ds(pl.multiple_of(kb * TILE, TILE), TILE), :]
            raw = dot_nt(stacked, keys)
            if masked:
                k_pos = kb * TILE + lax.broadcasted_iota(jnp.int32, (big, TILE), 1)
                q_row = lax.broadcasted_iota(jnp.int32, (big, TILE), 0) & (TILE - 1)
                allowed = (k_pos >= begin) & (k_pos <= qb * TILE + q_row)
                raw = jnp.where(allowed, raw, MASKED)
            scores[kb] = raw
            best = raw[:, :128]
            for c in range(1, TILE // 128):
                best = jnp.maximum(best, raw[:, c * 128 : (c + 1) * 128])
            top[...] = jnp.maximum(top[...], best)

        def masked_step(kb, _):
            score(kb, True)
            return 0

        def plain_step(kb, _):
            score(kb, False)
            return 0

        lax.fori_loop(first[qb], full[qb], masked_step, 0)
        lax.fori_loop(full[qb], qb, plain_step, 0)
        score(qb, True)
        peak = jnp.max(top[...], axis=1, keepdims=True)
        top[...] = jnp.broadcast_to(peak, top.shape)
        total[...] = jnp.zeros_like(total)

        def weigh(kb, carry):
            vals = value[pl.ds(pl.multiple_of(kb * TILE, TILE), TILE), :]
            pieces = []
            summed = total[...]
            for c in range(TILE // 128):
                piece = jnp.exp(scores[kb, :, c * 128 : (c + 1) * 128] - top[...])
                summed = summed + piece
                pieces.append(piece.astype(bf16))
            total[...] = summed
            return carry + dot_nn(jnp.concatenate(pieces, axis=1), vals)

        gathered = lax.fori_loop(first[qb], qb + 1, weigh, jnp.zeros((big, width), f32))
        denom = jnp.sum(total[...], axis=1, keepdims=True)
        fine[rows, :] = merge_heads(gathered / denom, masks, TILE)
        logs = jnp.broadcast_to(peak + jnp.log(denom), (big, width))
        logsum[rows, :] = merge_heads(logs, masks, TILE)
        return 0

    lax.fori_loop(0, seq_len // TILE, query_tile, 0)

    def emit(j, _):
        where = pl.ds(pl.multiple_of(send[j] * blk, blk), blk)
        attended[pl.ds(pl.multiple_of(j * blk, blk), blk), :] = fine[where, :].astype(bf16)
        return 0

    lax.fori_loop(0, seq_len // blk, emit, 0)


def backward_kernel(
    rel, send, first, full, query, key, value, fine, logsum, grad_in, weight, start,
    partial, grads,
    grad_at, grad_q, grad_k, grad_v, grad_q2,
):
    seq_len, width = query.shape
    heads = width // HEAD_DIM
    blk = TILE // 2
    big = heads * TILE

    def place(j, _):
        where = pl.ds(pl.multiple_of(send[j] * blk, blk), blk)
        grad_at[where, :] = grad_in[pl.ds(pl.multiple_of(j * blk, blk), blk), :]
        return 0

    lax.fori_loop(0, seq_len // blk, place, 0)
    grad_k[...] = jnp.zeros_like(grad_k)
    grad_v[...] = jnp.zeros_like(grad_v)
    masks = head_masks(TILE, width)

    def flip(values):
        if width < 128:
            values = jnp.concatenate([values, jnp.zeros((TILE, 128 - width), f32)], axis=1)
        return values.T

    def query_tile(qb, _):
        rows = pl.ds(pl.multiple_of(qb * TILE, TILE), TILE)
        stacked = stack_heads(query[rows, :], masks)
        grad_rows = grad_at[rows, :]
        grad_stacked = stack_heads(grad_rows, masks)
        products = flip(grad_rows.astype(f32) * fine[rows, :])
        logs = flip(logsum[rows, :])
        delta = jnp.concatenate(
            [
                jnp.sum(products[h * HEAD_DIM : (h + 1) * HEAD_DIM], axis=0, keepdims=True)
                for h in range(heads)
            ],
            axis=1,
        )
        log_row = jnp.concatenate(
            [logs[h * HEAD_DIM : h * HEAD_DIM + 1] for h in range(heads)], axis=1
        )
        begin = jnp.concatenate([start[qb]] * heads, axis=1)
        grad_q2[...] = jnp.zeros_like(grad_q2)

        def step(kb, masked):
            where = pl.ds(pl.multiple_of(kb * TILE, TILE), TILE)
            keys = key[where, :]
            probs = jnp.exp(dot_nt(keys, stacked) - log_row)
            if masked:
                k_pos = kb * TILE + lax.broadcasted_iota(jnp.int32, (TILE, big), 0)
                q_row = lax.broadcasted_iota(jnp.int32, (TILE, big), 1) & (TILE - 1)
                allowed = (k_pos >= begin) & (k_pos <= qb * TILE + q_row)
                probs = jnp.where(allowed, probs, 0.0)
            slope = (probs * (dot_nt(value[where, :], grad_stacked) - delta)).astype(bf16)
            grad_v[where, :] += dot_nn(probs.astype(bf16), grad_stacked)
            grad_k[where, :] += dot_nn(slope, stacked)
            grad_q2[...] += dot_tn(slope, keys)

        def masked_step(kb, _):
            step(kb, True)
            return 0

        def plain_step(kb, _):
            step(kb, False)
            return 0

        lax.fori_loop(first[qb], full[qb], masked_step, 0)
        lax.fori_loop(full[qb], qb, plain_step, 0)
        step(qb, True)
        grad_q[rows, :] = (merge_heads(grad_q2[...], masks, TILE) * 0.125).astype(bf16)
        return 0

    lax.fori_loop(0, seq_len // TILE, query_tile, 0)

    tiles = seq_len // TILE

    def project(t, _):
        rows = pl.ds(pl.multiple_of(t * TILE, TILE), TILE)
        for h in range(2):
            where = pl.ds(pl.multiple_of(rel[t * 2 + h] * blk, blk), blk)
            here = pl.ds(pl.multiple_of(t * TILE + h * blk, blk), blk)
            grads[here, :width] = grad_q[where, :]
            grads[here, width : 2 * width] = grad_k[where, :].astype(bf16)
            grads[here, 2 * width :] = grad_v[where, :].astype(bf16)
        partial[rows, :] = dot_nt(grads[rows, :], weight[...]).astype(bf16)
        return 0

    lax.fori_loop(0, tiles, project, 0)


def smem():
    return pl.BlockSpec(memory_space=pltpu.SMEM)


def vmem():
    return pl.BlockSpec(memory_space=pltpu.VMEM)


LIMIT = pltpu.CompilerParams(vmem_limit_bytes=56 * 2**20)


def attend_forward(tables, x_near, x_far, weight, gain, start, width):
    half_rows, feats = x_near.shape
    seq_len = 2 * half_rows
    big = (width // HEAD_DIM) * TILE
    shape = jax.ShapeDtypeStruct
    narrow = shape((seq_len, width), bf16)
    wide = shape((seq_len, width), f32)
    pairs = seq_len * seq_len * width // 2
    return pl.pallas_call(
        forward_kernel,
        out_shape=(narrow, narrow, narrow, shape((2, half_rows, feats), bf16), narrow, wide, wide),
        in_specs=[smem()] * 4 + [vmem()] * 5,
        out_specs=[vmem()] * 7,
        scratch_shapes=[
            pltpu.VMEM((seq_len // TILE, big, TILE), f32),
            pltpu.VMEM((big, 128), f32),
            pltpu.VMEM((big, 128), f32),
        ],
        compiler_params=LIMIT,
        cost_estimate=pl.CostEstimate(
            flops=6 * seq_len * feats * width + 16 * pairs,
            bytes_accessed=6 * seq_len * feats,
            transcendentals=pairs // HEAD_DIM,
        ),
        name="attend_forward",
    )(*tables, x_near, x_far, weight, gain, start)


def attend_backward(tables, saved, grad_in, weight, start):
    query = saved[0]
    seq_len, width = query.shape
    feats = weight.shape[0]
    big = (width // HEAD_DIM) * TILE
    shape = jax.ShapeDtypeStruct
    pairs = seq_len * seq_len * width // 2
    return pl.pallas_call(
        backward_kernel,
        out_shape=(shape((seq_len, feats), bf16), shape((seq_len, 3 * width), bf16)),
        in_specs=[smem()] * 4 + [vmem()] * 8,
        out_specs=[vmem()] * 2,
        scratch_shapes=[
            pltpu.VMEM((seq_len, width), bf16),
            pltpu.VMEM((seq_len, width), bf16),
            pltpu.VMEM((seq_len, width), f32),
            pltpu.VMEM((seq_len, width), f32),
            pltpu.VMEM((big, width), f32),
        ],
        compiler_params=LIMIT,
        cost_estimate=pl.CostEstimate(
            flops=6 * seq_len * feats * width + 32 * pairs,
            bytes_accessed=4 * seq_len * feats,
            transcendentals=pairs // HEAD_DIM,
        ),
        name="attend_backward",
    )(*tables, *saved, grad_in, weight, start)


def per_device(
    inputs, w_query, w_key, w_value, w_out, w_gate, w_up, w_down,
    gain_attn, gain_ffn, segments, deal_order, cotangent,
):
    rows, seqs, feats = inputs.shape
    chips = lax.axis_size("chip")
    groups = 2 * chips
    shards = lax.axis_size("fsdp")
    chip = lax.axis_index("chip")
    core = lax.axis_index("core")
    rank = chip * 2 + core
    width = feats // groups
    hidden_width = w_gate.shape[1] // groups
    per_shard = hidden_width // shards
    seq_len = rows * groups
    blocks = deal_order.shape[0]
    blk = rows // 2
    tokens = chips * rows

    near_ids = jnp.arange(chips, dtype=jnp.int32) ^ chip
    pair = jnp.arange(2, dtype=jnp.int32)
    rel_dev = (near_ids[None, :] * 2) + (pair[:, None] ^ core)
    rel_slot = (rel_dev[:, :, None] * 2 + pair[None, None, :]).reshape(-1)
    send_dev = jnp.arange(chips, dtype=jnp.int32)[:, None] * 2 + (pair[None, :] ^ core)
    send_slot = (send_dev[:, :, None] * 2 + pair[None, None, :]).reshape(-1)
    ids = jnp.arange(blocks, dtype=jnp.int32)

    def look_up(slots):
        return jnp.sum(
            jnp.where(slots[:, None] == ids[None, :], deal_order[None, :], 0), axis=1
        ).astype(jnp.int32)

    rel_table = look_up(rel_slot)
    send_table = look_up(send_slot)
    earlier = (segments[None, :, :] < segments[:, None, :]).astype(jnp.int32)
    slot_start = jnp.sum(earlier, axis=1).astype(jnp.int32).reshape(blocks, blk, seqs)
    start = jnp.sum(
        jnp.where((deal_order[None, :] == ids[:, None])[:, :, None, None], slot_start[None], 0),
        axis=1,
    ).astype(jnp.int32)
    start = start.transpose(2, 0, 1).reshape(seqs, seq_len)
    tiles = seq_len // TILE
    tiled = start.reshape(seqs, tiles, TILE)
    first = tiled[:, :, 0] // TILE
    full = jnp.minimum(
        jnp.arange(tiles, dtype=jnp.int32)[None, :], (tiled[:, :, -1] + TILE - 1) // TILE
    )

    def take(weight, axis, index, size):
        return lax.dynamic_slice_in_dim(weight, index * size, size, axis)

    own_qkv = jnp.concatenate([take(w, 1, rank, width) for w in (w_query, w_key, w_value)], axis=1)

    def hidden_columns(weight):
        grid = weight.reshape(weight.shape[0], shards, groups, per_shard)
        return take(grid, 2, rank, 1).reshape(weight.shape[0], hidden_width)

    own_gate_up = jnp.concatenate([hidden_columns(w_gate), hidden_columns(w_up)], axis=1)
    own_down = take(w_down, 0, rank, per_shard)
    out_grid = w_out.reshape(-1, 2, width, feats)
    own_out = take(out_grid, 1, core, 1).reshape(-1, feats)

    def gather_rows(value):
        return lax.all_gather(value, "fsdp", axis=0, tiled=True)

    gains = gather_rows(jnp.stack([gain_attn, gain_ffn], axis=1))
    gain_one, gain_two = gains[:, 0][None, :], gains[:, 1][None, :]
    qkv = gather_rows(own_qkv)
    out_half = gather_rows(own_out)
    gate_up = gather_rows(own_gate_up)
    down = gather_rows(own_down)

    outputs, grad_inputs = [], []
    grad_qkv = grad_gate_up = grad_down = grad_out = 0.0
    gain_sums_one = gain_sums_two = 0.0
    kept = []
    for b in range(seqs):
        x_own = inputs[:, b]
        x_near, x_far = gather_all(x_own)
        tables = (rel_table, send_table, first[b], full[b])
        query, key, value, normed, sent, fine, logsum = attend_forward(
            tables,
            x_near.reshape(tokens, feats),
            x_far.reshape(tokens, feats),
            qkv,
            gain_one,
            start[b][:, None],
            width,
        )
        got = lax.all_to_all(sent.reshape(chips, 2 * rows, width), "chip", 0, 0)
        attended = got.transpose(1, 0, 2).reshape(2 * rows, chips * width)
        mixed = dot_nn(attended, out_half)
        middle = x_own.astype(f32) + mixed[:rows] + swap_core(mixed[rows:])
        scale_two = row_scale(middle)
        unit_two = middle * scale_two
        normed_mid = (unit_two * gain_two.astype(f32)).astype(bf16)
        kept.append((x_own, query, key, value, normed, fine, logsum, attended, middle,
                     scale_two, unit_two, normed_mid, tables))

    for b in range(seqs):
        (x_own, query, key, value, normed, fine, logsum, attended, middle,
         scale_two, unit_two, normed_mid, tables) = kept[b]
        cot_own = cotangent[:, b]
        cots = gather_all(cot_own)
        mids = gather_all(normed_mid)
        out_parts, mid_parts = [], []
        for cot, mid in zip(cots, mids):
            cot = cot.reshape(tokens, feats)
            mid = mid.reshape(tokens, feats)
            pre = dot_nn(mid, gate_up)
            gate_pre, up_pre = pre[:, :hidden_width], pre[:, hidden_width:]
            sigma = jax.nn.sigmoid(gate_pre)
            active = gate_pre * sigma
            hidden = (active * up_pre).astype(bf16)
            out_parts.append(dot_nn(hidden, down).astype(bf16).reshape(chips, rows, feats))
            grad_hidden = dot_nt(cot, down)
            grad_gate = grad_hidden * up_pre * sigma * (1.0 + gate_pre * (1.0 - sigma))
            grad_up = grad_hidden * active
            grad_pre = jnp.concatenate([grad_gate, grad_up], axis=1).astype(bf16)
            mid_parts.append(dot_nt(grad_pre, gate_up).astype(bf16).reshape(chips, rows, feats))
            grad_gate_up = grad_gate_up + dot_tn(mid, grad_pre)
            grad_down = grad_down + dot_tn(hidden, cot)
        grad_normed_mid = plane_reduce(*mid_parts)
        outputs.append((middle + plane_reduce(*out_parts)).astype(bf16))
        gain_sums_two = gain_sums_two + jnp.sum(grad_normed_mid * unit_two, axis=0)
        scaled_two = grad_normed_mid * gain_two.astype(f32)
        grad_middle = cot_own.astype(f32) + scale_two * (
            scaled_two - unit_two * jnp.mean(scaled_two * unit_two, axis=-1, keepdims=True)
        )
        branch_own = grad_middle.astype(bf16)
        branch = jnp.concatenate([branch_own, swap_core(branch_own)])
        grad_att = dot_nt(branch, out_half).astype(bf16)
        grad_out = grad_out + dot_tn(attended.astype(bf16), branch)
        grad_sent = lax.all_to_all(
            grad_att.reshape(2 * rows, chips, width).transpose(1, 0, 2), "chip", 0, 0
        )
        partial, grads = attend_backward(
            tables,
            (query, key, value, fine, logsum),
            grad_sent.reshape(seq_len, width),
            qkv,
            tiled[b][:, None, :],
        )
        grad_qkv = grad_qkv + dot_tn(normed.reshape(seq_len, feats), grads)
        parts = partial.reshape(2, chips, rows, feats)
        grad_normed_in = plane_reduce(parts[0], parts[1])
        flat_in = x_own.astype(f32)
        scale_one = row_scale(flat_in)
        unit_one = flat_in * scale_one
        gain_sums_one = gain_sums_one + jnp.sum(grad_normed_in * unit_one, axis=0)
        scaled_one = grad_normed_in * gain_one.astype(f32)
        grad_inputs.append(
            (
                grad_middle
                + scale_one
                * (scaled_one - unit_one * jnp.mean(scaled_one * unit_one, axis=-1, keepdims=True))
            ).astype(bf16)
        )

    def to_shard(value):
        return lax.psum_scatter(value.astype(bf16), "fsdp", scatter_dimension=0, tiled=True)

    def collect(value):
        return lax.all_gather(value, PLANE, axis=0)

    own_rows = feats // shards
    s_gate_up = collect(to_shard(grad_gate_up))
    s_gate_up = s_gate_up.reshape(groups, own_rows, 2, shards, per_shard)
    g_gate_up = s_gate_up.transpose(2, 1, 3, 0, 4).reshape(2, own_rows, -1).astype(f32)
    g_down = collect(to_shard(grad_down)).reshape(-1, feats).astype(f32)
    s_qkv = collect(to_shard(grad_qkv)).reshape(groups, own_rows, 3, width)
    g_qkv = s_qkv.transpose(2, 1, 0, 3).reshape(3, own_rows, feats).astype(f32)
    part_out = lax.psum(to_shard(grad_out), "chip")
    s_out = lax.all_gather(part_out.reshape(-1, width, feats), "core", axis=1)
    g_out = s_out.reshape(own_rows, feats).astype(f32)
    gain_sums = lax.psum(jnp.stack([gain_sums_one, gain_sums_two]), PLANE + ("fsdp",))
    g_gains = lax.dynamic_slice_in_dim(gain_sums, lax.axis_index("fsdp") * own_rows, own_rows, 1)

    return (
        jnp.stack(outputs, axis=1),
        jnp.stack(grad_inputs, axis=1),
        g_qkv[0],
        g_qkv[1],
        g_qkv[2],
        g_out,
        g_gate_up[0],
        g_gate_up[1],
        g_down,
        g_gains[0],
        g_gains[1],
    )


def solution(mesh):
    names = mesh.axis_names
    ctx, shards = mesh.shape[names[0]], mesh.shape[names[1]]
    fine_mesh = Mesh(mesh.devices.reshape(ctx // 2, 2, shards), ("chip", "core", "fsdp"))
    by_row = P("fsdp", None)
    by_token = P(PLANE, "fsdp", None)
    return jax.shard_map(
        per_device,
        mesh=fine_mesh,
        in_specs=(by_token,) + (by_row,) * 7 + (P("fsdp"), P("fsdp"), P(None, "fsdp"), P(), by_token),
        out_specs=(by_token, by_token) + (by_row,) * 7 + (P("fsdp"), P("fsdp")),
        check_vma=False,
    )
```

time: 1910 us -> 813 us (0.43)
  waiting for transfers between devices: 1120 us -> 247 us
  matrix products: 509 us -> 104 us
  Pallas kernels: 0 us -> 125 us
  starting transfers between devices: 0.72 us -> 70.2 us
  blocking collectives: 44.1 us -> 71.4 us
  other arithmetic: 83.8 us -> 61.5 us
    reduce_scatter x8 -> x4, waiting for transfers between devices: 579 us -> 46.1 us  [to_shard(): lax.psum_scatter(value.astype(bf16), 'fsdp', scatter_dimension=0, tiled=T...]
    all_gather x9 -> x6, waiting for transfers between devices: 461 us -> 0.03 us  [the longest x3 0.02 us: gather_rows(): return lax.all_gather(value, 'fsdp', axis=0, tiled=True)]
    dot_general x53 -> x32, matrix products: 509 us -> 104 us  [the longest x12 46.6 us: dot_tn(): lax.dot_general(left_op, right_op, (((0,), (0,)), ((), ())), preferred_el...]
    ppermute x0 -> x64, waiting for transfers between devices: none -> 162 us  [the longest x48 162 us: swap_chip(): return lax.ppermute(value, 'chip', [(i, i ^ mask) for i in range(count)])]
    pallas_call x0 -> x4, Pallas kernels: none -> 125 us  [the longest x2 63 us: attend_backward(): pl.pallas_call(backward_kernel, out_shape=(shape((seq_len, feats), bf16),...]
    ppermute x0 -> x64, starting transfers between devices: none -> 53.8 us  [the longest x48 51.9 us: swap_chip(): return lax.ppermute(value, 'chip', [(i, i ^ mask) for i in range(count)])]
    psum x1, waiting for transfers between devices: 80.3 us -> 27.7 us  [per_device(): part_out = lax.psum(to_shard(grad_out), 'chip')]
    slice x4 -> x29, local copies, waits for them, and re-layouts: 5.19 us -> 43.3 us  [the longest x2 12.8 us: per_device(): g_gate_up[1]]
  transfers between devices with their start and end apart: 18 -> 79, of which waited for: 14 -> 38; matrix products, arithmetic and copies ran while one was open for 24% -> 29% of each run, Pallas kernels for 0% -> 16%
where the time goes in v1:
time: 813 us; the launch traced here: 803 us
  waiting for transfers between devices  247 us (30%)
  Pallas kernels  125 us (15%)
  local copies, waits for them, and re-layouts  109 us (13%)
  matrix products  104 us (13%)
  blocking collectives  71.4 us (9%)
  starting transfers between devices  70.2 us (9%)
  other arithmetic  61.5 us (8%)
  between operations  15.7 us (2%)
    ppermute x48, waiting for transfers between devices, swap_chip(): return lax.ppermute(value, 'chip', [(i, i ^ mask) for i in range(count)])  162 us
    pallas_call x2, Pallas kernels, attend_backward(): pl.pallas_call(backward_kernel, out_shape=(shape((seq_len, feats), bf16),...  63 us
    pallas_call x2, Pallas kernels, attend_forward(): pl.pallas_call(forward_kernel, out_shape=(narrow, narrow, narrow, shape((...  61.5 us
    ppermute x48, starting transfers between devices, swap_chip(): return lax.ppermute(value, 'chip', [(i, i ^ mask) for i in range(count)])  51.9 us
    dot_general x12, matrix products, dot_tn(): lax.dot_general(left_op, right_op, (((0,), (0,)), ((), ())), preferred_el...  46.6 us
    reduce_scatter x4, waiting for transfers between devices, to_shard(): lax.psum_scatter(value.astype(bf16), 'fsdp', scatter_dimension=0, tiled=T...  46.1 us
    psum x1, blocking collectives, per_device(): lax.psum(jnp.stack([gain_sums_one, gain_sums_two]), PLANE + ('fsdp',))  39.8 us
    all_gather x2, blocking collectives, gather_rows(): return lax.all_gather(value, 'fsdp', axis=0, tiled=True)  29.2 us
  transfers between devices with their start and end apart: 79, of which 38 were waited for; matrix products, arithmetic and copies ran while one was open for 29% of the time, Pallas kernels for 16%

profile of v1, /device:TPU:0, one launch (start us, length us, event | category | flops | bytes accessed | tf_op | source)
XLA Modules:
  0.0 803.2 jit_solution(2139190083935245795)
XLA Ops:
  7.2 4.0 fusion.91
  17.7 4.0 convert_reduce_fusion
  27.0 9.2 %collective-permute-done.3 = bf16[2,128,1024]{2,1,0:T(8,128)(2,1)} collective-permute-done((bf16[2,128,1024]{2,1,0:T(8,128)(2,1)}, bf16[2,128,1024]{2,1,0:T(8,128)(2,1)}, u32[]{:S(2)}, u32[]{:S(2)}) %collective-permute-start.3) | collective-permute-done | bytes 524320 | tf_op jit(solution)/shard_map/ppermute | solution.py:42
  42.9 11.2 %all_gather.37 = bf16[1024,2]{0,1:T(2,128)(2,1)S(1)} all-gather(bf16[256,2]{0,1:T(2,128)(2,1)S(1)} %pad_maximum_fusion.45), channel_id=1, replica_groups=mesh['chip'=4,'core'=2,'fsdp'=4] {'fsdp'}, dimensions={0}, use_global_device_ids=true | all-gather | bytes 5120 | tf_op jit(solution)/shard_map/all_gather | solution.py:424
  58.6 18.0 %all_gather.36.weight = bf16[1024,384]{1,0:T(8,128)(2,1)} all-gather(bf16[256,384]{1,0:T(8,128)(2,1)S(1)} %pad_maximum_fusion.43), channel_id=1, replica_groups=mesh['chip'=4,'core'=2,'fsdp'=4] {'fsdp'}, dimensions={0}, use_global_device_ids=true | all-gather | bytes 983040 | tf_op jit(solution)/shard_map/all_gather | solution.py:424
  76.7 30.7 %attend_forward.2 = (bf16[2048,128]{1,0:T(8,128)(2,1)}, bf16[2048,128]{1,0:T(8,128)(2,1)}, bf16[2048,128]{1,0:T(8,128)(2,1)}, bf16[2,1024,1024]{2,1,0:T(8,128)(2...) custom-call(s32[16]{0:T(128)} %get-tuple-element.113.rel, s32[16]{0:T(128)} %get-tuple-element.112.send, ...), custom_call_target="tpu_custom_call" | custom-call | flops 5905580032 | bytes 12582912 | tf_op jit(solution)/shard_map/attend_forward/pallas_call | solution.py:312
  109.4 3.5 all-to-all-start
  117.7 4.1 copy.141
  121.8 4.1 copy.142
  136.4 8.5 %collective-permute-done.19 = bf16[2,128,1024]{2,1,0:T(8,128)(2,1)S(1)} collective-permute-done((bf16[2,128,1024]{2,1,0:T(8,128)(2,1)S(1)}, bf16[2,128,1024]{2,1,0:T(8,128)(2,1)S(1)}, u32[]{:S(2)}, u32[]{:S(2)}) %collective-permute-start.19) | collective-permute-done | bytes 524320 | tf_op jit(solution)/shard_map/ppermute | solution.py:42
  146.2 4.6 collective-permute-done.17
  162.8 5.5 collective-permute-done.34
  168.9 9.9 %collective-permute-done.32 = bf16[128,1024]{1,0:T(8,128)(2,1)S(1)} collective-permute-done((bf16[128,1024]{1,0:T(8,128)(2,1)S(1)}, bf16[128,1024]{1,0:T(8,128)(2,1)S(1)}, u32[]{:S(2)}, u32[]{:S(2)}) %collective-permute-start.32) | collective-permute-done | bytes 262176 | tf_op jit(solution)/shard_map/ppermute | solution.py:42
  182.0 10.4 %collective-permute-done.35 = bf16[2,128,1024]{2,1,0:T(8,128)(2,1)S(1)} collective-permute-done((bf16[2,128,1024]{2,1,0:T(8,128)(2,1)S(1)}, bf16[2,128,1024]{2,1,0:T(8,128)(2,1)S(1)}, u32[]{:S(2)}, u32[]{:S(2)}) %collective-permute-start.35) | collective-permute-done | bytes 524320 | tf_op jit(solution)/shard_map/ppermute | solution.py:42
  198.0 30.8 %attend_forward.3 = (bf16[2048,128]{1,0:T(8,128)(2,1)}, bf16[2048,128]{1,0:T(8,128)(2,1)}, bf16[2048,128]{1,0:T(8,128)(2,1)}, bf16[2,1024,1024]{2,1,0:T(8,128)(2...) custom-call(s32[16]{0:T(128)} %get-tuple-element.113.rel, s32[16]{0:T(128)} %get-tuple-element.112.send, ...), custom_call_target="tpu_custom_call" | custom-call | flops 5905580032 | bytes 12582912 | tf_op jit(solution)/shard_map/attend_forward/pallas_call | solution.py:312
  231.0 3.5 all-to-all-start.1
  238.8 4.6 all-to-all-done.1
  247.5 6.6 fusion.101
  254.1 5.3 multiply_convert_fusion.5
  262.5 4.1 fusion.100
  268.0 3.6 multiply_convert_fusion.7
  283.5 7.9 collective-permute-done.38
  295.3 7.4 collective-permute-done.12
  310.5 4.2 collective-permute-done.13
  325.1 13.8 %collective-permute-done.22 = bf16[128,1024]{1,0:T(8,128)(2,1)S(1)} collective-permute-done((bf16[128,1024]{1,0:T(8,128)(2,1)S(1)}, bf16[128,1024]{1,0:T(8,128)(2,1)S(1)}, u32[]{:S(2)}, u32[]{:S(2)}) %collective-permute-start.22) | collective-permute-done | bytes 262176 | tf_op jit(solution)/shard_map/ppermute | solution.py:42
  340.4 4.0 collective-permute-done.48
  346.1 7.7 collective-permute-done.25
  355.3 5.0 collective-permute-done.49
  362.6 6.0 fusion.18
  369.1 4.2 fusion.105
  373.3 4.3 fusion.106
  379.5 3.5 all-to-all-start.2
  383.4 4.7 fusion.102
  388.2 4.1 fusion.103
  392.3 3.6 multiply_convert_fusion.1
  400.4 3.6 multiply_convert_fusion.3
  418.8 7.9 collective-permute-done.54
  431.9 4.0 add_convert_fusion.1
  454.1 31.5 %attend_backward.2 = (bf16[2048,1024]{1,0:T(8,128)(2,1)}, bf16[2048,384]{1,0:T(8,128)(2,1)}) custom-call(s32[16]{0:T(128)} %get-tuple-element.113.rel, s32[16]{0:T(128)} %get-tuple-element.112.send, s32[8]{0:T(128)} %get-tuple-element.246.first, s32[8]{0:T(128)} %get-tuple-element.244.full, bf16[2048,128]{1,0:T(8,128)(2,1)} %get-tuple-element.31.query, ...), custom_call_target="tpu_custom_call" | custom-call | flops 10200547328 | bytes 8388608 | tf_op jit(solution)/shard_map/attend_backward/pallas_call | solution.py:339
  488.6 4.1 all-to-all-start.3
  496.9 4.9 all-to-all-done.3
  501.8 31.5 %attend_backward.3 = (bf16[2048,1024]{1,0:T(8,128)(2,1)}, bf16[2048,384]{1,0:T(8,128)(2,1)}) custom-call(s32[16]{0:T(128)} %get-tuple-element.113.rel, s32[16]{0:T(128)} %get-tuple-element.112.send, s32[8]{0:T(128)} %get-tuple-element.247.first, s32[8]{0:T(128)} %get-tuple-element.245.full, bf16[2048,128]{1,0:T(8,128)(2,1)} %get-tuple-element.37.query, ...), custom_call_target="tpu_custom_call" | custom-call | flops 10200547328 | bytes 8388608 | tf_op jit(solution)/shard_map/attend_backward/pallas_call | solution.py:339
  533.4 3.9 fusion.104
  537.3 3.3 add_convert_fusion.3
  541.1 4.7 fusion.17
  545.9 4.1 fusion.16
  550.0 5.4 add_convert_fusion
  556.9 4.9 reduce-scatter.5.cloned.1.call-done
  562.1 4.6 fusion.79
  566.8 41.2 %reduce-scatter.9.cloned.1.call-done = bf16[256,1024]{1,0:T(8,128)(2,1)} async-done(((bf16[1024,1024]{1,0:T(8,128)(2,1)}), bf16[256,1024]{1,0:T(8,128)(2,1)}) %reduce-scatter.9.cloned.1.call-update) | async-done | bytes 524304 | tf_op jit(solution)/shard_map/reduce_scatter | solution.py:521
  608.0 4.8 fusion.80
  619.8 14.2 %collective-permute-done.44 = bf16[2,128,1024]{2,1,0:T(8,128)(2,1)S(1)} collective-permute-done((bf16[2,128,1024]{2,1,0:T(8,128)(2,1)S(1)}, bf16[2,128,1024]{2,1,0:T(8,128)(2,1)S(1)}, u32[]{:S(2)}, u32[]{:S(2)}) %collective-permute-start.44) | collective-permute-done | bytes 524320 | tf_op jit(solution)/shard_map/ppermute | solution.py:42
  638.3 6.5 collective-permute-done.45
  656.0 4.1 convert_element_type.716
  660.1 27.7 %all-reduce.2.cloned.1.call-done = bf16[1,1,128,1024]{3,2,1,0:T(8,128)(2,1)} async-done(((bf16[1,1,128,1024]{3,2,1,0:T(8,128)(2,1)}), bf16[1,1,128,1024]{3,2,1,0:T(8,128)(2,1)}) %all-reduce.2.cloned.1.call-update) | async-done | bytes 262160 | tf_op jit(solution)/shard_map/psum | solution.py:533
  694.7 5.9 collective-permute-done.61
  708.1 39.8 %psum.15 = f32[2,1024]{1,0:T(2,128)S(1)} all-reduce(f32[2,1024]{1,0:T(2,128)S(1)} %pad_maximum_fusion.44), channel_id=1, replica_groups=mesh['chip'=4,'core'=2,'fsdp'=4] {'chip','core','fsdp'}, use_global_device_ids=true, to_apply=%region_21.22 | all-reduce | flops 2048 | bytes 16384 | tf_op jit(solution)/shard_map/psum | solution.py:536
  751.7 3.4 copy.181
  760.3 8.8 %reshape.553 = f32[8,256,2,4,128]{4,3,2,1,0:T(4,128)} reshape(bf16[2048,1024]{1,0:T(8,128)(2,1)} %all-gather.19.cloned.1.call-done) | data formatting | bytes 12582912 | tf_op jit(solution)/shard_map/convert_element_type | solution.py:529
  769.1 6.2 fusion.78
  775.3 4.4 copy.161
  779.7 4.9 squeeze.38
  784.7 6.6 copy.162
  791.3 5.1 squeeze.39
  (456 shorter events, 218.8 us)
Async XLA Ops:
  7.2 120.9 %all-gather.15.cloned.1.call-start = ((), (), s32[]{:S(2)}) async-start(), calls=%async_computation.15 | async-start | bytes 1310720 | tf_op jit(solution)/shard_map/all_gather | solution.py:424
  22.8 13.4 %collective-permute-start.3 = (bf16[2,128,1024]{2,1,0:T(8,128)(2,1)}, bf16[2,128,1024]{2,1,0:T(8,128)(2,1)}, u32[]{:S(2)}, u32[]{:S(2)}) collective-permute-start(bf16[2,128,1024]{2,1,0:T(8,128)(2,1)} %pad_maximum_fusion.25), channel_id=1, source_target_pairs={{0,8},{8,0},{16,24},{24,16},{1,9},{9,1},{17,25},{25,17},{2,10},{10... | collective-permute-start | bytes 1572872 | tf_op jit(solution)/shard_map/ppermute | solution.py:42
  25.4 13.1 %collective-permute-start.1 = (bf16[2,128,1024]{2,1,0:T(8,128)(2,1)}, bf16[2,128,1024]{2,1,0:T(8,128)(2,1)}, u32[]{:S(2)}, u32[]{:S(2)}) collective-permute-start(bf16[2,128,1024]{2,1,0:T(8,128)(2,1)} %pad_maximum_fusion.24), channel_id=1, source_target_pairs={{0,16},{8,24},{16,0},{24,8},{1,17},{9,25},{17,1},{25,9},{2,18},{10... | collective-permute-start | bytes 1572872 | tf_op jit(solution)/shard_map/ppermute | solution.py:42
  40.9 35.8 %collective-permute-start.4 = (bf16[4,256,1024]{2,1,0:T(8,128)(2,1)}, bf16[4,256,1024]{2,1,0:T(8,128)(2,1)}, u32[]{:S(2)}, u32[]{:S(2)}) collective-permute-start(bf16[4,256,1024]{2,1,0:T(8,128)(2,1)} %maximum_maximum_fusion), channel_id=1, source_target_pairs={{0,4},{4,0},{1,5},{5,1},{2,6},{6,2},{3,7},{7,3},{8,12},{12,8},{9,1... | collective-permute-start | bytes 6291464 | tf_op jit(solution)/shard_map/ppermute | solution.py:37
  109.4 18.6 %all-to-all-start = ((bf16[4,512,128]{1,2,0:T(8,128)(2,1)}), bf16[4,512,128]{1,2,0:T(8,128)(2,1)S(1)}, u32[]{:S(2)}, u32[]{:S(2)}) async-start(bf16[4,512,128]{1,2,0:T(8,128)(2,1)} %copy.140), calls=%async_computation | async-start | bytes 1048576 | tf_op jit(solution)/shard_map/all_to_all | solution.py:450
  112.9 134.6 %all-gather.11.cloned.1.call-start = ((), (), s32[]{:S(2)}) async-start(), calls=%async_computation.8 | async-start | bytes 2621440 | tf_op jit(solution)/shard_map/all_gather | solution.py:424
  113.1 17.4 %collective-permute-start.18 = (bf16[128,1024]{1,0:T(8,128)(2,1)S(1)}, bf16[128,1024]{1,0:T(8,128)(2,1)S(1)}, u32[]{:S(2)}, u32[]{:S(2)}) collective-permute-start(bf16[128,1024]{1,0:T(8,128)(2,1)S(1)} %bitcast.310), channel_id=1, source_target_pairs={{0,16},{8,24},{16,0},{24,8},{1,17},{9,25},{17,1},{25,9},{2,18},{10... | collective-permute-start | bytes 786440 | tf_op jit(solution)/shard_map/ppermute | solution.py:42
  116.2 18.5 %collective-permute-start.16 = (bf16[128,1024]{1,0:T(8,128)(2,1)S(1)}, bf16[128,1024]{1,0:T(8,128)(2,1)}, u32[]{:S(2)}, u32[]{:S(2)}) collective-permute-start(bf16[128,1024]{1,0:T(8,128)(2,1)S(1)} %bitcast.313), channel_id=1, source_target_pairs={{0,8},{8,0},{16,24},{24,16},{1,9},{9,1},{17,25},{25,17},{2,10},{10... | collective-permute-start | bytes 786440 | tf_op jit(solution)/shard_map/ppermute | solution.py:42
  127.8 126.3 %all-gather.13.cloned.1.call-start = ((), (), s32[]{:S(2)}) async-start(), calls=%async_computation.9 | async-start | bytes 1310720 | tf_op jit(solution)/shard_map/all_gather | solution.py:424
  130.4 14.6 %collective-permute-start.5 = (f32[256,1024]{1,0:T(8,128)S(1)}, f32[256,1024]{1,0:T(8,128)S(1)}, u32[]{:S(2)}, u32[]{:S(2)}) collective-permute-start(f32[256,1024]{1,0:T(8,128)S(1)} %slice.642), channel_id=1, source_target_pairs={{0,4},{4,0},{1,5},{5,1},{2,6},{6,2},{3,7},{7,3},{8,12},{12,8},{9,1... | collective-permute-start | bytes 3145736 | tf_op jit(solution)/shard_map/ppermute | solution.py:37
  130.5 14.4 %collective-permute-start.19 = (bf16[2,128,1024]{2,1,0:T(8,128)(2,1)S(1)}, bf16[2,128,1024]{2,1,0:T(8,128)(2,1)S(1)}, u32[]{:S(2)}, u32[]{:S(2)}) collective-permute-start(bf16[2,128,1024]{2,1,0:T(8,128)(2,1)S(1)} %pad_maximum_fusion.31), channel_id=1, source_target_pairs={{0,8},{8,0},{16,24},{24,16},{1,9},{9,1},{17,25},{25,17},{2,10},{10... | collective-permute-start | bytes 1572872 | tf_op jit(solution)/shard_map/ppermute | solution.py:42
  135.9 14.9 %collective-permute-start.17 = (bf16[2,128,1024]{2,1,0:T(8,128)(2,1)S(1)}, bf16[2,128,1024]{2,1,0:T(8,128)(2,1)S(1)}, u32[]{:S(2)}, u32[]{:S(2)}) collective-permute-start(bf16[2,128,1024]{2,1,0:T(8,128)(2,1)S(1)} %pad_maximum_fusion.30), channel_id=1, source_target_pairs={{0,16},{8,24},{16,0},{24,8},{1,17},{9,25},{17,1},{25,9},{2,18},{10... | collective-permute-start | bytes 1572872 | tf_op jit(solution)/shard_map/ppermute | solution.py:42
  153.2 44.8 %collective-permute-start.20 = (bf16[4,256,1024]{2,1,0:T(8,128)(2,1)}, bf16[4,256,1024]{2,1,0:T(8,128)(2,1)}, u32[]{:S(2)}, u32[]{:S(2)}) collective-permute-start(bf16[4,256,1024]{2,1,0:T(8,128)(2,1)} %maximum_maximum_fusion.2), channel_id=1, source_target_pairs={{0,4},{4,0},{1,5},{5,1},{2,6},{6,2},{3,7},{7,3},{8,12},{12,8},{9,1... | collective-permute-start | bytes 6291464 | tf_op jit(solution)/shard_map/ppermute | solution.py:37
  155.2 24.6 %collective-permute-start.9 = (bf16[2,128,1024]{2,1,0:T(8,128)(2,1)S(1)}, bf16[2,128,1024]{2,1,0:T(8,128)(2,1)S(1)}, u32[]{:S(2)}, u32[]{:S(2)}) collective-permute-start(bf16[2,128,1024]{2,1,0:T(8,128)(2,1)S(1)} %pad_maximum_fusion.27), channel_id=1, source_target_pairs={{0,8},{8,0},{16,24},{24,16},{1,9},{9,1},{17,25},{25,17},{2,10},{10... | collective-permute-start | bytes 1572872 | tf_op jit(solution)/shard_map/ppermute | solution.py:42
  159.7 19.1 %collective-permute-start.32 = (bf16[128,1024]{1,0:T(8,128)(2,1)S(1)}, bf16[128,1024]{1,0:T(8,128)(2,1)S(1)}, u32[]{:S(2)}, u32[]{:S(2)}) collective-permute-start(bf16[128,1024]{1,0:T(8,128)(2,1)S(1)} %bitcast.325), channel_id=1, source_target_pairs={{0,8},{8,0},{16,24},{24,16},{1,9},{9,1},{17,25},{25,17},{2,10},{10... | collective-permute-start | bytes 786440 | tf_op jit(solution)/shard_map/ppermute | solution.py:42
  162.4 18.1 %collective-permute-start.7 = (bf16[2,128,1024]{2,1,0:T(8,128)(2,1)S(1)}, bf16[2,128,1024]{2,1,0:T(8,128)(2,1)S(1)}, u32[]{:S(2)}, u32[]{:S(2)}) collective-permute-start(bf16[2,128,1024]{2,1,0:T(8,128)(2,1)S(1)} %pad_maximum_fusion.26), channel_id=1, source_target_pairs={{0,16},{8,24},{16,0},{24,8},{1,17},{9,25},{17,1},{25,9},{2,18},{10... | collective-permute-start | bytes 1572872 | tf_op jit(solution)/shard_map/ppermute | solution.py:42
  168.3 149.0 %collective-permute-start.50 = (bf16[128,1024]{1,0:T(8,128)(2,1)S(1)}, bf16[128,1024]{1,0:T(8,128)(2,1)}, u32[]{:S(2)}, u32[]{:S(2)}) collective-permute-start(bf16[128,1024]{1,0:T(8,128)(2,1)S(1)} %bitcast.307), channel_id=1, source_target_pairs={{0,16},{8,24},{16,0},{24,8},{1,17},{9,25},{17,1},{25,9},{2,18},{10... | collective-permute-start | bytes 786440 | tf_op jit(solution)/shard_map/ppermute | solution.py:42
  178.8 13.6 %collective-permute-start.35 = (bf16[2,128,1024]{2,1,0:T(8,128)(2,1)S(1)}, bf16[2,128,1024]{2,1,0:T(8,128)(2,1)S(1)}, u32[]{:S(2)}, u32[]{:S(2)}) collective-permute-start(bf16[2,128,1024]{2,1,0:T(8,128)(2,1)S(1)} %pad_maximum_fusion.36), channel_id=1, source_target_pairs={{0,8},{8,0},{16,24},{24,16},{1,9},{9,1},{17,25},{25,17},{2,10},{10... | collective-permute-start | bytes 1572872 | tf_op jit(solution)/shard_map/ppermute | solution.py:42
  179.8 14.7 %collective-permute-start.33 = (bf16[2,128,1024]{2,1,0:T(8,128)(2,1)S(1)}, bf16[2,128,1024]{2,1,0:T(8,128)(2,1)S(1)}, u32[]{:S(2)}, u32[]{:S(2)}) collective-permute-start(bf16[2,128,1024]{2,1,0:T(8,128)(2,1)S(1)} %pad_maximum_fusion.35), channel_id=1, source_target_pairs={{0,16},{8,24},{16,0},{24,8},{1,17},{9,25},{17,1},{25,9},{2,18},{10... | collective-permute-start | bytes 1572872 | tf_op jit(solution)/shard_map/ppermute | solution.py:42
  182.0 65.5 %collective-permute-start.10 = (bf16[4,256,1024]{2,1,0:T(8,128)(2,1)}, bf16[4,256,1024]{2,1,0:T(8,128)(2,1)}, u32[]{:S(2)}, u32[]{:S(2)}) collective-permute-start(bf16[4,256,1024]{2,1,0:T(8,128)(2,1)} %maximum_maximum_fusion.1), channel_id=1, source_target_pairs={{0,4},{4,0},{1,5},{5,1},{2,6},{6,2},{3,7},{7,3},{8,12},{12,8},{9,1... | collective-permute-start | bytes 6291464 | tf_op jit(solution)/shard_map/ppermute | solution.py:37
  196.0 58.2 %collective-permute-start.36 = (bf16[4,256,1024]{2,1,0:T(8,128)(2,1)}, bf16[4,256,1024]{2,1,0:T(8,128)(2,1)}, u32[]{:S(2)}, u32[]{:S(2)}) collective-permute-start(bf16[4,256,1024]{2,1,0:T(8,128)(2,1)} %maximum_maximum_fusion.4), channel_id=1, source_target_pairs={{0,4},{4,0},{1,5},{5,1},{2,6},{6,2},{3,7},{7,3},{8,12},{12,8},{9,1... | collective-permute-start | bytes 6291464 | tf_op jit(solution)/shard_map/ppermute | solution.py:37
  231.0 12.4 %all-to-all-start.1 = ((bf16[4,512,128]{1,2,0:T(8,128)(2,1)}), bf16[4,512,128]{1,2,0:T(8,128)(2,1)S(1)}, u32[]{:S(2)}, u32[]{:S(2)}) async-start(bf16[4,512,128]{1,2,0:T(8,128)(2,1)} %copy.147), calls=%async_computation.1 | async-start | bytes 1048576 | tf_op jit(solution)/shard_map/all_to_all | solution.py:450
  247.5 34.0 %collective-permute-start.21 = (f32[256,1024]{1,0:T(8,128)}, f32[256,1024]{1,0:T(8,128)}, u32[]{:S(2)}, u32[]{:S(2)}) collective-permute-start(f32[256,1024]{1,0:T(8,128)} %slice.666), channel_id=1, source_target_pairs={{0,4},{4,0},{1,5},{5,1},{2,6},{6,2},{3,7},{7,3},{8,12},{12,8},{9,1... | collective-permute-start | bytes 3145736 | tf_op jit(solution)/shard_map/ppermute | solution.py:37
  261.9 13.6 %collective-permute-start.37 = (bf16[4,256,1024]{2,1,0:T(8,128)(2,1)S(1)}, bf16[4,256,1024]{2,1,0:T(8,128)(2,1)S(1)}, u32[]{:S(2)}, u32[]{:S(2)}) collective-permute-start(bf16[4,256,1024]{2,1,0:T(8,128)(2,1)S(1)} %bitcast.384), channel_id=1, source_target_pairs={{0,4},{4,0},{1,5},{5,1},{2,6},{6,2},{3,7},{7,3},{8,12},{12,8},{9,1... | collective-permute-start | bytes 6291464 | tf_op jit(solution)/shard_map/ppermute | solution.py:37
  267.9 10.8 %collective-permute-start.11 = (bf16[4,256,1024]{2,1,0:T(8,128)(2,1)S(1)}, bf16[4,256,1024]{2,1,0:T(8,128)(2,1)S(1)}, u32[]{:S(2)}, u32[]{:S(2)}) collective-permute-start(bf16[4,256,1024]{2,1,0:T(8,128)(2,1)S(1)} %bitcast.382), channel_id=1, source_target_pairs={{0,4},{4,0},{1,5},{5,1},{2,6},{6,2},{3,7},{7,3},{8,12},{12,8},{9,1... | collective-permute-start | bytes 6291464 | tf_op jit(solution)/shard_map/ppermute | solution.py:37
  276.7 14.8 %collective-permute-start.38 = (bf16[2,128,1024]{2,1,0:T(8,128)(2,1)S(1)}, bf16[2,128,1024]{2,1,0:T(8,128)(2,1)S(1)}, u32[]{:S(2)}, u32[]{:S(2)}) collective-permute-start(bf16[2,128,1024]{2,1,0:T(8,128)(2,1)S(1)} %pad_maximum_fusion.37), channel_id=1, source_target_pairs={{0,8},{8,0},{16,24},{24,16},{1,9},{9,1},{17,25},{25,17},{2,10},{10... | collective-permute-start | bytes 1572872 | tf_op jit(solution)/shard_map/ppermute | solution.py:42
  278.2 14.8 %collective-permute-start.40 = (bf16[2,128,1024]{2,1,0:T(8,128)(2,1)S(1)}, bf16[2,128,1024]{2,1,0:T(8,128)(2,1)S(1)}, u32[]{:S(2)}, u32[]{:S(2)}) collective-permute-start(bf16[2,128,1024]{2,1,0:T(8,128)(2,1)S(1)} %stack.314), channel_id=1, source_target_pairs={{0,16},{8,24},{16,0},{24,8},{1,17},{9,25},{17,1},{25,9},{2,18},{10... | collective-permute-start | bytes 1572872 | tf_op jit(solution)/shard_map/ppermute | solution.py:42
  279.9 22.8 %collective-permute-start.12 = (bf16[2,128,1024]{2,1,0:T(8,128)(2,1)S(1)}, bf16[2,128,1024]{2,1,0:T(8,128)(2,1)S(1)}, u32[]{:S(2)}, u32[]{:S(2)}) collective-permute-start(bf16[2,128,1024]{2,1,0:T(8,128)(2,1)S(1)} %pad_maximum_fusion.29), channel_id=1, source_target_pairs={{0,8},{8,0},{16,24},{24,16},{1,9},{9,1},{17,25},{25,17},{2,10},{10... | collective-permute-start | bytes 1572872 | tf_op jit(solution)/shard_map/ppermute | solution.py:42
  281.4 22.7 %collective-permute-start.14 = (bf16[2,128,1024]{2,1,0:T(8,128)(2,1)S(1)}, bf16[2,128,1024]{2,1,0:T(8,128)(2,1)S(1)}, u32[]{:S(2)}, u32[]{:S(2)}) collective-permute-start(bf16[2,128,1024]{2,1,0:T(8,128)(2,1)S(1)} %stack.312), channel_id=1, source_target_pairs={{0,16},{8,24},{16,0},{24,8},{1,17},{9,25},{17,1},{25,9},{2,18},{10... | collective-permute-start | bytes 1572872 | tf_op jit(solution)/shard_map/ppermute | solution.py:42
  293.1 16.7 %collective-permute-start.39 = (bf16[128,1024]{1,0:T(8,128)(2,1)S(1)}, bf16[128,1024]{1,0:T(8,128)(2,1)S(1)}, u32[]{:S(2)}, u32[]{:S(2)}) collective-permute-start(bf16[128,1024]{1,0:T(8,128)(2,1)S(1)} %get-tuple-element.155), channel_id=1, source_target_pairs={{0,16},{8,24},{16,0},{24,8},{1,17},{9,25},{17,1},{25,9},{2,18},{10... | collective-permute-start | bytes 786440 | tf_op jit(solution)/shard_map/ppermute | solution.py:42
  293.7 16.0 %collective-permute-start.41 = (bf16[128,1024]{1,0:T(8,128)(2,1)S(1)}, bf16[128,1024]{1,0:T(8,128)(2,1)S(1)}, u32[]{:S(2)}, u32[]{:S(2)}) collective-permute-start(bf16[128,1024]{1,0:T(8,128)(2,1)S(1)} %get-tuple-element.156), channel_id=1, source_target_pairs={{0,8},{8,0},{16,24},{24,16},{1,9},{9,1},{17,25},{25,17},{2,10},{10... | collective-permute-start | bytes 786440 | tf_op jit(solution)/shard_map/ppermute | solution.py:42
  318.3 27.8 %collective-permute-start.51 = (bf16[2,128,1024]{2,1,0:T(8,128)(2,1)S(1)}, bf16[2,128,1024]{2,1,0:T(8,128)(2,1)S(1)}, u32[]{:S(2)}, u32[]{:S(2)}) collective-permute-start(bf16[2,128,1024]{2,1,0:T(8,128)(2,1)S(1)} %pad_maximum_fusion.40), channel_id=1, source_target_pairs={{0,8},{8,0},{16,24},{24,16},{1,9},{9,1},{17,25},{25,17},{2,10},{10... | collective-permute-start | bytes 1572872 | tf_op jit(solution)/shard_map/ppermute | solution.py:42
  319.9 19.0 %collective-permute-start.22 = (bf16[128,1024]{1,0:T(8,128)(2,1)S(1)}, bf16[128,1024]{1,0:T(8,128)(2,1)S(1)}, u32[]{:S(2)}, u32[]{:S(2)}) collective-permute-start(bf16[128,1024]{1,0:T(8,128)(2,1)S(1)} %get-tuple-element.224), channel_id=1, source_target_pairs={{0,8},{8,0},{16,24},{24,16},{1,9},{9,1},{17,25},{25,17},{2,10},{10... | collective-permute-start | bytes 786440 | tf_op jit(solution)/shard_map/ppermute | solution.py:42
  320.5 24.0 %collective-permute-start.48 = (bf16[128,1024]{1,0:T(8,128)(2,1)S(1)}, bf16[128,1024]{1,0:T(8,128)(2,1)S(1)}, u32[]{:S(2)}, u32[]{:S(2)}) collective-permute-start(bf16[128,1024]{1,0:T(8,128)(2,1)S(1)} %bitcast.328), channel_id=1, source_target_pairs={{0,8},{8,0},{16,24},{24,16},{1,9},{9,1},{17,25},{25,17},{2,10},{10... | collective-permute-start | bytes 786440 | tf_op jit(solution)/shard_map/ppermute | solution.py:42
  324.4 29.4 %collective-permute-start.25 = (bf16[2,128,1024]{2,1,0:T(8,128)(2,1)S(1)}, bf16[2,128,1024]{2,1,0:T(8,128)(2,1)S(1)}, u32[]{:S(2)}, u32[]{:S(2)}) collective-permute-start(bf16[2,128,1024]{2,1,0:T(8,128)(2,1)S(1)} %pad_maximum_fusion.33), channel_id=1, source_target_pairs={{0,8},{8,0},{16,24},{24,16},{1,9},{9,1},{17,25},{25,17},{2,10},{10... | collective-permute-start | bytes 1572872 | tf_op jit(solution)/shard_map/ppermute | solution.py:42
  338.9 14.9 %collective-permute-start.23 = (bf16[2,128,1024]{2,1,0:T(8,128)(2,1)S(1)}, bf16[2,128,1024]{2,1,0:T(8,128)(2,1)S(1)}, u32[]{:S(2)}, u32[]{:S(2)}) collective-permute-start(bf16[2,128,1024]{2,1,0:T(8,128)(2,1)S(1)} %pad_maximum_fusion.32), channel_id=1, source_target_pairs={{0,16},{8,24},{16,0},{24,8},{1,17},{9,25},{17,1},{25,9},{2,18},{10... | collective-permute-start | bytes 1572872 | tf_op jit(solution)/shard_map/ppermute | solution.py:42
  344.5 15.8 %collective-permute-start.49 = (bf16[2,128,1024]{2,1,0:T(8,128)(2,1)S(1)}, bf16[2,128,1024]{2,1,0:T(8,128)(2,1)S(1)}, u32[]{:S(2)}, u32[]{:S(2)}) collective-permute-start(bf16[2,128,1024]{2,1,0:T(8,128)(2,1)S(1)} %pad_maximum_fusion.39), channel_id=1, source_target_pairs={{0,16},{8,24},{16,0},{24,8},{1,17},{9,25},{17,1},{25,9},{2,18},{10... | collective-permute-start | bytes 1572872 | tf_op jit(solution)/shard_map/ppermute | solution.py:42
  355.3 32.9 %collective-permute-start.26 = (bf16[4,256,1024]{2,1,0:T(8,128)(2,1)}, bf16[4,256,1024]{2,1,0:T(8,128)(2,1)}, u32[]{:S(2)}, u32[]{:S(2)}) collective-permute-start(bf16[4,256,1024]{2,1,0:T(8,128)(2,1)} %maximum_maximum_fusion.3), channel_id=1, source_target_pairs={{0,4},{4,0},{1,5},{5,1},{2,6},{6,2},{3,7},{7,3},{8,12},{12,8},{9,1... | collective-permute-start | bytes 6291464 | tf_op jit(solution)/shard_map/ppermute | solution.py:37
  362.6 29.7 %collective-permute-start.52 = (bf16[4,256,1024]{2,1,0:T(8,128)(2,1)}, bf16[4,256,1024]{2,1,0:T(8,128)(2,1)}, u32[]{:S(2)}, u32[]{:S(2)}) collective-permute-start(bf16[4,256,1024]{2,1,0:T(8,128)(2,1)} %maximum_maximum_fusion.5), channel_id=1, source_target_pairs={{0,4},{4,0},{1,5},{5,1},{2,6},{6,2},{3,7},{7,3},{8,12},{12,8},{9,1... | collective-permute-start | bytes 6291464 | tf_op jit(solution)/shard_map/ppermute | solution.py:37
  379.5 73.8 %all-to-all-start.2 = ((bf16[4,512,128]{2,1,0:T(8,128)(2,1)}), bf16[4,512,128]{2,1,0:T(8,128)(2,1)S(1)}, u32[]{:S(2)}, u32[]{:S(2)}) async-start(bf16[4,512,128]{2,1,0:T(8,128)(2,1)} %bitcast.82), calls=%async_computation.2 | async-start | bytes 1048576 | tf_op jit(solution)/shard_map/all_to_all | solution.py:494
  383.0 172.5 %reduce-scatter.11.cloned.1.call-start = ((), (), s32[]{:S(2)}) async-start(), calls=%async_computation.14 | async-start | bytes 1310720 | tf_op jit(solution)/shard_map/reduce_scatter | solution.py:521
  398.5 12.3 %collective-permute-start.53 = (bf16[4,256,1024]{2,1,0:T(8,128)(2,1)S(1)}, bf16[4,256,1024]{2,1,0:T(8,128)(2,1)S(1)}, u32[]{:S(2)}, u32[]{:S(2)}) collective-permute-start(bf16[4,256,1024]{2,1,0:T(8,128)(2,1)S(1)} %bitcast.383), channel_id=1, source_target_pairs={{0,4},{4,0},{1,5},{5,1},{2,6},{6,2},{3,7},{7,3},{8,12},{12,8},{9,1... | collective-permute-start | bytes 6291464 | tf_op jit(solution)/shard_map/ppermute | solution.py:37
  399.8 15.6 %collective-permute-start.27 = (bf16[4,256,1024]{2,1,0:T(8,128)(2,1)S(1)}, bf16[4,256,1024]{2,1,0:T(8,128)(2,1)S(1)}, u32[]{:S(2)}, u32[]{:S(2)}) collective-permute-start(bf16[4,256,1024]{2,1,0:T(8,128)(2,1)S(1)} %bitcast.381), channel_id=1, source_target_pairs={{0,4},{4,0},{1,5},{5,1},{2,6},{6,2},{3,7},{7,3},{8,12},{12,8},{9,1... | collective-permute-start | bytes 6291464 | tf_op jit(solution)/shard_map/ppermute | solution.py:37
  412.0 14.8 %collective-permute-start.54 = (bf16[2,128,1024]{2,1,0:T(8,128)(2,1)S(1)}, bf16[2,128,1024]{2,1,0:T(8,128)(2,1)S(1)}, u32[]{:S(2)}, u32[]{:S(2)}) collective-permute-start(bf16[2,128,1024]{2,1,0:T(8,128)(2,1)S(1)} %pad_maximum_fusion.41), channel_id=1, source_target_pairs={{0,8},{8,0},{16,24},{24,16},{1,9},{9,1},{17,25},{25,17},{2,10},{10... | collective-permute-start | bytes 1572872 | tf_op jit(solution)/shard_map/ppermute | solution.py:42
  414.0 14.8 %collective-permute-start.56 = (bf16[2,128,1024]{2,1,0:T(8,128)(2,1)S(1)}, bf16[2,128,1024]{2,1,0:T(8,128)(2,1)S(1)}, u32[]{:S(2)}, u32[]{:S(2)}) collective-permute-start(bf16[2,128,1024]{2,1,0:T(8,128)(2,1)S(1)} %stack.316), channel_id=1, source_target_pairs={{0,16},{8,24},{16,0},{24,8},{1,17},{9,25},{17,1},{25,9},{2,18},{10... | collective-permute-start | bytes 1572872 | tf_op jit(solution)/shard_map/ppermute | solution.py:42
  418.2 19.9 %collective-permute-start.28 = (bf16[2,128,1024]{2,1,0:T(8,128)(2,1)}, bf16[2,128,1024]{2,1,0:T(8,128)(2,1)}, u32[]{:S(2)}, u32[]{:S(2)}) collective-permute-start(bf16[2,128,1024]{2,1,0:T(8,128)(2,1)} %pad_maximum_fusion.34), channel_id=1, source_target_pairs={{0,8},{8,0},{16,24},{24,16},{1,9},{9,1},{17,25},{25,17},{2,10},{10... | collective-permute-start | bytes 1572872 | tf_op jit(solution)/shard_map/ppermute | solution.py:42
  418.8 21.4 %collective-permute-start.30 = (bf16[2,128,1024]{2,1,0:T(8,128)(2,1)}, bf16[2,128,1024]{2,1,0:T(8,128)(2,1)}, u32[]{:S(2)}, u32[]{:S(2)}) collective-permute-start(bf16[2,128,1024]{2,1,0:T(8,128)(2,1)} %stack.313), channel_id=1, source_target_pairs={{0,16},{8,24},{16,0},{24,8},{1,17},{9,25},{17,1},{25,9},{2,18},{10... | collective-permute-start | bytes 1572872 | tf_op jit(solution)/shard_map/ppermute | solution.py:42
  429.8 15.8 %collective-permute-start.55 = (bf16[128,1024]{1,0:T(8,128)(2,1)}, bf16[128,1024]{1,0:T(8,128)(2,1)S(1)}, u32[]{:S(2)}, u32[]{:S(2)}) collective-permute-start(bf16[128,1024]{1,0:T(8,128)(2,1)} %get-tuple-element.167), channel_id=1, source_target_pairs={{0,16},{8,24},{16,0},{24,8},{1,17},{9,25},{17,1},{25,9},{2,18},{10... | collective-permute-start | bytes 786440 | tf_op jit(solution)/shard_map/ppermute | solution.py:42
  431.3 14.3 %collective-permute-start.57 = (bf16[128,1024]{1,0:T(8,128)(2,1)}, bf16[128,1024]{1,0:T(8,128)(2,1)}, u32[]{:S(2)}, u32[]{:S(2)}) collective-permute-start(bf16[128,1024]{1,0:T(8,128)(2,1)} %get-tuple-element.168), channel_id=1, source_target_pairs={{0,8},{8,0},{16,24},{24,16},{1,9},{9,1},{17,25},{25,17},{2,10},{10... | collective-permute-start | bytes 786440 | tf_op jit(solution)/shard_map/ppermute | solution.py:42
  453.3 32.3 %collective-permute-start.58 = (bf16[256,1024]{1,0:T(8,128)(2,1)}, bf16[256,1024]{1,0:T(8,128)(2,1)S(1)}, u32[]{:S(2)}, u32[]{:S(2)}) collective-permute-start(bf16[256,1024]{1,0:T(8,128)(2,1)} %get-tuple-element.120), channel_id=1, source_target_pairs={{0,4},{4,0},{1,5},{5,1},{2,6},{6,2},{3,7},{7,3},{8,12},{12,8},{9,1... | collective-permute-start | bytes 1572872 | tf_op jit(solution)/shard_map/ppermute | solution.py:37
  488.6 13.2 %all-to-all-start.3 = ((bf16[4,512,128]{2,1,0:T(8,128)(2,1)}), bf16[4,512,128]{2,1,0:T(8,128)(2,1)}, u32[]{:S(2)}, u32[]{:S(2)}) async-start(bf16[4,512,128]{2,1,0:T(8,128)(2,1)} %bitcast.110), calls=%async_computation.3 | async-start | bytes 1048576 | tf_op jit(solution)/shard_map/all_to_all | solution.py:494
  492.8 63.4 %reduce-scatter.7.cloned.1.call-start = ((), (), s32[]{:S(2)}) async-start(), calls=%async_computation.11 | async-start | bytes 1310720 | tf_op jit(solution)/shard_map/reduce_scatter | solution.py:521
  496.9 65.0 %reduce-scatter.5.cloned.1.call-start = ((), (), s32[]{:S(2)}) async-start(), calls=%async_computation.10 | async-start | bytes 983040 | tf_op jit(solution)/shard_map/reduce_scatter | solution.py:521
  540.6 67.3 %reduce-scatter.9.cloned.1.call-start = ((), (), s32[]{:S(2)}) async-start(), calls=%async_computation.13 | async-start | bytes 2621440 | tf_op jit(solution)/shard_map/reduce_scatter | solution.py:521
  555.4 100.6 %all-gather.21.cloned.1.call-start = ((), (), s32[]{:S(2)}) async-start(), calls=%async_computation.18 | async-start | bytes 2359296 | tf_op jit(solution)/shard_map/all_gather | solution.py:524
  556.2 131.7 %all-reduce.2.cloned.1.call-start = ((), (), s32[]{:S(2)}) async-start(), calls=%async_computation.12 | async-start | bytes 524288 | tf_op jit(solution)/shard_map/psum | solution.py:533
  556.9 191.7 %all-gather.17.cloned.1.call-start = ((), (), s32[]{:S(2)}) async-start(), calls=%async_computation.16 | async-start | bytes 1769472 | tf_op jit(solution)/shard_map/all_gather | solution.py:524
  561.9 198.4 %all-gather.19.cloned.1.call-start = ((), (), s32[]{:S(2)}) async-start(), calls=%async_computation.17 | async-start | bytes 4718592 | tf_op jit(solution)/shard_map/all_gather | solution.py:524
  566.8 46.0 %collective-permute-start.43 = (bf16[4,256,1024]{2,1,0:T(8,128)(2,1)}, bf16[4,256,1024]{2,1,0:T(8,128)(2,1)S(1)}, u32[]{:S(2)}, u32[]{:S(2)}) collective-permute-start(bf16[4,256,1024]{2,1,0:T(8,128)(2,1)} %bitcast.86), channel_id=1, source_target_pairs={{0,4},{4,0},{1,5},{5,1},{2,6},{6,2},{3,7},{7,3},{8,12},{12,8},{9,1... | collective-permute-start | bytes 6291464 | tf_op jit(solution)/shard_map/ppermute | solution.py:37
  612.8 33.9 %collective-permute-start.59 = (bf16[4,256,1024]{2,1,0:T(8,128)(2,1)}, bf16[4,256,1024]{2,1,0:T(8,128)(2,1)}, u32[]{:S(2)}, u32[]{:S(2)}) collective-permute-start(bf16[4,256,1024]{2,1,0:T(8,128)(2,1)} %bitcast.114), channel_id=1, source_target_pairs={{0,4},{4,0},{1,5},{5,1},{2,6},{6,2},{3,7},{7,3},{8,12},{12,8},{9,1... | collective-permute-start | bytes 6291464 | tf_op jit(solution)/shard_map/ppermute | solution.py:37
  616.8 17.2 %collective-permute-start.44 = (bf16[2,128,1024]{2,1,0:T(8,128)(2,1)S(1)}, bf16[2,128,1024]{2,1,0:T(8,128)(2,1)S(1)}, u32[]{:S(2)}, u32[]{:S(2)}) collective-permute-start(bf16[2,128,1024]{2,1,0:T(8,128)(2,1)S(1)} %pad_maximum_fusion.38), channel_id=1, source_target_pairs={{0,8},{8,0},{16,24},{24,16},{1,9},{9,1},{17,25},{25,17},{2,10},{10... | collective-permute-start | bytes 1572872 | tf_op jit(solution)/shard_map/ppermute | solution.py:42
  618.4 16.2 %collective-permute-start.46 = (bf16[2,128,1024]{2,1,0:T(8,128)(2,1)S(1)}, bf16[2,128,1024]{2,1,0:T(8,128)(2,1)S(1)}, u32[]{:S(2)}, u32[]{:S(2)}) collective-permute-start(bf16[2,128,1024]{2,1,0:T(8,128)(2,1)S(1)} %stack.315), channel_id=1, source_target_pairs={{0,16},{8,24},{16,0},{24,8},{1,17},{9,25},{17,1},{25,9},{2,18},{10... | collective-permute-start | bytes 1572872 | tf_op jit(solution)/shard_map/ppermute | solution.py:42
  651.3 38.9 %collective-permute-start.60 = (bf16[2,128,1024]{2,1,0:T(8,128)(2,1)}, bf16[2,128,1024]{2,1,0:T(8,128)(2,1)}, u32[]{:S(2)}, u32[]{:S(2)}) collective-permute-start(bf16[2,128,1024]{2,1,0:T(8,128)(2,1)} %pad_maximum_fusion.42), channel_id=1, source_target_pairs={{0,8},{8,0},{16,24},{24,16},{1,9},{9,1},{17,25},{25,17},{2,10},{10... | collective-permute-start | bytes 1572872 | tf_op jit(solution)/shard_map/ppermute | solution.py:42
  652.3 37.9 %collective-permute-start.62 = (bf16[2,128,1024]{2,1,0:T(8,128)(2,1)}, bf16[2,128,1024]{2,1,0:T(8,128)(2,1)}, u32[]{:S(2)}, u32[]{:S(2)}) collective-permute-start(bf16[2,128,1024]{2,1,0:T(8,128)(2,1)} %stack.317), channel_id=1, source_target_pairs={{0,16},{8,24},{16,0},{24,8},{1,17},{9,25},{17,1},{25,9},{2,18},{10... | collective-permute-start | bytes 1572872 | tf_op jit(solution)/shard_map/ppermute | solution.py:42
  (89 other events, 870.7 us)
Sparse Core Ops, SparseCore 0:
  17.8 27.2 all-gather.14
  127.9 43.2 all-gather.10
  196.8 25.1 all-gather.12
  436.0 25.0 reduce-scatter.10
  497.0 26.3 reduce-scatter.6
  540.8 21.0 reduce-scatter.4
  564.7 43.1 reduce-scatter.8
  610.0 31.1 all-gather.20
  644.4 43.4 all-reduce.1
  689.5 27.0 all-gather.16
  718.5 37.6 all-gather.18

commit v2 on v1

--- a/solution.py
+++ b/solution.py
@@ -42,48 +42,49 @@
     return lax.ppermute(value, "chip", [(i, i ^ mask) for i in range(count)])
 
 
-def plane_gather(value):
+def swap_shard(value, mask):
+    count = lax.axis_size("fsdp")
+    return lax.ppermute(value, "fsdp", [(i, i ^ mask) for i in range(count)])
+
+
+def hold(value, *deps):
+    return lax.optimization_barrier((value, deps))[0]
+
+
+def spread(value):
     count = lax.axis_size("chip")
-    if count != 4:
-        return jnp.stack([value] + [swap_chip(value, r) for r in range(1, count)])
-    half = value.shape[0] // 2
-    top, low = value[:half], value[half:]
-    top_x = swap_chip(top, 1)
-    low_y = swap_chip(low, 2)
-    top_y = swap_chip(jnp.stack([top, top_x]), 2)
-    low_x = swap_chip(jnp.stack([low, low_y]), 1)
-    tops = jnp.stack([top, top_x, top_y[0], top_y[1]])
-    lows = jnp.stack([low, low_x[0], low_y, low_x[1]])
-    return jnp.concatenate([tops, lows], axis=1)
-
-
-def gather_all(value):
-    near = plane_gather(value)
-    return near, swap_core(near)
-
-
-def plane_reduce(own, other):
-    count = lax.axis_size("chip")
-    total = (own.astype(f32) + swap_core(other).astype(f32)).astype(bf16)
-    if count != 4:
-        result = total[0].astype(f32)
-        for r in range(1, count):
-            result = result + swap_chip(total[r], r).astype(f32)
-        return result
-    half = own.shape[1] // 2
-    top, low = total[:, :half], total[:, half:]
-    got_x = swap_chip(jnp.stack([top[1], top[3]]), 1)
-    got_y = swap_chip(jnp.stack([low[2], low[3]]), 2)
-    top_two = (top[2].astype(f32) + got_x[1].astype(f32)).astype(bf16)
-    low_one = (low[1].astype(f32) + got_y[1].astype(f32)).astype(bf16)
-    last_y = swap_chip(top_two, 2)
-    last_x = swap_chip(low_one, 1)
-    return jnp.concatenate(
-        [
-            top[0].astype(f32) + got_x[0].astype(f32) + last_y.astype(f32),
-            low[0].astype(f32) + got_y[0].astype(f32) + last_x.astype(f32),
-        ]
-    )
+    return exchange(jnp.broadcast_to(value, (count,) + value.shape))
+
+
+def exchange(value):
+    return lax.all_to_all(value, "chip", 0, 0)
+
+
+def core_sum(own, swapped):
+    return (own.astype(f32) + swapped.astype(f32)).astype(bf16)
+
+
+def last_sum(value):
+    return jnp.sum(value.astype(f32), axis=0)
+
+
+def shard_pieces(value):
+    return [value] + [swap_shard(value, r) for r in range(1, lax.axis_size("fsdp"))]
+
+
+def shard_sum(pieces):
+    return add_pieces(pieces[0], send_pieces(pieces))
+
+
+def send_pieces(pieces):
+    return [swap_shard(pieces[r], r) for r in range(1, len(pieces))]
+
+
+def add_pieces(own, received):
+    total = own.astype(f32)
+    for piece in received:
+        total = total + piece.astype(f32)
+    return total.astype(bf16)
 
 
 def head_masks(rows, width):
@@ -121,7 +122,7 @@
             rows_in = source[rows, :].astype(f32)
             tile = (rows_in * row_scale(rows_in) * gain_row).astype(bf16)
             normed[s, rows, :] = tile
-            mixed = dot_nn(tile, weight[...])
+            mixed = dot_nn(tile, weight[:, : 3 * width])
             for h in range(2):
                 place = rel[(s * tiles + t) * 2 + h]
                 where = pl.ds(pl.multiple_of(place * blk, blk), blk)
@@ -201,7 +202,7 @@
 
 def backward_kernel(
     rel, send, first, full, query, key, value, fine, logsum, grad_in, weight, start,
-    partial, grads,
+    part_near, part_far, grads,
     grad_at, grad_q, grad_k, grad_v, grad_q2,
 ):
     seq_len, width = query.shape
@@ -274,20 +275,152 @@
 
     lax.fori_loop(0, seq_len // TILE, query_tile, 0)
 
-    tiles = seq_len // TILE
-
-    def project(t, _):
+    tiles = seq_len // TILE // 2
+
+    def project(t, side, part):
         rows = pl.ds(pl.multiple_of(t * TILE, TILE), TILE)
+        base = side * tiles + t
         for h in range(2):
-            where = pl.ds(pl.multiple_of(rel[t * 2 + h] * blk, blk), blk)
+            where = pl.ds(pl.multiple_of(rel[base * 2 + h] * blk, blk), blk)
             here = pl.ds(pl.multiple_of(t * TILE + h * blk, blk), blk)
-            grads[here, :width] = grad_q[where, :]
-            grads[here, width : 2 * width] = grad_k[where, :].astype(bf16)
-            grads[here, 2 * width :] = grad_v[where, :].astype(bf16)
-        partial[rows, :] = dot_nt(grads[rows, :], weight[...]).astype(bf16)
+            grads[side, here, :width] = grad_q[where, :]
+            grads[side, here, width : 2 * width] = grad_k[where, :].astype(bf16)
+            grads[side, here, 2 * width :] = grad_v[where, :].astype(bf16)
+        part[rows, :] = dot_nt(grads[side, rows, :], weight[:, : 3 * width]).astype(bf16)
         return 0
 
-    lax.fori_loop(0, tiles, project, 0)
+    for side, part in ((0, part_near), (1, part_far)):
+        lax.fori_loop(0, tiles, lambda t, _, s=side, p=part: project(t, s, p), 0)
+
+
+def place_pieces(target, pieces, shard, begin, count):
+    for r, piece in enumerate(pieces):
+        at = pl.multiple_of((shard ^ r) * count, count)
+        target[pl.ds(at, count), :] = piece[begin : begin + count, :]
+
+
+def mix_kernel(ids, got, *refs):
+    pieces, (attended, own, other, weight) = refs[:-4], refs[-4:]
+    rows = own.shape[0]
+    place_pieces(weight, pieces, ids[1], 0, pieces[0].shape[0])
+    joined = jnp.concatenate([got[p] for p in range(got.shape[0])], axis=1)
+    attended[...] = joined
+    own[...] = dot_nn(joined[:rows], weight[...])
+    other[...] = dot_nn(joined[rows:], weight[...])
+
+
+def unmix_kernel(ids, own, other, attended, *refs):
+    pieces, (grad_sent, grad_weight, weight) = refs[:-3], refs[-3:]
+    place_pieces(weight, pieces, ids[1], 0, pieces[0].shape[0])
+    branch = jnp.concatenate([own[...], other[...]], axis=0)
+    spread = dot_nt(branch, weight[...]).astype(bf16)
+    width = grad_sent.shape[2]
+    for p in range(grad_sent.shape[0]):
+        grad_sent[p] = spread[:, p * width : (p + 1) * width]
+    grad_weight[...] = dot_tn(attended[...], branch)
+
+
+def ffn_kernel(ids, x_near, x_far, cot_ref, *refs, split):
+    outs = 7 + split
+    pieces, out_parts = refs[:-outs], refs[-outs : 1 + split - outs]
+    mid_near, mid_far, hidden, grad_pre, gate_up, down = refs[-6:]
+    t = pl.program_id(0)
+    half = pl.num_programs(0) // 2
+    feats, size = gate_up.shape[0], gate_up.shape[1] // 2
+    shards = pieces[0].shape[0]
+    rows, more = feats // shards, size // shards
+    begin = rows if len(pieces) == 1 else 0
+
+    @pl.when(t == 0)
+    def _():
+        for z in range(shards):
+            gate_up[z * rows : (z + 1) * rows, :] = pieces[0][z, :rows, :]
+            down[z * more : (z + 1) * more, :] = pieces[-1][z, begin : begin + more, :]
+
+    tile = jnp.where(t < half, x_near[...], x_far[...])
+    cot = cot_ref[...].reshape(tile.shape)
+    pre = dot_nn(tile, gate_up[...])
+    gate_pre, up_pre = pre[:, :size], pre[:, size:]
+    sigma = jax.nn.sigmoid(gate_pre)
+    active = gate_pre * sigma
+    low = (active * up_pre).astype(bf16)
+    grad_hidden = dot_nt(cot, down[...])
+    hidden[...] = low
+    out_part = dot_nn(low, down[...]).astype(bf16)
+    grad_gate = grad_hidden * up_pre * sigma * (1.0 + gate_pre * (1.0 - sigma))
+    grad_up = grad_hidden * active
+    grads = jnp.concatenate([grad_gate.astype(bf16), grad_up.astype(bf16)], axis=1)
+    grad_pre[...] = grads
+    mid_part = dot_nt(grads, gate_up[...]).astype(bf16)
+
+    if not split:
+        out_parts[0][...] = out_part.reshape(out_parts[0].shape)
+
+    @pl.when(t < half)
+    def _():
+        mid_near[...] = mid_part
+        if split:
+            out_parts[0][...] = out_part
+
+    @pl.when(t >= half)
+    def _():
+        mid_far[...] = mid_part
+        if split:
+            out_parts[1][...] = out_part
+
+
+def weight_kernel(ids, *refs, streams, shards):
+    ins, outs, (wide, down) = refs[: 5 * streams], refs[5 * streams : -2], refs[-2:]
+    t = pl.program_id(0)
+    per = pl.num_programs(0) // streams
+
+    @pl.when(t == 0)
+    def _():
+        wide[...] = jnp.zeros_like(wide)
+        down[...] = jnp.zeros_like(down)
+
+    for b in range(streams):
+        x_near, x_far, cot, hidden, grad_pre = ins[5 * b : 5 * b + 5]
+
+        @pl.when((t >= b * per) & (t < (b + 1) * per))
+        def _(b=b, x_near=x_near, x_far=x_far, cot=cot, hidden=hidden, grad_pre=grad_pre):
+            tile = jnp.where(t < b * per + per // 2, x_near[...], x_far[...])
+            wide[...] += dot_tn(tile, grad_pre[...])
+            down[...] += dot_tn(hidden[...], cot[...].reshape(tile.shape))
+
+    @pl.when(t == pl.num_programs(0) - 1)
+    def _():
+        rows, more = wide.shape[0] // shards, down.shape[0] // shards
+        begin = rows if len(outs) == 1 else 0
+        for z in range(shards):
+            outs[0][z, :rows, :] = wide[z * rows : (z + 1) * rows, :].astype(bf16)
+            piece = down[z * more : (z + 1) * more, :]
+            outs[-1][z, begin : begin + more, :] = piece.astype(bf16)
+
+
+def assemble_kernel(*refs, kinds, shards, with_down):
+    parts, gain = refs[:2]
+    weights = refs[2 : 2 + kinds]
+    rest = refs[2 + kinds :]
+    if with_down:
+        down_part, rest = rest[0], rest[1:]
+    outs, gain_out = rest[:kinds], rest[kinds]
+    groups, _, size = parts.shape
+    pieces = size // kinds
+    lanes = pieces // shards
+    sums = 0.0
+    for k in range(kinds):
+        columns = []
+        for z in range(shards):
+            for i in range(groups):
+                at = k * pieces + z * lanes
+                columns.append(parts[i, :, at : at + lanes].astype(f32))
+        full = jnp.concatenate(columns, axis=1)
+        outs[k][...] = full
+        sums = sums + jnp.sum(full * weights[k][...].astype(f32), axis=1, keepdims=True)
+    gain_out[...] = sums / gain[...].astype(f32)
+    if with_down:
+        rest[kinds + 1][...] = down_part[...].astype(f32)
 
 
 def smem():
@@ -296,6 +429,10 @@
 
 def vmem():
     return pl.BlockSpec(memory_space=pltpu.VMEM)
+
+
+def cost(micros):
+    return pl.CostEstimate(flops=micros * 10**9, bytes_accessed=2**20, transcendentals=0)
 
 
 LIMIT = pltpu.CompilerParams(vmem_limit_bytes=56 * 2**20)
@@ -320,11 +457,7 @@
             pltpu.VMEM((big, 128), f32),
         ],
         compiler_params=LIMIT,
-        cost_estimate=pl.CostEstimate(
-            flops=6 * seq_len * feats * width + 16 * pairs,
-            bytes_accessed=6 * seq_len * feats,
-            transcendentals=pairs // HEAD_DIM,
-        ),
+        cost_estimate=cost(31),
         name="attend_forward",
     )(*tables, x_near, x_far, weight, gain, start)
 
@@ -338,9 +471,13 @@
     pairs = seq_len * seq_len * width // 2
     return pl.pallas_call(
         backward_kernel,
-        out_shape=(shape((seq_len, feats), bf16), shape((seq_len, 3 * width), bf16)),
+        out_shape=(
+            shape((seq_len // 2, feats), bf16),
+            shape((seq_len // 2, feats), bf16),
+            shape((2, seq_len // 2, 3 * width), bf16),
+        ),
         in_specs=[smem()] * 4 + [vmem()] * 8,
-        out_specs=[vmem()] * 2,
+        out_specs=[vmem()] * 3,
         scratch_shapes=[
             pltpu.VMEM((seq_len, width), bf16),
             pltpu.VMEM((seq_len, width), bf16),
@@ -349,13 +486,177 @@
             pltpu.VMEM((big, width), f32),
         ],
         compiler_params=LIMIT,
-        cost_estimate=pl.CostEstimate(
-            flops=6 * seq_len * feats * width + 32 * pairs,
-            bytes_accessed=4 * seq_len * feats,
-            transcendentals=pairs // HEAD_DIM,
-        ),
+        cost_estimate=cost(31),
         name="attend_backward",
     )(*tables, *saved, grad_in, weight, start)
+
+
+def mix(ids, got, pieces):
+    chips, doubled, width = got.shape
+    feats = pieces[0].shape[1]
+    size = chips * width
+    shape = jax.ShapeDtypeStruct
+    return pl.pallas_call(
+        mix_kernel,
+        out_shape=(
+            shape((doubled, size), bf16),
+            shape((doubled // 2, feats), f32),
+            shape((doubled // 2, feats), f32),
+        ),
+        in_specs=[smem()] + [vmem()] * (1 + len(pieces)),
+        out_specs=[vmem()] * 3,
+        scratch_shapes=[pltpu.VMEM((size, feats), bf16)],
+        compiler_params=LIMIT,
+        cost_estimate=cost(3),
+        name="mix",
+    )(ids, got, *pieces)
+
+
+def unmix(ids, own, other, attended, pieces, chips):
+    rows, feats = own.shape
+    size = attended.shape[1]
+    shape = jax.ShapeDtypeStruct
+    return pl.pallas_call(
+        unmix_kernel,
+        out_shape=(shape((chips, 2 * rows, size // chips), bf16), shape((size, feats), f32)),
+        in_specs=[smem()] + [vmem()] * (3 + len(pieces)),
+        out_specs=[vmem()] * 2,
+        scratch_shapes=[pltpu.VMEM((size, feats), bf16)],
+        compiler_params=LIMIT,
+        cost_estimate=cost(4),
+        name="unmix",
+    )(ids, own, other, attended, *pieces)
+
+
+ROWS = 512
+
+
+def feed_forward(ids, mids, cot, pieces, size, split):
+    tokens, feats = mids[0].shape
+    chips, _, rows, _ = cot.shape
+    half = tokens // ROWS
+    shape = jax.ShapeDtypeStruct
+    near = pl.BlockSpec((ROWS, feats), lambda t, ids: (jnp.minimum(t, half - 1), 0))
+    far = pl.BlockSpec((ROWS, feats), lambda t, ids: (jnp.maximum(t - half, 0), 0))
+    by_device = pl.BlockSpec(
+        (ROWS // rows, None, rows, feats),
+        lambda t, ids: (lax.rem(t, half), ids[0] ^ lax.div(t, half), 0, 0),
+    )
+
+    def tiles(width):
+        return pl.BlockSpec((ROWS, width), lambda t, ids: (t, 0))
+
+    side = shape((tokens, feats), bf16)
+    return pl.pallas_call(
+        functools.partial(ffn_kernel, split=split),
+        grid_spec=pltpu.PrefetchScalarGridSpec(
+            num_scalar_prefetch=1,
+            grid=(2 * half,),
+            in_specs=[near, far, by_device]
+            + [pl.BlockSpec(piece.shape, lambda t, ids: (0, 0, 0)) for piece in pieces],
+            out_specs=([near, far] if split else [by_device])
+            + [near, far, tiles(size), tiles(2 * size)],
+            scratch_shapes=[
+                pltpu.VMEM((feats, 2 * size), bf16),
+                pltpu.VMEM((size, feats), bf16),
+            ],
+        ),
+        out_shape=([side, side] if split else [shape(cot.shape, bf16)])
+        + [
+            side,
+            side,
+            shape((2 * tokens, size), bf16),
+            shape((2 * tokens, 2 * size), bf16),
+        ],
+        compiler_params=LIMIT,
+        cost_estimate=cost(20),
+        name="feed_forward",
+    )(ids, *mids, cot, *pieces)
+
+
+def weight_sums(ids, streams, shards):
+    tokens, feats = streams[0][0].shape
+    size = streams[0][3].shape[1]
+    rows = streams[0][2].shape[2]
+    half = tokens // ROWS
+    per = 2 * half
+    shape = jax.ShapeDtypeStruct
+    specs = []
+    for b in range(len(streams)):
+
+        def local(t, b=b):
+            return jnp.clip(t - b * per, 0, per - 1)
+
+        specs += [
+            pl.BlockSpec((ROWS, feats), lambda t, ids, f=local: (jnp.minimum(f(t), half - 1), 0)),
+            pl.BlockSpec((ROWS, feats), lambda t, ids, f=local: (jnp.maximum(f(t) - half, 0), 0)),
+            pl.BlockSpec(
+                (ROWS // rows, None, rows, feats),
+                lambda t, ids, f=local: (
+                    lax.rem(f(t), half),
+                    ids[0] ^ lax.div(f(t), half),
+                    0,
+                    0,
+                ),
+            ),
+            pl.BlockSpec((ROWS, size), lambda t, ids, f=local: (f(t), 0)),
+            pl.BlockSpec((ROWS, 2 * size), lambda t, ids, f=local: (f(t), 0)),
+        ]
+    if 2 * size == feats:
+        outs = [(shards, (feats + size) // shards, feats)]
+    else:
+        outs = [(shards, feats // shards, 2 * size), (shards, size // shards, feats)]
+    return pl.pallas_call(
+        functools.partial(weight_kernel, streams=len(streams), shards=shards),
+        grid_spec=pltpu.PrefetchScalarGridSpec(
+            num_scalar_prefetch=1,
+            grid=(per * len(streams),),
+            in_specs=specs,
+            out_specs=[pl.BlockSpec(out, lambda t, ids: (0, 0, 0)) for out in outs],
+            scratch_shapes=[pltpu.VMEM((feats, 2 * size), f32), pltpu.VMEM((size, feats), f32)],
+        ),
+        out_shape=[shape(out, bf16) for out in outs],
+        compiler_params=LIMIT,
+        cost_estimate=cost(23),
+        name="weight_sums",
+    )(ids, *[value for stream in streams for value in stream])
+
+
+STEPS = 4
+
+
+def assemble(parts, gain, weights, shards, downs=None, begin=0, down_rows=0):
+    rows, columns = weights[0].shape
+    step = rows // STEPS
+    shape = jax.ShapeDtypeStruct
+    groups, _, size = parts.shape
+    row_block = pl.BlockSpec((step, columns), lambda t: (t, 0))
+    thin = pl.BlockSpec((step, 1), lambda t: (t, 0))
+    count = len(weights)
+    args = [parts, gain[:, None], *weights]
+    in_specs = [pl.BlockSpec((groups, step, size), lambda t: (0, t, 0)), thin] + [row_block] * count
+    out_shape = [shape((rows, columns), f32)] * count + [shape((rows, 1), f32)]
+    out_specs = [row_block] * count + [thin]
+    if down_rows:
+        share, feats = groups // STEPS, downs.shape[2]
+        args.append(downs)
+        in_specs.append(
+            pl.BlockSpec((share, down_rows, feats), lambda t: (t, begin // down_rows, 0))
+        )
+        out_shape.append(shape((groups, down_rows, feats), f32))
+        out_specs.append(pl.BlockSpec((share, down_rows, feats), lambda t: (t, 0, 0)))
+    outs = pl.pallas_call(
+        functools.partial(
+            assemble_kernel, kinds=count, shards=shards, with_down=bool(down_rows)
+        ),
+        grid=(STEPS,),
+        out_shape=out_shape,
+        in_specs=in_specs,
+        out_specs=out_specs,
+        compiler_params=LIMIT,
+        name="assemble",
+    )(*args)
+    return outs[:count], outs[count][:, 0], outs[count + 1 :]
 
 
 def per_device(
@@ -377,17 +678,17 @@
     blk = rows // 2
     tokens = chips * rows
 
-    near_ids = jnp.arange(chips, dtype=jnp.int32) ^ chip
+    ids = jnp.stack([core, lax.axis_index("fsdp")]).astype(jnp.int32)
     pair = jnp.arange(2, dtype=jnp.int32)
-    rel_dev = (near_ids[None, :] * 2) + (pair[:, None] ^ core)
+    rel_dev = (jnp.arange(chips, dtype=jnp.int32)[None, :] * 2) + (pair[:, None] ^ core)
     rel_slot = (rel_dev[:, :, None] * 2 + pair[None, None, :]).reshape(-1)
     send_dev = jnp.arange(chips, dtype=jnp.int32)[:, None] * 2 + (pair[None, :] ^ core)
     send_slot = (send_dev[:, :, None] * 2 + pair[None, None, :]).reshape(-1)
-    ids = jnp.arange(blocks, dtype=jnp.int32)
+    spots = jnp.arange(blocks, dtype=jnp.int32)
 
     def look_up(slots):
         return jnp.sum(
-            jnp.where(slots[:, None] == ids[None, :], deal_order[None, :], 0), axis=1
+            jnp.where(slots[:, None] == spots[None, :], deal_order[None, :], 0), axis=1
         ).astype(jnp.int32)
 
     rel_table = look_up(rel_slot)
@@ -395,7 +696,7 @@
     earlier = (segments[None, :, :] < segments[:, None, :]).astype(jnp.int32)
     slot_start = jnp.sum(earlier, axis=1).astype(jnp.int32).reshape(blocks, blk, seqs)
     start = jnp.sum(
-        jnp.where((deal_order[None, :] == ids[:, None])[:, :, None, None], slot_start[None], 0),
+        jnp.where((deal_order[None, :] == spots[:, None])[:, :, None, None], slot_start[None], 0),
         axis=1,
     ).astype(jnp.int32)
     start = start.transpose(2, 0, 1).reshape(seqs, seq_len)
@@ -409,145 +710,191 @@
     def take(weight, axis, index, size):
         return lax.dynamic_slice_in_dim(weight, index * size, size, axis)
 
-    own_qkv = jnp.concatenate([take(w, 1, rank, width) for w in (w_query, w_key, w_value)], axis=1)
+    both = jnp.stack([gain_attn, gain_ffn], axis=1)
+    spare = jnp.zeros((both.shape[0], -(3 * width + 2) % 128), bf16)
+    own_qkv = jnp.concatenate(
+        [take(w, 1, rank, width) for w in (w_query, w_key, w_value)] + [both, spare], axis=1
+    )
 
     def hidden_columns(weight):
-        grid = weight.reshape(weight.shape[0], shards, groups, per_shard)
-        return take(grid, 2, rank, 1).reshape(weight.shape[0], hidden_width)
-
-    own_gate_up = jnp.concatenate([hidden_columns(w_gate), hidden_columns(w_up)], axis=1)
+        return [take(weight, 1, rank + z * groups, per_shard) for z in range(shards)]
+
+    own_gate_up = jnp.concatenate(hidden_columns(w_gate) + hidden_columns(w_up), axis=1)
     own_down = take(w_down, 0, rank, per_shard)
     out_grid = w_out.reshape(-1, 2, width, feats)
     own_out = take(out_grid, 1, core, 1).reshape(-1, feats)
 
-    def gather_rows(value):
-        return lax.all_gather(value, "fsdp", axis=0, tiled=True)
-
-    gains = gather_rows(jnp.stack([gain_attn, gain_ffn], axis=1))
-    gain_one, gain_two = gains[:, 0][None, :], gains[:, 1][None, :]
-    qkv = gather_rows(own_qkv)
-    out_half = gather_rows(own_out)
-    gate_up = gather_rows(own_gate_up)
-    down = gather_rows(own_down)
-
-    outputs, grad_inputs = [], []
-    grad_qkv = grad_gate_up = grad_down = grad_out = 0.0
-    gain_sums_one = gain_sums_two = 0.0
-    kept = []
-    for b in range(seqs):
-        x_own = inputs[:, b]
-        x_near, x_far = gather_all(x_own)
-        tables = (rel_table, send_table, first[b], full[b])
+    qkv = lax.all_gather(own_qkv, "fsdp", axis=0, tiled=True)
+    gain_one, gain_two = qkv[:, 3 * width][None, :], qkv[:, 3 * width + 1][None, :]
+    out_pieces = shard_pieces(own_out)
+    merged = 2 * hidden_width == feats
+    if merged:
+        ffn_own = [jnp.concatenate([own_gate_up, own_down])]
+    else:
+        ffn_own = [own_gate_up, own_down]
+    ffn_pieces = [lax.all_gather(value, "fsdp", axis=0) for value in ffn_own]
+
+    def flat(*pair):
+        return [value.reshape(tokens, feats) for value in pair]
+
+    def by_chip(value):
+        return value.reshape(chips, rows, feats)
+
+    x_zero, x_one = [inputs[:, b] for b in range(seqs)]
+    cot_all = [cotangent[:, b] for b in range(seqs)]
+    cots = [
+        lax.all_gather(c, PLANE, axis=0).reshape(chips, 2, rows, feats) for c in cot_all
+    ]
+    tables = [(rel_table, send_table, first[b], full[b]) for b in range(seqs)]
+
+    def forward(b, near, far):
         query, key, value, normed, sent, fine, logsum = attend_forward(
-            tables,
-            x_near.reshape(tokens, feats),
-            x_far.reshape(tokens, feats),
-            qkv,
-            gain_one,
-            start[b][:, None],
-            width,
+            tables[b], *flat(near, far), qkv, gain_one, start[b][:, None], width
         )
-        got = lax.all_to_all(sent.reshape(chips, 2 * rows, width), "chip", 0, 0)
-        attended = got.transpose(1, 0, 2).reshape(2 * rows, chips * width)
-        mixed = dot_nn(attended, out_half)
-        middle = x_own.astype(f32) + mixed[:rows] + swap_core(mixed[rows:])
+        return (query, key, value, fine, logsum), normed, sent.reshape(chips, 2 * rows, width)
+
+    def mid_norm(x_own, own, swapped):
+        middle = x_own.astype(f32) + own + swapped
+        return middle, (middle * row_scale(middle) * gain_two.astype(f32)).astype(bf16)
+
+    near_zero = spread(x_zero)
+    near_one = spread(hold(x_one, near_zero))
+    saved_zero, normed_zero, sent_zero = forward(0, near_zero, swap_core(near_zero))
+    near_one, out_pieces = hold((near_one, out_pieces), sent_zero)
+    got_zero = exchange(sent_zero)
+    saved_one, normed_one, sent_one = forward(1, near_one, swap_core(near_one))
+    got_zero = hold(got_zero, sent_one)
+    got_one = exchange(sent_one)
+    att_zero, own, other = mix(ids, got_zero, out_pieces)
+    mid_zero, norm_zero = mid_norm(x_zero, own, swap_core(other))
+    got_one = hold(got_one, norm_zero)
+    near_zero = spread(hold(norm_zero, got_one))
+    att_one, own, other = mix(ids, got_one, out_pieces)
+    mid_one, norm_one = mid_norm(x_one, own, swap_core(other))
+    near_zero = hold(near_zero, norm_one)
+    near_one = spread(hold(norm_one, near_zero))
+
+    def ffn(b, near, far, split):
+        mids = flat(near, far)
+        *out_part, mid_near, mid_far, hidden, grad_pre = feed_forward(
+            ids, mids, cots[b], ffn_pieces, hidden_width, split
+        )
+        return out_part, by_chip(mid_near), by_chip(mid_far), (*mids, cots[b], hidden, grad_pre)
+
+    out_zero, own_zero, far_zero, stream_zero = ffn(0, near_zero, swap_core(near_zero), False)
+    near_one = hold(near_one, stream_zero[3])
+    total_zero = core_sum(own_zero, swap_core(far_zero))
+    near_far = hold((near_one, swap_core(near_one)), total_zero)
+    out_one, own_one, far_one, stream_one = ffn(1, *near_far, True)
+    sums_zero = hold(exchange(total_zero), stream_one[3])
+    total_one = core_sum(own_one, swap_core(far_one))
+
+    out_sum_zero = lax.psum_scatter(
+        out_zero[0].reshape(groups * rows, feats), PLANE, scatter_dimension=0, tiled=True
+    )
+
+    def mid_backward(b, grad_normed_mid, middle):
         scale_two = row_scale(middle)
         unit_two = middle * scale_two
-        normed_mid = (unit_two * gain_two.astype(f32)).astype(bf16)
-        kept.append((x_own, query, key, value, normed, fine, logsum, attended, middle,
-                     scale_two, unit_two, normed_mid, tables))
-
-    for b in range(seqs):
-        (x_own, query, key, value, normed, fine, logsum, attended, middle,
-         scale_two, unit_two, normed_mid, tables) = kept[b]
-        cot_own = cotangent[:, b]
-        cots = gather_all(cot_own)
-        mids = gather_all(normed_mid)
-        out_parts, mid_parts = [], []
-        for cot, mid in zip(cots, mids):
-            cot = cot.reshape(tokens, feats)
-            mid = mid.reshape(tokens, feats)
-            pre = dot_nn(mid, gate_up)
-            gate_pre, up_pre = pre[:, :hidden_width], pre[:, hidden_width:]
-            sigma = jax.nn.sigmoid(gate_pre)
-            active = gate_pre * sigma
-            hidden = (active * up_pre).astype(bf16)
-            out_parts.append(dot_nn(hidden, down).astype(bf16).reshape(chips, rows, feats))
-            grad_hidden = dot_nt(cot, down)
-            grad_gate = grad_hidden * up_pre * sigma * (1.0 + gate_pre * (1.0 - sigma))
-            grad_up = grad_hidden * active
-            grad_pre = jnp.concatenate([grad_gate, grad_up], axis=1).astype(bf16)
-            mid_parts.append(dot_nt(grad_pre, gate_up).astype(bf16).reshape(chips, rows, feats))
-            grad_gate_up = grad_gate_up + dot_tn(mid, grad_pre)
-            grad_down = grad_down + dot_tn(hidden, cot)
-        grad_normed_mid = plane_reduce(*mid_parts)
-        outputs.append((middle + plane_reduce(*out_parts)).astype(bf16))
-        gain_sums_two = gain_sums_two + jnp.sum(grad_normed_mid * unit_two, axis=0)
         scaled_two = grad_normed_mid * gain_two.astype(f32)
-        grad_middle = cot_own.astype(f32) + scale_two * (
+        grad_middle = cot_all[b].astype(f32) + scale_two * (
             scaled_two - unit_two * jnp.mean(scaled_two * unit_two, axis=-1, keepdims=True)
         )
-        branch_own = grad_middle.astype(bf16)
-        branch = jnp.concatenate([branch_own, swap_core(branch_own)])
-        grad_att = dot_nt(branch, out_half).astype(bf16)
-        grad_out = grad_out + dot_tn(attended.astype(bf16), branch)
-        grad_sent = lax.all_to_all(
-            grad_att.reshape(2 * rows, chips, width).transpose(1, 0, 2), "chip", 0, 0
+        return grad_middle, grad_middle.astype(bf16)
+
+    def backward(b, saved, grad_got):
+        return attend_backward(
+            tables[b], saved, grad_got.reshape(seq_len, width), qkv, tiled[b][:, None, :]
         )
-        partial, grads = attend_backward(
-            tables,
-            (query, key, value, fine, logsum),
-            grad_sent.reshape(seq_len, width),
-            qkv,
-            tiled[b][:, None, :],
-        )
-        grad_qkv = grad_qkv + dot_tn(normed.reshape(seq_len, feats), grads)
-        parts = partial.reshape(2, chips, rows, feats)
-        grad_normed_in = plane_reduce(parts[0], parts[1])
+
+    def qkv_sums(normed, grads):
+        return dot_tn(normed.reshape(seq_len, feats), grads.reshape(seq_len, 3 * width))
+
+    def in_backward(grad_normed_in, grad_middle, x_own):
         flat_in = x_own.astype(f32)
         scale_one = row_scale(flat_in)
         unit_one = flat_in * scale_one
-        gain_sums_one = gain_sums_one + jnp.sum(grad_normed_in * unit_one, axis=0)
         scaled_one = grad_normed_in * gain_one.astype(f32)
-        grad_inputs.append(
-            (
-                grad_middle
-                + scale_one
-                * (scaled_one - unit_one * jnp.mean(scaled_one * unit_one, axis=-1, keepdims=True))
-            ).astype(bf16)
-        )
-
-    def to_shard(value):
-        return lax.psum_scatter(value.astype(bf16), "fsdp", scatter_dimension=0, tiled=True)
-
-    def collect(value):
-        return lax.all_gather(value, PLANE, axis=0)
+        return (
+            grad_middle
+            + scale_one
+            * (scaled_one - unit_one * jnp.mean(scaled_one * unit_one, axis=-1, keepdims=True))
+        ).astype(bf16)
+
+    grad_mid_zero, branch = mid_backward(0, last_sum(sums_zero), mid_zero)
+    grad_sent, grad_out_zero = unmix(ids, branch, swap_core(branch), att_zero, out_pieces, chips)
+    streams = hold((stream_zero, stream_one), grad_sent)
+    ffn_sums = weight_sums(ids, streams, shards)
+    grad_got_zero, out_sum_zero = hold((exchange(grad_sent), out_sum_zero), ffn_sums[0])
+    grad_got_zero = hold(grad_got_zero, out_sum_zero)
+    shares = [lax.psum_scatter(value, "fsdp", scatter_dimension=0) for value in ffn_sums]
+    sums_one = exchange(hold(total_one, grad_got_zero))
+    part_near, part_far, grads_zero = backward(0, saved_zero, grad_got_zero)
+    sums_one = hold(sums_one, grads_zero)
+    far_swapped = swap_core(by_chip(part_far))
+    grad_mid_one, branch = mid_backward(1, last_sum(sums_one), mid_one)
+    grad_sent, grad_out_one = unmix(ids, branch, swap_core(branch), att_one, out_pieces, chips)
+    grad_got_one = exchange(grad_sent)
+    far_swapped = hold(far_swapped, grad_sent)
+    total_zero = core_sum(by_chip(part_near), far_swapped)
+    sums_zero = exchange(hold(total_zero, grad_got_one))
 
     own_rows = feats // shards
-    s_gate_up = collect(to_shard(grad_gate_up))
-    s_gate_up = s_gate_up.reshape(groups, own_rows, 2, shards, per_shard)
-    g_gate_up = s_gate_up.transpose(2, 1, 3, 0, 4).reshape(2, own_rows, -1).astype(f32)
-    g_down = collect(to_shard(grad_down)).reshape(-1, feats).astype(f32)
-    s_qkv = collect(to_shard(grad_qkv)).reshape(groups, own_rows, 3, width)
-    g_qkv = s_qkv.transpose(2, 1, 0, 3).reshape(3, own_rows, feats).astype(f32)
-    part_out = lax.psum(to_shard(grad_out), "chip")
-    s_out = lax.all_gather(part_out.reshape(-1, width, feats), "core", axis=1)
-    g_out = s_out.reshape(own_rows, feats).astype(f32)
-    gain_sums = lax.psum(jnp.stack([gain_sums_one, gain_sums_two]), PLANE + ("fsdp",))
-    g_gains = lax.dynamic_slice_in_dim(gain_sums, lax.axis_index("fsdp") * own_rows, own_rows, 1)
+
+    def rel_rows(value):
+        value = value.astype(bf16)
+        count = value.shape[0] // shards
+        return [take(value, 0, ids[1] ^ r, count) for r in range(shards)]
+
+    out_rel = rel_rows(grad_out_zero + grad_out_one)
+    out_sent = send_pieces(out_rel)
+    grad_got_one, shares = hold((grad_got_one, shares), total_zero)
+    full_ffn = [lax.all_gather(share, PLANE, axis=0) for share in shares]
+    part_near, part_far, grads_one = backward(1, saved_one, grad_got_one)
+    part_near, part_far, grads_one, sums_zero, out_sent = lax.optimization_barrier(
+        (part_near, part_far, grads_one, sums_zero, out_sent)
+    )
+    far_swapped = swap_core(by_chip(part_far))
+    grad_qkv = qkv_sums(normed_zero, grads_zero) + qkv_sums(normed_one, grads_one)
+    far_swapped = hold(far_swapped, full_ffn)
+    sums_one = exchange(core_sum(by_chip(part_near), far_swapped))
+    out_near, out_far = [by_chip(part) for part in out_one]
+    total_out = hold(core_sum(out_near, swap_core(out_far)), sums_one)
+    out_sum_one = last_sum(exchange(total_out))
+    share_out = lax.all_gather(add_pieces(out_rel[0], out_sent), PLANE, axis=0).astype(f32)
+    full_qkv = lax.all_gather(shard_sum(rel_rows(grad_qkv)), PLANE, axis=0)
+
+    outputs = [
+        (mid_zero + out_sum_zero.astype(f32)).astype(bf16),
+        (mid_one + out_sum_one).astype(bf16),
+    ]
+    grad_inputs = [
+        in_backward(last_sum(sums_zero), grad_mid_zero, x_zero),
+        in_backward(last_sum(sums_one), grad_mid_one, x_one),
+    ]
+    g_gate_up, g_gain_two, (g_down,) = assemble(
+        full_ffn[0],
+        gain_ffn,
+        (w_gate, w_up),
+        shards,
+        full_ffn[-1],
+        own_rows if merged else 0,
+        per_shard,
+    )
+    g_down = g_down.reshape(-1, feats)
+    g_qkv, g_gain_one, _ = assemble(full_qkv, gain_attn, (w_query, w_key, w_value), 1)
+    share_out = share_out.reshape(chips, 2, -1, width, feats)
+    g_out = jnp.sum(share_out, axis=0).transpose(1, 0, 2, 3).reshape(own_rows, feats)
 
     return (
         jnp.stack(outputs, axis=1),
         jnp.stack(grad_inputs, axis=1),
-        g_qkv[0],
-        g_qkv[1],
-        g_qkv[2],
+        *g_qkv,
         g_out,
-        g_gate_up[0],
-        g_gate_up[1],
+        *g_gate_up,
         g_down,
-        g_gains[0],
-        g_gains[1],
+        g_gain_one,
+        g_gain_two,
     )
 
 

time: 813 us -> 603 us (0.74)
  Pallas kernels: 125 us -> 221 us
  matrix products: 104 us -> 12 us
  waiting for transfers between devices: 247 us -> 156 us
  blocking collectives: 71.4 us -> 0 us
  local copies, waits for them, and re-layouts: 109 us -> 49.1 us
    ppermute x48 -> x9, waiting for transfers between devices: 162 us -> 11.8 us  [swap_shard(): return lax.ppermute(value, 'fsdp', [(i, i ^ mask) for i in range(count)])]
    all_to_all x4 -> x13, waiting for transfers between devices: 9.47 us -> 114 us  [exchange(): return lax.all_to_all(value, 'chip', 0, 0)]
    pallas_call x2 -> x11, Pallas kernels: 63 us -> 159 us  [the longest x2 62.8 us: attend_backward(): pl.pallas_call(backward_kernel, out_shape=(shape((seq_len // 2, feats), b...]
    dot_general x20 -> x0, matrix products: 57.7 us -> none  [the longest x10 29.2 us: dot_nn(): lax.dot_general(left_op, right_op, (((1,), (0,)), ((), ())), preferred_el...]
    reduce_scatter x4 -> x2, waiting for transfers between devices: 46.1 us -> 0.01 us  [the longest x1 0.01 us: per_device(): lax.psum_scatter(value, 'fsdp', scatter_dimension=0)]
    all_to_all x4 -> x13, starting transfers between devices: 14.5 us -> 57.2 us  [exchange(): return lax.all_to_all(value, 'chip', 0, 0)]
    psum x1 -> x0, blocking collectives: 39.8 us -> none  [per_device(): lax.psum(jnp.stack([gain_sums_one, gain_sums_two]), PLANE + ('fsdp',))]
    ppermute x48 -> x9, starting transfers between devices: 51.9 us -> 14.1 us  [swap_shard(): return lax.ppermute(value, 'fsdp', [(i, i ^ mask) for i in range(count)])]
  transfers between devices with their start and end apart: 79 -> 44, of which waited for: 38 -> 16; matrix products, arithmetic and copies ran while one was open for 29% -> 18% of each run, Pallas kernels for 16% -> 37%
where the time goes in v2:
time: 603 us; the launch traced here: 593 us
  Pallas kernels  221 us (37%)
  waiting for transfers between devices  156 us (26%)
  starting transfers between devices  75 us (12%)
  other arithmetic  64.8 us (11%)
  local copies, waits for them, and re-layouts  49.1 us (8%)
  between operations  15.2 us (3%)
  matrix products  12 us (2%)
    all_to_all x13, waiting for transfers between devices, exchange(): return lax.all_to_all(value, 'chip', 0, 0)  114 us
    pallas_call x2, Pallas kernels, attend_backward(): pl.pallas_call(backward_kernel, out_shape=(shape((seq_len // 2, feats), b...  62.8 us
    pallas_call x2, Pallas kernels, attend_forward(): pl.pallas_call(forward_kernel, out_shape=(narrow, narrow, narrow, shape((...  61.8 us
    all_to_all x13, starting transfers between devices, exchange(): return lax.all_to_all(value, 'chip', 0, 0)  57.2 us
    pallas_call x2, Pallas kernels, feed_forward(): pl.pallas_call(functools.partial(ffn_kernel, split=split), grid_spec=pltp...  44.4 us
    all_gather x1, waiting for transfers between devices, per_device(): lax.all_gather(add_pieces(out_rel[0], out_sent), PLANE, axis=0).astype(f32)  25.6 us
    convert_element_type x5, other arithmetic, core_sum(): return (own.astype(f32) + swapped.astype(f32)).astype(bf16)  23.1 us
    pallas_call x1, Pallas kernels, weight_sums(): pl.pallas_call(functools.partial(weight_kernel, streams=len(streams), sha...  22.9 us
  transfers between devices with their start and end apart: 44, of which 16 were waited for; matrix products, arithmetic and copies ran while one was open for 18% of the time, Pallas kernels for 37%

profile of v2, /device:TPU:0, one launch (start us, length us, event | category | flops | bytes accessed | tf_op | source)
XLA Modules:
  0.0 592.9 jit_solution(2328350487419653167)
XLA Ops:
  8.4 5.1 collective-permute-start.3
  21.2 2.3 fusion.35
  25.9 4.5 all-to-all-start
  38.5 3.9 convert_reduce_fusion
  42.7 12.3 %all-to-all-done = bf16[4,256,1024]{2,1,0:T(8,128)(2,1)} async-done(((bf16[4,256,1024]{2,1,0:T(8,128)(2,1)}), bf16[4,256,1024]{2,1,0:T(8,128)(2,1)}, u32[]{:S(2)}, u32[]{:S(2)}) %all-to-all-start) | async-done | bytes 2097184 | tf_op jit(solution)/shard_map/all_to_all | solution.py:60
  63.8 4.5 all-to-all-start.2
  68.3 30.9 %attend_forward.2 = (bf16[2048,128]{1,0:T(8,128)(2,1)}, bf16[2048,128]{1,0:T(8,128)(2,1)}, bf16[2048,128]{1,0:T(8,128)(2,1)}, bf16[2,1024,1024]{2,1,0:T(8,128)(2...) custom-call(s32[16]{0:T(128)} %get-tuple-element.246.rel, s32[16]{0:T(128)} %get-tuple-element.245.send, ...), custom_call_target="tpu_custom_call" | custom-call | flops 31000000512 | bytes 1048576 | tf_op jit(solution)/shard_map/attend_forward/pallas_call | solution.py:449
  99.8 3.4 fusion.34
  107.1 4.0 all-to-all-start.1
  111.1 30.8 %attend_forward.3 = (bf16[2048,128]{1,0:T(8,128)(2,1)}, bf16[2048,128]{1,0:T(8,128)(2,1)}, bf16[2048,128]{1,0:T(8,128)(2,1)}, bf16[2,1024,1024]{2,1,0:T(8,128)(2...) custom-call(s32[16]{0:T(128)} %get-tuple-element.246.rel, s32[16]{0:T(128)} %get-tuple-element.245.send, ...), custom_call_target="tpu_custom_call" | custom-call | flops 31000000512 | bytes 1048576 | tf_op jit(solution)/shard_map/attend_forward/pallas_call | solution.py:449
  142.8 3.4 mix.2
  147.0 4.2 all-to-all-start.3
  154.2 6.3 %all-to-all-done.3.got = bf16[4,512,128]{2,1,0:T(8,128)(2,1)} async-done(((bf16[4,512,128]{2,1,0:T(8,128)(2,1)}), bf16[4,512,128]{2,1,0:T(8,128)(2,1)}, u32[]{:S(2)}, u32[]{:S(2)}) %all-to-all-start.3) | async-done | bytes 524320 | tf_op jit(solution)/shard_map/all_to_all | solution.py:60
  160.5 3.3 mix.3
  165.4 4.5 all-to-all-start.4
  172.9 28.4 %all-to-all-done.4 = bf16[4,256,1024]{2,1,0:T(8,128)(2,1)} async-done(((bf16[4,256,1024]{2,1,0:T(8,128)(2,1)}), bf16[4,256,1024]{2,1,0:T(8,128)(2,1)}, u32[]{:S(2)}, u32[]{:S(2)}) %all-to-all-start.4) | async-done | bytes 2097184 | tf_op jit(solution)/shard_map/all_to_all | solution.py:60
  203.0 4.5 all-to-all-start.6
  207.5 21.6 %feed_forward.2 = (bf16[4,2,256,1024]{3,2,1,0:T(8,128)(2,1)}, bf16[1024,1024]{1,0:T(8,128)(2,1)}, bf16[1024,1024]{1,0:T(8,128)(2,1)}, bf16[2048,512]{1,0:T(8,128)(2,1)}, bf16[2048,1024]{1,0:T(8,128)(2,1)}) custom-call(s32[2]{0:T(128)} %pad_add_fusion.ids, bf16[1024,1024]{1,0:T(8,128)(2,1)} %bitcast.20.x_near.refs_0_, ...), custom_call_target="tpu_custom_call" | custom-call | flops 20000000000 | bytes 1048576 | tf_op jit(solution)/shard_map/feed_forward/pallas_call | solution.py:550
  229.6 13.2 %all-to-all-done.6 = bf16[4,256,1024]{2,1,0:T(8,128)(2,1)} async-done(((bf16[4,256,1024]{2,1,0:T(8,128)(2,1)}), bf16[4,256,1024]{2,1,0:T(8,128)(2,1)}, u32[]{:S(2)}, u32[]{:S(2)}) %all-to-all-start.6) | async-done | bytes 2097184 | tf_op jit(solution)/shard_map/all_to_all | solution.py:60
  242.9 4.6 fusion.4
  247.5 4.5 all-to-all-start.5
  252.4 22.8 %feed_forward.3 = (bf16[1024,1024]{1,0:T(8,128)(2,1)}, bf16[1024,1024]{1,0:T(8,128)(2,1)}, bf16[1024,1024]{1,0:T(8,128)(2,1)}, bf16[1024,1024]{1,0:T(8,128)(2,1)...) custom-call(s32[2]{0:T(128)} %pad_add_fusion.ids, bf16[1024,1024]{1,0:T(8,128)(2,1)} %bitcast.26.x_near.refs_5_, ...), custom_call_target="tpu_custom_call" | custom-call | flops 20000000000 | bytes 1048576 | tf_op jit(solution)/shard_map/feed_forward/pallas_call | solution.py:550
  275.2 10.7 %all-to-all-done.5 = bf16[4,256,1024]{2,1,0:T(8,128)(2,1)} async-done(((bf16[4,256,1024]{2,1,0:T(8,128)(2,1)}), bf16[4,256,1024]{2,1,0:T(8,128)(2,1)}, u32[]{:S(2)}, u32[]{:S(2)}) %all-to-all-start.5) | async-done | bytes 2097184 | tf_op jit(solution)/shard_map/all_to_all | solution.py:60
  285.9 2.2 convert_reduce_fusion.6
  291.6 4.4 unmix.2
  296.0 22.9 %weight_sums.1 = bf16[4,384,1024]{2,1,0:T(8,128)(2,1)} custom-call(s32[2]{0:T(128)} %pad_add_fusion.ids, bf16[1024,1024]{1,0:T(8,128)(2,1)} %bitcast.20.x_near.refs_0_, bf16[1024,1024]{1,0:T(8,128)(2,1)} %bitcast.21.x_far.refs_1_, bf16[4,2,256,1024]{3,2,1,0:T(8,128)(2,1)} %bitcast.124, bf16[2048,512]{1,0:T(8,128)(2,1)} %get-tuple-element.136.refs_3_, ...), custom_call_target="tpu_custom_call" | custom-call | flops 23000000512 | bytes 1048576 | tf_op jit(solution)/shard_map/weight_sums/pallas_call | solution.py:609
  318.9 4.2 all-to-all-start.7
  323.1 4.8 fusion.2
  327.9 3.9 all-to-all-done.7
  331.8 4.6 all-to-all-start.8
  336.4 31.5 %attend_backward.2 = (bf16[1024,1024]{1,0:T(8,128)(2,1)}, bf16[1024,1024]{1,0:T(8,128)(2,1)}, bf16[2,1024,384]{2,1,0:T(8,128)(2,1)}) custom-call(s32[16]{0:T(128)} %get-tuple-element.246.rel, s32[16]{0:T(128)} %get-tuple-element.245.send, s32[8]{0:T(128)} %get-tuple-element.275.first, s32[8]{0:T(128)} %get-tuple-element.273.full, ...), custom_call_target="tpu_custom_call" | custom-call | flops 31000000512 | bytes 1048576 | tf_op jit(solution)/shard_map/attend_backward/pallas_call | solution.py:472
  367.9 2.2 convert_reduce_fusion.5
  373.9 4.4 unmix.3
  378.3 4.1 all-to-all-start.9
  382.5 4.5 fusion.1
  387.0 4.4 all-to-all-done.9
  391.5 6.4 %fusion.37 = f32[1024,384,1]{1,0,2:T(8,128)} fusion(bf16[2,1024,1024]{2,1,0:T(8,128)(2,1)} %get-tuple-element.181, bf16[2,1024,384]{2,1,0:T(8,128)(2,1)} %get-tuple-element.161), kind=kOutput, calls=%fused_computation.132 | convolution fusion | flops 1610612736 | bytes 7340032 | tf_op jit(solution)/shard_map/dot_general | solution.py:29
  400.3 3.3 collective-permute-start.17
  404.7 4.4 all-to-all-start.10
  409.4 31.4 %attend_backward.3 = (bf16[1024,1024]{1,0:T(8,128)(2,1)}, bf16[1024,1024]{1,0:T(8,128)(2,1)}, bf16[2,1024,384]{2,1,0:T(8,128)(2,1)}) custom-call(s32[16]{0:T(128)} %get-tuple-element.246.rel, s32[16]{0:T(128)} %get-tuple-element.245.send, s32[8]{0:T(128)} %get-tuple-element.276.first, s32[8]{0:T(128)} %get-tuple-element.274.full, ...), custom_call_target="tpu_custom_call" | custom-call | flops 31000000512 | bytes 1048576 | tf_op jit(solution)/shard_map/attend_backward/pallas_call | solution.py:472
  440.8 9.5 %all-to-all-done.10 = bf16[4,256,1024]{2,1,0:T(8,128)(2,1)} async-done(((bf16[4,256,1024]{2,1,0:T(8,128)(2,1)}), bf16[4,256,1024]{2,1,0:T(8,128)(2,1)}, u32[]{:S(2)}, u32[]{:S(2)}) %all-to-all-start.10) | async-done | bytes 2097184 | tf_op jit(solution)/shard_map/all_to_all | solution.py:60
  450.3 5.6 fusion.5
  458.4 2.6 collective-permute-start.21
  461.5 3.3 collective-permute-done.19
  464.8 2.3 collective-permute-done.21
  467.1 6.2 %collective-permute-done.20 = bf16[256,384]{1,0:T(8,128)(2,1)} collective-permute-done((bf16[256,384]{1,0:T(8,128)(2,1)}, bf16[256,384]{1,0:T(8,128)(2,1)}, u32[]{:S(2)}, u32[]{:S(2)}) %collective-permute-start.20) | collective-permute-done | bytes 196640 | tf_op jit(solution)/shard_map/ppermute | solution.py:47
  473.3 2.0 add_convert_fusion.4
  475.4 2.0 add_convert_fusion.3
  478.0 1.9 collective-permute-done.18
  479.9 4.6 fusion
  484.6 4.6 all-to-all-start.11
  489.2 4.5 fusion.3
  493.7 25.1 %all-to-all-done.11 = bf16[4,256,1024]{2,1,0:T(8,128)(2,1)} async-done(((bf16[4,256,1024]{2,1,0:T(8,128)(2,1)}), bf16[4,256,1024]{2,1,0:T(8,128)(2,1)}, u32[]{:S(2)}, u32[]{:S(2)}) %all-to-all-start.11) | async-done | bytes 2097184 | tf_op jit(solution)/shard_map/all_to_all | solution.py:60
  518.8 4.7 all-to-all-start.12
  523.6 3.1 convert_reduce_fusion.3
  526.6 4.2 assemble.2
  532.4 25.6 %all-gather.26.cloned.1.call-done = bf16[1024,1024]{1,0:T(8,128)(2,1)} async-done(((bf16[128,1024]{1,0:T(8,128)(2,1)}), bf16[1024,1024]{1,0:T(8,128)(2,1)}) %all-gather.26.cloned.1.call-update) | async-done | bytes 2097168 | tf_op jit(solution)/shard_map/all_gather | solution.py:864
  558.0 3.0 convert_reduce_fusion.1
  561.1 9.0 %assemble.3 = (f32[256,4096]{1,0:T(8,128)}, f32[256,4096]{1,0:T(8,128)}, f32[256,1]{1,0:T(8,128)}, f32[8,128,1024]{2,1,0:T(8,128)}) custom-call(bf16[8,384,1024]{2,1,0:T(8,128)(2,1)} %bitcast.102, bf16[256,1]{1,0:T(8,128)(2,1)} %copy-done.26, bf16[256,4096]{1,0:T(8,128)(2,1)} %refs_2_.3, bf16[256,4096]{1,0:T(8,128)(2,1)} %refs_3_.3, ...), custom_call_target="tpu_custom_call" | custom-call | tf_op jit(solution)/shard_map/assemble/pallas_call | solution.py:648
  571.6 2.3 convert_reduce_fusion.2
  577.3 2.3 convert_reduce_fusion.4
  579.6 2.1 fusion.27
  581.8 2.0 copy.80
  583.9 2.0 copy.79
  (224 shorter events, 66.0 us)
Async XLA Ops:
  7.2 30.2 %copy-start = (bf16[1024,1024]{1,0:T(8,128)(2,1)S(1)}, bf16[1024,1024]{1,0:T(8,128)(2,1)}, u32[]{:S(2)}) copy-start(bf16[1024,1024]{1,0:T(8,128)(2,1)} %param.20) | copy-start | bytes 6291460
  7.2 14.0 %copy-start.18 = (bf16[256,2,1024]{2,1,0:T(2,128)(2,1)S(1)}, bf16[256,2,1024]{2,1,0:T(2,128)(2,1)}, u32[]{:S(2)}) copy-start(bf16[256,2,1024]{2,1,0:T(2,128)(2,1)} %param.13) | copy-start | bytes 3145732
  7.2 53.1 %all-gather.14.cloned.1.call-start = ((), (), s32[]{:S(2)}) async-start(), calls=%async_computation.15 | async-start | bytes 1310720 | tf_op jit(solution)/shard_map/all_gather | solution.py:727
  8.4 15.1 %copy-start.33 = (bf16[128,1024]{1,0:T(8,128)(2,1)}, bf16[128,1024]{1,0:T(8,128)(2,1)S(1)}, u32[]{:S(2)}) copy-start(bf16[128,1024]{1,0:T(8,128)(2,1)S(1)} %dynamic-slice_bitcast_fusion.refs_0_) | copy-start | bytes 786436
  8.4 90.8 %collective-permute-start.3 = (bf16[128,1024]{1,0:T(8,128)(2,1)S(1)}, bf16[128,1024]{1,0:T(8,128)(2,1)}, u32[]{:S(2)}, u32[]{:S(2)}) collective-permute-start(bf16[128,1024]{1,0:T(8,128)(2,1)S(1)} %dynamic-slice_bitcast_fusion.refs_0_), channel_id=1, source_target_pairs={{0,3},{1,2},{2,1},{3,0},{4,7},{5,6},{6,5},{7,4},{8,11},{9,10},{10,... | collective-permute-start | bytes 786440 | tf_op jit(solution)/shard_map/ppermute | solution.py:47
  13.5 85.7 %collective-permute-start.2 = (bf16[128,1024]{1,0:T(8,128)(2,1)S(1)}, bf16[128,1024]{1,0:T(8,128)(2,1)}, u32[]{:S(2)}, u32[]{:S(2)}) collective-permute-start(bf16[128,1024]{1,0:T(8,128)(2,1)S(1)} %dynamic-slice_bitcast_fusion.refs_0_), channel_id=1, source_target_pairs={{0,2},{1,3},{2,0},{3,1},{4,6},{5,7},{6,4},{7,5},{8,10},{9,11},{10,... | collective-permute-start | bytes 786440 | tf_op jit(solution)/shard_map/ppermute | solution.py:47
  13.5 85.7 %collective-permute-start.1 = (bf16[128,1024]{1,0:T(8,128)(2,1)S(1)}, bf16[128,1024]{1,0:T(8,128)(2,1)}, u32[]{:S(2)}, u32[]{:S(2)}) collective-permute-start(bf16[128,1024]{1,0:T(8,128)(2,1)S(1)} %dynamic-slice_bitcast_fusion.refs_0_), channel_id=1, source_target_pairs={{0,1},{1,0},{2,3},{3,2},{4,5},{5,4},{6,7},{7,6},{8,9},{9,8},{10,11... | collective-permute-start | bytes 786440 | tf_op jit(solution)/shard_map/ppermute | solution.py:47
  14.9 8.6 %copy-start.27 = (bf16[256,1]{1,0:T(8,128)(2,1)}, bf16[256,1]{1,0:T(8,128)(2,1)S(1)}, u32[]{:S(2)}) copy-start(bf16[256,1]{1,0:T(8,128)(2,1)S(1)} %stack.44.refs_1_) | copy-start | bytes 1540
  15.7 7.8 %copy-start.26 = (bf16[256,1]{1,0:T(8,128)(2,1)}, bf16[256,1]{1,0:T(8,128)(2,1)S(1)}, u32[]{:S(2)}) copy-start(bf16[256,1]{1,0:T(8,128)(2,1)S(1)} %stack.45.refs_1_) | copy-start | bytes 1540
  24.3 127.9 %copy-start.13 = (bf16[256,1024]{1,0:T(8,128)(2,1)}, bf16[256,1024]{1,0:T(8,128)(2,1)S(1)}, u32[]{:S(2)}) copy-start(bf16[256,1024]{1,0:T(8,128)(2,1)S(1)} %get-tuple-element.250) | copy-start | bytes 1572868
  25.9 29.1 %all-to-all-start = ((bf16[4,256,1024]{2,1,0:T(8,128)(2,1)}), bf16[4,256,1024]{2,1,0:T(8,128)(2,1)}, u32[]{:S(2)}, u32[]{:S(2)}) async-start(bf16[4,256,1024]{2,1,0:T(8,128)(2,1)} %broadcast_in_dim.54), calls=%async_computation | async-start | bytes 4194304 | tf_op jit(solution)/shard_map/all_to_all | solution.py:60
  30.4 8.1 %copy-start.40 = (s32[2048,2]{0,1:T(2,128)S(1)}, s32[2048,2]{0,1:T(2,128)}, u32[]{:S(2)}) copy-start(s32[2048,2]{0,1:T(2,128)} %param.23) | copy-start | bytes 49156
  30.4 12.0 %copy-start.37 = (s32[16]{0:T(128)S(1)}, s32[16]{0:T(128)}, u32[]{:S(2)}) copy-start(s32[16]{0:T(128)} %param.24) | copy-start | bytes 196
  30.4 177.1 %all-gather.18.cloned.1.call-start = ((), (), s32[]{:S(2)}) async-start(), calls=%async_computation.19 | async-start | bytes 3932160 | tf_op jit(solution)/shard_map/all_gather | solution.py:735
  37.4 22.0 %copy-start.19 = (bf16[256,1,1024]{2,1,0:T(2,128)(2,1)S(1)}, bf16[256,1,1024]{2,1,0:T(2,128)(2,1)}, u32[]{:S(2)}) copy-start(bf16[256,1,1024]{2,1,0:T(2,128)(2,1)} %get-tuple-element.265) | copy-start | bytes 1572868
  55.0 13.3 %collective-permute-start = (bf16[4,256,1024]{2,1,0:T(8,128)(2,1)}, bf16[4,256,1024]{2,1,0:T(8,128)(2,1)}, u32[]{:S(2)}, u32[]{:S(2)}) collective-permute-start(bf16[4,256,1024]{2,1,0:T(8,128)(2,1)} %all-to-all-done), channel_id=1, source_target_pairs={{0,4},{4,0},{1,5},{5,1},{2,6},{6,2},{3,7},{7,3},{8,12},{12,8},{9,1... | collective-permute-start | bytes 6291464 | tf_op jit(solution)/shard_map/ppermute | solution.py:37
  60.3 110.7 %copy-start.10 = (bf16[256,1024]{1,0:T(8,128)(2,1)}, bf16[256,1024]{1,0:T(8,128)(2,1)S(1)}, u32[]{:S(2)}) copy-start(bf16[256,1024]{1,0:T(8,128)(2,1)S(1)} %get-tuple-element.104) | copy-start | bytes 1572868
  63.8 35.5 %all-to-all-start.2 = ((bf16[4,256,1024]{2,1,0:T(8,128)(2,1)}), bf16[4,256,1024]{2,1,0:T(8,128)(2,1)}, u32[]{:S(2)}, u32[]{:S(2)}) async-start(bf16[4,256,1024]{2,1,0:T(8,128)(2,1)} %broadcast_in_dim.56), calls=%async_computation.2 | async-start | bytes 4194304 | tf_op jit(solution)/shard_map/all_to_all | solution.py:60
  68.2 139.3 %all-gather.16.cloned.1.call-start = ((), (), s32[]{:S(2)}) async-start(), calls=%async_computation.18 | async-start | bytes 4718592 | tf_op jit(solution)/shard_map/all_gather | solution.py:746
  99.2 11.9 %collective-permute-start.4 = (bf16[4,256,1024]{2,1,0:T(8,128)(2,1)}, bf16[4,256,1024]{2,1,0:T(8,128)(2,1)}, u32[]{:S(2)}, u32[]{:S(2)}) collective-permute-start(bf16[4,256,1024]{2,1,0:T(8,128)(2,1)} %all-to-all-done.2), channel_id=1, source_target_pairs={{0,4},{4,0},{1,5},{5,1},{2,6},{6,2},{3,7},{7,3},{8,12},{12,8},{9,1... | collective-permute-start | bytes 6291464 | tf_op jit(solution)/shard_map/ppermute | solution.py:37
  103.2 66.7 %copy-start.4 = (bf16[256,1,1024]{2,1,0:T(2,128)(2,1)}, bf16[256,1,1024]{2,1,0:T(2,128)(2,1)S(1)}, u32[]{:S(2)}) copy-start(bf16[256,1,1024]{2,1,0:T(2,128)(2,1)S(1)} %get-tuple-element.262) | copy-start | bytes 1572868
  107.1 34.9 %all-to-all-start.1 = ((bf16[4,512,128]{2,1,0:T(8,128)(2,1)}), bf16[4,512,128]{2,1,0:T(8,128)(2,1)S(1)}, u32[]{:S(2)}, u32[]{:S(2)}) async-start(bf16[4,512,128]{2,1,0:T(8,128)(2,1)} %bitcast.114), calls=%async_computation.1 | async-start | bytes 1048576 | tf_op jit(solution)/shard_map/all_to_all | solution.py:60
  142.8 3.4 copy-start.28
  146.2 5.1 collective-permute-start.5
  147.0 13.4 %all-to-all-start.3 = ((bf16[4,512,128]{2,1,0:T(8,128)(2,1)}), bf16[4,512,128]{2,1,0:T(8,128)(2,1)}, u32[]{:S(2)}, u32[]{:S(2)}) async-start(bf16[4,512,128]{2,1,0:T(8,128)(2,1)} %bitcast.115), calls=%async_computation.3 | async-start | bytes 1048576 | tf_op jit(solution)/shard_map/all_to_all | solution.py:60
  163.8 7.2 %collective-permute-start.6 = (f32[256,1024]{1,0:T(8,128)}, f32[256,1024]{1,0:T(8,128)}, u32[]{:S(2)}, u32[]{:S(2)}) collective-permute-start(f32[256,1024]{1,0:T(8,128)} %get-tuple-element.117), channel_id=1, source_target_pairs={{0,4},{4,0},{1,5},{5,1},{2,6},{6,2},{3,7},{7,3},{8,12},{12,8},{9,1... | collective-permute-start | bytes 3145736 | tf_op jit(solution)/shard_map/ppermute | solution.py:37
  165.4 36.0 %all-to-all-start.4 = ((bf16[4,256,1024]{2,1,0:T(8,128)(2,1)}), bf16[4,256,1024]{2,1,0:T(8,128)(2,1)}, u32[]{:S(2)}, u32[]{:S(2)}) async-start(bf16[4,256,1024]{2,1,0:T(8,128)(2,1)} %broadcast_in_dim.92), calls=%async_computation.4 | async-start | bytes 4194304 | tf_op jit(solution)/shard_map/all_to_all | solution.py:60
  169.9 82.5 %all-gather.20.cloned.1.call-start = ((), (), s32[]{:S(2)}) async-start(), calls=%async_computation.20 | async-start | bytes 4718592 | tf_op jit(solution)/shard_map/all_gather | solution.py:746
  201.4 6.2 %collective-permute-start.7 = (bf16[4,256,1024]{2,1,0:T(8,128)(2,1)}, bf16[4,256,1024]{2,1,0:T(8,128)(2,1)}, u32[]{:S(2)}, u32[]{:S(2)}) collective-permute-start(bf16[4,256,1024]{2,1,0:T(8,128)(2,1)} %all-to-all-done.4), channel_id=1, source_target_pairs={{0,4},{4,0},{1,5},{5,1},{2,6},{6,2},{3,7},{7,3},{8,12},{12,8},{9,1... | collective-permute-start | bytes 6291464 | tf_op jit(solution)/shard_map/ppermute | solution.py:37
  203.0 39.9 %all-to-all-start.6 = ((bf16[4,256,1024]{2,1,0:T(8,128)(2,1)}), bf16[4,256,1024]{2,1,0:T(8,128)(2,1)}, u32[]{:S(2)}, u32[]{:S(2)}) async-start(bf16[4,256,1024]{2,1,0:T(8,128)(2,1)} %broadcast_in_dim.93), calls=%async_computation.6 | async-start | bytes 4194304 | tf_op jit(solution)/shard_map/all_to_all | solution.py:60
  207.4 124.3 %reduce-scatter.3.cloned.1.call-start = ((), (), s32[]{:S(2)}) async-start(), calls=%async_computation.16 | async-start | bytes 4718592 | tf_op jit(solution)/shard_map/reduce_scatter | solution.py:792
  229.1 13.7 %collective-permute-start.8 = (bf16[4,256,1024]{2,1,0:T(8,128)(2,1)}, bf16[4,256,1024]{2,1,0:T(8,128)(2,1)}, u32[]{:S(2)}, u32[]{:S(2)}) collective-permute-start(bf16[4,256,1024]{2,1,0:T(8,128)(2,1)} %bitcast.133), channel_id=1, source_target_pairs={{0,4},{4,0},{1,5},{5,1},{2,6},{6,2},{3,7},{7,3},{8,12},{12,8},{9,1... | collective-permute-start | bytes 6291464 | tf_op jit(solution)/shard_map/ppermute | solution.py:37
  242.8 9.5 %collective-permute-start.9 = (bf16[4,256,1024]{2,1,0:T(8,128)(2,1)}, bf16[4,256,1024]{2,1,0:T(8,128)(2,1)}, u32[]{:S(2)}, u32[]{:S(2)}) collective-permute-start(bf16[4,256,1024]{2,1,0:T(8,128)(2,1)} %all-to-all-done.6), channel_id=1, source_target_pairs={{0,4},{4,0},{1,5},{5,1},{2,6},{6,2},{3,7},{7,3},{8,12},{12,8},{9,1... | collective-permute-start | bytes 6291464 | tf_op jit(solution)/shard_map/ppermute | solution.py:37
  247.5 38.5 %all-to-all-start.5 = ((bf16[4,256,1024]{2,1,0:T(8,128)(2,1)}), bf16[4,256,1024]{2,1,0:T(8,128)(2,1)}, u32[]{:S(2)}, u32[]{:S(2)}) async-start(bf16[4,256,1024]{2,1,0:T(8,128)(2,1)} %fusion.4), calls=%async_computation.5 | async-start | bytes 4194304 | tf_op jit(solution)/shard_map/all_to_all | solution.py:60
  251.9 139.5 %reduce-scatter.5.cloned.1.call-start = ((), (), s32[]{:S(2)}) async-start(), calls=%async_computation.17 | async-start | bytes 3932160 | tf_op jit(solution)/shard_map/reduce_scatter | solution.py:830
  285.9 2.4 copy-start.8
  288.8 2.0 collective-permute-start.10
  288.9 34.2 %collective-permute-start.12 = (bf16[4,256,1024]{2,1,0:T(8,128)(2,1)}, bf16[4,256,1024]{2,1,0:T(8,128)(2,1)}, u32[]{:S(2)}, u32[]{:S(2)}) collective-permute-start(bf16[4,256,1024]{2,1,0:T(8,128)(2,1)} %bitcast.35), channel_id=1, source_target_pairs={{0,4},{4,0},{1,5},{5,1},{2,6},{6,2},{3,7},{7,3},{8,12},{12,8},{9,1... | collective-permute-start | bytes 6291464 | tf_op jit(solution)/shard_map/ppermute | solution.py:37
  318.9 12.8 %all-to-all-start.7 = ((bf16[4,512,128]{2,1,0:T(8,128)(2,1)}), bf16[4,512,128]{2,1,0:T(8,128)(2,1)}, u32[]{:S(2)}, u32[]{:S(2)}) async-start(bf16[4,512,128]{2,1,0:T(8,128)(2,1)} %get-tuple-element.129), calls=%async_computation.7 | async-start | bytes 1048576 | tf_op jit(solution)/shard_map/all_to_all | solution.py:60
  331.8 36.1 %all-to-all-start.8 = ((bf16[4,256,1024]{2,1,0:T(8,128)(2,1)}), bf16[4,256,1024]{2,1,0:T(8,128)(2,1)}, u32[]{:S(2)}, u32[]{:S(2)}) async-start(bf16[4,256,1024]{2,1,0:T(8,128)(2,1)} %fusion.2), calls=%async_computation.9 | async-start | bytes 4194304 | tf_op jit(solution)/shard_map/all_to_all | solution.py:60
  367.9 14.6 %collective-permute-start.14 = (bf16[4,256,1024]{2,1,0:T(8,128)(2,1)}, bf16[4,256,1024]{2,1,0:T(8,128)(2,1)}, u32[]{:S(2)}, u32[]{:S(2)}) collective-permute-start(bf16[4,256,1024]{2,1,0:T(8,128)(2,1)} %bitcast.132), channel_id=1, source_target_pairs={{0,4},{4,0},{1,5},{5,1},{2,6},{6,2},{3,7},{7,3},{8,12},{12,8},{9,1... | collective-permute-start | bytes 6291464 | tf_op jit(solution)/shard_map/ppermute | solution.py:37
  367.9 2.5 copy-start.5
  371.1 2.0 collective-permute-start.13
  378.3 13.2 %all-to-all-start.9 = ((bf16[4,512,128]{2,1,0:T(8,128)(2,1)}), bf16[4,512,128]{2,1,0:T(8,128)(2,1)}, u32[]{:S(2)}, u32[]{:S(2)}) async-start(bf16[4,512,128]{2,1,0:T(8,128)(2,1)} %get-tuple-element.164), calls=%async_computation.10 | async-start | bytes 1048576 | tf_op jit(solution)/shard_map/all_to_all | solution.py:60
  382.4 97.5 %all-gather.22.cloned.1.call-start = ((), (), s32[]{:S(2)}) async-start(), calls=%async_computation.21 | async-start | bytes 7077888 | tf_op jit(solution)/shard_map/all_gather | solution.py:852
  391.5 6.4 %copy-start.20 = (f32[512,1024]{1,0:T(8,128)S(1)}, f32[512,1024]{1,0:T(8,128)}, u32[]{:S(2)}) copy-start(f32[512,1024]{1,0:T(8,128)} %get-tuple-element.173) | copy-start | bytes 6291460
  391.5 6.4 %copy-start.21 = (f32[512,1024]{1,0:T(8,128)S(1)}, f32[512,1024]{1,0:T(8,128)}, u32[]{:S(2)}) copy-start(f32[512,1024]{1,0:T(8,128)} %get-tuple-element.174) | copy-start | bytes 6291460
  400.3 40.5 %collective-permute-start.17 = (bf16[128,1024]{1,0:T(8,128)(2,1)}, bf16[128,1024]{1,0:T(8,128)(2,1)S(1)}, u32[]{:S(2)}, u32[]{:S(2)}) collective-permute-start(bf16[128,1024]{1,0:T(8,128)(2,1)} %get-tuple-element.259), channel_id=1, source_target_pairs={{0,3},{1,2},{2,1},{3,0},{4,7},{5,6},{6,5},{7,4},{8,11},{9,10},{10,... | collective-permute-start | bytes 786440 | tf_op jit(solution)/shard_map/ppermute | solution.py:47
  403.6 37.1 %collective-permute-start.16 = (bf16[128,1024]{1,0:T(8,128)(2,1)}, bf16[128,1024]{1,0:T(8,128)(2,1)}, u32[]{:S(2)}, u32[]{:S(2)}) collective-permute-start(bf16[128,1024]{1,0:T(8,128)(2,1)} %get-tuple-element.260), channel_id=1, source_target_pairs={{0,2},{1,3},{2,0},{3,1},{4,6},{5,7},{6,4},{7,5},{8,10},{9,11},{10,... | collective-permute-start | bytes 786440 | tf_op jit(solution)/shard_map/ppermute | solution.py:47
  403.6 37.1 %collective-permute-start.15 = (bf16[128,1024]{1,0:T(8,128)(2,1)}, bf16[128,1024]{1,0:T(8,128)(2,1)}, u32[]{:S(2)}, u32[]{:S(2)}) collective-permute-start(bf16[128,1024]{1,0:T(8,128)(2,1)} %get-tuple-element.261), channel_id=1, source_target_pairs={{0,1},{1,0},{2,3},{3,2},{4,5},{5,4},{6,7},{7,6},{8,9},{9,8},{10,11... | collective-permute-start | bytes 786440 | tf_op jit(solution)/shard_map/ppermute | solution.py:47
  404.7 45.6 %all-to-all-start.10 = ((bf16[4,256,1024]{2,1,0:T(8,128)(2,1)}), bf16[4,256,1024]{2,1,0:T(8,128)(2,1)}, u32[]{:S(2)}, u32[]{:S(2)}) async-start(bf16[4,256,1024]{2,1,0:T(8,128)(2,1)} %fusion.1), calls=%async_computation.12 | async-start | bytes 4194304 | tf_op jit(solution)/shard_map/all_to_all | solution.py:60
  409.1 117.5 %all-gather.24.cloned.1.call-start = ((), (), s32[]{:S(2)}) async-start(), calls=%async_computation.22 | async-start | bytes 1769472 | tf_op jit(solution)/shard_map/all_gather | solution.py:865
  457.6 7.3 %collective-permute-start.19 = (bf16[256,384]{1,0:T(8,128)(2,1)}, bf16[256,384]{1,0:T(8,128)(2,1)}, u32[]{:S(2)}, u32[]{:S(2)}) collective-permute-start(bf16[256,384]{1,0:T(8,128)(2,1)} %get-tuple-element.266), channel_id=1, source_target_pairs={{0,1},{1,0},{2,3},{3,2},{4,5},{5,4},{6,7},{7,6},{8,9},{9,8},{10,11... | collective-permute-start | bytes 589832 | tf_op jit(solution)/shard_map/ppermute | solution.py:47
  458.4 8.8 %collective-permute-start.21 = (bf16[256,384]{1,0:T(8,128)(2,1)}, bf16[256,384]{1,0:T(8,128)(2,1)}, u32[]{:S(2)}, u32[]{:S(2)}) collective-permute-start(bf16[256,384]{1,0:T(8,128)(2,1)} %get-tuple-element.267), channel_id=1, source_target_pairs={{0,3},{1,2},{2,1},{3,0},{4,7},{5,6},{6,5},{7,4},{8,11},{9,10},{10,... | collective-permute-start | bytes 589832 | tf_op jit(solution)/shard_map/ppermute | solution.py:47
  460.9 12.3 %collective-permute-start.20 = (bf16[256,384]{1,0:T(8,128)(2,1)}, bf16[256,384]{1,0:T(8,128)(2,1)}, u32[]{:S(2)}, u32[]{:S(2)}) collective-permute-start(bf16[256,384]{1,0:T(8,128)(2,1)} %get-tuple-element.268), channel_id=1, source_target_pairs={{0,2},{1,3},{2,0},{3,1},{4,6},{5,7},{6,4},{7,5},{8,10},{9,11},{10,... | collective-permute-start | bytes 589832 | tf_op jit(solution)/shard_map/ppermute | solution.py:47
  475.3 82.7 %all-gather.26.cloned.1.call-start = ((), (), s32[]{:S(2)}) async-start(), calls=%async_computation.23 | async-start | bytes 2359296 | tf_op jit(solution)/shard_map/all_gather | solution.py:864
  475.4 4.6 collective-permute-start.18
  477.4 11.7 %collective-permute-start.11 = (bf16[4,256,1024]{2,1,0:T(8,128)(2,1)}, bf16[4,256,1024]{2,1,0:T(8,128)(2,1)}, u32[]{:S(2)}, u32[]{:S(2)}) collective-permute-start(bf16[4,256,1024]{2,1,0:T(8,128)(2,1)} %bitcast.130), channel_id=1, source_target_pairs={{0,4},{4,0},{1,5},{5,1},{2,6},{6,2},{3,7},{7,3},{8,12},{12,8},{9,1... | collective-permute-start | bytes 6291464 | tf_op jit(solution)/shard_map/ppermute | solution.py:37
  484.6 4.6 copy-start.35
  484.6 4.6 copy-start.36
  484.6 34.3 %all-to-all-start.11 = ((bf16[4,256,1024]{2,1,0:T(8,128)(2,1)}), bf16[4,256,1024]{2,1,0:T(8,128)(2,1)}, u32[]{:S(2)}, u32[]{:S(2)}) async-start(bf16[4,256,1024]{2,1,0:T(8,128)(2,1)} %fusion), calls=%async_computation.13 | async-start | bytes 4194304 | tf_op jit(solution)/shard_map/all_to_all | solution.py:60
  518.8 58.4 %all-to-all-start.12 = ((bf16[4,256,1024]{2,1,0:T(8,128)(2,1)}), bf16[4,256,1024]{2,1,0:T(8,128)(2,1)}, u32[]{:S(2)}, u32[]{:S(2)}) async-start(bf16[4,256,1024]{2,1,0:T(8,128)(2,1)} %fusion.3), calls=%async_computation.14 | async-start | bytes 4194304 | tf_op jit(solution)/shard_map/all_to_all | solution.py:60
  570.0 3.9 copy-start.34
  571.6 2.3 copy-start.15
  (21 other events, 33.4 us)
Sparse Core Ops, SparseCore 0:
  21.3 31.7 all-gather.13
  54.7 63.5 all-gather.17
  120.2 35.3 all-gather.15
  172.3 70.6 all-gather.19
  246.1 58.4 reduce-scatter.2
  319.0 60.2 reduce-scatter.4
  391.6 60.3 all-gather.21
  475.4 38.7 all-gather.23
  516.9 41.1 all-gather.25

commit v3 on v2

--- a/solution.py
+++ b/solution.py
@@ -11,6 +11,9 @@
 EPSILON = 1e-05
 MASKED = -1e30
 TILE = 256
+PROJ = 512
+Q_FORE, K_FORE = 512, 512
+Q_BACK, K_BACK = 512, 512
 PLANE = ("chip", "core")
 
 bf16 = jnp.bfloat16
@@ -60,8 +63,26 @@
     return lax.all_to_all(value, "chip", 0, 0)
 
 
+def add_kernel(own, other, total):
+    total[...] = (own[...].astype(f32) + other[...].astype(f32)).astype(bf16)
+
+
+def exchange_pieces(pieces):
+    return [pieces[0]] + [swap_chip(pieces[r], r) for r in range(1, len(pieces))]
+
+
 def core_sum(own, swapped):
-    return (own.astype(f32) + swapped.astype(f32)).astype(bf16)
+    chips, rows, width = own.shape
+    block = pl.BlockSpec((chips // 2, rows, width), lambda t: (t, 0, 0))
+    return pl.pallas_call(
+        add_kernel,
+        grid=(2,),
+        out_shape=jax.ShapeDtypeStruct(own.shape, bf16),
+        in_specs=[block, block],
+        out_specs=block,
+        cost_estimate=cost(3),
+        name="core_sum",
+    )(own, swapped)
 
 
 def last_sum(value):
@@ -74,6 +95,12 @@
 
 def shard_sum(pieces):
     return add_pieces(pieces[0], send_pieces(pieces))
+
+
+def in_order(pieces, shard):
+    stacked = jnp.stack(pieces)
+    rows = [lax.dynamic_index_in_dim(stacked, shard ^ z, keepdims=False) for z in range(len(pieces))]
+    return jnp.concatenate(rows)
 
 
 def send_pieces(pieces):
@@ -106,25 +133,26 @@
 
 def forward_kernel(
     rel, send, first, full, x_near, x_far, weight, gain, start,
-    query, key, value, normed, attended, fine, logsum,
-    scores, top, total,
+    query, key, value, normed, fine, logsum, *refs,
 ):
+    attended, (scores, top, total) = refs[:-3], refs[-3:]
     width = query.shape[1]
     seq_len = query.shape[0]
     heads = width // HEAD_DIM
     blk = TILE // 2
-    tiles = x_near.shape[0] // TILE
+    tiles = x_near.shape[0] // PROJ
+    blocks = PROJ // blk
     gain_row = gain[...].astype(f32)
     for s, source in ((0, x_near), (1, x_far)):
 
         def project(t, _, s=s, source=source):
-            rows = pl.ds(pl.multiple_of(t * TILE, TILE), TILE)
+            rows = pl.ds(pl.multiple_of(t * PROJ, PROJ), PROJ)
             rows_in = source[rows, :].astype(f32)
             tile = (rows_in * row_scale(rows_in) * gain_row).astype(bf16)
             normed[s, rows, :] = tile
             mixed = dot_nn(tile, weight[:, : 3 * width])
-            for h in range(2):
-                place = rel[(s * tiles + t) * 2 + h]
+            for h in range(blocks):
+                place = rel[(s * tiles + t) * blocks + h]
                 where = pl.ds(pl.multiple_of(place * blk, blk), blk)
                 part = mixed[h * blk : (h + 1) * blk]
                 query[where, :] = (part[:, :width].astype(bf16) * 0.125).astype(bf16)
@@ -134,26 +162,28 @@
 
         lax.fori_loop(0, tiles, project, 0)
 
-    masks = head_masks(TILE, width)
-    big = heads * TILE
+    masks = head_masks(Q_FORE, width)
+    big = heads * Q_FORE
 
     def query_tile(qb, _):
-        rows = pl.ds(pl.multiple_of(qb * TILE, TILE), TILE)
+        rows = pl.ds(pl.multiple_of(qb * Q_FORE, Q_FORE), Q_FORE)
         stacked = stack_heads(query[rows, :], masks)
         top[...] = jnp.full_like(top, MASKED)
         begin = jnp.concatenate([start[rows, :]] * heads, axis=0)
+        diagonal = qb * Q_FORE // K_FORE
+        last = (qb * Q_FORE + Q_FORE + K_FORE - 1) // K_FORE
 
         def score(kb, masked):
-            keys = key[pl.ds(pl.multiple_of(kb * TILE, TILE), TILE), :]
+            keys = key[pl.ds(pl.multiple_of(kb * K_FORE, K_FORE), K_FORE), :]
             raw = dot_nt(stacked, keys)
             if masked:
-                k_pos = kb * TILE + lax.broadcasted_iota(jnp.int32, (big, TILE), 1)
-                q_row = lax.broadcasted_iota(jnp.int32, (big, TILE), 0) & (TILE - 1)
-                allowed = (k_pos >= begin) & (k_pos <= qb * TILE + q_row)
+                k_pos = kb * K_FORE + lax.broadcasted_iota(jnp.int32, (big, K_FORE), 1)
+                q_row = lax.broadcasted_iota(jnp.int32, (big, K_FORE), 0) & (Q_FORE - 1)
+                allowed = (k_pos >= begin) & (k_pos <= qb * Q_FORE + q_row)
                 raw = jnp.where(allowed, raw, MASKED)
             scores[kb] = raw
             best = raw[:, :128]
-            for c in range(1, TILE // 128):
+            for c in range(1, K_FORE // 128):
                 best = jnp.maximum(best, raw[:, c * 128 : (c + 1) * 128])
             top[...] = jnp.maximum(top[...], best)
 
@@ -166,67 +196,65 @@
             return 0
 
         lax.fori_loop(first[qb], full[qb], masked_step, 0)
-        lax.fori_loop(full[qb], qb, plain_step, 0)
-        score(qb, True)
+        lax.fori_loop(full[qb], diagonal, plain_step, 0)
+        lax.fori_loop(diagonal, last, masked_step, 0)
         peak = jnp.max(top[...], axis=1, keepdims=True)
         top[...] = jnp.broadcast_to(peak, top.shape)
         total[...] = jnp.zeros_like(total)
 
         def weigh(kb, carry):
-            vals = value[pl.ds(pl.multiple_of(kb * TILE, TILE), TILE), :]
+            vals = value[pl.ds(pl.multiple_of(kb * K_FORE, K_FORE), K_FORE), :]
             pieces = []
             summed = total[...]
-            for c in range(TILE // 128):
+            for c in range(K_FORE // 128):
                 piece = jnp.exp(scores[kb, :, c * 128 : (c + 1) * 128] - top[...])
                 summed = summed + piece
                 pieces.append(piece.astype(bf16))
             total[...] = summed
             return carry + dot_nn(jnp.concatenate(pieces, axis=1), vals)
 
-        gathered = lax.fori_loop(first[qb], qb + 1, weigh, jnp.zeros((big, width), f32))
+        gathered = lax.fori_loop(first[qb], last, weigh, jnp.zeros((big, width), f32))
         denom = jnp.sum(total[...], axis=1, keepdims=True)
-        fine[rows, :] = merge_heads(gathered / denom, masks, TILE)
+        fine[rows, :] = merge_heads(gathered / denom, masks, Q_FORE)
         logs = jnp.broadcast_to(peak + jnp.log(denom), (big, width))
-        logsum[rows, :] = merge_heads(logs, masks, TILE)
+        logsum[rows, :] = merge_heads(logs, masks, Q_FORE)
         return 0
 
-    lax.fori_loop(0, seq_len // TILE, query_tile, 0)
-
-    def emit(j, _):
-        where = pl.ds(pl.multiple_of(send[j] * blk, blk), blk)
-        attended[pl.ds(pl.multiple_of(j * blk, blk), blk), :] = fine[where, :].astype(bf16)
-        return 0
-
-    lax.fori_loop(0, seq_len // blk, emit, 0)
+    lax.fori_loop(0, seq_len // Q_FORE, query_tile, 0)
+
+    count = seq_len // blk // len(attended)
+    for r, piece in enumerate(attended):
+        for j in range(count):
+            where = pl.ds(pl.multiple_of(send[r * count + j] * blk, blk), blk)
+            piece[j * blk : (j + 1) * blk, :] = fine[where, :].astype(bf16)
 
 
 def backward_kernel(
-    rel, send, first, full, query, key, value, fine, logsum, grad_in, weight, start,
-    part_near, part_far, grads,
-    grad_at, grad_q, grad_k, grad_v, grad_q2,
+    rel, send, first, full, query, key, value, fine, logsum, weight, start, *refs
 ):
+    grad_in, refs = refs[:-8], refs[-8:]
+    part_near, part_far, grads, grad_at, grad_q, grad_k, grad_v, grad_q2 = refs
     seq_len, width = query.shape
     heads = width // HEAD_DIM
     blk = TILE // 2
-    big = heads * TILE
-
-    def place(j, _):
-        where = pl.ds(pl.multiple_of(send[j] * blk, blk), blk)
-        grad_at[where, :] = grad_in[pl.ds(pl.multiple_of(j * blk, blk), blk), :]
-        return 0
-
-    lax.fori_loop(0, seq_len // blk, place, 0)
+    big = heads * Q_BACK
+
+    count = seq_len // blk // len(grad_in)
+    for r, piece in enumerate(grad_in):
+        for j in range(count):
+            where = pl.ds(pl.multiple_of(send[r * count + j] * blk, blk), blk)
+            grad_at[where, :] = piece[j * blk : (j + 1) * blk, :]
     grad_k[...] = jnp.zeros_like(grad_k)
     grad_v[...] = jnp.zeros_like(grad_v)
-    masks = head_masks(TILE, width)
+    masks = head_masks(Q_BACK, width)
 
     def flip(values):
         if width < 128:
-            values = jnp.concatenate([values, jnp.zeros((TILE, 128 - width), f32)], axis=1)
+            values = jnp.concatenate([values, jnp.zeros((Q_BACK, 128 - width), f32)], axis=1)
         return values.T
 
     def query_tile(qb, _):
-        rows = pl.ds(pl.multiple_of(qb * TILE, TILE), TILE)
+        rows = pl.ds(pl.multiple_of(qb * Q_BACK, Q_BACK), Q_BACK)
         stacked = stack_heads(query[rows, :], masks)
         grad_rows = grad_at[rows, :]
         grad_stacked = stack_heads(grad_rows, masks)
@@ -244,15 +272,17 @@
         )
         begin = jnp.concatenate([start[qb]] * heads, axis=1)
         grad_q2[...] = jnp.zeros_like(grad_q2)
+        diagonal = qb * Q_BACK // K_BACK
+        last = (qb * Q_BACK + Q_BACK + K_BACK - 1) // K_BACK
 
         def step(kb, masked):
-            where = pl.ds(pl.multiple_of(kb * TILE, TILE), TILE)
+            where = pl.ds(pl.multiple_of(kb * K_BACK, K_BACK), K_BACK)
             keys = key[where, :]
             probs = jnp.exp(dot_nt(keys, stacked) - log_row)
             if masked:
-                k_pos = kb * TILE + lax.broadcasted_iota(jnp.int32, (TILE, big), 0)
-                q_row = lax.broadcasted_iota(jnp.int32, (TILE, big), 1) & (TILE - 1)
-                allowed = (k_pos >= begin) & (k_pos <= qb * TILE + q_row)
+                k_pos = kb * K_BACK + lax.broadcasted_iota(jnp.int32, (K_BACK, big), 0)
+                q_row = lax.broadcasted_iota(jnp.int32, (K_BACK, big), 1) & (Q_BACK - 1)
+                allowed = (k_pos >= begin) & (k_pos <= qb * Q_BACK + q_row)
                 probs = jnp.where(allowed, probs, 0.0)
             slope = (probs * (dot_nt(value[where, :], grad_stacked) - delta)).astype(bf16)
             grad_v[where, :] += dot_nn(probs.astype(bf16), grad_stacked)
@@ -268,21 +298,22 @@
             return 0
 
         lax.fori_loop(first[qb], full[qb], masked_step, 0)
-        lax.fori_loop(full[qb], qb, plain_step, 0)
-        step(qb, True)
-        grad_q[rows, :] = (merge_heads(grad_q2[...], masks, TILE) * 0.125).astype(bf16)
+        lax.fori_loop(full[qb], diagonal, plain_step, 0)
+        lax.fori_loop(diagonal, last, masked_step, 0)
+        grad_q[rows, :] = (merge_heads(grad_q2[...], masks, Q_BACK) * 0.125).astype(bf16)
         return 0
 
-    lax.fori_loop(0, seq_len // TILE, query_tile, 0)
-
-    tiles = seq_len // TILE // 2
+    lax.fori_loop(0, seq_len // Q_BACK, query_tile, 0)
+
+    tiles = seq_len // PROJ // 2
+    blocks = PROJ // blk
 
     def project(t, side, part):
-        rows = pl.ds(pl.multiple_of(t * TILE, TILE), TILE)
+        rows = pl.ds(pl.multiple_of(t * PROJ, PROJ), PROJ)
         base = side * tiles + t
-        for h in range(2):
-            where = pl.ds(pl.multiple_of(rel[base * 2 + h] * blk, blk), blk)
-            here = pl.ds(pl.multiple_of(t * TILE + h * blk, blk), blk)
+        for h in range(blocks):
+            where = pl.ds(pl.multiple_of(rel[base * blocks + h] * blk, blk), blk)
+            here = pl.ds(pl.multiple_of(t * PROJ + h * blk, blk), blk)
             grads[side, here, :width] = grad_q[where, :]
             grads[side, here, width : 2 * width] = grad_k[where, :].astype(bf16)
             grads[side, here, 2 * width :] = grad_v[where, :].astype(bf16)
@@ -299,28 +330,60 @@
         target[pl.ds(at, count), :] = piece[begin : begin + count, :]
 
 
-def mix_kernel(ids, got, *refs):
-    pieces, (attended, own, other, weight) = refs[:-4], refs[-4:]
+def near_first(target, source, chip, count):
+    for r in range(count):
+        rows = target.shape[0] // count
+        at = pl.multiple_of((chip ^ r) * rows, rows)
+        target[r * rows : (r + 1) * rows, :] = source[pl.ds(at, rows), :]
+
+
+def mix_kernel(ids, *refs, chips):
+    got, pieces, (attended, own, other, whole, weight) = refs[:chips], refs[chips:-5], refs[-5:]
     rows = own.shape[0]
-    place_pieces(weight, pieces, ids[1], 0, pieces[0].shape[0])
-    joined = jnp.concatenate([got[p] for p in range(got.shape[0])], axis=1)
+    place_pieces(whole, pieces, ids[1], 0, pieces[0].shape[0])
+    near_first(weight, whole, ids[2], chips)
+    joined = jnp.concatenate([piece[...] for piece in got], axis=1)
     attended[...] = joined
     own[...] = dot_nn(joined[:rows], weight[...])
     other[...] = dot_nn(joined[rows:], weight[...])
 
 
-def unmix_kernel(ids, own, other, attended, *refs):
-    pieces, (grad_sent, grad_weight, weight) = refs[:-3], refs[-3:]
-    place_pieces(weight, pieces, ids[1], 0, pieces[0].shape[0])
+def unmix_kernel(ids, own, other, attended, *refs, chips):
+    outs = chips + 3
+    pieces, grad_sent, (grad_weight, whole, weight) = refs[:-outs], refs[-outs:-3], refs[-3:]
+    place_pieces(whole, pieces, ids[1], 0, pieces[0].shape[0])
+    near_first(weight, whole, ids[2], chips)
     branch = jnp.concatenate([own[...], other[...]], axis=0)
-    spread = dot_nt(branch, weight[...]).astype(bf16)
-    width = grad_sent.shape[2]
-    for p in range(grad_sent.shape[0]):
-        grad_sent[p] = spread[:, p * width : (p + 1) * width]
-    grad_weight[...] = dot_tn(attended[...], branch)
-
-
-def ffn_kernel(ids, x_near, x_far, cot_ref, *refs, split):
+    mixed = dot_nt(branch, weight[...]).astype(bf16)
+    sums = dot_tn(attended[...], branch)
+    width = grad_sent[0].shape[1]
+    for r in range(chips):
+        grad_sent[r][...] = mixed[:, r * width : (r + 1) * width]
+        at = pl.multiple_of((ids[2] ^ r) * width, width)
+        grad_weight[pl.ds(at, width), :] = sums[r * width : (r + 1) * width]
+
+
+def qkv_kernel(ids, *refs):
+    normed, grads, before = refs[:3]
+    outs, total = refs[3:-1], refs[-1]
+    t = pl.program_id(0)
+
+    @pl.when(t == 0)
+    def _():
+        total[...] = before[...]
+
+    total[...] += dot_tn(normed[...], grads[...])
+
+    @pl.when(t == pl.num_programs(0) - 1)
+    def _():
+        rows = outs[0].shape[0]
+        for r, out in enumerate(outs):
+            at = pl.multiple_of((ids[1] ^ r) * rows, rows)
+            out[...] = total[pl.ds(at, rows), :].astype(bf16)
+
+
+def ffn_kernel(ids, x_near, x_far, *refs, split, sides):
+    cot_refs, refs = refs[:sides], refs[sides:]
     outs = 7 + split
     pieces, out_parts = refs[:-outs], refs[-outs : 1 + split - outs]
     mid_near, mid_far, hidden, grad_pre, gate_up, down = refs[-6:]
@@ -338,7 +401,9 @@
             down[z * more : (z + 1) * more, :] = pieces[-1][z, begin : begin + more, :]
 
     tile = jnp.where(t < half, x_near[...], x_far[...])
-    cot = cot_ref[...].reshape(tile.shape)
+    cot = cot_refs[0][...].reshape(tile.shape)
+    if sides == 2:
+        cot = jnp.where(t < half, cot, cot_refs[1][...])
     pre = dot_nn(tile, gate_up[...])
     gate_pre, up_pre = pre[:, :size], pre[:, size:]
     sigma = jax.nn.sigmoid(gate_pre)
@@ -369,8 +434,9 @@
             out_parts[1][...] = out_part
 
 
-def weight_kernel(ids, *refs, streams, shards):
-    ins, outs, (wide, down) = refs[: 5 * streams], refs[5 * streams : -2], refs[-2:]
+def weight_kernel(ids, *refs, counts, shards):
+    streams = len(counts)
+    ins, outs, (wide, down) = refs[: sum(counts)], refs[sum(counts) : -2], refs[-2:]
     t = pl.program_id(0)
     per = pl.num_programs(0) // streams
 
@@ -380,13 +446,18 @@
         down[...] = jnp.zeros_like(down)
 
     for b in range(streams):
-        x_near, x_far, cot, hidden, grad_pre = ins[5 * b : 5 * b + 5]
+        mine = ins[sum(counts[:b]) : sum(counts[: b + 1])]
 
         @pl.when((t >= b * per) & (t < (b + 1) * per))
-        def _(b=b, x_near=x_near, x_far=x_far, cot=cot, hidden=hidden, grad_pre=grad_pre):
-            tile = jnp.where(t < b * per + per // 2, x_near[...], x_far[...])
+        def _(b=b, mine=mine):
+            x_near, x_far, hidden, grad_pre = mine[:4]
+            near = t < b * per + per // 2
+            tile = jnp.where(near, x_near[...], x_far[...])
+            cot = mine[4][...].reshape(tile.shape)
+            if len(mine) == 6:
+                cot = jnp.where(near, cot, mine[5][...])
             wide[...] += dot_tn(tile, grad_pre[...])
-            down[...] += dot_tn(hidden[...], cot[...].reshape(tile.shape))
+            down[...] += dot_tn(hidden[...], cot)
 
     @pl.when(t == pl.num_programs(0) - 1)
     def _():
@@ -438,21 +509,22 @@
 LIMIT = pltpu.CompilerParams(vmem_limit_bytes=56 * 2**20)
 
 
-def attend_forward(tables, x_near, x_far, weight, gain, start, width):
+def attend_forward(tables, x_near, x_far, weight, gain, start, width, chips):
     half_rows, feats = x_near.shape
     seq_len = 2 * half_rows
-    big = (width // HEAD_DIM) * TILE
+    big = (width // HEAD_DIM) * Q_FORE
     shape = jax.ShapeDtypeStruct
     narrow = shape((seq_len, width), bf16)
     wide = shape((seq_len, width), f32)
     pairs = seq_len * seq_len * width // 2
     return pl.pallas_call(
         forward_kernel,
-        out_shape=(narrow, narrow, narrow, shape((2, half_rows, feats), bf16), narrow, wide, wide),
+        out_shape=[narrow, narrow, narrow, shape((2, half_rows, feats), bf16), wide, wide]
+        + [shape((seq_len // chips, width), bf16)] * chips,
         in_specs=[smem()] * 4 + [vmem()] * 5,
-        out_specs=[vmem()] * 7,
+        out_specs=[vmem()] * (6 + chips),
         scratch_shapes=[
-            pltpu.VMEM((seq_len // TILE, big, TILE), f32),
+            pltpu.VMEM((seq_len // K_FORE, big, K_FORE), f32),
             pltpu.VMEM((big, 128), f32),
             pltpu.VMEM((big, 128), f32),
         ],
@@ -466,7 +538,7 @@
     query = saved[0]
     seq_len, width = query.shape
     feats = weight.shape[0]
-    big = (width // HEAD_DIM) * TILE
+    big = (width // HEAD_DIM) * Q_BACK
     shape = jax.ShapeDtypeStruct
     pairs = seq_len * seq_len * width // 2
     return pl.pallas_call(
@@ -476,7 +548,7 @@
             shape((seq_len // 2, feats), bf16),
             shape((2, seq_len // 2, 3 * width), bf16),
         ),
-        in_specs=[smem()] * 4 + [vmem()] * 8,
+        in_specs=[smem()] * 4 + [vmem()] * (7 + len(grad_in)),
         out_specs=[vmem()] * 3,
         scratch_shapes=[
             pltpu.VMEM((seq_len, width), bf16),
@@ -488,44 +560,46 @@
         compiler_params=LIMIT,
         cost_estimate=cost(31),
         name="attend_backward",
-    )(*tables, *saved, grad_in, weight, start)
+    )(*tables, *saved, weight, start, *grad_in)
 
 
 def mix(ids, got, pieces):
-    chips, doubled, width = got.shape
+    chips = len(got)
+    doubled, width = got[0].shape
     feats = pieces[0].shape[1]
     size = chips * width
     shape = jax.ShapeDtypeStruct
     return pl.pallas_call(
-        mix_kernel,
+        functools.partial(mix_kernel, chips=chips),
         out_shape=(
             shape((doubled, size), bf16),
             shape((doubled // 2, feats), f32),
             shape((doubled // 2, feats), f32),
         ),
-        in_specs=[smem()] + [vmem()] * (1 + len(pieces)),
+        in_specs=[smem()] + [vmem()] * (chips + len(pieces)),
         out_specs=[vmem()] * 3,
-        scratch_shapes=[pltpu.VMEM((size, feats), bf16)],
+        scratch_shapes=[pltpu.VMEM((size, feats), bf16)] * 2,
         compiler_params=LIMIT,
         cost_estimate=cost(3),
         name="mix",
-    )(ids, got, *pieces)
+    )(ids, *got, *pieces)
 
 
 def unmix(ids, own, other, attended, pieces, chips):
     rows, feats = own.shape
     size = attended.shape[1]
     shape = jax.ShapeDtypeStruct
-    return pl.pallas_call(
-        unmix_kernel,
-        out_shape=(shape((chips, 2 * rows, size // chips), bf16), shape((size, feats), f32)),
+    outs = pl.pallas_call(
+        functools.partial(unmix_kernel, chips=chips),
+        out_shape=[shape((2 * rows, size // chips), bf16)] * chips + [shape((size, feats), f32)],
         in_specs=[smem()] + [vmem()] * (3 + len(pieces)),
-        out_specs=[vmem()] * 2,
-        scratch_shapes=[pltpu.VMEM((size, feats), bf16)],
+        out_specs=[vmem()] * (chips + 1),
+        scratch_shapes=[pltpu.VMEM((size, feats), bf16)] * 2,
         compiler_params=LIMIT,
         cost_estimate=cost(4),
         name="unmix",
     )(ids, own, other, attended, *pieces)
+    return outs[:-1], outs[-1]
 
 
 ROWS = 512
@@ -533,7 +607,8 @@
 
 def feed_forward(ids, mids, cot, pieces, size, split):
     tokens, feats = mids[0].shape
-    chips, _, rows, _ = cot.shape
+    rows = ROWS // 2
+    chips = tokens // rows
     half = tokens // ROWS
     shape = jax.ShapeDtypeStruct
     near = pl.BlockSpec((ROWS, feats), lambda t, ids: (jnp.minimum(t, half - 1), 0))
@@ -542,17 +617,18 @@
         (ROWS // rows, None, rows, feats),
         lambda t, ids: (lax.rem(t, half), ids[0] ^ lax.div(t, half), 0, 0),
     )
+    cot_specs = [by_device] if len(cot) == 1 else [near, far]
 
     def tiles(width):
         return pl.BlockSpec((ROWS, width), lambda t, ids: (t, 0))
 
     side = shape((tokens, feats), bf16)
     return pl.pallas_call(
-        functools.partial(ffn_kernel, split=split),
+        functools.partial(ffn_kernel, split=split, sides=len(cot)),
         grid_spec=pltpu.PrefetchScalarGridSpec(
             num_scalar_prefetch=1,
             grid=(2 * half,),
-            in_specs=[near, far, by_device]
+            in_specs=[near, far, *cot_specs]
             + [pl.BlockSpec(piece.shape, lambda t, ids: (0, 0, 0)) for piece in pieces],
             out_specs=([near, far] if split else [by_device])
             + [near, far, tiles(size), tiles(2 * size)],
@@ -561,7 +637,7 @@
                 pltpu.VMEM((size, feats), bf16),
             ],
         ),
-        out_shape=([side, side] if split else [shape(cot.shape, bf16)])
+        out_shape=([side, side] if split else [shape((chips, 2, rows, feats), bf16)])
         + [
             side,
             side,
@@ -571,13 +647,13 @@
         compiler_params=LIMIT,
         cost_estimate=cost(20),
         name="feed_forward",
-    )(ids, *mids, cot, *pieces)
+    )(ids, *mids, *cot, *pieces)
 
 
 def weight_sums(ids, streams, shards):
     tokens, feats = streams[0][0].shape
-    size = streams[0][3].shape[1]
-    rows = streams[0][2].shape[2]
+    size = streams[0][2].shape[1]
+    rows = ROWS // 2
     half = tokens // ROWS
     per = 2 * half
     shape = jax.ShapeDtypeStruct
@@ -587,27 +663,29 @@
         def local(t, b=b):
             return jnp.clip(t - b * per, 0, per - 1)
 
+        near = pl.BlockSpec(
+            (ROWS, feats), lambda t, ids, f=local: (jnp.minimum(f(t), half - 1), 0)
+        )
+        far = pl.BlockSpec(
+            (ROWS, feats), lambda t, ids, f=local: (jnp.maximum(f(t) - half, 0), 0)
+        )
+        by_device = pl.BlockSpec(
+            (ROWS // rows, None, rows, feats),
+            lambda t, ids, f=local: (lax.rem(f(t), half), ids[0] ^ lax.div(f(t), half), 0, 0),
+        )
         specs += [
-            pl.BlockSpec((ROWS, feats), lambda t, ids, f=local: (jnp.minimum(f(t), half - 1), 0)),
-            pl.BlockSpec((ROWS, feats), lambda t, ids, f=local: (jnp.maximum(f(t) - half, 0), 0)),
-            pl.BlockSpec(
-                (ROWS // rows, None, rows, feats),
-                lambda t, ids, f=local: (
-                    lax.rem(f(t), half),
-                    ids[0] ^ lax.div(f(t), half),
-                    0,
-                    0,
-                ),
-            ),
+            near,
+            far,
             pl.BlockSpec((ROWS, size), lambda t, ids, f=local: (f(t), 0)),
             pl.BlockSpec((ROWS, 2 * size), lambda t, ids, f=local: (f(t), 0)),
         ]
+        specs += [by_device] if len(streams[b]) == 5 else [near, far]
     if 2 * size == feats:
         outs = [(shards, (feats + size) // shards, feats)]
     else:
         outs = [(shards, feats // shards, 2 * size), (shards, size // shards, feats)]
     return pl.pallas_call(
-        functools.partial(weight_kernel, streams=len(streams), shards=shards),
+        functools.partial(weight_kernel, counts=[len(v) for v in streams], shards=shards),
         grid_spec=pltpu.PrefetchScalarGridSpec(
             num_scalar_prefetch=1,
             grid=(per * len(streams),),
@@ -620,6 +698,56 @@
         cost_estimate=cost(23),
         name="weight_sums",
     )(ids, *[value for stream in streams for value in stream])
+
+
+def qkv_first(normed, grads):
+    tokens, feats = normed.shape
+    size = grads.shape[1]
+
+    def kernel(normed_ref, grads_ref, total):
+        @pl.when(pl.program_id(0) == 0)
+        def _():
+            total[...] = jnp.zeros_like(total)
+
+        total[...] += dot_tn(normed_ref[...], grads_ref[...])
+
+    return pl.pallas_call(
+        kernel,
+        grid=(tokens // ROWS,),
+        out_shape=jax.ShapeDtypeStruct((feats, size), f32),
+        in_specs=[
+            pl.BlockSpec((ROWS, feats), lambda t: (t, 0)),
+            pl.BlockSpec((ROWS, size), lambda t: (t, 0)),
+        ],
+        out_specs=pl.BlockSpec((feats, size), lambda t: (0, 0)),
+        compiler_params=LIMIT,
+        cost_estimate=cost(6),
+        name="qkv_first",
+    )(normed, grads)
+
+
+def qkv_sums(ids, normed, grads, before, shards):
+    tokens, feats = normed.shape
+    size = grads.shape[1]
+    out = (feats // shards, size)
+    return pl.pallas_call(
+        qkv_kernel,
+        grid_spec=pltpu.PrefetchScalarGridSpec(
+            num_scalar_prefetch=1,
+            grid=(tokens // ROWS,),
+            in_specs=[
+                pl.BlockSpec((ROWS, feats), lambda t, ids: (t, 0)),
+                pl.BlockSpec((ROWS, size), lambda t, ids: (t, 0)),
+                pl.BlockSpec((feats, size), lambda t, ids: (0, 0)),
+            ],
+            out_specs=[pl.BlockSpec(out, lambda t, ids: (0, 0))] * shards,
+            scratch_shapes=[pltpu.VMEM((feats, size), f32)],
+        ),
+        out_shape=[jax.ShapeDtypeStruct(out, bf16)] * shards,
+        compiler_params=LIMIT,
+        cost_estimate=cost(6),
+        name="qkv_sums",
+    )(ids, normed, grads, before)
 
 
 STEPS = 4
@@ -678,11 +806,22 @@
     blk = rows // 2
     tokens = chips * rows
 
-    ids = jnp.stack([core, lax.axis_index("fsdp")]).astype(jnp.int32)
+    def take(weight, axis, index, size):
+        return lax.dynamic_slice_in_dim(weight, index * size, size, axis)
+
+    x_zero, x_one = [inputs[:, b] for b in range(seqs)]
+    x_spread = jnp.broadcast_to(x_zero, (chips,) + x_zero.shape)
+    near_zero = exchange(x_spread)
+    w_query, w_key, w_value, w_out, w_gate, w_up, w_down, segments, deal_order = hold(
+        (w_query, w_key, w_value, w_out, w_gate, w_up, w_down, segments, deal_order), x_spread
+    )
+
+    ids = jnp.stack([core, lax.axis_index("fsdp"), chip]).astype(jnp.int32)
     pair = jnp.arange(2, dtype=jnp.int32)
     rel_dev = (jnp.arange(chips, dtype=jnp.int32)[None, :] * 2) + (pair[:, None] ^ core)
     rel_slot = (rel_dev[:, :, None] * 2 + pair[None, None, :]).reshape(-1)
-    send_dev = jnp.arange(chips, dtype=jnp.int32)[:, None] * 2 + (pair[None, :] ^ core)
+    near_chips = jnp.arange(chips, dtype=jnp.int32) ^ chip
+    send_dev = near_chips[:, None] * 2 + (pair[None, :] ^ core)
     send_slot = (send_dev[:, :, None] * 2 + pair[None, None, :]).reshape(-1)
     spots = jnp.arange(blocks, dtype=jnp.int32)
 
@@ -700,15 +839,16 @@
         axis=1,
     ).astype(jnp.int32)
     start = start.transpose(2, 0, 1).reshape(seqs, seq_len)
-    tiles = seq_len // TILE
-    tiled = start.reshape(seqs, tiles, TILE)
-    first = tiled[:, :, 0] // TILE
-    full = jnp.minimum(
-        jnp.arange(tiles, dtype=jnp.int32)[None, :], (tiled[:, :, -1] + TILE - 1) // TILE
-    )
-
-    def take(weight, axis, index, size):
-        return lax.dynamic_slice_in_dim(weight, index * size, size, axis)
+
+    def ranges(q_rows, k_rows):
+        tiled = start.reshape(seqs, seq_len // q_rows, q_rows)
+        begins = jnp.arange(seq_len // q_rows, dtype=jnp.int32) * q_rows // k_rows
+        first = tiled[:, :, 0] // k_rows
+        full = jnp.minimum(begins[None, :], (tiled[:, :, -1] + k_rows - 1) // k_rows)
+        return tiled, first, full
+
+    _, first, full = ranges(Q_FORE, K_FORE)
+    tiled, first_back, full_back = ranges(Q_BACK, K_BACK)
 
     both = jnp.stack([gain_attn, gain_ffn], axis=1)
     spare = jnp.zeros((both.shape[0], -(3 * width + 2) % 128), bf16)
@@ -724,70 +864,86 @@
     out_grid = w_out.reshape(-1, 2, width, feats)
     own_out = take(out_grid, 1, core, 1).reshape(-1, feats)
 
-    qkv = lax.all_gather(own_qkv, "fsdp", axis=0, tiled=True)
-    gain_one, gain_two = qkv[:, 3 * width][None, :], qkv[:, 3 * width + 1][None, :]
-    out_pieces = shard_pieces(own_out)
     merged = 2 * hidden_width == feats
     if merged:
         ffn_own = [jnp.concatenate([own_gate_up, own_down])]
     else:
         ffn_own = [own_gate_up, own_down]
-    ffn_pieces = [lax.all_gather(value, "fsdp", axis=0) for value in ffn_own]
-
+    qkv_pieces = shard_pieces(own_qkv)
+    x_spread_one = jnp.broadcast_to(x_one, (chips,) + x_one.shape)
+    cot_all = [cotangent[:, b] for b in range(seqs)]
+    (
+        near_zero, qkv_pieces, start, tiled, first, full, first_back, full_back, rel_table, send_table,
+        x_spread_one, cot_all, own_out, ffn_own,
+    ) = hold(
+        (
+            near_zero, qkv_pieces, start, tiled, first, full, first_back, full_back, rel_table, send_table,
+            x_spread_one, cot_all, own_out, ffn_own,
+        )
+    )
+    qkv = in_order(qkv_pieces, ids[1])
+    gain_one, gain_two = qkv[:, 3 * width][None, :], qkv[:, 3 * width + 1][None, :]
     def flat(*pair):
         return [value.reshape(tokens, feats) for value in pair]
 
     def by_chip(value):
         return value.reshape(chips, rows, feats)
 
-    x_zero, x_one = [inputs[:, b] for b in range(seqs)]
-    cot_all = [cotangent[:, b] for b in range(seqs)]
-    cots = [
-        lax.all_gather(c, PLANE, axis=0).reshape(chips, 2, rows, feats) for c in cot_all
-    ]
+    def spread_cot(own):
+        return lax.all_gather(own, PLANE, axis=0).reshape(chips, 2, rows, feats)
+
     tables = [(rel_table, send_table, first[b], full[b]) for b in range(seqs)]
+    tables_back = [(rel_table, send_table, first_back[b], full_back[b]) for b in range(seqs)]
 
     def forward(b, near, far):
-        query, key, value, normed, sent, fine, logsum = attend_forward(
-            tables[b], *flat(near, far), qkv, gain_one, start[b][:, None], width
+        query, key, value, normed, fine, logsum, *sent = attend_forward(
+            tables[b], *flat(near, far), qkv, gain_one, start[b][:, None], width, chips
         )
-        return (query, key, value, fine, logsum), normed, sent.reshape(chips, 2 * rows, width)
+        return (query, key, value, fine, logsum), normed, sent
 
     def mid_norm(x_own, own, swapped):
         middle = x_own.astype(f32) + own + swapped
         return middle, (middle * row_scale(middle) * gain_two.astype(f32)).astype(bf16)
 
-    near_zero = spread(x_zero)
-    near_one = spread(hold(x_one, near_zero))
+    near_one = exchange(x_spread_one)
+    out_pieces = shard_pieces(own_out)
+    ffn_pieces = [lax.all_gather(value, "fsdp", axis=0) for value in ffn_own]
     saved_zero, normed_zero, sent_zero = forward(0, near_zero, swap_core(near_zero))
-    near_one, out_pieces = hold((near_one, out_pieces), sent_zero)
-    got_zero = exchange(sent_zero)
+    near_one, sent_zero, out_pieces, cot_zero, cot_one = hold(
+        (near_one, sent_zero, out_pieces, cot_all[0], cot_all[1])
+    )
+    near_cot = spread(cot_zero)
+    got_zero = exchange_pieces(sent_zero)
     saved_one, normed_one, sent_one = forward(1, near_one, swap_core(near_one))
-    got_zero = hold(got_zero, sent_one)
-    got_one = exchange(sent_one)
+    got_zero, sent_one, near_cot = hold((got_zero, sent_one, near_cot))
+    got_one = exchange_pieces(sent_one)
     att_zero, own, other = mix(ids, got_zero, out_pieces)
     mid_zero, norm_zero = mid_norm(x_zero, own, swap_core(other))
-    got_one = hold(got_one, norm_zero)
-    near_zero = spread(hold(norm_zero, got_one))
-    att_one, own, other = mix(ids, got_one, out_pieces)
+    norm_zero, got_one = hold((norm_zero, got_one))
+    near_zero = spread(norm_zero)
+    att_one, own, other = mix(ids, hold(got_one, near_zero), out_pieces)
     mid_one, norm_one = mid_norm(x_one, own, swap_core(other))
-    near_zero = hold(near_zero, norm_one)
-    near_one = spread(hold(norm_one, near_zero))
+    near_one = spread(norm_one)
+    cots = (flat(near_cot, swap_core(near_cot)), [spread_cot(hold(cot_one, near_zero))])
 
     def ffn(b, near, far, split):
         mids = flat(near, far)
         *out_part, mid_near, mid_far, hidden, grad_pre = feed_forward(
             ids, mids, cots[b], ffn_pieces, hidden_width, split
         )
-        return out_part, by_chip(mid_near), by_chip(mid_far), (*mids, cots[b], hidden, grad_pre)
+        return out_part, by_chip(mid_near), by_chip(mid_far), (*mids, hidden, grad_pre, *cots[b])
 
     out_zero, own_zero, far_zero, stream_zero = ffn(0, near_zero, swap_core(near_zero), False)
-    near_one = hold(near_one, stream_zero[3])
+    near_one = hold(near_one, stream_zero[2])
     total_zero = core_sum(own_zero, swap_core(far_zero))
     near_far = hold((near_one, swap_core(near_one)), total_zero)
     out_one, own_one, far_one, stream_one = ffn(1, *near_far, True)
-    sums_zero = hold(exchange(total_zero), stream_one[3])
-    total_one = core_sum(own_one, swap_core(far_one))
+    sums_zero = hold(exchange(total_zero), stream_one[2])
+    far_one = swap_core(far_one)
+    ffn_sums = weight_sums(ids, (stream_zero, stream_one), shards)
+    shares = [lax.psum_scatter(value, "fsdp", scatter_dimension=0) for value in ffn_sums]
+    sums_zero, far_one = hold((sums_zero, far_one), ffn_sums[0])
+    total_one = core_sum(own_one, far_one)
 
     out_sum_zero = lax.psum_scatter(
         out_zero[0].reshape(groups * rows, feats), PLANE, scatter_dimension=0, tiled=True
@@ -804,11 +960,11 @@
 
     def backward(b, saved, grad_got):
         return attend_backward(
-            tables[b], saved, grad_got.reshape(seq_len, width), qkv, tiled[b][:, None, :]
+            tables_back[b], saved, grad_got, qkv, tiled[b][:, None, :]
         )
 
-    def qkv_sums(normed, grads):
-        return dot_tn(normed.reshape(seq_len, feats), grads.reshape(seq_len, 3 * width))
+    def qkv_stream(normed, grads):
+        return normed.reshape(seq_len, feats), grads.reshape(seq_len, 3 * width)
 
     def in_backward(grad_normed_in, grad_middle, x_own):
         flat_in = x_own.astype(f32)
@@ -823,21 +979,18 @@
 
     grad_mid_zero, branch = mid_backward(0, last_sum(sums_zero), mid_zero)
     grad_sent, grad_out_zero = unmix(ids, branch, swap_core(branch), att_zero, out_pieces, chips)
-    streams = hold((stream_zero, stream_one), grad_sent)
-    ffn_sums = weight_sums(ids, streams, shards)
-    grad_got_zero, out_sum_zero = hold((exchange(grad_sent), out_sum_zero), ffn_sums[0])
-    grad_got_zero = hold(grad_got_zero, out_sum_zero)
-    shares = [lax.psum_scatter(value, "fsdp", scatter_dimension=0) for value in ffn_sums]
-    sums_one = exchange(hold(total_one, grad_got_zero))
+    total_one = hold(total_one, grad_sent)
+    grad_got_zero = hold(exchange_pieces(grad_sent), out_sum_zero)
+    sums_one = exchange(total_one)
     part_near, part_far, grads_zero = backward(0, saved_zero, grad_got_zero)
     sums_one = hold(sums_one, grads_zero)
     far_swapped = swap_core(by_chip(part_far))
     grad_mid_one, branch = mid_backward(1, last_sum(sums_one), mid_one)
     grad_sent, grad_out_one = unmix(ids, branch, swap_core(branch), att_one, out_pieces, chips)
-    grad_got_one = exchange(grad_sent)
+    grad_got_one = exchange_pieces(grad_sent)
     far_swapped = hold(far_swapped, grad_sent)
     total_zero = core_sum(by_chip(part_near), far_swapped)
-    sums_zero = exchange(hold(total_zero, grad_got_one))
+    sums_zero = exchange(total_zero)
 
     own_rows = feats // shards
 
@@ -851,27 +1004,15 @@
     grad_got_one, shares = hold((grad_got_one, shares), total_zero)
     full_ffn = [lax.all_gather(share, PLANE, axis=0) for share in shares]
     part_near, part_far, grads_one = backward(1, saved_one, grad_got_one)
-    part_near, part_far, grads_one, sums_zero, out_sent = lax.optimization_barrier(
+    part_near, part_far, grads_one, sums_zero, out_sent = hold(
         (part_near, part_far, grads_one, sums_zero, out_sent)
     )
-    far_swapped = swap_core(by_chip(part_far))
-    grad_qkv = qkv_sums(normed_zero, grads_zero) + qkv_sums(normed_one, grads_one)
-    far_swapped = hold(far_swapped, full_ffn)
-    sums_one = exchange(core_sum(by_chip(part_near), far_swapped))
-    out_near, out_far = [by_chip(part) for part in out_one]
-    total_out = hold(core_sum(out_near, swap_core(out_far)), sums_one)
-    out_sum_one = last_sum(exchange(total_out))
-    share_out = lax.all_gather(add_pieces(out_rel[0], out_sent), PLANE, axis=0).astype(f32)
-    full_qkv = lax.all_gather(shard_sum(rel_rows(grad_qkv)), PLANE, axis=0)
-
-    outputs = [
-        (mid_zero + out_sum_zero.astype(f32)).astype(bf16),
-        (mid_one + out_sum_one).astype(bf16),
-    ]
-    grad_inputs = [
-        in_backward(last_sum(sums_zero), grad_mid_zero, x_zero),
-        in_backward(last_sum(sums_one), grad_mid_one, x_one),
-    ]
+    total_one = core_sum(by_chip(part_near), swap_core(by_chip(part_far)))
+    qkv_one = qkv_first(*qkv_stream(normed_one, grads_one))
+    total_one, qkv_one, grads_zero = hold((total_one, qkv_one, grads_zero))
+    sums_one = exchange(total_one)
+    grad_qkv = qkv_sums(ids, *qkv_stream(normed_zero, grads_zero), qkv_one, shards)
+    own_rows = feats // shards
     g_gate_up, g_gain_two, (g_down,) = assemble(
         full_ffn[0],
         gain_ffn,
@@ -882,6 +1023,28 @@
         per_shard,
     )
     g_down = g_down.reshape(-1, feats)
+    sums_one, g_gate_up, g_gain_two, g_down = hold((sums_one, g_gate_up, g_gain_two, g_down))
+    out_near, out_far = [by_chip(part) for part in out_one]
+    total_out = core_sum(out_near, swap_core(out_far))
+    share_qkv = add_pieces(grad_qkv[0], send_pieces(grad_qkv))
+    near_qkv = spread(hold(share_qkv, sums_one))
+    sums_out = exchange(hold(total_out, near_qkv))
+    share_out = lax.all_gather(add_pieces(out_rel[0], out_sent), PLANE, axis=0)
+    share_out = share_out.astype(f32)
+
+    outputs = [
+        (mid_zero + out_sum_zero.astype(f32)).astype(bf16),
+        (mid_one + last_sum(sums_out)).astype(bf16),
+    ]
+    grad_inputs = [
+        in_backward(last_sum(sums_zero), grad_mid_zero, x_zero),
+        in_backward(last_sum(sums_one), grad_mid_one, x_one),
+    ]
+    far_qkv = swap_core(near_qkv)
+    full_qkv = jnp.stack(
+        [jnp.where(core == 0, near_qkv, far_qkv), jnp.where(core == 0, far_qkv, near_qkv)], axis=1
+    )
+    full_qkv = full_qkv.reshape(groups, own_rows, 3 * width)
     g_qkv, g_gain_one, _ = assemble(full_qkv, gain_attn, (w_query, w_key, w_value), 1)
     share_out = share_out.reshape(chips, 2, -1, width, feats)
     g_out = jnp.sum(share_out, axis=0).transpose(1, 0, 2, 3).reshape(own_rows, feats)

time: 603 us -> 521 us (0.86)
  waiting for transfers between devices: 156 us -> 63 us
  blocking collectives: 0 us -> 40 us
  other arithmetic: 64.8 us -> 45.5 us
  matrix products: 12 us -> 0 us
    all_to_all x13 -> x10, waiting for transfers between devices: 114 us -> 31.1 us  [exchange(): return lax.all_to_all(value, 'chip', 0, 0)]
    all_to_all x0 -> x1, blocking collectives: none -> 40 us  [exchange(): return lax.all_to_all(value, 'chip', 0, 0)]
    all_gather x5 -> x2, waiting for transfers between devices: 25.6 us -> 0.02 us  [the longest x1 0.02 us: spread_cot(): return lax.all_gather(own, PLANE, axis=0).reshape(chips, 2, rows, feats)]
    convert_element_type x5 -> x0, other arithmetic: 23.1 us -> none  [core_sum(): return (own.astype(f32) + swapped.astype(f32)).astype(bf16)]
    pallas_call x9 -> x16, Pallas kernels: 145 us -> 160 us  [the longest x2 45.9 us: attend_forward(): pl.pallas_call(forward_kernel, out_shape=[narrow, narrow, narrow, shape((...]
    ppermute x0 -> x12, starting transfers between devices: none -> 14 us  [swap_chip(): return lax.ppermute(value, 'chip', [(i, i ^ mask) for i in range(count)])]
    all_to_all x13 -> x10, starting transfers between devices: 57.2 us -> 45.1 us  [exchange(): return lax.all_to_all(value, 'chip', 0, 0)]
    dot_general x2 -> x0, matrix products: 12 us -> none  [dot_tn(): lax.dot_general(left_op, right_op, (((0,), (0,)), ((), ())), preferred_el...]
  transfers between devices with their start and end apart: 44 -> 55, of which waited for: 16 -> 14; matrix products, arithmetic and copies ran while one was open for 18% -> 13% of each run, Pallas kernels for 37% -> 44%
where the time goes in v3:
time: 521 us; the launch traced here: 515 us
  Pallas kernels  226 us (43%)
  starting transfers between devices  80.8 us (16%)
  waiting for transfers between devices  63 us (12%)
  other arithmetic  45.5 us (9%)
  local copies, waits for them, and re-layouts  43.6 us (8%)
  blocking collectives  40 us (8%)
  between operations  15.4 us (3%)
    pallas_call x2, Pallas kernels, attend_backward(): pl.pallas_call(backward_kernel, out_shape=(shape((seq_len // 2, feats), b...  52.9 us
    pallas_call x2, Pallas kernels, attend_forward(): pl.pallas_call(forward_kernel, out_shape=[narrow, narrow, narrow, shape((...  45.9 us
    all_to_all x10, starting transfers between devices, exchange(): return lax.all_to_all(value, 'chip', 0, 0)  45.1 us
    pallas_call x2, Pallas kernels, feed_forward(): pl.pallas_call(functools.partial(ffn_kernel, split=split, sides=len(cot))...  44.1 us
    all_to_all x1, blocking collectives, exchange(): return lax.all_to_all(value, 'chip', 0, 0)  40 us
    all_to_all x10, waiting for transfers between devices, exchange(): return lax.all_to_all(value, 'chip', 0, 0)  31.1 us
    pallas_call x1, Pallas kernels, weight_sums(): pl.pallas_call(functools.partial(weight_kernel, counts=[len(v) for v in s...  23.3 us
    ppermute x12, starting transfers between devices, swap_shard(): return lax.ppermute(value, 'fsdp', [(i, i ^ mask) for i in range(count)])  18.2 us
  transfers between devices with their start and end apart: 55, of which 14 were waited for; matrix products, arithmetic and copies ran while one was open for 13% of the time, Pallas kernels for 44%

profile of v3, /device:TPU:0, one launch (start us, length us, event | category | flops | bytes accessed | tf_op | source)
XLA Modules:
  0.0 514.6 jit_solution(16175892682985338602)
XLA Ops:
  7.2 4.2 fusion.29
  13.8 5.3 %all-to-all-start = ((bf16[4,256,1024]{2,1,0:T(8,128)(2,1)}), bf16[4,256,1024]{2,1,0:T(8,128)(2,1)}, u32[]{:S(2)}, u32[]{:S(2)}) async-start(bf16[4,256,1024]{2,1,0:T(8,128)(2,1)} %broadcast_in_dim.50), calls=%async_computation | async-start | bytes 4194304 | tf_op jit(solution)/shard_map/all_to_all | solution.py:63
  21.3 4.4 collective-permute-start.2
  26.8 4.0 convert_reduce_fusion
  38.9 1.7 dynamic-slice_bitcast_fusion.4.refs_4_.refs_0_
  45.9 2.2 collective-permute-done.1
  49.7 2.5 collective-permute-start.6
  52.2 1.9 collective-permute-start.4
  54.1 4.4 all-to-all-start.1
  63.7 22.9 %attend_forward.2 = (bf16[2048,128]{1,0:T(8,128)(2,1)}, bf16[2048,128]{1,0:T(8,128)(2,1)}, bf16[2048,128]{1,0:T(8,128)(2,1)}, bf16[2,1024,1024]{2,1,0:T(8,128)(2...) custom-call(s32[16]{0:T(128)} %get-tuple-element.178.rel, ...), custom_call_target="tpu_custom_call" | custom-call | flops 31000000512 | bytes 1048576 | tf_op jit(solution)/shard_map/attend_forward/pallas_call | solution.py:520
  88.8 1.9 collective-permute-start.7
  93.9 4.1 all-to-all-start.2
  98.0 23.0 %attend_forward.3 = (bf16[2048,128]{1,0:T(8,128)(2,1)}, bf16[2048,128]{1,0:T(8,128)(2,1)}, bf16[2048,128]{1,0:T(8,128)(2,1)}, bf16[2,1024,1024]{2,1,0:T(8,128)(2...) custom-call(s32[16]{0:T(128)} %get-tuple-element.178.rel, ...), custom_call_target="tpu_custom_call" | custom-call | flops 31000000512 | bytes 1048576 | tf_op jit(solution)/shard_map/attend_forward/pallas_call | solution.py:520
  121.0 1.7 all-to-all-done.2
  124.1 3.5 mix.2
  134.7 3.6 collective-permute-done.13.refs_2_
  139.0 40.0 %all_to_all.55 = bf16[4,256,1024]{2,1,0:T(8,128)(2,1)} all-to-all(bf16[4,256,1024]{2,1,0:T(8,128)(2,1)S(1)} %broadcast_in_dim.59), channel_id=1, replica_groups=mesh['chip'=4,'core'=2,'fsdp'=4] {'chip'}, dimensions={0} | all-to-all | bytes 4194304 | tf_op jit(solution)/shard_map/all_to_all | solution.py:63
  179.6 3.4 mix.3
  183.1 4.9 collective-permute-done.17
  189.7 1.6 broadcast_in_dim.98
  191.3 4.4 all-to-all-start.4
  195.8 21.8 %feed_forward.2 = (bf16[4,2,256,1024]{3,2,1,0:T(8,128)(2,1)}, bf16[1024,1024]{1,0:T(8,128)(2,1)}, bf16[1024,1024]{1,0:T(8,128)(2,1)}, bf16[2048,512]{1,0:T(8,128)(2,1)}, bf16[2048,1024]{1,0:T(8,128)(2,1)}) custom-call(s32[3]{0:T(128)} %pad_add_fusion.ids, bf16[1024,1024]{1,0:T(8,128)(2,1)} %bitcast.116, bf16[1024,1024]{1,0:T(8,128)(2,1)} %bitcast.30.x_far.refs_1_, ...), custom_call_target="tpu_custom_call" | custom-call | flops 20000000000 | bytes 1048576 | tf_op jit(solution)/shard_map/feed_forward/pallas_call | solution.py:626
  217.9 14.6 %all-to-all-done.4 = bf16[4,256,1024]{2,1,0:T(8,128)(2,1)} async-done(((bf16[4,256,1024]{2,1,0:T(8,128)(2,1)}), bf16[4,256,1024]{2,1,0:T(8,128)(2,1)}, u32[]{:S(2)}, u32[]{:S(2)}) %all-to-all-start.4) | async-done | bytes 2097184 | tf_op jit(solution)/shard_map/all_to_all | solution.py:63
  232.5 3.5 core_sum.5
  236.0 4.5 all-to-all-start.5
  240.5 22.3 %feed_forward.3 = (bf16[1024,1024]{1,0:T(8,128)(2,1)}, bf16[1024,1024]{1,0:T(8,128)(2,1)}, bf16[1024,1024]{1,0:T(8,128)(2,1)}, bf16[1024,1024]{1,0:T(8,128)(2,1)...) custom-call(s32[3]{0:T(128)} %pad_add_fusion.ids, bf16[1024,1024]{1,0:T(8,128)(2,1)} %bitcast.38.x_near.refs_6_, ...), custom_call_target="tpu_custom_call" | custom-call | flops 20000000000 | bytes 1048576 | tf_op jit(solution)/shard_map/feed_forward/pallas_call | solution.py:626
  262.8 6.6 %all-to-all-done.5 = bf16[4,256,1024]{2,1,0:T(8,128)(2,1)} async-done(((bf16[4,256,1024]{2,1,0:T(8,128)(2,1)}), bf16[4,256,1024]{2,1,0:T(8,128)(2,1)}, u32[]{:S(2)}, u32[]{:S(2)}) %all-to-all-start.5) | async-done | bytes 2097184 | tf_op jit(solution)/shard_map/all_to_all | solution.py:63
  269.4 23.3 %weight_sums.1 = bf16[4,384,1024]{2,1,0:T(8,128)(2,1)} custom-call(s32[3]{0:T(128)} %pad_add_fusion.ids, bf16[1024,1024]{1,0:T(8,128)(2,1)} %bitcast.117, bf16[1024,1024]{1,0:T(8,128)(2,1)} %bitcast.30.x_far.refs_1_, bf16[2048,512]{1,0:T(8,128)(2,1)} %get-tuple-element.233.refs_2_, bf16[2048,1024]{1,0:T(8,128)(2,1)} %get-tuple-element.256.refs_3_, ...), custom_call_target="tpu_custom_call" | custom-call | flops 23000000512 | bytes 1048576 | tf_op jit(solution)/shard_map/weight_sums/pallas_call | solution.py:687
  292.7 2.1 convert_reduce_fusion.6
  298.6 4.5 unmix.2
  304.7 1.9 collective-permute-start.25
  306.5 3.4 core_sum.7
  309.9 4.4 all-to-all-start.6
  315.6 26.3 %attend_backward.2 = (bf16[1024,1024]{1,0:T(8,128)(2,1)}, bf16[1024,1024]{1,0:T(8,128)(2,1)}, bf16[2,1024,384]{2,1,0:T(8,128)(2,1)}) custom-call(s32[16]{0:T(128)} %get-tuple-element.178.rel, s32[16]{0:T(128)} %get-tuple-element.179.send, s32[4]{0:T(128)} %get-tuple-element.408.first, s32[4]{0:T(128)} %get-tuple-element.406.full, ...), custom_call_target="tpu_custom_call" | custom-call | flops 31000000512 | bytes 1048576 | tf_op jit(solution)/shard_map/attend_backward/pallas_call | solution.py:544
  341.9 2.2 convert_reduce_fusion.5
  347.9 4.4 unmix.3
  352.2 2.0 collective-permute-start.27
  355.7 3.4 core_sum.8
  359.1 3.5 collective-permute-done.28.refs_2_
  362.7 2.5 add_convert_fusion
  368.8 2.8 collective-permute-start.31
  371.6 4.4 all-to-all-start.7
  376.2 26.6 %attend_backward.3 = (bf16[1024,1024]{1,0:T(8,128)(2,1)}, bf16[1024,1024]{1,0:T(8,128)(2,1)}, bf16[2,1024,384]{2,1,0:T(8,128)(2,1)}) custom-call(s32[16]{0:T(128)} %get-tuple-element.178.rel, s32[16]{0:T(128)} %get-tuple-element.179.send, s32[4]{0:T(128)} %get-tuple-element.409.first, s32[4]{0:T(128)} %get-tuple-element.407.full, ...), custom_call_target="tpu_custom_call" | custom-call | flops 31000000512 | bytes 1048576 | tf_op jit(solution)/shard_map/attend_backward/pallas_call | solution.py:544
  403.0 2.1 add_convert_fusion.3
  405.6 6.3 %qkv_first.1.refs_2_ = f32[1024,384]{1,0:T(8,128)} custom-call(bf16[2048,1024]{1,0:T(8,128)(2,1)} %bitcast.137, bf16[2048,384]{1,0:T(8,128)(2,1)} %bitcast.144), custom_call_target="tpu_custom_call" | custom-call | flops 6000000000 | bytes 1048576 | tf_op jit(solution)/shard_map/qkv_first/pallas_call | solution.py:714
  411.9 3.6 core_sum.9
  415.4 4.6 all-to-all-start.8
  420.1 7.3 %qkv_sums.1 = (bf16[256,384]{1,0:T(8,128)(2,1)}, bf16[256,384]{1,0:T(8,128)(2,1)}, bf16[256,384]{1,0:T(8,128)(2,1)}, bf16[256,384]{1,0:T(8,128)(2,1)}) custom-call(s32[3]{0:T(128)} %pad_add_fusion.ids, bf16[2048,1024]{1,0:T(8,128)(2,1)} %bitcast.136, bf16[2048,384]{1,0:T(8,128)(2,1)} %bitcast.143, f32[1024,384]{1,0:T(8,128)} %qkv_first.1.refs_2_), custom_call_target="tpu_custom_call" | custom-call | flops 6000000000 | bytes 1048576 | tf_op jit(solution)/shard_map/qkv_sums/pallas_call | solution.py:733
  428.7 2.4 collective-permute-start.36
  431.8 6.0 %collective-permute-done.35 = bf16[256,384]{1,0:T(8,128)(2,1)S(1)} collective-permute-done((bf16[256,384]{1,0:T(8,128)(2,1)}, bf16[256,384]{1,0:T(8,128)(2,1)S(1)}, u32[]{:S(2)}, u32[]{:S(2)}) %collective-permute-start.35) | collective-permute-done | bytes 196640 | tf_op jit(solution)/shard_map/ppermute | solution.py:50
  437.7 8.4 %collective-permute-done.36 = bf16[256,384]{1,0:T(8,128)(2,1)S(1)} collective-permute-done((bf16[256,384]{1,0:T(8,128)(2,1)}, bf16[256,384]{1,0:T(8,128)(2,1)S(1)}, u32[]{:S(2)}, u32[]{:S(2)}) %collective-permute-start.36) | collective-permute-done | bytes 196640 | tf_op jit(solution)/shard_map/ppermute | solution.py:50
  447.2 9.2 %assemble.2 = (f32[256,4096]{1,0:T(8,128)}, f32[256,4096]{1,0:T(8,128)}, f32[256,1]{1,0:T(8,128)}, f32[8,128,1024]{2,1,0:T(8,128)}) custom-call(bf16[8,384,1024]{2,1,0:T(8,128)(2,1)} %bitcast.109, bf16[256,1]{1,0:T(8,128)(2,1)} %copy-done.25, bf16[256,4096]{1,0:T(8,128)(2,1)} %refs_2_, bf16[256,4096]{1,0:T(8,128)(2,1)} %refs_3_, bf16[8,384,1024]{2,1,0:T(8,128)(2,1)} %bitcast.110), custom_call_target="tpu_custom_call" | custom-call | tf_op jit(solution)/shard_map/assemble/pallas_call | solution.py:776
  458.9 4.3 all-to-all-start.9
  463.2 3.5 core_sum.6
  466.6 3.0 convert_reduce_fusion.3
  469.7 3.0 convert_reduce_fusion.1
  472.7 4.7 all-to-all-start.10
  477.5 2.2 convert_reduce_fusion.2
  485.8 4.2 assemble.3
  490.0 1.7 reduce.7
  491.7 8.2 %all-to-all-done.10 = bf16[4,256,1024]{2,1,0:T(8,128)(2,1)} async-done(((bf16[4,256,1024]{2,1,0:T(8,128)(2,1)}), bf16[4,256,1024]{2,1,0:T(8,128)(2,1)}, u32[]{:S(2)}, u32[]{:S(2)}) %all-to-all-start.10) | async-done | bytes 2097184 | tf_op jit(solution)/shard_map/all_to_all | solution.py:63
  499.9 2.2 convert_reduce_fusion.4
  503.3 2.0 copy.82
  505.5 2.0 copy.81
  (285 shorter events, 71.7 us)
Async XLA Ops:
  7.2 24.7 %copy-start = (bf16[1024,1024]{1,0:T(8,128)(2,1)S(1)}, bf16[1024,1024]{1,0:T(8,128)(2,1)}, u32[]{:S(2)}) copy-start(bf16[1024,1024]{1,0:T(8,128)(2,1)} %param.20) | copy-start | bytes 6291460
  12.2 119.7 %copy-start.4 = (bf16[256,1024]{1,0:T(8,128)(2,1)}, bf16[256,1024]{1,0:T(8,128)(2,1)S(1)}, u32[]{:S(2)}) copy-start(bf16[256,1024]{1,0:T(8,128)(2,1)S(1)} %get-tuple-element.380) | copy-start | bytes 1572868
  13.8 13.0 %copy-start.38 = (s32[16]{0:T(128)S(1)}, s32[16]{0:T(128)}, u32[]{:S(2)}) copy-start(s32[16]{0:T(128)} %param.24) | copy-start | bytes 196
  13.8 13.1 %copy-start.55 = (s32[2048,2]{0,1:T(2,128)S(1)}, s32[2048,2]{0,1:T(2,128)}, u32[]{:S(2)}) copy-start(s32[2048,2]{0,1:T(2,128)} %param.23) | copy-start | bytes 49156
  13.8 34.3 %all-to-all-start = ((bf16[4,256,1024]{2,1,0:T(8,128)(2,1)}), bf16[4,256,1024]{2,1,0:T(8,128)(2,1)}, u32[]{:S(2)}, u32[]{:S(2)}) async-start(bf16[4,256,1024]{2,1,0:T(8,128)(2,1)} %broadcast_in_dim.50), calls=%async_computation | async-start | bytes 4194304 | tf_op jit(solution)/shard_map/all_to_all | solution.py:63
  21.3 24.6 %collective-permute-start.2 = (bf16[256,512]{1,0:T(8,128)(2,1)S(1)}, bf16[256,512]{1,0:T(8,128)(2,1)}, u32[]{:S(2)}, u32[]{:S(2)}) collective-permute-start(bf16[256,512]{1,0:T(8,128)(2,1)S(1)} %concatenate.12), channel_id=1, source_target_pairs={{0,3},{1,2},{2,1},{3,0},{4,7},{5,6},{6,5},{7,4},{8,11},{9,10},{10,... | collective-permute-start | bytes 786440 | tf_op jit(solution)/shard_map/ppermute | solution.py:50
  25.7 22.4 %collective-permute-start.1 = (bf16[256,512]{1,0:T(8,128)(2,1)S(1)}, bf16[256,512]{1,0:T(8,128)(2,1)}, u32[]{:S(2)}, u32[]{:S(2)}) collective-permute-start(bf16[256,512]{1,0:T(8,128)(2,1)S(1)} %concatenate.12), channel_id=1, source_target_pairs={{0,2},{1,3},{2,0},{3,1},{4,6},{5,7},{6,4},{7,5},{8,10},{9,11},{10,... | collective-permute-start | bytes 786440 | tf_op jit(solution)/shard_map/ppermute | solution.py:50
  25.7 22.4 %collective-permute-start = (bf16[256,512]{1,0:T(8,128)(2,1)S(1)}, bf16[256,512]{1,0:T(8,128)(2,1)}, u32[]{:S(2)}, u32[]{:S(2)}) collective-permute-start(bf16[256,512]{1,0:T(8,128)(2,1)S(1)} %concatenate.12), channel_id=1, source_target_pairs={{0,1},{1,0},{2,3},{3,2},{4,5},{5,4},{6,7},{7,6},{8,9},{9,8},{10,11... | collective-permute-start | bytes 786440 | tf_op jit(solution)/shard_map/ppermute | solution.py:50
  41.6 21.0 %copy-start.34 = (s32[2,4]{1,0:T(2,128)}, s32[2,4]{1,0:T(2,128)S(1)}, u32[]{:S(2)}) copy-start(s32[2,4]{1,0:T(2,128)S(1)} %get-tuple-element.180) | copy-start | bytes 100
  41.6 21.5 %copy-start.32 = (s32[2,4]{1,0:T(2,128)}, s32[2,4]{1,0:T(2,128)S(1)}, u32[]{:S(2)}) copy-start(s32[2,4]{1,0:T(2,128)S(1)} %get-tuple-element.181) | copy-start | bytes 100
  44.3 48.0 %copy-start.12 = (bf16[256,1024]{1,0:T(8,128)(2,1)}, bf16[256,1024]{1,0:T(8,128)(2,1)S(1)}, u32[]{:S(2)}) copy-start(bf16[256,1024]{1,0:T(8,128)(2,1)S(1)} %get-tuple-element.204) | copy-start | bytes 1572868
  45.9 142.1 %copy-start.6 = (bf16[256,1024]{1,0:T(8,128)(2,1)}, bf16[256,1024]{1,0:T(8,128)(2,1)S(1)}, u32[]{:S(2)}) copy-start(bf16[256,1024]{1,0:T(8,128)(2,1)S(1)} %get-tuple-element.378) | copy-start | bytes 1572868
  49.7 14.0 %collective-permute-start.3 = (bf16[4,256,1024]{2,1,0:T(8,128)(2,1)}, bf16[4,256,1024]{2,1,0:T(8,128)(2,1)}, u32[]{:S(2)}, u32[]{:S(2)}) collective-permute-start(bf16[4,256,1024]{2,1,0:T(8,128)(2,1)} %all-to-all-done), channel_id=1, source_target_pairs={{0,4},{4,0},{1,5},{5,1},{2,6},{6,2},{3,7},{7,3},{8,12},{12,8},{9,1... | collective-permute-start | bytes 6291464 | tf_op jit(solution)/shard_map/ppermute | solution.py:40
  49.7 36.9 %collective-permute-start.6 = (bf16[128,1024]{1,0:T(8,128)(2,1)}, bf16[128,1024]{1,0:T(8,128)(2,1)}, u32[]{:S(2)}, u32[]{:S(2)}) collective-permute-start(bf16[128,1024]{1,0:T(8,128)(2,1)} %dynamic-slice_bitcast_fusion.4.refs_4_.refs_0_), channel_id=1, source_target_pairs={{0,3},{1,2},{2,1},{3,0},{4,7},{5,6},{6,5},{7,4},{8,11},{9,10},{10,... | collective-permute-start | bytes 786440 | tf_op jit(solution)/shard_map/ppermute | solution.py:50
  52.2 34.5 %collective-permute-start.5 = (bf16[128,1024]{1,0:T(8,128)(2,1)}, bf16[128,1024]{1,0:T(8,128)(2,1)}, u32[]{:S(2)}, u32[]{:S(2)}) collective-permute-start(bf16[128,1024]{1,0:T(8,128)(2,1)} %dynamic-slice_bitcast_fusion.4.refs_4_.refs_0_), channel_id=1, source_target_pairs={{0,2},{1,3},{2,0},{3,1},{4,6},{5,7},{6,4},{7,5},{8,10},{9,11},{10,... | collective-permute-start | bytes 786440 | tf_op jit(solution)/shard_map/ppermute | solution.py:50
  52.2 34.5 %collective-permute-start.4 = (bf16[128,1024]{1,0:T(8,128)(2,1)}, bf16[128,1024]{1,0:T(8,128)(2,1)}, u32[]{:S(2)}, u32[]{:S(2)}) collective-permute-start(bf16[128,1024]{1,0:T(8,128)(2,1)} %dynamic-slice_bitcast_fusion.4.refs_4_.refs_0_), channel_id=1, source_target_pairs={{0,1},{1,0},{2,3},{3,2},{4,5},{5,4},{6,7},{7,6},{8,9},{9,8},{10,11... | collective-permute-start | bytes 786440 | tf_op jit(solution)/shard_map/ppermute | solution.py:50
  54.1 32.6 %all-to-all-start.1 = ((bf16[4,256,1024]{2,1,0:T(8,128)(2,1)}), bf16[4,256,1024]{2,1,0:T(8,128)(2,1)}, u32[]{:S(2)}, u32[]{:S(2)}) async-start(bf16[4,256,1024]{2,1,0:T(8,128)(2,1)} %broadcast_in_dim.57), calls=%async_computation.1 | async-start | bytes 4194304 | tf_op jit(solution)/shard_map/all_to_all | solution.py:63
  58.5 137.2 %all-gather.9.cloned.1.call-start = ((), (), s32[]{:S(2)}) async-start(), calls=%async_computation.15 | async-start | bytes 3932160 | tf_op jit(solution)/shard_map/all_gather | solution.py:910
  86.7 11.3 %collective-permute-start.10 = (bf16[4,256,1024]{2,1,0:T(8,128)(2,1)}, bf16[4,256,1024]{2,1,0:T(8,128)(2,1)}, u32[]{:S(2)}, u32[]{:S(2)}) collective-permute-start(bf16[4,256,1024]{2,1,0:T(8,128)(2,1)} %all-to-all-done.1), channel_id=1, source_target_pairs={{0,4},{4,0},{1,5},{5,1},{2,6},{6,2},{3,7},{7,3},{8,12},{12,8},{9,1... | collective-permute-start | bytes 6291464 | tf_op jit(solution)/shard_map/ppermute | solution.py:40
  88.8 32.2 %collective-permute-start.7 = (bf16[512,128]{1,0:T(8,128)(2,1)}, bf16[512,128]{1,0:T(8,128)(2,1)S(1)}, u32[]{:S(2)}, u32[]{:S(2)}) collective-permute-start(bf16[512,128]{1,0:T(8,128)(2,1)} %get-tuple-element.196), channel_id=1, source_target_pairs={{0,8},{8,0},{16,24},{24,16},{1,9},{9,1},{17,25},{25,17},{2,10},{10... | collective-permute-start | bytes 393224 | tf_op jit(solution)/shard_map/ppermute | solution.py:45
  90.7 30.2 %collective-permute-start.8 = (bf16[512,128]{1,0:T(8,128)(2,1)}, bf16[512,128]{1,0:T(8,128)(2,1)S(1)}, u32[]{:S(2)}, u32[]{:S(2)}) collective-permute-start(bf16[512,128]{1,0:T(8,128)(2,1)} %get-tuple-element.197), channel_id=1, source_target_pairs={{0,16},{8,24},{16,0},{24,8},{1,17},{9,25},{17,1},{25,9},{2,18},{10... | collective-permute-start | bytes 393224 | tf_op jit(solution)/shard_map/ppermute | solution.py:45
  92.2 28.8 %collective-permute-start.9 = (bf16[512,128]{1,0:T(8,128)(2,1)}, bf16[512,128]{1,0:T(8,128)(2,1)S(1)}, u32[]{:S(2)}, u32[]{:S(2)}) collective-permute-start(bf16[512,128]{1,0:T(8,128)(2,1)} %get-tuple-element.198), channel_id=1, source_target_pairs={{0,24},{8,16},{16,8},{24,0},{1,25},{9,17},{17,9},{25,1},{2,26},{10... | collective-permute-start | bytes 393224 | tf_op jit(solution)/shard_map/ppermute | solution.py:45
  93.9 28.8 %all-to-all-start.2 = ((bf16[4,256,1024]{2,1,0:T(8,128)(2,1)}), bf16[4,256,1024]{2,1,0:T(8,128)(2,1)S(1)}, u32[]{:S(2)}, u32[]{:S(2)}) async-start(bf16[4,256,1024]{2,1,0:T(8,128)(2,1)} %broadcast_in_dim.58), calls=%async_computation.2 | async-start | bytes 4194304 | tf_op jit(solution)/shard_map/all_to_all | solution.py:63
  98.0 142.5 %all-gather.11.cloned.1.call-start = ((), (), s32[]{:S(2)}) async-start(), calls=%async_computation.16 | async-start | bytes 4718592 | tf_op jit(solution)/shard_map/all_gather | solution.py:893
  127.6 4.3 collective-permute-start.11
  128.4 6.3 %collective-permute-start.12 = (bf16[512,128]{1,0:T(8,128)(2,1)S(1)}, bf16[512,128]{1,0:T(8,128)(2,1)S(1)}, u32[]{:S(2)}, u32[]{:S(2)}) collective-permute-start(bf16[512,128]{1,0:T(8,128)(2,1)S(1)} %copy-done.46), channel_id=1, source_target_pairs={{0,8},{8,0},{16,24},{24,16},{1,9},{9,1},{17,25},{25,17},{2,10},{10... | collective-permute-start | bytes 393224 | tf_op jit(solution)/shard_map/ppermute | solution.py:45
  129.8 8.4 %collective-permute-start.13 = (bf16[512,128]{1,0:T(8,128)(2,1)S(1)}, bf16[512,128]{1,0:T(8,128)(2,1)S(1)}, u32[]{:S(2)}, u32[]{:S(2)}) collective-permute-start(bf16[512,128]{1,0:T(8,128)(2,1)S(1)} %copy-done.45), channel_id=1, source_target_pairs={{0,16},{8,24},{16,0},{24,8},{1,17},{9,25},{17,1},{25,9},{2,18},{10... | collective-permute-start | bytes 393224 | tf_op jit(solution)/shard_map/ppermute | solution.py:45
  130.4 7.9 %collective-permute-start.14 = (bf16[512,128]{1,0:T(8,128)(2,1)S(1)}, bf16[512,128]{1,0:T(8,128)(2,1)S(1)}, u32[]{:S(2)}, u32[]{:S(2)}) collective-permute-start(bf16[512,128]{1,0:T(8,128)(2,1)S(1)} %copy-done.44), channel_id=1, source_target_pairs={{0,24},{8,16},{16,8},{24,0},{1,25},{9,17},{17,9},{25,1},{2,26},{10... | collective-permute-start | bytes 393224 | tf_op jit(solution)/shard_map/ppermute | solution.py:45
  134.7 44.3 %copy-start.49 = (bf16[512,128]{1,0:T(8,128)(2,1)}, bf16[512,128]{1,0:T(8,128)(2,1)S(1)}, u32[]{:S(2)}) copy-start(bf16[512,128]{1,0:T(8,128)(2,1)S(1)} %collective-permute-done.12.refs_1_) | copy-start | bytes 393220
  179.0 16.8 %collective-permute-start.16 = (bf16[4,256,1024]{2,1,0:T(8,128)(2,1)}, bf16[4,256,1024]{2,1,0:T(8,128)(2,1)}, u32[]{:S(2)}, u32[]{:S(2)}) collective-permute-start(bf16[4,256,1024]{2,1,0:T(8,128)(2,1)} %copy-done.22), channel_id=1, source_target_pairs={{0,4},{4,0},{1,5},{5,1},{2,6},{6,2},{3,7},{7,3},{8,12},{12,8},{9,1... | collective-permute-start | bytes 6291464 | tf_op jit(solution)/shard_map/ppermute | solution.py:40
  179.1 16.7 %collective-permute-start.15 = (bf16[4,256,1024]{2,1,0:T(8,128)(2,1)}, bf16[4,256,1024]{2,1,0:T(8,128)(2,1)}, u32[]{:S(2)}, u32[]{:S(2)}) collective-permute-start(bf16[4,256,1024]{2,1,0:T(8,128)(2,1)} %all_to_all.55), channel_id=1, source_target_pairs={{0,4},{4,0},{1,5},{5,1},{2,6},{6,2},{3,7},{7,3},{8,12},{12,8},{9,1... | collective-permute-start | bytes 6291464 | tf_op jit(solution)/shard_map/ppermute | solution.py:40
  183.0 5.0 collective-permute-start.17
  191.3 41.2 %all-to-all-start.4 = ((bf16[4,256,1024]{2,1,0:T(8,128)(2,1)}), bf16[4,256,1024]{2,1,0:T(8,128)(2,1)}, u32[]{:S(2)}, u32[]{:S(2)}) async-start(bf16[4,256,1024]{2,1,0:T(8,128)(2,1)} %broadcast_in_dim.98), calls=%async_computation.5 | async-start | bytes 4194304 | tf_op jit(solution)/shard_map/all_to_all | solution.py:63
  195.7 119.1 %reduce-scatter.3.cloned.1.call-start = ((), (), s32[]{:S(2)}) async-start(), calls=%async_computation.13 | async-start | bytes 4718592 | tf_op jit(solution)/shard_map/reduce_scatter | solution.py:948
  217.6 14.9 %collective-permute-start.19 = (bf16[4,256,1024]{2,1,0:T(8,128)(2,1)}, bf16[4,256,1024]{2,1,0:T(8,128)(2,1)}, u32[]{:S(2)}, u32[]{:S(2)}) collective-permute-start(bf16[4,256,1024]{2,1,0:T(8,128)(2,1)} %bitcast.135), channel_id=1, source_target_pairs={{0,4},{4,0},{1,5},{5,1},{2,6},{6,2},{3,7},{7,3},{8,12},{12,8},{9,1... | collective-permute-start | bytes 6291464 | tf_op jit(solution)/shard_map/ppermute | solution.py:40
  232.5 8.0 %collective-permute-start.18 = (bf16[4,256,1024]{2,1,0:T(8,128)(2,1)}, bf16[4,256,1024]{2,1,0:T(8,128)(2,1)}, u32[]{:S(2)}, u32[]{:S(2)}) collective-permute-start(bf16[4,256,1024]{2,1,0:T(8,128)(2,1)} %all-to-all-done.4), channel_id=1, source_target_pairs={{0,4},{4,0},{1,5},{5,1},{2,6},{6,2},{3,7},{7,3},{8,12},{12,8},{9,1... | collective-permute-start | bytes 6291464 | tf_op jit(solution)/shard_map/ppermute | solution.py:40
  236.0 33.4 %all-to-all-start.5 = ((bf16[4,256,1024]{2,1,0:T(8,128)(2,1)}), bf16[4,256,1024]{2,1,0:T(8,128)(2,1)}, u32[]{:S(2)}, u32[]{:S(2)}) async-start(bf16[4,256,1024]{2,1,0:T(8,128)(2,1)} %core_sum.5), calls=%async_computation.6 | async-start | bytes 4194304 | tf_op jit(solution)/shard_map/all_to_all | solution.py:63
  240.5 122.2 %reduce-scatter.5.cloned.1.call-start = ((), (), s32[]{:S(2)}) async-start(), calls=%async_computation.14 | async-start | bytes 3932160 | tf_op jit(solution)/shard_map/reduce_scatter | solution.py:944
  269.4 23.3 %collective-permute-start.21 = (bf16[4,256,1024]{2,1,0:T(8,128)(2,1)}, bf16[4,256,1024]{2,1,0:T(8,128)(2,1)}, u32[]{:S(2)}, u32[]{:S(2)}) collective-permute-start(bf16[4,256,1024]{2,1,0:T(8,128)(2,1)} %bitcast.134), channel_id=1, source_target_pairs={{0,4},{4,0},{1,5},{5,1},{2,6},{6,2},{3,7},{7,3},{8,12},{12,8},{9,1... | collective-permute-start | bytes 6291464 | tf_op jit(solution)/shard_map/ppermute | solution.py:40
  296.3 2.3 collective-permute-start.22
  303.0 11.8 %collective-permute-start.23 = (bf16[512,128]{1,0:T(8,128)(2,1)}, bf16[512,128]{1,0:T(8,128)(2,1)S(1)}, u32[]{:S(2)}, u32[]{:S(2)}) collective-permute-start(bf16[512,128]{1,0:T(8,128)(2,1)} %get-tuple-element.262), channel_id=1, source_target_pairs={{0,8},{8,0},{16,24},{24,16},{1,9},{9,1},{17,25},{25,17},{2,10},{10... | collective-permute-start | bytes 393224 | tf_op jit(solution)/shard_map/ppermute | solution.py:45
  304.6 10.3 %collective-permute-start.24 = (bf16[512,128]{1,0:T(8,128)(2,1)}, bf16[512,128]{1,0:T(8,128)(2,1)S(1)}, u32[]{:S(2)}, u32[]{:S(2)}) collective-permute-start(bf16[512,128]{1,0:T(8,128)(2,1)} %get-tuple-element.263), channel_id=1, source_target_pairs={{0,16},{8,24},{16,0},{24,8},{1,17},{9,25},{17,1},{25,9},{2,18},{10... | collective-permute-start | bytes 393224 | tf_op jit(solution)/shard_map/ppermute | solution.py:45
  304.7 10.2 %collective-permute-start.25 = (bf16[512,128]{1,0:T(8,128)(2,1)}, bf16[512,128]{1,0:T(8,128)(2,1)}, u32[]{:S(2)}, u32[]{:S(2)}) collective-permute-start(bf16[512,128]{1,0:T(8,128)(2,1)} %get-tuple-element.264), channel_id=1, source_target_pairs={{0,24},{8,16},{16,8},{24,0},{1,25},{9,17},{17,9},{25,1},{2,26},{10... | collective-permute-start | bytes 393224 | tf_op jit(solution)/shard_map/ppermute | solution.py:45
  309.9 31.9 %all-to-all-start.6 = ((bf16[4,256,1024]{2,1,0:T(8,128)(2,1)}), bf16[4,256,1024]{2,1,0:T(8,128)(2,1)}, u32[]{:S(2)}, u32[]{:S(2)}) async-start(bf16[4,256,1024]{2,1,0:T(8,128)(2,1)} %core_sum.7), calls=%async_computation.7 | async-start | bytes 4194304 | tf_op jit(solution)/shard_map/all_to_all | solution.py:63
  314.4 132.8 %all-gather.13.cloned.1.call-start = ((), (), s32[]{:S(2)}) async-start(), calls=%async_computation.17 | async-start | bytes 7077888 | tf_op jit(solution)/shard_map/all_gather | solution.py:1005
  341.9 13.9 %collective-permute-start.30 = (bf16[4,256,1024]{2,1,0:T(8,128)(2,1)}, bf16[4,256,1024]{2,1,0:T(8,128)(2,1)}, u32[]{:S(2)}, u32[]{:S(2)}) collective-permute-start(bf16[4,256,1024]{2,1,0:T(8,128)(2,1)} %bitcast.133), channel_id=1, source_target_pairs={{0,4},{4,0},{1,5},{5,1},{2,6},{6,2},{3,7},{7,3},{8,12},{12,8},{9,1... | collective-permute-start | bytes 6291464 | tf_op jit(solution)/shard_map/ppermute | solution.py:40
  345.1 2.0 collective-permute-start.26
  352.2 6.9 %collective-permute-start.27 = (bf16[512,128]{1,0:T(8,128)(2,1)}, bf16[512,128]{1,0:T(8,128)(2,1)S(1)}, u32[]{:S(2)}, u32[]{:S(2)}) collective-permute-start(bf16[512,128]{1,0:T(8,128)(2,1)} %get-tuple-element.279), channel_id=1, source_target_pairs={{0,8},{8,0},{16,24},{24,16},{1,9},{9,1},{17,25},{25,17},{2,10},{10... | collective-permute-start | bytes 393224 | tf_op jit(solution)/shard_map/ppermute | solution.py:45
  354.2 8.5 %collective-permute-start.28 = (bf16[512,128]{1,0:T(8,128)(2,1)}, bf16[512,128]{1,0:T(8,128)(2,1)S(1)}, u32[]{:S(2)}, u32[]{:S(2)}) collective-permute-start(bf16[512,128]{1,0:T(8,128)(2,1)} %get-tuple-element.280), channel_id=1, source_target_pairs={{0,16},{8,24},{16,0},{24,8},{1,17},{9,25},{17,1},{25,9},{2,18},{10... | collective-permute-start | bytes 393224 | tf_op jit(solution)/shard_map/ppermute | solution.py:45
  355.6 7.0 %collective-permute-start.29 = (bf16[512,128]{1,0:T(8,128)(2,1)}, bf16[512,128]{1,0:T(8,128)(2,1)}, u32[]{:S(2)}, u32[]{:S(2)}) collective-permute-start(bf16[512,128]{1,0:T(8,128)(2,1)} %get-tuple-element.281), channel_id=1, source_target_pairs={{0,24},{8,16},{16,8},{24,0},{1,25},{9,17},{17,9},{25,1},{2,26},{10... | collective-permute-start | bytes 393224 | tf_op jit(solution)/shard_map/ppermute | solution.py:45
  367.2 35.7 %collective-permute-start.33 = (bf16[128,1024]{1,0:T(8,128)(2,1)}, bf16[128,1024]{1,0:T(8,128)(2,1)}, u32[]{:S(2)}, u32[]{:S(2)}) collective-permute-start(bf16[128,1024]{1,0:T(8,128)(2,1)} %get-tuple-element.391), channel_id=1, source_target_pairs={{0,3},{1,2},{2,1},{3,0},{4,7},{5,6},{6,5},{7,4},{8,11},{9,10},{10,... | collective-permute-start | bytes 786440 | tf_op jit(solution)/shard_map/ppermute | solution.py:50
  368.7 34.1 %collective-permute-start.32 = (bf16[128,1024]{1,0:T(8,128)(2,1)}, bf16[128,1024]{1,0:T(8,128)(2,1)}, u32[]{:S(2)}, u32[]{:S(2)}) collective-permute-start(bf16[128,1024]{1,0:T(8,128)(2,1)} %get-tuple-element.392), channel_id=1, source_target_pairs={{0,2},{1,3},{2,0},{3,1},{4,6},{5,7},{6,4},{7,5},{8,10},{9,11},{10,... | collective-permute-start | bytes 786440 | tf_op jit(solution)/shard_map/ppermute | solution.py:50
  368.8 34.1 %collective-permute-start.31 = (bf16[128,1024]{1,0:T(8,128)(2,1)}, bf16[128,1024]{1,0:T(8,128)(2,1)}, u32[]{:S(2)}, u32[]{:S(2)}) collective-permute-start(bf16[128,1024]{1,0:T(8,128)(2,1)} %get-tuple-element.393), channel_id=1, source_target_pairs={{0,1},{1,0},{2,3},{3,2},{4,5},{5,4},{6,7},{7,6},{8,9},{9,8},{10,11... | collective-permute-start | bytes 786440 | tf_op jit(solution)/shard_map/ppermute | solution.py:50
  371.6 31.3 %all-to-all-start.7 = ((bf16[4,256,1024]{2,1,0:T(8,128)(2,1)}), bf16[4,256,1024]{2,1,0:T(8,128)(2,1)}, u32[]{:S(2)}, u32[]{:S(2)}) async-start(bf16[4,256,1024]{2,1,0:T(8,128)(2,1)} %core_sum.8), calls=%async_computation.9 | async-start | bytes 4194304 | tf_op jit(solution)/shard_map/all_to_all | solution.py:63
  376.0 93.7 %all-gather.15.cloned.1.call-start = ((), (), s32[]{:S(2)}) async-start(), calls=%async_computation.18 | async-start | bytes 2359296 | tf_op jit(solution)/shard_map/all_gather | solution.py:1032
  402.9 9.0 %collective-permute-start.34 = (bf16[4,256,1024]{2,1,0:T(8,128)(2,1)}, bf16[4,256,1024]{2,1,0:T(8,128)(2,1)}, u32[]{:S(2)}, u32[]{:S(2)}) collective-permute-start(bf16[4,256,1024]{2,1,0:T(8,128)(2,1)} %bitcast.132), channel_id=1, source_target_pairs={{0,4},{4,0},{1,5},{5,1},{2,6},{6,2},{3,7},{7,3},{8,12},{12,8},{9,1... | collective-permute-start | bytes 6291464 | tf_op jit(solution)/shard_map/ppermute | solution.py:40
  405.0 58.1 %collective-permute-start.20 = (bf16[4,256,1024]{2,1,0:T(8,128)(2,1)}, bf16[4,256,1024]{2,1,0:T(8,128)(2,1)}, u32[]{:S(2)}, u32[]{:S(2)}) collective-permute-start(bf16[4,256,1024]{2,1,0:T(8,128)(2,1)} %bitcast.131), channel_id=1, source_target_pairs={{0,4},{4,0},{1,5},{5,1},{2,6},{6,2},{3,7},{7,3},{8,12},{12,8},{9,1... | collective-permute-start | bytes 6291464 | tf_op jit(solution)/shard_map/ppermute | solution.py:40
  415.4 42.5 %all-to-all-start.8 = ((bf16[4,256,1024]{2,1,0:T(8,128)(2,1)}), bf16[4,256,1024]{2,1,0:T(8,128)(2,1)}, u32[]{:S(2)}, u32[]{:S(2)}) async-start(bf16[4,256,1024]{2,1,0:T(8,128)(2,1)} %core_sum.9), calls=%async_computation.10 | async-start | bytes 4194304 | tf_op jit(solution)/shard_map/all_to_all | solution.py:63
  427.4 10.4 %collective-permute-start.35 = (bf16[256,384]{1,0:T(8,128)(2,1)}, bf16[256,384]{1,0:T(8,128)(2,1)S(1)}, u32[]{:S(2)}, u32[]{:S(2)}) collective-permute-start(bf16[256,384]{1,0:T(8,128)(2,1)} %get-tuple-element.301), channel_id=1, source_target_pairs={{0,1},{1,0},{2,3},{3,2},{4,5},{5,4},{6,7},{7,6},{8,9},{9,8},{10,11... | collective-permute-start | bytes 589832 | tf_op jit(solution)/shard_map/ppermute | solution.py:50
  428.7 17.4 %collective-permute-start.36 = (bf16[256,384]{1,0:T(8,128)(2,1)}, bf16[256,384]{1,0:T(8,128)(2,1)S(1)}, u32[]{:S(2)}, u32[]{:S(2)}) collective-permute-start(bf16[256,384]{1,0:T(8,128)(2,1)} %get-tuple-element.302), channel_id=1, source_target_pairs={{0,2},{1,3},{2,0},{3,1},{4,6},{5,7},{6,4},{7,5},{8,10},{9,11},{10,... | collective-permute-start | bytes 589832 | tf_op jit(solution)/shard_map/ppermute | solution.py:50
  431.2 15.0 %collective-permute-start.37 = (bf16[256,384]{1,0:T(8,128)(2,1)}, bf16[256,384]{1,0:T(8,128)(2,1)S(1)}, u32[]{:S(2)}, u32[]{:S(2)}) collective-permute-start(bf16[256,384]{1,0:T(8,128)(2,1)} %get-tuple-element.303), channel_id=1, source_target_pairs={{0,3},{1,2},{2,1},{3,0},{4,7},{5,6},{6,5},{7,4},{8,11},{9,10},{10,... | collective-permute-start | bytes 589832 | tf_op jit(solution)/shard_map/ppermute | solution.py:50
  458.9 13.8 %all-to-all-start.9 = ((bf16[4,256,384]{2,1,0:T(8,128)(2,1)}), bf16[4,256,384]{2,1,0:T(8,128)(2,1)}, u32[]{:S(2)}, u32[]{:S(2)}) async-start(bf16[4,256,384]{2,1,0:T(8,128)(2,1)} %broadcast_in_dim.99), calls=%async_computation.11 | async-start | bytes 1572864 | tf_op jit(solution)/shard_map/all_to_all | solution.py:63
  472.7 27.2 %all-to-all-start.10 = ((bf16[4,256,1024]{2,1,0:T(8,128)(2,1)}), bf16[4,256,1024]{2,1,0:T(8,128)(2,1)}, u32[]{:S(2)}, u32[]{:S(2)}) async-start(bf16[4,256,1024]{2,1,0:T(8,128)(2,1)} %core_sum.6), calls=%async_computation.12 | async-start | bytes 4194304 | tf_op jit(solution)/shard_map/all_to_all | solution.py:63
  480.7 2.5 collective-permute-start.38
  (47 other events, 177.0 us)
Sparse Core Ops, SparseCore 0:
  87.6 64.1 all-gather.8
  179.2 57.4 all-gather.10
  240.1 52.1 reduce-scatter.2
  297.4 58.4 reduce-scatter.4
  362.8 58.7 all-gather.12
  424.1 38.6 all-gather.14

commit v4 on v3

--- a/solution.py
+++ b/solution.py
@@ -61,6 +61,28 @@
 
 def exchange(value):
     return lax.all_to_all(value, "chip", 0, 0)
+
+
+def arrange_kernel(ids, *refs):
+    out = refs[-1]
+    for r, piece in enumerate(refs[:-1]):
+        out[ids[2] ^ r] = piece[...]
+
+
+def arrange(ids, pieces):
+    return pl.pallas_call(
+        arrange_kernel,
+        out_shape=jax.ShapeDtypeStruct((len(pieces),) + pieces[0].shape, bf16),
+        in_specs=[smem()] + [vmem()] * len(pieces),
+        out_specs=vmem(),
+        compiler_params=LIMIT,
+        cost_estimate=cost(3),
+        name="arrange",
+    )(ids, *pieces)
+
+
+def send_copies(value):
+    return exchange_pieces([value] * lax.axis_size("chip"))
 
 
 def add_kernel(own, other, total):
@@ -133,9 +155,11 @@
 
 def forward_kernel(
     rel, send, first, full, x_near, x_far, weight, gain, start,
-    query, key, value, normed, fine, logsum, *refs,
+    query_out, key_out, value_out, normed, fine_out, logsum_out, *refs,
 ):
-    attended, (scores, top, total) = refs[:-3], refs[-3:]
+    attended, refs = refs[:-13], refs[-13:]
+    query, key, value, fine, logsum, x_tiles, normed_tiles, scores, top, total = refs[:10]
+    in_sems, normed_sems, out_sems = refs[10:]
     width = query.shape[1]
     seq_len = query.shape[0]
     heads = width // HEAD_DIM
@@ -143,24 +167,35 @@
     tiles = x_near.shape[0] // PROJ
     blocks = PROJ // blk
     gain_row = gain[...].astype(f32)
-    for s, source in ((0, x_near), (1, x_far)):
-
-        def project(t, _, s=s, source=source):
-            rows = pl.ds(pl.multiple_of(t * PROJ, PROJ), PROJ)
-            rows_in = source[rows, :].astype(f32)
-            tile = (rows_in * row_scale(rows_in) * gain_row).astype(bf16)
-            normed[s, rows, :] = tile
-            mixed = dot_nn(tile, weight[:, : 3 * width])
-            for h in range(blocks):
-                place = rel[(s * tiles + t) * blocks + h]
-                where = pl.ds(pl.multiple_of(place * blk, blk), blk)
-                part = mixed[h * blk : (h + 1) * blk]
-                query[where, :] = (part[:, :width].astype(bf16) * 0.125).astype(bf16)
-                key[where, :] = part[:, width : 2 * width].astype(bf16)
-                value[where, :] = part[:, 2 * width :].astype(bf16)
-            return 0
-
-        lax.fori_loop(0, tiles, project, 0)
+    loads, stores = [], []
+    for i in range(2 * tiles):
+        rows = pl.ds(i % tiles * PROJ, PROJ)
+        source = x_near if i < tiles else x_far
+        loads.append(pltpu.make_async_copy(source.at[rows], x_tiles.at[i], in_sems.at[i]))
+        stores.append(
+            pltpu.make_async_copy(
+                normed_tiles.at[i], normed.at[i // tiles, rows], normed_sems.at[i]
+            )
+        )
+        loads[i].start()
+    for i in range(2 * tiles):
+        loads[i].wait()
+        rows_in = x_tiles[i].astype(f32)
+        tile = (rows_in * row_scale(rows_in) * gain_row).astype(bf16)
+        normed_tiles[i] = tile
+        stores[i].start()
+        mixed = dot_nn(tile, weight[:, : 3 * width])
+        for h in range(blocks):
+            where = pl.ds(pl.multiple_of(rel[i * blocks + h] * blk, blk), blk)
+            part = mixed[h * blk : (h + 1) * blk]
+            query[where, :] = (part[:, :width].astype(bf16) * 0.125).astype(bf16)
+            key[where, :] = part[:, width : 2 * width].astype(bf16)
+            value[where, :] = part[:, 2 * width :].astype(bf16)
+    for i, (source, target) in enumerate(
+        ((query, query_out), (key, key_out), (value, value_out))
+    ):
+        stores.append(pltpu.make_async_copy(source, target, out_sems.at[i]))
+        stores[-1].start()
 
     masks = head_masks(Q_FORE, width)
     big = heads * Q_FORE
@@ -221,19 +256,27 @@
         return 0
 
     lax.fori_loop(0, seq_len // Q_FORE, query_tile, 0)
+    for i, (source, target) in enumerate(((fine, fine_out), (logsum, logsum_out))):
+        stores.append(pltpu.make_async_copy(source, target, out_sems.at[3 + i]))
+        stores[-1].start()
 
     count = seq_len // blk // len(attended)
     for r, piece in enumerate(attended):
         for j in range(count):
             where = pl.ds(pl.multiple_of(send[r * count + j] * blk, blk), blk)
             piece[j * blk : (j + 1) * blk, :] = fine[where, :].astype(bf16)
+    for copy in stores:
+        copy.wait()
 
 
 def backward_kernel(
     rel, send, first, full, query, key, value, fine, logsum, weight, start, *refs
 ):
-    grad_in, refs = refs[:-8], refs[-8:]
-    part_near, part_far, grads, grad_at, grad_q, grad_k, grad_v, grad_q2 = refs
+    grad_in, refs = refs[:-13], refs[-13:]
+    part_near, part_far, grads_out, grad_at, grad_q, grad_k, grad_v, grad_q2 = refs[:8]
+    parts, grads, local_weight, sems, weight_sem = refs[8:]
+    load = pltpu.make_async_copy(weight, local_weight, weight_sem)
+    load.start()
     seq_len, width = query.shape
     heads = width // HEAD_DIM
     blk = TILE // 2
@@ -307,21 +350,25 @@
 
     tiles = seq_len // PROJ // 2
     blocks = PROJ // blk
-
-    def project(t, side, part):
-        rows = pl.ds(pl.multiple_of(t * PROJ, PROJ), PROJ)
-        base = side * tiles + t
+    load.wait()
+    stores = []
+    for i in range(2 * tiles):
+        rows = pl.ds(i % tiles * PROJ, PROJ)
         for h in range(blocks):
-            where = pl.ds(pl.multiple_of(rel[base * blocks + h] * blk, blk), blk)
-            here = pl.ds(pl.multiple_of(t * PROJ + h * blk, blk), blk)
-            grads[side, here, :width] = grad_q[where, :]
-            grads[side, here, width : 2 * width] = grad_k[where, :].astype(bf16)
-            grads[side, here, 2 * width :] = grad_v[where, :].astype(bf16)
-        part[rows, :] = dot_nt(grads[side, rows, :], weight[:, : 3 * width]).astype(bf16)
-        return 0
-
-    for side, part in ((0, part_near), (1, part_far)):
-        lax.fori_loop(0, tiles, lambda t, _, s=side, p=part: project(t, s, p), 0)
+            where = pl.ds(pl.multiple_of(rel[i * blocks + h] * blk, blk), blk)
+            here = pl.ds(h * blk, blk)
+            grads[i, here, :width] = grad_q[where, :]
+            grads[i, here, width : 2 * width] = grad_k[where, :].astype(bf16)
+            grads[i, here, 2 * width :] = grad_v[where, :].astype(bf16)
+        target = grads_out.at[i // tiles, rows]
+        stores.append(pltpu.make_async_copy(grads.at[i], target, sems.at[0, i]))
+        stores[-1].start()
+        parts[i] = dot_nt(grads[i], local_weight[:, : 3 * width]).astype(bf16)
+        target = (part_near if i < tiles else part_far).at[rows]
+        stores.append(pltpu.make_async_copy(parts.at[i], target, sems.at[1, i]))
+        stores[-1].start()
+    for copy in stores:
+        copy.wait()
 
 
 def place_pieces(target, pieces, shard, begin, count):
@@ -469,14 +516,25 @@
             outs[-1][z, begin : begin + more, :] = piece.astype(bf16)
 
 
-def assemble_kernel(*refs, kinds, shards, with_down):
-    parts, gain = refs[:2]
+def assemble_kernel(*refs, kinds, shards, with_down, sides):
+    sources, gain = refs[:sides], refs[sides]
+    if sides == 1:
+        parts = sources[0]
+    else:
+        ids, near, far = sources
+        parts = []
+        for p in range(near.shape[0]):
+            own, other = near[p], far[p]
+            parts.append(jnp.where(ids[0] == 0, own, other))
+            parts.append(jnp.where(ids[0] == 0, other, own))
+    refs = refs[sides - 1 :]
     weights = refs[2 : 2 + kinds]
     rest = refs[2 + kinds :]
     if with_down:
         down_part, rest = rest[0], rest[1:]
     outs, gain_out = rest[:kinds], rest[kinds]
-    groups, _, size = parts.shape
+    groups = len(parts) if sides > 1 else parts.shape[0]
+    size = sources[-1].shape[2]
     pieces = size // kinds
     lanes = pieces // shards
     sums = 0.0
@@ -485,7 +543,7 @@
         for z in range(shards):
             for i in range(groups):
                 at = k * pieces + z * lanes
-                columns.append(parts[i, :, at : at + lanes].astype(f32))
+                columns.append(parts[i][:, at : at + lanes].astype(f32))
         full = jnp.concatenate(columns, axis=1)
         outs[k][...] = full
         sums = sums + jnp.sum(full * weights[k][...].astype(f32), axis=1, keepdims=True)
@@ -496,6 +554,10 @@
 
 def smem():
     return pl.BlockSpec(memory_space=pltpu.SMEM)
+
+
+def hbm():
+    return pl.BlockSpec(memory_space=pl.ANY)
 
 
 def vmem():
@@ -521,12 +583,22 @@
         forward_kernel,
         out_shape=[narrow, narrow, narrow, shape((2, half_rows, feats), bf16), wide, wide]
         + [shape((seq_len // chips, width), bf16)] * chips,
-        in_specs=[smem()] * 4 + [vmem()] * 5,
-        out_specs=[vmem()] * (6 + chips),
+        in_specs=[smem()] * 4 + [hbm()] * 2 + [vmem()] * 3,
+        out_specs=[hbm()] * 6 + [vmem()] * chips,
         scratch_shapes=[
+            pltpu.VMEM((seq_len, width), bf16),
+            pltpu.VMEM((seq_len, width), bf16),
+            pltpu.VMEM((seq_len, width), bf16),
+            pltpu.VMEM((seq_len, width), f32),
+            pltpu.VMEM((seq_len, width), f32),
+            pltpu.VMEM((seq_len // PROJ, PROJ, feats), bf16),
+            pltpu.VMEM((seq_len // PROJ, PROJ, feats), bf16),
             pltpu.VMEM((seq_len // K_FORE, big, K_FORE), f32),
             pltpu.VMEM((big, 128), f32),
             pltpu.VMEM((big, 128), f32),
+            pltpu.SemaphoreType.DMA((seq_len // PROJ,)),
+            pltpu.SemaphoreType.DMA((seq_len // PROJ,)),
+            pltpu.SemaphoreType.DMA((5,)),
         ],
         compiler_params=LIMIT,
         cost_estimate=cost(31),
@@ -548,14 +620,19 @@
             shape((seq_len // 2, feats), bf16),
             shape((2, seq_len // 2, 3 * width), bf16),
         ),
-        in_specs=[smem()] * 4 + [vmem()] * (7 + len(grad_in)),
-        out_specs=[vmem()] * 3,
+        in_specs=[smem()] * 4 + [vmem()] * 5 + [hbm()] + [vmem()] * (1 + len(grad_in)),
+        out_specs=[hbm()] * 3,
         scratch_shapes=[
             pltpu.VMEM((seq_len, width), bf16),
             pltpu.VMEM((seq_len, width), bf16),
             pltpu.VMEM((seq_len, width), f32),
             pltpu.VMEM((seq_len, width), f32),
             pltpu.VMEM((big, width), f32),
+            pltpu.VMEM((seq_len // PROJ, PROJ, feats), bf16),
+            pltpu.VMEM((seq_len // PROJ, PROJ, 3 * width), bf16),
+            pltpu.VMEM(weight.shape, bf16),
+            pltpu.SemaphoreType.DMA((2, seq_len // PROJ)),
+            pltpu.SemaphoreType.DMA,
         ],
         compiler_params=LIMIT,
         cost_estimate=cost(31),
@@ -757,12 +834,15 @@
     rows, columns = weights[0].shape
     step = rows // STEPS
     shape = jax.ShapeDtypeStruct
-    groups, _, size = parts.shape
+    sides = len(parts)
+    groups, size = parts[-1].shape[0] * min(2, sides), parts[-1].shape[2]
     row_block = pl.BlockSpec((step, columns), lambda t: (t, 0))
     thin = pl.BlockSpec((step, 1), lambda t: (t, 0))
     count = len(weights)
-    args = [parts, gain[:, None], *weights]
-    in_specs = [pl.BlockSpec((groups, step, size), lambda t: (0, t, 0)), thin] + [row_block] * count
+    args = [*parts, gain[:, None], *weights]
+    share_spec = pl.BlockSpec((parts[-1].shape[0], step, size), lambda t: (0, t, 0))
+    in_specs = [share_spec] if sides == 1 else [smem(), share_spec, share_spec]
+    in_specs += [thin] + [row_block] * count
     out_shape = [shape((rows, columns), f32)] * count + [shape((rows, 1), f32)]
     out_specs = [row_block] * count + [thin]
     if down_rows:
@@ -775,7 +855,7 @@
         out_specs.append(pl.BlockSpec((share, down_rows, feats), lambda t: (t, 0, 0)))
     outs = pl.pallas_call(
         functools.partial(
-            assemble_kernel, kinds=count, shards=shards, with_down=bool(down_rows)
+            assemble_kernel, kinds=count, shards=shards, with_down=bool(down_rows), sides=sides
         ),
         grid=(STEPS,),
         out_shape=out_shape,
@@ -920,11 +1000,14 @@
     att_zero, own, other = mix(ids, got_zero, out_pieces)
     mid_zero, norm_zero = mid_norm(x_zero, own, swap_core(other))
     norm_zero, got_one = hold((norm_zero, got_one))
-    near_zero = spread(norm_zero)
+    pieces_zero = send_copies(norm_zero)
+    pieces_zero, got_one = hold((pieces_zero, got_one))
+    near_zero = arrange(ids, pieces_zero)
     att_one, own, other = mix(ids, hold(got_one, near_zero), out_pieces)
     mid_one, norm_one = mid_norm(x_one, own, swap_core(other))
-    near_one = spread(norm_one)
-    cots = (flat(near_cot, swap_core(near_cot)), [spread_cot(hold(cot_one, near_zero))])
+    cot_one, near_zero = hold((cot_one, near_zero))
+    pieces_one = send_copies(norm_one)
+    cots = (flat(near_cot, swap_core(near_cot)), [spread_cot(cot_one)])
 
     def ffn(b, near, far, split):
         mids = flat(near, far)
@@ -934,10 +1017,10 @@
         return out_part, by_chip(mid_near), by_chip(mid_far), (*mids, hidden, grad_pre, *cots[b])
 
     out_zero, own_zero, far_zero, stream_zero = ffn(0, near_zero, swap_core(near_zero), False)
-    near_one = hold(near_one, stream_zero[2])
+    near_one = arrange(ids, hold(pieces_one, stream_zero[2]))
     total_zero = core_sum(own_zero, swap_core(far_zero))
     near_far = hold((near_one, swap_core(near_one)), total_zero)
-    out_one, own_one, far_one, stream_one = ffn(1, *near_far, True)
+    out_one, own_one, far_one, stream_one = ffn(1, *near_far, False)
     sums_zero = hold(exchange(total_zero), stream_one[2])
     far_one = swap_core(far_one)
     ffn_sums = weight_sums(ids, (stream_zero, stream_one), shards)
@@ -945,9 +1028,11 @@
     sums_zero, far_one = hold((sums_zero, far_one), ffn_sums[0])
     total_one = core_sum(own_one, far_one)
 
-    out_sum_zero = lax.psum_scatter(
-        out_zero[0].reshape(groups * rows, feats), PLANE, scatter_dimension=0, tiled=True
-    )
+    def collect_out(part):
+        flat_part = part.reshape(groups * rows, feats)
+        return lax.psum_scatter(flat_part, PLANE, scatter_dimension=0, tiled=True)
+
+    out_sum_zero = collect_out(out_zero[0])
 
     def mid_backward(b, grad_normed_mid, middle):
         scale_two = row_scale(middle)
@@ -1014,7 +1099,7 @@
     grad_qkv = qkv_sums(ids, *qkv_stream(normed_zero, grads_zero), qkv_one, shards)
     own_rows = feats // shards
     g_gate_up, g_gain_two, (g_down,) = assemble(
-        full_ffn[0],
+        [full_ffn[0]],
         gain_ffn,
         (w_gate, w_up),
         shards,
@@ -1023,31 +1108,40 @@
         per_shard,
     )
     g_down = g_down.reshape(-1, feats)
-    sums_one, g_gate_up, g_gain_two, g_down = hold((sums_one, g_gate_up, g_gain_two, g_down))
-    out_near, out_far = [by_chip(part) for part in out_one]
-    total_out = core_sum(out_near, swap_core(out_far))
-    share_qkv = add_pieces(grad_qkv[0], send_pieces(grad_qkv))
-    near_qkv = spread(hold(share_qkv, sums_one))
-    sums_out = exchange(hold(total_out, near_qkv))
-    share_out = lax.all_gather(add_pieces(out_rel[0], out_sent), PLANE, axis=0)
-    share_out = share_out.astype(f32)
+    sent_qkv = send_pieces(grad_qkv)
+    sent_qkv, g_gate_up, g_gain_two, g_down = hold((sent_qkv, g_gate_up, g_gain_two, g_down))
+    share_qkv = add_pieces(grad_qkv[0], sent_qkv)
+    out_sum_one = collect_out(hold(out_one[0], full_ffn, grad_qkv))
+    share_out = add_pieces(out_rel[0], out_sent)
+    spare = share_out.size // rows
+    if share_qkv.shape[0] == rows and spare % 128 == 0:
+        beside = jnp.concatenate([share_qkv, share_out.reshape(rows, spare)], axis=1)
+        mixed = spread(hold(beside, sums_one))
+        near_qkv = mixed[:, :, : 3 * width]
+        own_sum = last_sum(mixed[:, :, 3 * width :]).reshape(-1, width, feats)
+        other_sum = swap_core(own_sum)
+        sides = (own_sum, other_sum)
+        g_out = jnp.stack(
+            [jnp.where(core == 0, *sides), jnp.where(core == 0, *sides[::-1])], axis=1
+        ).reshape(own_rows, feats)
+    else:
+        near_qkv = spread(hold(share_qkv, sums_one))
+        all_out = lax.all_gather(share_out, PLANE, axis=0).astype(f32)
+        all_out = all_out.reshape(chips, 2, -1, width, feats)
+        g_out = jnp.sum(all_out, axis=0).transpose(1, 0, 2, 3).reshape(own_rows, feats)
 
     outputs = [
         (mid_zero + out_sum_zero.astype(f32)).astype(bf16),
-        (mid_one + last_sum(sums_out)).astype(bf16),
+        (mid_one + out_sum_one.astype(f32)).astype(bf16),
     ]
     grad_inputs = [
         in_backward(last_sum(sums_zero), grad_mid_zero, x_zero),
         in_backward(last_sum(sums_one), grad_mid_one, x_one),
     ]
     far_qkv = swap_core(near_qkv)
-    full_qkv = jnp.stack(
-        [jnp.where(core == 0, near_qkv, far_qkv), jnp.where(core == 0, far_qkv, near_qkv)], axis=1
+    g_qkv, g_gain_one, _ = assemble(
+        [ids, near_qkv, far_qkv], gain_attn, (w_query, w_key, w_value), 1
     )
-    full_qkv = full_qkv.reshape(groups, own_rows, 3 * width)
-    g_qkv, g_gain_one, _ = assemble(full_qkv, gain_attn, (w_query, w_key, w_value), 1)
-    share_out = share_out.reshape(chips, 2, -1, width, feats)
-    g_out = jnp.sum(share_out, axis=0).transpose(1, 0, 2, 3).reshape(own_rows, feats)
 
     return (
         jnp.stack(outputs, axis=1),

time: 521 us -> 506 us (0.971)
  blocking collectives: 40 us -> 0 us
  waiting for transfers between devices: 63 us -> 86.5 us
  local copies, waits for them, and re-layouts: 43.6 us -> 49.3 us
    all_to_all x1 -> x0, blocking collectives: 40 us -> none  [exchange(): return lax.all_to_all(value, 'chip', 0, 0)]
    ppermute x12 -> x18, waiting for transfers between devices: 8.26 us -> 33 us  [swap_chip(): return lax.ppermute(value, 'chip', [(i, i ^ mask) for i in range(count)])]
    ppermute x12, waiting for transfers between devices: 16.6 us -> 2.57 us  [swap_shard(): return lax.ppermute(value, 'fsdp', [(i, i ^ mask) for i in range(count)])]
    all_to_all x10 -> x8, waiting for transfers between devices: 31.1 us -> 40.1 us  [exchange(): return lax.all_to_all(value, 'chip', 0, 0)]
    all_to_all x10 -> x8, starting transfers between devices: 45.1 us -> 36.4 us  [exchange(): return lax.all_to_all(value, 'chip', 0, 0)]
    ppermute x12 -> x18, starting transfers between devices: 14 us -> 21 us  [swap_chip(): return lax.ppermute(value, 'chip', [(i, i ^ mask) for i in range(count)])]
    pallas_call x0 -> x2, Pallas kernels: none -> 6.07 us  [arrange(): pl.pallas_call(arrange_kernel, out_shape=jax.ShapeDtypeStruct((len(pieces...]
    pallas_call x5 -> x4, Pallas kernels: 17.3 us -> 13.8 us  [core_sum(): pl.pallas_call(add_kernel, grid=(2,), out_shape=jax.ShapeDtypeStruct(own....]
  transfers between devices with their start and end apart: 55 -> 59, of which waited for: 14 -> 18; matrix products, arithmetic and copies ran while one was open for 13% -> 14% of each run, Pallas kernels for 44% -> 45%
where the time goes in v4:
time: 506 us; the launch traced here: 498 us
  Pallas kernels  222 us (44%)
  waiting for transfers between devices  86.5 us (17%)
  starting transfers between devices  80.6 us (16%)
  local copies, waits for them, and re-layouts  49.3 us (10%)
  other arithmetic  44.2 us (9%)
  between operations  15.4 us (3%)
    pallas_call x2, Pallas kernels, attend_backward(): pl.pallas_call(backward_kernel, out_shape=(shape((seq_len // 2, feats), b...  48 us
    pallas_call x2, Pallas kernels, attend_forward(): pl.pallas_call(forward_kernel, out_shape=[narrow, narrow, narrow, shape((...  43.8 us
    pallas_call x2, Pallas kernels, feed_forward(): pl.pallas_call(functools.partial(ffn_kernel, split=split, sides=len(cot))...  43.5 us
    all_to_all x8, waiting for transfers between devices, exchange(): return lax.all_to_all(value, 'chip', 0, 0)  40.1 us
    all_to_all x8, starting transfers between devices, exchange(): return lax.all_to_all(value, 'chip', 0, 0)  36.4 us
    ppermute x18, waiting for transfers between devices, swap_chip(): return lax.ppermute(value, 'chip', [(i, i ^ mask) for i in range(count)])  33 us
    pallas_call x1, Pallas kernels, weight_sums(): pl.pallas_call(functools.partial(weight_kernel, counts=[len(v) for v in s...  23.1 us
    ppermute x18, starting transfers between devices, swap_chip(): return lax.ppermute(value, 'chip', [(i, i ^ mask) for i in range(count)])  21 us
  transfers between devices with their start and end apart: 59, of which 18 were waited for; matrix products, arithmetic and copies ran while one was open for 14% of the time, Pallas kernels for 45%

profile of v4, /device:TPU:0, one launch (start us, length us, event | category | flops | bytes accessed | tf_op | source)
XLA Modules:
  0.0 497.5 jit_solution(5113398266344736397)
XLA Ops:
  7.2 4.2 fusion.29
  13.7 5.3 %all-to-all-start = ((bf16[4,256,1024]{2,1,0:T(8,128)(2,1)}), bf16[4,256,1024]{2,1,0:T(8,128)(2,1)}, u32[]{:S(2)}, u32[]{:S(2)}) async-start(bf16[4,256,1024]{2,1,0:T(8,128)(2,1)} %broadcast_in_dim.46), calls=%async_computation | async-start | bytes 4194304 | tf_op jit(solution)/shard_map/all_to_all | solution.py:63
  21.2 4.4 collective-permute-start.2
  26.8 4.0 convert_reduce_fusion
  45.9 2.2 collective-permute-done.1
  49.6 2.5 collective-permute-start.6
  52.1 1.9 collective-permute-start.4
  54.0 4.4 all-to-all-start.1
  63.9 21.9 %attend_forward.2 = (bf16[2048,128]{1,0:T(8,128)(2,1)}, bf16[2048,128]{1,0:T(8,128)(2,1)}, bf16[2048,128]{1,0:T(8,128)(2,1)}, bf16[2,1024,1024]{2,1,0:T(8,128)(2...) custom-call(s32[16]{0:T(128)} %get-tuple-element.191.rel, ...), custom_call_target="tpu_custom_call" | custom-call | flops 31000000512 | bytes 1048576 | tf_op jit(solution)/shard_map/attend_forward/pallas_call | solution.py:582
  87.9 1.9 collective-permute-start.7
  93.0 4.1 all-to-all-start.2
  97.3 21.9 %attend_forward.3 = (bf16[2048,128]{1,0:T(8,128)(2,1)}, bf16[2048,128]{1,0:T(8,128)(2,1)}, bf16[2048,128]{1,0:T(8,128)(2,1)}, bf16[2,1024,1024]{2,1,0:T(8,128)(2...) custom-call(s32[16]{0:T(128)} %get-tuple-element.191.rel, ...), custom_call_target="tpu_custom_call" | custom-call | flops 31000000512 | bytes 1048576 | tf_op jit(solution)/shard_map/attend_forward/pallas_call | solution.py:582
  119.3 2.6 all-to-all-done.2
  123.2 3.5 mix.2
  133.8 3.6 collective-permute-done.13.refs_2_
  141.6 12.3 %collective-permute-done.17.refs_3_ = bf16[256,1024]{1,0:T(8,128)(2,1)S(1)} collective-permute-done((bf16[256,1024]{1,0:T(8,128)(2,1)S(1)}, bf16[256,1024]{1,0:T(8,128)(2,1)S(1)}, u32[]{:S(2)}, u32[]{:S(2)}) %collective-permute-start.17) | collective-permute-done | bytes 524320 | tf_op jit(solution)/shard_map/ppermute | solution.py:45
  153.9 9.7 %collective-permute-done.16.refs_2_ = bf16[256,1024]{1,0:T(8,128)(2,1)S(1)} collective-permute-done((bf16[256,1024]{1,0:T(8,128)(2,1)S(1)}, bf16[256,1024]{1,0:T(8,128)(2,1)S(1)}, u32[]{:S(2)}, u32[]{:S(2)}) %collective-permute-start.16) | collective-permute-done | bytes 524320 | tf_op jit(solution)/shard_map/ppermute | solution.py:45
  165.2 3.1 arrange.2
  169.1 3.4 mix.3
  172.6 4.9 collective-permute-done.20
  182.8 21.9 %feed_forward.2 = (bf16[4,2,256,1024]{3,2,1,0:T(8,128)(2,1)}, bf16[1024,1024]{1,0:T(8,128)(2,1)}, bf16[1024,1024]{1,0:T(8,128)(2,1)}, bf16[2048,512]{1,0:T(8,128)(2,1)}, bf16[2048,1024]{1,0:T(8,128)(2,1)}) custom-call(s32[3]{0:T(128)} %pad_add_fusion.ids.refs_0_, bf16[1024,1024]{1,0:T(8,128)(2,1)} %bitcast.122, bf16[1024,1024]{1,0:T(8,128)(2,1)} %bitcast.30.x_far.refs_1_, ...), custom_call_target="tpu_custom_call" | custom-call | flops 20000000000 | bytes 1048576 | tf_op jit(solution)/shard_map/feed_forward/pallas_call | solution.py:703
  204.7 2.6 collective-permute-done.22.refs_2_
  207.3 3.0 arrange.3
  211.9 3.5 core_sum.4
  215.4 4.5 all-to-all-start.3
  220.2 21.6 %feed_forward.3 = (bf16[4,2,256,1024]{3,2,1,0:T(8,128)(2,1)}, bf16[1024,1024]{1,0:T(8,128)(2,1)}, bf16[1024,1024]{1,0:T(8,128)(2,1)}, bf16[2048,512]{1,0:T(8,128)(2,1)}, bf16[2048,1024]{1,0:T(8,128)(2,1)}) custom-call(s32[3]{0:T(128)} %pad_add_fusion.ids.refs_0_, bf16[1024,1024]{1,0:T(8,128)(2,1)} %bitcast.125, bf16[1024,1024]{1,0:T(8,128)(2,1)} %bitcast.39.x_far.refs_7_, ...), custom_call_target="tpu_custom_call" | custom-call | flops 20000000000 | bytes 1048576 | tf_op jit(solution)/shard_map/feed_forward/pallas_call | solution.py:703
  241.8 3.6 all-to-all-done.3
  245.4 23.1 %weight_sums.1 = bf16[4,384,1024]{2,1,0:T(8,128)(2,1)} custom-call(s32[3]{0:T(128)} %pad_add_fusion.ids.refs_0_, bf16[1024,1024]{1,0:T(8,128)(2,1)} %bitcast.123, bf16[1024,1024]{1,0:T(8,128)(2,1)} %bitcast.30.x_far.refs_1_, bf16[2048,512]{1,0:T(8,128)(2,1)} %get-tuple-element.256.refs_2_, bf16[2048,1024]{1,0:T(8,128)(2,1)} %get-tuple-element.271.refs_3_, ...), custom_call_target="tpu_custom_call" | custom-call | flops 23000000512 | bytes 1048576 | tf_op jit(solution)/shard_map/weight_sums/pallas_call | solution.py:764
  268.5 2.1 convert_reduce_fusion.4
  274.5 4.4 unmix.2
  282.5 3.4 core_sum.5
  285.9 4.4 all-to-all-start.4
  291.6 24.0 %attend_backward.2 = (bf16[1024,1024]{1,0:T(8,128)(2,1)}, bf16[1024,1024]{1,0:T(8,128)(2,1)}, bf16[2,1024,384]{2,1,0:T(8,128)(2,1)}) custom-call(s32[16]{0:T(128)} %get-tuple-element.191.rel, s32[16]{0:T(128)} %get-tuple-element.192.send, s32[4]{0:T(128)} %get-tuple-element.435.first, s32[4]{0:T(128)} %get-tuple-element.433.full, ...), custom_call_target="tpu_custom_call" | custom-call | flops 31000000512 | bytes 1048576 | tf_op jit(solution)/shard_map/attend_backward/pallas_call | solution.py:616
  315.7 2.2 convert_reduce_fusion.3
  321.7 4.3 unmix.3
  326.1 1.9 collective-permute-start.32
  329.6 3.4 core_sum.6
  333.0 3.6 collective-permute-done.33.refs_2_
  336.7 2.5 add_convert_fusion
  341.1 3.5 collective-permute-start.38
  345.5 4.4 all-to-all-start.5
  350.2 24.0 %attend_backward.3 = (bf16[1024,1024]{1,0:T(8,128)(2,1)}, bf16[1024,1024]{1,0:T(8,128)(2,1)}, bf16[2,1024,384]{2,1,0:T(8,128)(2,1)}) custom-call(s32[16]{0:T(128)} %get-tuple-element.191.rel, s32[16]{0:T(128)} %get-tuple-element.192.send, s32[4]{0:T(128)} %get-tuple-element.434.first, s32[4]{0:T(128)} %get-tuple-element.432.full, ...), custom_call_target="tpu_custom_call" | custom-call | flops 31000000512 | bytes 1048576 | tf_op jit(solution)/shard_map/attend_backward/pallas_call | solution.py:616
  374.2 5.8 %all-to-all-done.5 = bf16[4,256,1024]{2,1,0:T(8,128)(2,1)} async-done(((bf16[4,256,1024]{2,1,0:T(8,128)(2,1)}), bf16[4,256,1024]{2,1,0:T(8,128)(2,1)}, u32[]{:S(2)}, u32[]{:S(2)}) %all-to-all-start.5) | async-done | bytes 2097184 | tf_op jit(solution)/shard_map/all_to_all | solution.py:63
  380.1 6.3 %qkv_first.1.refs_2_ = f32[1024,384]{1,0:T(8,128)} custom-call(bf16[2048,1024]{1,0:T(8,128)(2,1)} %bitcast.131, bf16[2048,384]{1,0:T(8,128)(2,1)} %bitcast.137), custom_call_target="tpu_custom_call" | custom-call | flops 6000000000 | bytes 1048576 | tf_op jit(solution)/shard_map/qkv_first/pallas_call | solution.py:791
  386.4 3.5 core_sum.7
  389.8 7.4 %qkv_sums.1 = (bf16[256,384]{1,0:T(8,128)(2,1)}, bf16[256,384]{1,0:T(8,128)(2,1)}, bf16[256,384]{1,0:T(8,128)(2,1)}, bf16[256,384]{1,0:T(8,128)(2,1)}) custom-call(s32[3]{0:T(128)} %pad_add_fusion.ids.refs_0_, bf16[2048,1024]{1,0:T(8,128)(2,1)} %bitcast.130, bf16[2048,384]{1,0:T(8,128)(2,1)} %bitcast.136, f32[1024,384]{1,0:T(8,128)} %qkv_first.1.refs_2_), custom_call_target="tpu_custom_call" | custom-call | flops 6000000000 | bytes 1048576 | tf_op jit(solution)/shard_map/qkv_sums/pallas_call | solution.py:810
  397.2 3.0 all-gather.11.cloned.1.call-done
  400.2 4.5 all-to-all-start.6
  406.3 2.4 collective-permute-start.41
  409.2 2.0 add_convert_fusion.3
  412.2 9.5 %assemble.2 = (f32[256,4096]{1,0:T(8,128)}, f32[256,4096]{1,0:T(8,128)}, f32[256,1]{1,0:T(8,128)}, f32[8,128,1024]{2,1,0:T(8,128)}) custom-call(bf16[8,384,1024]{2,1,0:T(8,128)(2,1)} %bitcast.103, bf16[256,1]{1,0:T(8,128)(2,1)} %copy-done.27, bf16[256,4096]{1,0:T(8,128)(2,1)} %refs_2_, bf16[256,4096]{1,0:T(8,128)(2,1)} %refs_3_, bf16[8,384,1024]{2,1,0:T(8,128)(2,1)} %bitcast.104), custom_call_target="tpu_custom_call" | custom-call | tf_op jit(solution)/shard_map/assemble/pallas_call | solution.py:856
  425.9 7.1 %all-to-all-done.6 = bf16[4,256,1024]{2,1,0:T(8,128)(2,1)} async-done(((bf16[4,256,1024]{2,1,0:T(8,128)(2,1)}), bf16[4,256,1024]{2,1,0:T(8,128)(2,1)}, u32[]{:S(2)}, u32[]{:S(2)}) %all-to-all-start.6) | async-done | bytes 2097184 | tf_op jit(solution)/shard_map/all_to_all | solution.py:63
  433.0 2.4 broadcast_in_dim.55
  435.4 4.7 all-to-all-start.7
  440.2 2.1 convert_reduce_fusion.2
  442.3 2.6 convert_reduce_fusion.1
  445.9 21.0 %all-to-all-done.7 = bf16[4,256,896]{2,1,0:T(8,128)(2,1)} async-done(((bf16[4,256,896]{2,1,0:T(8,128)(2,1)}), bf16[4,256,896]{2,1,0:T(8,128)(2,1)}, u32[]{:S(2)}, u32[]{:S(2)}) %all-to-all-start.7) | async-done | bytes 1835040 | tf_op jit(solution)/shard_map/all_to_all | solution.py:63
  466.9 2.2 convert_reduce_fusion.5
  469.1 2.0 reshape.363
  472.9 2.9 fusion.20
  478.0 4.5 assemble.3
  484.1 2.0 fusion.21
  486.2 2.0 copy.78
  488.4 2.0 copy.77
  (310 shorter events, 86.1 us)
Async XLA Ops:
  12.1 118.9 %copy-start.4 = (bf16[256,1024]{1,0:T(8,128)(2,1)}, bf16[256,1024]{1,0:T(8,128)(2,1)S(1)}, u32[]{:S(2)}) copy-start(bf16[256,1024]{1,0:T(8,128)(2,1)S(1)} %get-tuple-element.406) | copy-start | bytes 1572868
  13.7 34.3 %all-to-all-start = ((bf16[4,256,1024]{2,1,0:T(8,128)(2,1)}), bf16[4,256,1024]{2,1,0:T(8,128)(2,1)}, u32[]{:S(2)}, u32[]{:S(2)}) async-start(bf16[4,256,1024]{2,1,0:T(8,128)(2,1)} %broadcast_in_dim.46), calls=%async_computation | async-start | bytes 4194304 | tf_op jit(solution)/shard_map/all_to_all | solution.py:63
  21.2 24.7 %collective-permute-start.2 = (bf16[256,512]{1,0:T(8,128)(2,1)S(1)}, bf16[256,512]{1,0:T(8,128)(2,1)}, u32[]{:S(2)}, u32[]{:S(2)}) collective-permute-start(bf16[256,512]{1,0:T(8,128)(2,1)S(1)} %concatenate.15), channel_id=1, source_target_pairs={{0,3},{1,2},{2,1},{3,0},{4,7},{5,6},{6,5},{7,4},{8,11},{9,10},{10,... | collective-permute-start | bytes 786440 | tf_op jit(solution)/shard_map/ppermute | solution.py:50
  25.6 22.4 %collective-permute-start.1 = (bf16[256,512]{1,0:T(8,128)(2,1)S(1)}, bf16[256,512]{1,0:T(8,128)(2,1)}, u32[]{:S(2)}, u32[]{:S(2)}) collective-permute-start(bf16[256,512]{1,0:T(8,128)(2,1)S(1)} %concatenate.15), channel_id=1, source_target_pairs={{0,2},{1,3},{2,0},{3,1},{4,6},{5,7},{6,4},{7,5},{8,10},{9,11},{10,... | collective-permute-start | bytes 786440 | tf_op jit(solution)/shard_map/ppermute | solution.py:50
  25.6 22.4 %collective-permute-start = (bf16[256,512]{1,0:T(8,128)(2,1)S(1)}, bf16[256,512]{1,0:T(8,128)(2,1)}, u32[]{:S(2)}, u32[]{:S(2)}) collective-permute-start(bf16[256,512]{1,0:T(8,128)(2,1)S(1)} %concatenate.15), channel_id=1, source_target_pairs={{0,1},{1,0},{2,3},{3,2},{4,5},{5,4},{6,7},{7,6},{8,9},{9,8},{10,11... | collective-permute-start | bytes 786440 | tf_op jit(solution)/shard_map/ppermute | solution.py:50
  44.3 47.1 %copy-start.14 = (bf16[256,1024]{1,0:T(8,128)(2,1)}, bf16[256,1024]{1,0:T(8,128)(2,1)S(1)}, u32[]{:S(2)}) copy-start(bf16[256,1024]{1,0:T(8,128)(2,1)S(1)} %get-tuple-element.217) | copy-start | bytes 1572868
  45.9 131.6 %copy-start.6 = (bf16[256,1024]{1,0:T(8,128)(2,1)}, bf16[256,1024]{1,0:T(8,128)(2,1)S(1)}, u32[]{:S(2)}) copy-start(bf16[256,1024]{1,0:T(8,128)(2,1)S(1)} %get-tuple-element.404) | copy-start | bytes 1572868
  49.6 14.3 %collective-permute-start.3 = (bf16[4,256,1024]{2,1,0:T(8,128)(2,1)}, bf16[4,256,1024]{2,1,0:T(8,128)(2,1)}, u32[]{:S(2)}, u32[]{:S(2)}) collective-permute-start(bf16[4,256,1024]{2,1,0:T(8,128)(2,1)} %all-to-all-done), channel_id=1, source_target_pairs={{0,4},{4,0},{1,5},{5,1},{2,6},{6,2},{3,7},{7,3},{8,12},{12,8},{9,1... | collective-permute-start | bytes 6291464 | tf_op jit(solution)/shard_map/ppermute | solution.py:40
  49.6 36.2 %collective-permute-start.6 = (bf16[128,1024]{1,0:T(8,128)(2,1)}, bf16[128,1024]{1,0:T(8,128)(2,1)}, u32[]{:S(2)}, u32[]{:S(2)}) collective-permute-start(bf16[128,1024]{1,0:T(8,128)(2,1)} %dynamic-slice_bitcast_fusion.4.refs_4_.refs_0_), channel_id=1, source_target_pairs={{0,3},{1,2},{2,1},{3,0},{4,7},{5,6},{6,5},{7,4},{8,11},{9,10},{10,... | collective-permute-start | bytes 786440 | tf_op jit(solution)/shard_map/ppermute | solution.py:50
  52.1 33.7 %collective-permute-start.5 = (bf16[128,1024]{1,0:T(8,128)(2,1)}, bf16[128,1024]{1,0:T(8,128)(2,1)}, u32[]{:S(2)}, u32[]{:S(2)}) collective-permute-start(bf16[128,1024]{1,0:T(8,128)(2,1)} %dynamic-slice_bitcast_fusion.4.refs_4_.refs_0_), channel_id=1, source_target_pairs={{0,2},{1,3},{2,0},{3,1},{4,6},{5,7},{6,4},{7,5},{8,10},{9,11},{10,... | collective-permute-start | bytes 786440 | tf_op jit(solution)/shard_map/ppermute | solution.py:50
  52.1 33.7 %collective-permute-start.4 = (bf16[128,1024]{1,0:T(8,128)(2,1)}, bf16[128,1024]{1,0:T(8,128)(2,1)}, u32[]{:S(2)}, u32[]{:S(2)}) collective-permute-start(bf16[128,1024]{1,0:T(8,128)(2,1)} %dynamic-slice_bitcast_fusion.4.refs_4_.refs_0_), channel_id=1, source_target_pairs={{0,1},{1,0},{2,3},{3,2},{4,5},{5,4},{6,7},{7,6},{8,9},{9,8},{10,11... | collective-permute-start | bytes 786440 | tf_op jit(solution)/shard_map/ppermute | solution.py:50
  54.0 31.8 %all-to-all-start.1 = ((bf16[4,256,1024]{2,1,0:T(8,128)(2,1)}), bf16[4,256,1024]{2,1,0:T(8,128)(2,1)}, u32[]{:S(2)}, u32[]{:S(2)}) async-start(bf16[4,256,1024]{2,1,0:T(8,128)(2,1)} %broadcast_in_dim.53), calls=%async_computation.1 | async-start | bytes 4194304 | tf_op jit(solution)/shard_map/all_to_all | solution.py:63
  58.5 124.3 %all-gather.7.cloned.1.call-start = ((), (), s32[]{:S(2)}) async-start(), calls=%async_computation.14 | async-start | bytes 3932160 | tf_op jit(solution)/shard_map/all_gather | solution.py:990
  85.9 11.5 %collective-permute-start.10 = (bf16[4,256,1024]{2,1,0:T(8,128)(2,1)}, bf16[4,256,1024]{2,1,0:T(8,128)(2,1)}, u32[]{:S(2)}, u32[]{:S(2)}) collective-permute-start(bf16[4,256,1024]{2,1,0:T(8,128)(2,1)} %all-to-all-done.1), channel_id=1, source_target_pairs={{0,4},{4,0},{1,5},{5,1},{2,6},{6,2},{3,7},{7,3},{8,12},{12,8},{9,1... | collective-permute-start | bytes 6291464 | tf_op jit(solution)/shard_map/ppermute | solution.py:40
  87.9 31.3 %collective-permute-start.7 = (bf16[512,128]{1,0:T(8,128)(2,1)}, bf16[512,128]{1,0:T(8,128)(2,1)S(1)}, u32[]{:S(2)}, u32[]{:S(2)}) collective-permute-start(bf16[512,128]{1,0:T(8,128)(2,1)} %get-tuple-element.209), channel_id=1, source_target_pairs={{0,8},{8,0},{16,24},{24,16},{1,9},{9,1},{17,25},{25,17},{2,10},{10... | collective-permute-start | bytes 393224 | tf_op jit(solution)/shard_map/ppermute | solution.py:45
  89.9 29.4 %collective-permute-start.8 = (bf16[512,128]{1,0:T(8,128)(2,1)}, bf16[512,128]{1,0:T(8,128)(2,1)S(1)}, u32[]{:S(2)}, u32[]{:S(2)}) collective-permute-start(bf16[512,128]{1,0:T(8,128)(2,1)} %get-tuple-element.210), channel_id=1, source_target_pairs={{0,16},{8,24},{16,0},{24,8},{1,17},{9,25},{17,1},{25,9},{2,18},{10... | collective-permute-start | bytes 393224 | tf_op jit(solution)/shard_map/ppermute | solution.py:45
  91.4 27.9 %collective-permute-start.9 = (bf16[512,128]{1,0:T(8,128)(2,1)}, bf16[512,128]{1,0:T(8,128)(2,1)S(1)}, u32[]{:S(2)}, u32[]{:S(2)}) collective-permute-start(bf16[512,128]{1,0:T(8,128)(2,1)} %get-tuple-element.211), channel_id=1, source_target_pairs={{0,24},{8,16},{16,8},{24,0},{1,25},{9,17},{17,9},{25,1},{2,26},{10... | collective-permute-start | bytes 393224 | tf_op jit(solution)/shard_map/ppermute | solution.py:45
  93.0 28.8 %all-to-all-start.2 = ((bf16[4,256,1024]{2,1,0:T(8,128)(2,1)}), bf16[4,256,1024]{2,1,0:T(8,128)(2,1)S(1)}, u32[]{:S(2)}, u32[]{:S(2)}) async-start(bf16[4,256,1024]{2,1,0:T(8,128)(2,1)} %broadcast_in_dim.54), calls=%async_computation.2 | async-start | bytes 4194304 | tf_op jit(solution)/shard_map/all_to_all | solution.py:63
  97.1 123.0 %all-gather.9.cloned.1.call-start = ((), (), s32[]{:S(2)}) async-start(), calls=%async_computation.15 | async-start | bytes 4718592 | tf_op jit(solution)/shard_map/all_gather | solution.py:973
  126.7 4.3 collective-permute-start.11
  127.5 6.3 %collective-permute-start.12 = (bf16[512,128]{1,0:T(8,128)(2,1)S(1)}, bf16[512,128]{1,0:T(8,128)(2,1)S(1)}, u32[]{:S(2)}, u32[]{:S(2)}) collective-permute-start(bf16[512,128]{1,0:T(8,128)(2,1)S(1)} %copy-done.56), channel_id=1, source_target_pairs={{0,8},{8,0},{16,24},{24,16},{1,9},{9,1},{17,25},{25,17},{2,10},{10... | collective-permute-start | bytes 393224 | tf_op jit(solution)/shard_map/ppermute | solution.py:45
  129.0 8.4 %collective-permute-start.13 = (bf16[512,128]{1,0:T(8,128)(2,1)S(1)}, bf16[512,128]{1,0:T(8,128)(2,1)S(1)}, u32[]{:S(2)}, u32[]{:S(2)}) collective-permute-start(bf16[512,128]{1,0:T(8,128)(2,1)S(1)} %copy-done.54), channel_id=1, source_target_pairs={{0,16},{8,24},{16,0},{24,8},{1,17},{9,25},{17,1},{25,9},{2,18},{10... | collective-permute-start | bytes 393224 | tf_op jit(solution)/shard_map/ppermute | solution.py:45
  129.5 7.9 %collective-permute-start.14 = (bf16[512,128]{1,0:T(8,128)(2,1)S(1)}, bf16[512,128]{1,0:T(8,128)(2,1)S(1)}, u32[]{:S(2)}, u32[]{:S(2)}) collective-permute-start(bf16[512,128]{1,0:T(8,128)(2,1)S(1)} %copy-done.52), channel_id=1, source_target_pairs={{0,24},{8,16},{16,8},{24,0},{1,25},{9,17},{17,9},{25,1},{2,26},{10... | collective-permute-start | bytes 393224 | tf_op jit(solution)/shard_map/ppermute | solution.py:45
  133.8 35.3 %copy-start.51 = (bf16[512,128]{1,0:T(8,128)(2,1)}, bf16[512,128]{1,0:T(8,128)(2,1)S(1)}, u32[]{:S(2)}) copy-start(bf16[512,128]{1,0:T(8,128)(2,1)S(1)} %collective-permute-done.12.refs_1_) | copy-start | bytes 393220
  137.4 31.7 %copy-start.53 = (bf16[512,128]{1,0:T(8,128)(2,1)}, bf16[512,128]{1,0:T(8,128)(2,1)S(1)}, u32[]{:S(2)}) copy-start(bf16[512,128]{1,0:T(8,128)(2,1)S(1)} %collective-permute-done.13.refs_2_) | copy-start | bytes 393220
  138.1 15.8 %collective-permute-start.17 = (bf16[256,1024]{1,0:T(8,128)(2,1)S(1)}, bf16[256,1024]{1,0:T(8,128)(2,1)S(1)}, u32[]{:S(2)}, u32[]{:S(2)}) collective-permute-start(bf16[256,1024]{1,0:T(8,128)(2,1)S(1)} %multiply_convert_fusion.1.refs_0_), channel_id=1, source_target_pairs={{0,24},{8,16},{16,8},{24,0},{1,25},{9,17},{17,9},{25,1},{2,26},{10... | collective-permute-start | bytes 1572872 | tf_op jit(solution)/shard_map/ppermute | solution.py:45
  139.6 24.0 %collective-permute-start.16 = (bf16[256,1024]{1,0:T(8,128)(2,1)S(1)}, bf16[256,1024]{1,0:T(8,128)(2,1)S(1)}, u32[]{:S(2)}, u32[]{:S(2)}) collective-permute-start(bf16[256,1024]{1,0:T(8,128)(2,1)S(1)} %multiply_convert_fusion.1.refs_0_), channel_id=1, source_target_pairs={{0,16},{8,24},{16,0},{24,8},{1,17},{9,25},{17,1},{25,9},{2,18},{10... | collective-permute-start | bytes 1572872 | tf_op jit(solution)/shard_map/ppermute | solution.py:45
  140.2 23.5 %collective-permute-start.15 = (bf16[256,1024]{1,0:T(8,128)(2,1)S(1)}, bf16[256,1024]{1,0:T(8,128)(2,1)S(1)}, u32[]{:S(2)}, u32[]{:S(2)}) collective-permute-start(bf16[256,1024]{1,0:T(8,128)(2,1)S(1)} %multiply_convert_fusion.1.refs_0_), channel_id=1, source_target_pairs={{0,8},{8,0},{16,24},{24,16},{1,9},{9,1},{17,25},{25,17},{2,10},{10... | collective-permute-start | bytes 1572872 | tf_op jit(solution)/shard_map/ppermute | solution.py:45
  168.3 122.6 %reduce-scatter.4.cloned.1.call-start = ((), (), s32[]{:S(2)}) async-start(), calls=%async_computation.11 | async-start | bytes 4718592 | tf_op jit(solution)/shard_map/reduce_scatter | solution.py:1033
  168.6 14.2 %collective-permute-start.19 = (bf16[4,256,1024]{2,1,0:T(8,128)(2,1)}, bf16[4,256,1024]{2,1,0:T(8,128)(2,1)}, u32[]{:S(2)}, u32[]{:S(2)}) collective-permute-start(bf16[4,256,1024]{2,1,0:T(8,128)(2,1)} %copy-done.23), channel_id=1, source_target_pairs={{0,4},{4,0},{1,5},{5,1},{2,6},{6,2},{3,7},{7,3},{8,12},{12,8},{9,1... | collective-permute-start | bytes 6291464 | tf_op jit(solution)/shard_map/ppermute | solution.py:40
  168.6 14.1 %collective-permute-start.18 = (bf16[4,256,1024]{2,1,0:T(8,128)(2,1)}, bf16[4,256,1024]{2,1,0:T(8,128)(2,1)}, u32[]{:S(2)}, u32[]{:S(2)}) collective-permute-start(bf16[4,256,1024]{2,1,0:T(8,128)(2,1)} %arrange.2), channel_id=1, source_target_pairs={{0,4},{4,0},{1,5},{5,1},{2,6},{6,2},{3,7},{7,3},{8,12},{12,8},{9,1... | collective-permute-start | bytes 6291464 | tf_op jit(solution)/shard_map/ppermute | solution.py:40
  172.5 5.0 %collective-permute-start.20 = (f32[256,1024]{1,0:T(8,128)}, f32[256,1024]{1,0:T(8,128)S(1)}, u32[]{:S(2)}, u32[]{:S(2)}) collective-permute-start(f32[256,1024]{1,0:T(8,128)} %get-tuple-element.255), channel_id=1, source_target_pairs={{0,4},{4,0},{1,5},{5,1},{2,6},{6,2},{3,7},{7,3},{8,12},{12,8},{9,1... | collective-permute-start | bytes 3145736 | tf_op jit(solution)/shard_map/ppermute | solution.py:40
  179.2 25.5 %collective-permute-start.23 = (bf16[256,1024]{1,0:T(8,128)(2,1)S(1)}, bf16[256,1024]{1,0:T(8,128)(2,1)S(1)}, u32[]{:S(2)}, u32[]{:S(2)}) collective-permute-start(bf16[256,1024]{1,0:T(8,128)(2,1)S(1)} %multiply_convert_fusion.refs_0_), channel_id=1, source_target_pairs={{0,24},{8,16},{16,8},{24,0},{1,25},{9,17},{17,9},{25,1},{2,26},{10... | collective-permute-start | bytes 1572872 | tf_op jit(solution)/shard_map/ppermute | solution.py:45
  180.7 26.6 %collective-permute-start.22 = (bf16[256,1024]{1,0:T(8,128)(2,1)S(1)}, bf16[256,1024]{1,0:T(8,128)(2,1)}, u32[]{:S(2)}, u32[]{:S(2)}) collective-permute-start(bf16[256,1024]{1,0:T(8,128)(2,1)S(1)} %multiply_convert_fusion.refs_0_), channel_id=1, source_target_pairs={{0,16},{8,24},{16,0},{24,8},{1,17},{9,25},{17,1},{25,9},{2,18},{10... | collective-permute-start | bytes 1572872 | tf_op jit(solution)/shard_map/ppermute | solution.py:45
  181.0 26.3 %collective-permute-start.21 = (bf16[256,1024]{1,0:T(8,128)(2,1)S(1)}, bf16[256,1024]{1,0:T(8,128)(2,1)}, u32[]{:S(2)}, u32[]{:S(2)}) collective-permute-start(bf16[256,1024]{1,0:T(8,128)(2,1)S(1)} %multiply_convert_fusion.refs_0_), channel_id=1, source_target_pairs={{0,8},{8,0},{16,24},{24,16},{1,9},{9,1},{17,25},{25,17},{2,10},{10... | collective-permute-start | bytes 1572872 | tf_op jit(solution)/shard_map/ppermute | solution.py:45
  207.3 4.6 collective-permute-start.25
  210.3 9.8 %collective-permute-start.24 = (bf16[4,256,1024]{2,1,0:T(8,128)(2,1)}, bf16[4,256,1024]{2,1,0:T(8,128)(2,1)}, u32[]{:S(2)}, u32[]{:S(2)}) collective-permute-start(bf16[4,256,1024]{2,1,0:T(8,128)(2,1)} %arrange.3), channel_id=1, source_target_pairs={{0,4},{4,0},{1,5},{5,1},{2,6},{6,2},{3,7},{7,3},{8,12},{12,8},{9,1... | collective-permute-start | bytes 6291464 | tf_op jit(solution)/shard_map/ppermute | solution.py:40
  215.4 30.0 %all-to-all-start.3 = ((bf16[4,256,1024]{2,1,0:T(8,128)(2,1)}), bf16[4,256,1024]{2,1,0:T(8,128)(2,1)}, u32[]{:S(2)}, u32[]{:S(2)}) async-start(bf16[4,256,1024]{2,1,0:T(8,128)(2,1)} %core_sum.4), calls=%async_computation.4 | async-start | bytes 4194304 | tf_op jit(solution)/shard_map/all_to_all | solution.py:63
  219.8 116.8 %reduce-scatter.6.cloned.1.call-start = ((), (), s32[]{:S(2)}) async-start(), calls=%async_computation.12 | async-start | bytes 3932160 | tf_op jit(solution)/shard_map/reduce_scatter | solution.py:1027
  245.4 23.1 %collective-permute-start.26 = (bf16[4,256,1024]{2,1,0:T(8,128)(2,1)}, bf16[4,256,1024]{2,1,0:T(8,128)(2,1)}, u32[]{:S(2)}, u32[]{:S(2)}) collective-permute-start(bf16[4,256,1024]{2,1,0:T(8,128)(2,1)} %bitcast.129), channel_id=1, source_target_pairs={{0,4},{4,0},{1,5},{5,1},{2,6},{6,2},{3,7},{7,3},{8,12},{12,8},{9,1... | collective-permute-start | bytes 6291464 | tf_op jit(solution)/shard_map/ppermute | solution.py:40
  272.1 2.4 collective-permute-start.27
  278.9 11.9 %collective-permute-start.28 = (bf16[512,128]{1,0:T(8,128)(2,1)}, bf16[512,128]{1,0:T(8,128)(2,1)S(1)}, u32[]{:S(2)}, u32[]{:S(2)}) collective-permute-start(bf16[512,128]{1,0:T(8,128)(2,1)} %get-tuple-element.277), channel_id=1, source_target_pairs={{0,8},{8,0},{16,24},{24,16},{1,9},{9,1},{17,25},{25,17},{2,10},{10... | collective-permute-start | bytes 393224 | tf_op jit(solution)/shard_map/ppermute | solution.py:45
  280.4 10.5 %collective-permute-start.29 = (bf16[512,128]{1,0:T(8,128)(2,1)}, bf16[512,128]{1,0:T(8,128)(2,1)S(1)}, u32[]{:S(2)}, u32[]{:S(2)}) collective-permute-start(bf16[512,128]{1,0:T(8,128)(2,1)} %get-tuple-element.278), channel_id=1, source_target_pairs={{0,16},{8,24},{16,0},{24,8},{1,17},{9,25},{17,1},{25,9},{2,18},{10... | collective-permute-start | bytes 393224 | tf_op jit(solution)/shard_map/ppermute | solution.py:45
  280.9 10.0 %collective-permute-start.30 = (bf16[512,128]{1,0:T(8,128)(2,1)}, bf16[512,128]{1,0:T(8,128)(2,1)S(1)}, u32[]{:S(2)}, u32[]{:S(2)}) collective-permute-start(bf16[512,128]{1,0:T(8,128)(2,1)} %get-tuple-element.279), channel_id=1, source_target_pairs={{0,24},{8,16},{16,8},{24,0},{1,25},{9,17},{17,9},{25,1},{2,26},{10... | collective-permute-start | bytes 393224 | tf_op jit(solution)/shard_map/ppermute | solution.py:45
  285.9 29.9 %all-to-all-start.4 = ((bf16[4,256,1024]{2,1,0:T(8,128)(2,1)}), bf16[4,256,1024]{2,1,0:T(8,128)(2,1)}, u32[]{:S(2)}, u32[]{:S(2)}) async-start(bf16[4,256,1024]{2,1,0:T(8,128)(2,1)} %core_sum.5), calls=%async_computation.5 | async-start | bytes 4194304 | tf_op jit(solution)/shard_map/all_to_all | solution.py:63
  290.3 109.9 %all-gather.11.cloned.1.call-start = ((), (), s32[]{:S(2)}) async-start(), calls=%async_computation.16 | async-start | bytes 7077888 | tf_op jit(solution)/shard_map/all_gather | solution.py:1090
  315.6 13.9 %collective-permute-start.35 = (bf16[4,256,1024]{2,1,0:T(8,128)(2,1)}, bf16[4,256,1024]{2,1,0:T(8,128)(2,1)}, u32[]{:S(2)}, u32[]{:S(2)}) collective-permute-start(bf16[4,256,1024]{2,1,0:T(8,128)(2,1)} %bitcast.124), channel_id=1, source_target_pairs={{0,4},{4,0},{1,5},{5,1},{2,6},{6,2},{3,7},{7,3},{8,12},{12,8},{9,1... | collective-permute-start | bytes 6291464 | tf_op jit(solution)/shard_map/ppermute | solution.py:40
  318.9 2.0 collective-permute-start.31
  326.1 6.9 %collective-permute-start.32 = (bf16[512,128]{1,0:T(8,128)(2,1)}, bf16[512,128]{1,0:T(8,128)(2,1)S(1)}, u32[]{:S(2)}, u32[]{:S(2)}) collective-permute-start(bf16[512,128]{1,0:T(8,128)(2,1)} %get-tuple-element.297), channel_id=1, source_target_pairs={{0,8},{8,0},{16,24},{24,16},{1,9},{9,1},{17,25},{25,17},{2,10},{10... | collective-permute-start | bytes 393224 | tf_op jit(solution)/shard_map/ppermute | solution.py:45
  328.0 8.6 %collective-permute-start.33 = (bf16[512,128]{1,0:T(8,128)(2,1)}, bf16[512,128]{1,0:T(8,128)(2,1)S(1)}, u32[]{:S(2)}, u32[]{:S(2)}) collective-permute-start(bf16[512,128]{1,0:T(8,128)(2,1)} %get-tuple-element.298), channel_id=1, source_target_pairs={{0,16},{8,24},{16,0},{24,8},{1,17},{9,25},{17,1},{25,9},{2,18},{10... | collective-permute-start | bytes 393224 | tf_op jit(solution)/shard_map/ppermute | solution.py:45
  329.5 7.1 %collective-permute-start.34 = (bf16[512,128]{1,0:T(8,128)(2,1)}, bf16[512,128]{1,0:T(8,128)(2,1)}, u32[]{:S(2)}, u32[]{:S(2)}) collective-permute-start(bf16[512,128]{1,0:T(8,128)(2,1)} %get-tuple-element.299), channel_id=1, source_target_pairs={{0,24},{8,16},{16,8},{24,0},{1,25},{9,17},{17,9},{25,1},{2,26},{10... | collective-permute-start | bytes 393224 | tf_op jit(solution)/shard_map/ppermute | solution.py:45
  341.1 33.1 %collective-permute-start.38 = (bf16[128,1024]{1,0:T(8,128)(2,1)}, bf16[128,1024]{1,0:T(8,128)(2,1)S(1)}, u32[]{:S(2)}, u32[]{:S(2)}) collective-permute-start(bf16[128,1024]{1,0:T(8,128)(2,1)} %get-tuple-element.417), channel_id=1, source_target_pairs={{0,3},{1,2},{2,1},{3,0},{4,7},{5,6},{6,5},{7,4},{8,11},{9,10},{10,... | collective-permute-start | bytes 786440 | tf_op jit(solution)/shard_map/ppermute | solution.py:50
  344.6 29.6 %collective-permute-start.37 = (bf16[128,1024]{1,0:T(8,128)(2,1)}, bf16[128,1024]{1,0:T(8,128)(2,1)}, u32[]{:S(2)}, u32[]{:S(2)}) collective-permute-start(bf16[128,1024]{1,0:T(8,128)(2,1)} %get-tuple-element.418), channel_id=1, source_target_pairs={{0,2},{1,3},{2,0},{3,1},{4,6},{5,7},{6,4},{7,5},{8,10},{9,11},{10,... | collective-permute-start | bytes 786440 | tf_op jit(solution)/shard_map/ppermute | solution.py:50
  344.6 29.6 %collective-permute-start.36 = (bf16[128,1024]{1,0:T(8,128)(2,1)}, bf16[128,1024]{1,0:T(8,128)(2,1)}, u32[]{:S(2)}, u32[]{:S(2)}) collective-permute-start(bf16[128,1024]{1,0:T(8,128)(2,1)} %get-tuple-element.419), channel_id=1, source_target_pairs={{0,1},{1,0},{2,3},{3,2},{4,5},{5,4},{6,7},{7,6},{8,9},{9,8},{10,11... | collective-permute-start | bytes 786440 | tf_op jit(solution)/shard_map/ppermute | solution.py:50
  345.5 34.6 %all-to-all-start.5 = ((bf16[4,256,1024]{2,1,0:T(8,128)(2,1)}), bf16[4,256,1024]{2,1,0:T(8,128)(2,1)}, u32[]{:S(2)}, u32[]{:S(2)}) async-start(bf16[4,256,1024]{2,1,0:T(8,128)(2,1)} %core_sum.6), calls=%async_computation.7 | async-start | bytes 4194304 | tf_op jit(solution)/shard_map/all_to_all | solution.py:63
  349.9 134.1 %reduce-scatter.8.cloned.1.call-start = ((), (), s32[]{:S(2)}) async-start(), calls=%async_computation.13 | async-start | bytes 4718592 | tf_op jit(solution)/shard_map/reduce_scatter | solution.py:1033
  380.1 6.3 %collective-permute-start.39 = (bf16[4,256,1024]{2,1,0:T(8,128)(2,1)}, bf16[4,256,1024]{2,1,0:T(8,128)(2,1)}, u32[]{:S(2)}, u32[]{:S(2)}) collective-permute-start(bf16[4,256,1024]{2,1,0:T(8,128)(2,1)} %bitcast.127), channel_id=1, source_target_pairs={{0,4},{4,0},{1,5},{5,1},{2,6},{6,2},{3,7},{7,3},{8,12},{12,8},{9,1... | collective-permute-start | bytes 6291464 | tf_op jit(solution)/shard_map/ppermute | solution.py:40
  400.2 32.7 %all-to-all-start.6 = ((bf16[4,256,1024]{2,1,0:T(8,128)(2,1)}), bf16[4,256,1024]{2,1,0:T(8,128)(2,1)}, u32[]{:S(2)}, u32[]{:S(2)}) async-start(bf16[4,256,1024]{2,1,0:T(8,128)(2,1)} %core_sum.7), calls=%async_computation.9 | async-start | bytes 4194304 | tf_op jit(solution)/shard_map/all_to_all | solution.py:63
  404.7 18.6 %collective-permute-start.40 = (bf16[256,384]{1,0:T(8,128)(2,1)}, bf16[256,384]{1,0:T(8,128)(2,1)}, u32[]{:S(2)}, u32[]{:S(2)}) collective-permute-start(bf16[256,384]{1,0:T(8,128)(2,1)} %get-tuple-element.326), channel_id=1, source_target_pairs={{0,1},{1,0},{2,3},{3,2},{4,5},{5,4},{6,7},{7,6},{8,9},{9,8},{10,11... | collective-permute-start | bytes 589832 | tf_op jit(solution)/shard_map/ppermute | solution.py:50
  406.3 17.4 %collective-permute-start.41 = (bf16[256,384]{1,0:T(8,128)(2,1)}, bf16[256,384]{1,0:T(8,128)(2,1)}, u32[]{:S(2)}, u32[]{:S(2)}) collective-permute-start(bf16[256,384]{1,0:T(8,128)(2,1)} %get-tuple-element.327), channel_id=1, source_target_pairs={{0,2},{1,3},{2,0},{3,1},{4,6},{5,7},{6,4},{7,5},{8,10},{9,11},{10,... | collective-permute-start | bytes 589832 | tf_op jit(solution)/shard_map/ppermute | solution.py:50
  408.7 15.0 %collective-permute-start.42 = (bf16[256,384]{1,0:T(8,128)(2,1)}, bf16[256,384]{1,0:T(8,128)(2,1)}, u32[]{:S(2)}, u32[]{:S(2)}) collective-permute-start(bf16[256,384]{1,0:T(8,128)(2,1)} %get-tuple-element.328), channel_id=1, source_target_pairs={{0,3},{1,2},{2,1},{3,0},{4,7},{5,6},{6,5},{7,4},{8,11},{9,10},{10,... | collective-permute-start | bytes 589832 | tf_op jit(solution)/shard_map/ppermute | solution.py:50
  435.4 31.5 %all-to-all-start.7 = ((bf16[4,256,896]{2,1,0:T(8,128)(2,1)}), bf16[4,256,896]{2,1,0:T(8,128)(2,1)}, u32[]{:S(2)}, u32[]{:S(2)}) async-start(bf16[4,256,896]{2,1,0:T(8,128)(2,1)} %broadcast_in_dim.55), calls=%async_computation.10 | async-start | bytes 3670016 | tf_op jit(solution)/shard_map/all_to_all | solution.py:63
  471.1 4.8 collective-permute-start.44
  472.4 4.7 collective-permute-start.43
  (59 other events, 329.9 us)
Sparse Core Ops, SparseCore 0:
  86.7 64.1 all-gather.6
  168.4 50.6 all-gather.8
  222.4 51.3 reduce-scatter.3
  276.1 60.2 reduce-scatter.5
  338.3 61.8 all-gather.10
  403.8 61.1 reduce-scatter.7

commit v5 on v4

--- a/solution.py
+++ b/solution.py
@@ -453,7 +453,7 @@
         cot = jnp.where(t < half, cot, cot_refs[1][...])
     pre = dot_nn(tile, gate_up[...])
     gate_pre, up_pre = pre[:, :size], pre[:, size:]
-    sigma = jax.nn.sigmoid(gate_pre)
+    sigma = 0.5 * jnp.tanh(0.5 * gate_pre) + 0.5
     active = gate_pre * sigma
     low = (active * up_pre).astype(bf16)
     grad_hidden = dot_nt(cot, down[...])
@@ -862,6 +862,7 @@
         in_specs=in_specs,
         out_specs=out_specs,
         compiler_params=LIMIT,
+        cost_estimate=cost(2),
         name="assemble",
     )(*args)
     return outs[:count], outs[count][:, 0], outs[count + 1 :]
@@ -1089,14 +1090,16 @@
     grad_got_one, shares = hold((grad_got_one, shares), total_zero)
     full_ffn = [lax.all_gather(share, PLANE, axis=0) for share in shares]
     part_near, part_far, grads_one = backward(1, saved_one, grad_got_one)
-    part_near, part_far, grads_one, sums_zero, out_sent = hold(
-        (part_near, part_far, grads_one, sums_zero, out_sent)
+    qkv_one = qkv_first(*qkv_stream(normed_one, grads_one))
+    part_near, part_far, qkv_one, sums_zero, out_sent = hold(
+        (part_near, part_far, qkv_one, sums_zero, out_sent)
     )
-    total_one = core_sum(by_chip(part_near), swap_core(by_chip(part_far)))
-    qkv_one = qkv_first(*qkv_stream(normed_one, grads_one))
-    total_one, qkv_one, grads_zero = hold((total_one, qkv_one, grads_zero))
+    far_swapped = swap_core(by_chip(part_far))
+    grad_qkv = qkv_sums(ids, *qkv_stream(normed_zero, grads_zero), qkv_one, shards)
+    part_near, far_swapped = hold((part_near, far_swapped), grad_qkv)
+    total_one = core_sum(by_chip(part_near), far_swapped)
     sums_one = exchange(total_one)
-    grad_qkv = qkv_sums(ids, *qkv_stream(normed_zero, grads_zero), qkv_one, shards)
+    full_ffn = hold(full_ffn, total_one)
     own_rows = feats // shards
     g_gate_up, g_gain_two, (g_down,) = assemble(
         [full_ffn[0]],
@@ -1109,9 +1112,9 @@
     )
     g_down = g_down.reshape(-1, feats)
     sent_qkv = send_pieces(grad_qkv)
-    sent_qkv, g_gate_up, g_gain_two, g_down = hold((sent_qkv, g_gate_up, g_gain_two, g_down))
+    sums_one, g_gate_up, g_gain_two, g_down = hold((sums_one, g_gate_up, g_gain_two, g_down))
     share_qkv = add_pieces(grad_qkv[0], sent_qkv)
-    out_sum_one = collect_out(hold(out_one[0], full_ffn, grad_qkv))
+    out_sum_one = collect_out(hold(out_one[0], g_down, sent_qkv))
     share_out = add_pieces(out_rel[0], out_sent)
     spare = share_out.size // rows
     if share_qkv.shape[0] == rows and spare % 128 == 0:

time: 506 us -> 504 us (level)
  transfers between devices with their start and end apart: 59 -> 59, of which waited for: 18 -> 16; matrix products, arithmetic and copies ran while one was open for 14% -> 14% of each run, Pallas kernels for 45% -> 44%
where the time goes in v5:
time: 504 us; the launch traced here: 496 us
  Pallas kernels  220 us (44%)
  waiting for transfers between devices  87.7 us (17%)
  starting transfers between devices  80.6 us (16%)
  local copies, waits for them, and re-layouts  48.3 us (10%)
  other arithmetic  43.7 us (9%)
  between operations  15.4 us (3%)
    pallas_call x2, Pallas kernels, attend_backward(): pl.pallas_call(backward_kernel, out_shape=(shape((seq_len // 2, feats), b...  48 us
    all_to_all x8, waiting for transfers between devices, exchange(): return lax.all_to_all(value, 'chip', 0, 0)  43.9 us
    pallas_call x2, Pallas kernels, attend_forward(): pl.pallas_call(forward_kernel, out_shape=[narrow, narrow, narrow, shape((...  43.8 us
    pallas_call x2, Pallas kernels, feed_forward(): pl.pallas_call(functools.partial(ffn_kernel, split=split, sides=len(cot))...  42.5 us
    all_to_all x8, starting transfers between devices, exchange(): return lax.all_to_all(value, 'chip', 0, 0)  36.6 us
    ppermute x18, waiting for transfers between devices, swap_chip(): return lax.ppermute(value, 'chip', [(i, i ^ mask) for i in range(count)])  33.5 us
    pallas_call x1, Pallas kernels, weight_sums(): pl.pallas_call(functools.partial(weight_kernel, counts=[len(v) for v in s...  23.1 us
    ppermute x18, starting transfers between devices, swap_chip(): return lax.ppermute(value, 'chip', [(i, i ^ mask) for i in range(count)])  21 us
  transfers between devices with their start and end apart: 59, of which 16 were waited for; matrix products, arithmetic and copies ran while one was open for 14% of the time, Pallas kernels for 44%

profile of v5, /device:TPU:0, one launch (start us, length us, event | category | flops | bytes accessed | tf_op | source)
XLA Modules:
  0.0 495.6 jit_solution(5667515042855249078)
XLA Ops:
  7.2 4.2 fusion.29
  13.7 5.3 %all-to-all-start = ((bf16[4,256,1024]{2,1,0:T(8,128)(2,1)}), bf16[4,256,1024]{2,1,0:T(8,128)(2,1)}, u32[]{:S(2)}, u32[]{:S(2)}) async-start(bf16[4,256,1024]{2,1,0:T(8,128)(2,1)} %broadcast_in_dim.46), calls=%async_computation | async-start | bytes 4194304 | tf_op jit(solution)/shard_map/all_to_all | solution.py:63
  21.2 4.4 collective-permute-start.2
  26.8 4.0 convert_reduce_fusion
  38.9 1.7 dynamic-slice_bitcast_fusion.4.refs_4_.refs_0_
  45.9 2.2 collective-permute-done.1
  48.0 1.6 broadcast_in_dim.53
  49.6 2.5 collective-permute-start.6
  52.1 1.9 collective-permute-start.4
  54.0 4.4 all-to-all-start.1
  63.9 21.9 %attend_forward.2 = (bf16[2048,128]{1,0:T(8,128)(2,1)}, bf16[2048,128]{1,0:T(8,128)(2,1)}, bf16[2048,128]{1,0:T(8,128)(2,1)}, bf16[2,1024,1024]{2,1,0:T(8,128)(2...) custom-call(s32[16]{0:T(128)} %get-tuple-element.189.rel, ...), custom_call_target="tpu_custom_call" | custom-call | flops 31000000512 | bytes 1048576 | tf_op jit(solution)/shard_map/attend_forward/pallas_call | solution.py:582
  87.9 1.9 collective-permute-start.7
  93.0 4.1 all-to-all-start.2
  97.3 21.9 %attend_forward.3 = (bf16[2048,128]{1,0:T(8,128)(2,1)}, bf16[2048,128]{1,0:T(8,128)(2,1)}, bf16[2048,128]{1,0:T(8,128)(2,1)}, bf16[2,1024,1024]{2,1,0:T(8,128)(2...) custom-call(s32[16]{0:T(128)} %get-tuple-element.189.rel, ...), custom_call_target="tpu_custom_call" | custom-call | flops 31000000512 | bytes 1048576 | tf_op jit(solution)/shard_map/attend_forward/pallas_call | solution.py:582
  119.3 2.6 all-to-all-done.2
  123.2 3.5 mix.2
  133.8 3.6 collective-permute-done.13.refs_2_
  141.6 12.3 %collective-permute-done.17.refs_3_ = bf16[256,1024]{1,0:T(8,128)(2,1)S(1)} collective-permute-done((bf16[256,1024]{1,0:T(8,128)(2,1)S(1)}, bf16[256,1024]{1,0:T(8,128)(2,1)S(1)}, u32[]{:S(2)}, u32[]{:S(2)}) %collective-permute-start.17) | collective-permute-done | bytes 524320 | tf_op jit(solution)/shard_map/ppermute | solution.py:45
  153.9 9.7 %collective-permute-done.16.refs_2_ = bf16[256,1024]{1,0:T(8,128)(2,1)S(1)} collective-permute-done((bf16[256,1024]{1,0:T(8,128)(2,1)S(1)}, bf16[256,1024]{1,0:T(8,128)(2,1)S(1)}, u32[]{:S(2)}, u32[]{:S(2)}) %collective-permute-start.16) | collective-permute-done | bytes 524320 | tf_op jit(solution)/shard_map/ppermute | solution.py:45
  165.2 3.1 arrange.2
  169.1 3.4 mix.3
  172.6 4.9 collective-permute-done.20
  181.0 1.8 collective-permute-start.21
  182.8 21.4 %feed_forward.2 = (bf16[4,2,256,1024]{3,2,1,0:T(8,128)(2,1)}, bf16[1024,1024]{1,0:T(8,128)(2,1)}, bf16[1024,1024]{1,0:T(8,128)(2,1)}, bf16[2048,512]{1,0:T(8,128)(2,1)}, bf16[2048,1024]{1,0:T(8,128)(2,1)}) custom-call(s32[3]{0:T(128)} %pad_add_fusion.ids.refs_0_, bf16[1024,1024]{1,0:T(8,128)(2,1)} %bitcast.122, bf16[1024,1024]{1,0:T(8,128)(2,1)} %bitcast.30.x_far.refs_1_, ...), custom_call_target="tpu_custom_call" | custom-call | flops 20000000000 | bytes 1048576 | tf_op jit(solution)/shard_map/feed_forward/pallas_call | solution.py:703
  204.2 3.1 collective-permute-done.22.refs_2_
  207.3 3.0 arrange.3
  211.9 3.5 core_sum.4
  215.4 4.5 all-to-all-start.3
  220.2 21.1 %feed_forward.3 = (bf16[4,2,256,1024]{3,2,1,0:T(8,128)(2,1)}, bf16[1024,1024]{1,0:T(8,128)(2,1)}, bf16[1024,1024]{1,0:T(8,128)(2,1)}, bf16[2048,512]{1,0:T(8,128)(2,1)}, bf16[2048,1024]{1,0:T(8,128)(2,1)}) custom-call(s32[3]{0:T(128)} %pad_add_fusion.ids.refs_0_, bf16[1024,1024]{1,0:T(8,128)(2,1)} %bitcast.125, bf16[1024,1024]{1,0:T(8,128)(2,1)} %bitcast.39.x_far.refs_7_, ...), custom_call_target="tpu_custom_call" | custom-call | flops 20000000000 | bytes 1048576 | tf_op jit(solution)/shard_map/feed_forward/pallas_call | solution.py:703
  241.3 4.1 all-to-all-done.3
  245.4 23.1 %weight_sums.1 = bf16[4,384,1024]{2,1,0:T(8,128)(2,1)} custom-call(s32[3]{0:T(128)} %pad_add_fusion.ids.refs_0_, bf16[1024,1024]{1,0:T(8,128)(2,1)} %bitcast.123, bf16[1024,1024]{1,0:T(8,128)(2,1)} %bitcast.30.x_far.refs_1_, bf16[2048,512]{1,0:T(8,128)(2,1)} %get-tuple-element.254.refs_2_, bf16[2048,1024]{1,0:T(8,128)(2,1)} %get-tuple-element.277.refs_3_, ...), custom_call_target="tpu_custom_call" | custom-call | flops 23000000512 | bytes 1048576 | tf_op jit(solution)/shard_map/weight_sums/pallas_call | solution.py:764
  268.5 2.1 convert_reduce_fusion.4
  274.5 4.4 unmix.2
  282.4 3.4 core_sum.5
  285.9 4.4 all-to-all-start.4
  291.6 24.0 %attend_backward.2 = (bf16[1024,1024]{1,0:T(8,128)(2,1)}, bf16[1024,1024]{1,0:T(8,128)(2,1)}, bf16[2,1024,384]{2,1,0:T(8,128)(2,1)}) custom-call(s32[16]{0:T(128)} %get-tuple-element.189.rel, s32[16]{0:T(128)} %get-tuple-element.190.send, s32[4]{0:T(128)} %get-tuple-element.430.first, s32[4]{0:T(128)} %get-tuple-element.428.full, ...), custom_call_target="tpu_custom_call" | custom-call | flops 31000000512 | bytes 1048576 | tf_op jit(solution)/shard_map/attend_backward/pallas_call | solution.py:616
  315.7 2.2 convert_reduce_fusion.3
  321.7 4.4 unmix.3
  326.1 1.9 collective-permute-start.32
  329.6 3.4 core_sum.6
  333.0 3.6 collective-permute-done.33.refs_2_
  336.6 2.5 add_convert_fusion
  341.1 3.5 collective-permute-start.38
  345.5 4.6 all-to-all-start.5
  350.1 24.0 %attend_backward.3 = (bf16[1024,1024]{1,0:T(8,128)(2,1)}, bf16[1024,1024]{1,0:T(8,128)(2,1)}, bf16[2,1024,384]{2,1,0:T(8,128)(2,1)}) custom-call(s32[16]{0:T(128)} %get-tuple-element.189.rel, s32[16]{0:T(128)} %get-tuple-element.190.send, s32[4]{0:T(128)} %get-tuple-element.431.first, s32[4]{0:T(128)} %get-tuple-element.429.full, ...), custom_call_target="tpu_custom_call" | custom-call | flops 31000000512 | bytes 1048576 | tf_op jit(solution)/shard_map/attend_backward/pallas_call | solution.py:616
  374.1 6.3 %qkv_first.1.refs_2_ = f32[1024,384]{1,0:T(8,128)} custom-call(bf16[2048,1024]{1,0:T(8,128)(2,1)} %bitcast.131, bf16[2048,384]{1,0:T(8,128)(2,1)} %bitcast.137), custom_call_target="tpu_custom_call" | custom-call | flops 6000000000 | bytes 1048576 | tf_op jit(solution)/shard_map/qkv_first/pallas_call | solution.py:791
  380.5 7.3 %qkv_sums.1 = (bf16[256,384]{1,0:T(8,128)(2,1)}, bf16[256,384]{1,0:T(8,128)(2,1)}, bf16[256,384]{1,0:T(8,128)(2,1)}, bf16[256,384]{1,0:T(8,128)(2,1)}) custom-call(s32[3]{0:T(128)} %pad_add_fusion.ids.refs_0_, bf16[2048,1024]{1,0:T(8,128)(2,1)} %bitcast.130, bf16[2048,384]{1,0:T(8,128)(2,1)} %bitcast.136, f32[1024,384]{1,0:T(8,128)} %qkv_first.1.refs_2_), custom_call_target="tpu_custom_call" | custom-call | flops 6000000000 | bytes 1048576 | tf_op jit(solution)/shard_map/qkv_sums/pallas_call | solution.py:810
  387.8 3.4 core_sum.7
  391.3 4.4 all-to-all-start.6
  397.0 2.8 collective-permute-start.41
  400.2 9.0 %assemble.2 = (f32[256,4096]{1,0:T(8,128)}, f32[256,4096]{1,0:T(8,128)}, f32[256,1]{1,0:T(8,128)}, f32[8,128,1024]{2,1,0:T(8,128)}) custom-call(bf16[8,384,1024]{2,1,0:T(8,128)(2,1)} %bitcast.103, bf16[256,1]{1,0:T(8,128)(2,1)} %copy-done.26, bf16[256,4096]{1,0:T(8,128)(2,1)} %refs_2_, bf16[256,4096]{1,0:T(8,128)(2,1)} %refs_3_, bf16[8,384,1024]{2,1,0:T(8,128)(2,1)} %bitcast.104), custom_call_target="tpu_custom_call" | custom-call | flops 2000000000 | bytes 1048576 | tf_op jit(solution)/shard_map/assemble/pallas_call | solution.py:856
  410.7 11.3 %all-to-all-done.6 = bf16[4,256,1024]{2,1,0:T(8,128)(2,1)} async-done(((bf16[4,256,1024]{2,1,0:T(8,128)(2,1)}), bf16[4,256,1024]{2,1,0:T(8,128)(2,1)}, u32[]{:S(2)}, u32[]{:S(2)}) %all-to-all-start.6) | async-done | bytes 2097184 | tf_op jit(solution)/shard_map/all_to_all | solution.py:63
  422.1 2.0 add_convert_fusion.3
  427.9 4.8 all-to-all-start.7
  432.7 2.4 convert_reduce_fusion.2
  435.1 2.6 convert_reduce_fusion.1
  438.7 25.9 %all-to-all-done.7 = bf16[4,256,896]{2,1,0:T(8,128)(2,1)} async-done(((bf16[4,256,896]{2,1,0:T(8,128)(2,1)}), bf16[4,256,896]{2,1,0:T(8,128)(2,1)}, u32[]{:S(2)}, u32[]{:S(2)}) %all-to-all-start.7) | async-done | bytes 1835040 | tf_op jit(solution)/shard_map/all_to_all | solution.py:63
  464.6 2.2 convert_reduce_fusion.5
  466.9 2.0 reshape.363
  470.7 2.9 fusion.20
  475.7 4.5 assemble.3
  482.1 2.0 fusion.21
  484.3 2.0 copy.78
  486.5 2.0 copy.77
  (310 shorter events, 81.1 us)
Async XLA Ops:
  12.1 118.9 %copy-start.4 = (bf16[256,1024]{1,0:T(8,128)(2,1)}, bf16[256,1024]{1,0:T(8,128)(2,1)S(1)}, u32[]{:S(2)}) copy-start(bf16[256,1024]{1,0:T(8,128)(2,1)S(1)} %get-tuple-element.402) | copy-start | bytes 1572868
  13.7 34.3 %all-to-all-start = ((bf16[4,256,1024]{2,1,0:T(8,128)(2,1)}), bf16[4,256,1024]{2,1,0:T(8,128)(2,1)}, u32[]{:S(2)}, u32[]{:S(2)}) async-start(bf16[4,256,1024]{2,1,0:T(8,128)(2,1)} %broadcast_in_dim.46), calls=%async_computation | async-start | bytes 4194304 | tf_op jit(solution)/shard_map/all_to_all | solution.py:63
  21.2 24.7 %collective-permute-start.2 = (bf16[256,512]{1,0:T(8,128)(2,1)S(1)}, bf16[256,512]{1,0:T(8,128)(2,1)}, u32[]{:S(2)}, u32[]{:S(2)}) collective-permute-start(bf16[256,512]{1,0:T(8,128)(2,1)S(1)} %concatenate.15), channel_id=1, source_target_pairs={{0,3},{1,2},{2,1},{3,0},{4,7},{5,6},{6,5},{7,4},{8,11},{9,10},{10,... | collective-permute-start | bytes 786440 | tf_op jit(solution)/shard_map/ppermute | solution.py:50
  25.6 22.4 %collective-permute-start.1 = (bf16[256,512]{1,0:T(8,128)(2,1)S(1)}, bf16[256,512]{1,0:T(8,128)(2,1)}, u32[]{:S(2)}, u32[]{:S(2)}) collective-permute-start(bf16[256,512]{1,0:T(8,128)(2,1)S(1)} %concatenate.15), channel_id=1, source_target_pairs={{0,2},{1,3},{2,0},{3,1},{4,6},{5,7},{6,4},{7,5},{8,10},{9,11},{10,... | collective-permute-start | bytes 786440 | tf_op jit(solution)/shard_map/ppermute | solution.py:50
  25.6 22.4 %collective-permute-start = (bf16[256,512]{1,0:T(8,128)(2,1)S(1)}, bf16[256,512]{1,0:T(8,128)(2,1)}, u32[]{:S(2)}, u32[]{:S(2)}) collective-permute-start(bf16[256,512]{1,0:T(8,128)(2,1)S(1)} %concatenate.15), channel_id=1, source_target_pairs={{0,1},{1,0},{2,3},{3,2},{4,5},{5,4},{6,7},{7,6},{8,9},{9,8},{10,11... | collective-permute-start | bytes 786440 | tf_op jit(solution)/shard_map/ppermute | solution.py:50
  44.3 47.1 %copy-start.14 = (bf16[256,1024]{1,0:T(8,128)(2,1)}, bf16[256,1024]{1,0:T(8,128)(2,1)S(1)}, u32[]{:S(2)}) copy-start(bf16[256,1024]{1,0:T(8,128)(2,1)S(1)} %get-tuple-element.215) | copy-start | bytes 1572868
  45.9 131.6 %copy-start.6 = (bf16[256,1024]{1,0:T(8,128)(2,1)}, bf16[256,1024]{1,0:T(8,128)(2,1)S(1)}, u32[]{:S(2)}) copy-start(bf16[256,1024]{1,0:T(8,128)(2,1)S(1)} %get-tuple-element.400) | copy-start | bytes 1572868
  49.6 14.3 %collective-permute-start.3 = (bf16[4,256,1024]{2,1,0:T(8,128)(2,1)}, bf16[4,256,1024]{2,1,0:T(8,128)(2,1)}, u32[]{:S(2)}, u32[]{:S(2)}) collective-permute-start(bf16[4,256,1024]{2,1,0:T(8,128)(2,1)} %all-to-all-done), channel_id=1, source_target_pairs={{0,4},{4,0},{1,5},{5,1},{2,6},{6,2},{3,7},{7,3},{8,12},{12,8},{9,1... | collective-permute-start | bytes 6291464 | tf_op jit(solution)/shard_map/ppermute | solution.py:40
  49.6 36.2 %collective-permute-start.6 = (bf16[128,1024]{1,0:T(8,128)(2,1)}, bf16[128,1024]{1,0:T(8,128)(2,1)}, u32[]{:S(2)}, u32[]{:S(2)}) collective-permute-start(bf16[128,1024]{1,0:T(8,128)(2,1)} %dynamic-slice_bitcast_fusion.4.refs_4_.refs_0_), channel_id=1, source_target_pairs={{0,3},{1,2},{2,1},{3,0},{4,7},{5,6},{6,5},{7,4},{8,11},{9,10},{10,... | collective-permute-start | bytes 786440 | tf_op jit(solution)/shard_map/ppermute | solution.py:50
  52.1 33.7 %collective-permute-start.5 = (bf16[128,1024]{1,0:T(8,128)(2,1)}, bf16[128,1024]{1,0:T(8,128)(2,1)}, u32[]{:S(2)}, u32[]{:S(2)}) collective-permute-start(bf16[128,1024]{1,0:T(8,128)(2,1)} %dynamic-slice_bitcast_fusion.4.refs_4_.refs_0_), channel_id=1, source_target_pairs={{0,2},{1,3},{2,0},{3,1},{4,6},{5,7},{6,4},{7,5},{8,10},{9,11},{10,... | collective-permute-start | bytes 786440 | tf_op jit(solution)/shard_map/ppermute | solution.py:50
  52.1 33.7 %collective-permute-start.4 = (bf16[128,1024]{1,0:T(8,128)(2,1)}, bf16[128,1024]{1,0:T(8,128)(2,1)}, u32[]{:S(2)}, u32[]{:S(2)}) collective-permute-start(bf16[128,1024]{1,0:T(8,128)(2,1)} %dynamic-slice_bitcast_fusion.4.refs_4_.refs_0_), channel_id=1, source_target_pairs={{0,1},{1,0},{2,3},{3,2},{4,5},{5,4},{6,7},{7,6},{8,9},{9,8},{10,11... | collective-permute-start | bytes 786440 | tf_op jit(solution)/shard_map/ppermute | solution.py:50
  54.0 31.8 %all-to-all-start.1 = ((bf16[4,256,1024]{2,1,0:T(8,128)(2,1)}), bf16[4,256,1024]{2,1,0:T(8,128)(2,1)}, u32[]{:S(2)}, u32[]{:S(2)}) async-start(bf16[4,256,1024]{2,1,0:T(8,128)(2,1)} %broadcast_in_dim.53), calls=%async_computation.1 | async-start | bytes 4194304 | tf_op jit(solution)/shard_map/all_to_all | solution.py:63
  58.5 124.3 %all-gather.7.cloned.1.call-start = ((), (), s32[]{:S(2)}) async-start(), calls=%async_computation.14 | async-start | bytes 3932160 | tf_op jit(solution)/shard_map/all_gather | solution.py:991
  85.8 11.5 %collective-permute-start.10 = (bf16[4,256,1024]{2,1,0:T(8,128)(2,1)}, bf16[4,256,1024]{2,1,0:T(8,128)(2,1)}, u32[]{:S(2)}, u32[]{:S(2)}) collective-permute-start(bf16[4,256,1024]{2,1,0:T(8,128)(2,1)} %all-to-all-done.1), channel_id=1, source_target_pairs={{0,4},{4,0},{1,5},{5,1},{2,6},{6,2},{3,7},{7,3},{8,12},{12,8},{9,1... | collective-permute-start | bytes 6291464 | tf_op jit(solution)/shard_map/ppermute | solution.py:40
  87.9 31.3 %collective-permute-start.7 = (bf16[512,128]{1,0:T(8,128)(2,1)}, bf16[512,128]{1,0:T(8,128)(2,1)S(1)}, u32[]{:S(2)}, u32[]{:S(2)}) collective-permute-start(bf16[512,128]{1,0:T(8,128)(2,1)} %get-tuple-element.207), channel_id=1, source_target_pairs={{0,8},{8,0},{16,24},{24,16},{1,9},{9,1},{17,25},{25,17},{2,10},{10... | collective-permute-start | bytes 393224 | tf_op jit(solution)/shard_map/ppermute | solution.py:45
  89.9 29.4 %collective-permute-start.8 = (bf16[512,128]{1,0:T(8,128)(2,1)}, bf16[512,128]{1,0:T(8,128)(2,1)S(1)}, u32[]{:S(2)}, u32[]{:S(2)}) collective-permute-start(bf16[512,128]{1,0:T(8,128)(2,1)} %get-tuple-element.208), channel_id=1, source_target_pairs={{0,16},{8,24},{16,0},{24,8},{1,17},{9,25},{17,1},{25,9},{2,18},{10... | collective-permute-start | bytes 393224 | tf_op jit(solution)/shard_map/ppermute | solution.py:45
  91.4 27.9 %collective-permute-start.9 = (bf16[512,128]{1,0:T(8,128)(2,1)}, bf16[512,128]{1,0:T(8,128)(2,1)S(1)}, u32[]{:S(2)}, u32[]{:S(2)}) collective-permute-start(bf16[512,128]{1,0:T(8,128)(2,1)} %get-tuple-element.209), channel_id=1, source_target_pairs={{0,24},{8,16},{16,8},{24,0},{1,25},{9,17},{17,9},{25,1},{2,26},{10... | collective-permute-start | bytes 393224 | tf_op jit(solution)/shard_map/ppermute | solution.py:45
  93.0 28.8 %all-to-all-start.2 = ((bf16[4,256,1024]{2,1,0:T(8,128)(2,1)}), bf16[4,256,1024]{2,1,0:T(8,128)(2,1)S(1)}, u32[]{:S(2)}, u32[]{:S(2)}) async-start(bf16[4,256,1024]{2,1,0:T(8,128)(2,1)} %broadcast_in_dim.54), calls=%async_computation.2 | async-start | bytes 4194304 | tf_op jit(solution)/shard_map/all_to_all | solution.py:63
  97.1 123.0 %all-gather.9.cloned.1.call-start = ((), (), s32[]{:S(2)}) async-start(), calls=%async_computation.15 | async-start | bytes 4718592 | tf_op jit(solution)/shard_map/all_gather | solution.py:974
  126.7 4.3 collective-permute-start.11
  127.5 6.3 %collective-permute-start.12 = (bf16[512,128]{1,0:T(8,128)(2,1)S(1)}, bf16[512,128]{1,0:T(8,128)(2,1)S(1)}, u32[]{:S(2)}, u32[]{:S(2)}) collective-permute-start(bf16[512,128]{1,0:T(8,128)(2,1)S(1)} %copy-done.56), channel_id=1, source_target_pairs={{0,8},{8,0},{16,24},{24,16},{1,9},{9,1},{17,25},{25,17},{2,10},{10... | collective-permute-start | bytes 393224 | tf_op jit(solution)/shard_map/ppermute | solution.py:45
  129.0 8.4 %collective-permute-start.13 = (bf16[512,128]{1,0:T(8,128)(2,1)S(1)}, bf16[512,128]{1,0:T(8,128)(2,1)S(1)}, u32[]{:S(2)}, u32[]{:S(2)}) collective-permute-start(bf16[512,128]{1,0:T(8,128)(2,1)S(1)} %copy-done.54), channel_id=1, source_target_pairs={{0,16},{8,24},{16,0},{24,8},{1,17},{9,25},{17,1},{25,9},{2,18},{10... | collective-permute-start | bytes 393224 | tf_op jit(solution)/shard_map/ppermute | solution.py:45
  129.5 7.9 %collective-permute-start.14 = (bf16[512,128]{1,0:T(8,128)(2,1)S(1)}, bf16[512,128]{1,0:T(8,128)(2,1)S(1)}, u32[]{:S(2)}, u32[]{:S(2)}) collective-permute-start(bf16[512,128]{1,0:T(8,128)(2,1)S(1)} %copy-done.52), channel_id=1, source_target_pairs={{0,24},{8,16},{16,8},{24,0},{1,25},{9,17},{17,9},{25,1},{2,26},{10... | collective-permute-start | bytes 393224 | tf_op jit(solution)/shard_map/ppermute | solution.py:45
  133.8 35.3 %copy-start.51 = (bf16[512,128]{1,0:T(8,128)(2,1)}, bf16[512,128]{1,0:T(8,128)(2,1)S(1)}, u32[]{:S(2)}) copy-start(bf16[512,128]{1,0:T(8,128)(2,1)S(1)} %collective-permute-done.12.refs_1_) | copy-start | bytes 393220
  137.4 31.7 %copy-start.53 = (bf16[512,128]{1,0:T(8,128)(2,1)}, bf16[512,128]{1,0:T(8,128)(2,1)S(1)}, u32[]{:S(2)}) copy-start(bf16[512,128]{1,0:T(8,128)(2,1)S(1)} %collective-permute-done.13.refs_2_) | copy-start | bytes 393220
  138.1 15.8 %collective-permute-start.17 = (bf16[256,1024]{1,0:T(8,128)(2,1)S(1)}, bf16[256,1024]{1,0:T(8,128)(2,1)S(1)}, u32[]{:S(2)}, u32[]{:S(2)}) collective-permute-start(bf16[256,1024]{1,0:T(8,128)(2,1)S(1)} %multiply_convert_fusion.1.refs_0_), channel_id=1, source_target_pairs={{0,24},{8,16},{16,8},{24,0},{1,25},{9,17},{17,9},{25,1},{2,26},{10... | collective-permute-start | bytes 1572872 | tf_op jit(solution)/shard_map/ppermute | solution.py:45
  139.6 24.0 %collective-permute-start.16 = (bf16[256,1024]{1,0:T(8,128)(2,1)S(1)}, bf16[256,1024]{1,0:T(8,128)(2,1)S(1)}, u32[]{:S(2)}, u32[]{:S(2)}) collective-permute-start(bf16[256,1024]{1,0:T(8,128)(2,1)S(1)} %multiply_convert_fusion.1.refs_0_), channel_id=1, source_target_pairs={{0,16},{8,24},{16,0},{24,8},{1,17},{9,25},{17,1},{25,9},{2,18},{10... | collective-permute-start | bytes 1572872 | tf_op jit(solution)/shard_map/ppermute | solution.py:45
  140.2 23.5 %collective-permute-start.15 = (bf16[256,1024]{1,0:T(8,128)(2,1)S(1)}, bf16[256,1024]{1,0:T(8,128)(2,1)S(1)}, u32[]{:S(2)}, u32[]{:S(2)}) collective-permute-start(bf16[256,1024]{1,0:T(8,128)(2,1)S(1)} %multiply_convert_fusion.1.refs_0_), channel_id=1, source_target_pairs={{0,8},{8,0},{16,24},{24,16},{1,9},{9,1},{17,25},{25,17},{2,10},{10... | collective-permute-start | bytes 1572872 | tf_op jit(solution)/shard_map/ppermute | solution.py:45
  168.3 122.5 %reduce-scatter.4.cloned.1.call-start = ((), (), s32[]{:S(2)}) async-start(), calls=%async_computation.11 | async-start | bytes 4718592 | tf_op jit(solution)/shard_map/reduce_scatter | solution.py:1034
  168.6 14.2 %collective-permute-start.19 = (bf16[4,256,1024]{2,1,0:T(8,128)(2,1)}, bf16[4,256,1024]{2,1,0:T(8,128)(2,1)}, u32[]{:S(2)}, u32[]{:S(2)}) collective-permute-start(bf16[4,256,1024]{2,1,0:T(8,128)(2,1)} %copy-done.22), channel_id=1, source_target_pairs={{0,4},{4,0},{1,5},{5,1},{2,6},{6,2},{3,7},{7,3},{8,12},{12,8},{9,1... | collective-permute-start | bytes 6291464 | tf_op jit(solution)/shard_map/ppermute | solution.py:40
  168.6 14.1 %collective-permute-start.18 = (bf16[4,256,1024]{2,1,0:T(8,128)(2,1)}, bf16[4,256,1024]{2,1,0:T(8,128)(2,1)}, u32[]{:S(2)}, u32[]{:S(2)}) collective-permute-start(bf16[4,256,1024]{2,1,0:T(8,128)(2,1)} %arrange.2), channel_id=1, source_target_pairs={{0,4},{4,0},{1,5},{5,1},{2,6},{6,2},{3,7},{7,3},{8,12},{12,8},{9,1... | collective-permute-start | bytes 6291464 | tf_op jit(solution)/shard_map/ppermute | solution.py:40
  172.5 5.0 %collective-permute-start.20 = (f32[256,1024]{1,0:T(8,128)}, f32[256,1024]{1,0:T(8,128)S(1)}, u32[]{:S(2)}, u32[]{:S(2)}) collective-permute-start(f32[256,1024]{1,0:T(8,128)} %get-tuple-element.253), channel_id=1, source_target_pairs={{0,4},{4,0},{1,5},{5,1},{2,6},{6,2},{3,7},{7,3},{8,12},{12,8},{9,1... | collective-permute-start | bytes 3145736 | tf_op jit(solution)/shard_map/ppermute | solution.py:40
  179.2 25.0 %collective-permute-start.23 = (bf16[256,1024]{1,0:T(8,128)(2,1)S(1)}, bf16[256,1024]{1,0:T(8,128)(2,1)S(1)}, u32[]{:S(2)}, u32[]{:S(2)}) collective-permute-start(bf16[256,1024]{1,0:T(8,128)(2,1)S(1)} %multiply_convert_fusion.refs_0_), channel_id=1, source_target_pairs={{0,24},{8,16},{16,8},{24,0},{1,25},{9,17},{17,9},{25,1},{2,26},{10... | collective-permute-start | bytes 1572872 | tf_op jit(solution)/shard_map/ppermute | solution.py:45
  180.7 26.6 %collective-permute-start.22 = (bf16[256,1024]{1,0:T(8,128)(2,1)S(1)}, bf16[256,1024]{1,0:T(8,128)(2,1)}, u32[]{:S(2)}, u32[]{:S(2)}) collective-permute-start(bf16[256,1024]{1,0:T(8,128)(2,1)S(1)} %multiply_convert_fusion.refs_0_), channel_id=1, source_target_pairs={{0,16},{8,24},{16,0},{24,8},{1,17},{9,25},{17,1},{25,9},{2,18},{10... | collective-permute-start | bytes 1572872 | tf_op jit(solution)/shard_map/ppermute | solution.py:45
  181.0 26.3 %collective-permute-start.21 = (bf16[256,1024]{1,0:T(8,128)(2,1)S(1)}, bf16[256,1024]{1,0:T(8,128)(2,1)}, u32[]{:S(2)}, u32[]{:S(2)}) collective-permute-start(bf16[256,1024]{1,0:T(8,128)(2,1)S(1)} %multiply_convert_fusion.refs_0_), channel_id=1, source_target_pairs={{0,8},{8,0},{16,24},{24,16},{1,9},{9,1},{17,25},{25,17},{2,10},{10... | collective-permute-start | bytes 1572872 | tf_op jit(solution)/shard_map/ppermute | solution.py:45
  207.3 4.6 collective-permute-start.25
  210.3 9.8 %collective-permute-start.24 = (bf16[4,256,1024]{2,1,0:T(8,128)(2,1)}, bf16[4,256,1024]{2,1,0:T(8,128)(2,1)}, u32[]{:S(2)}, u32[]{:S(2)}) collective-permute-start(bf16[4,256,1024]{2,1,0:T(8,128)(2,1)} %arrange.3), channel_id=1, source_target_pairs={{0,4},{4,0},{1,5},{5,1},{2,6},{6,2},{3,7},{7,3},{8,12},{12,8},{9,1... | collective-permute-start | bytes 6291464 | tf_op jit(solution)/shard_map/ppermute | solution.py:40
  215.4 30.0 %all-to-all-start.3 = ((bf16[4,256,1024]{2,1,0:T(8,128)(2,1)}), bf16[4,256,1024]{2,1,0:T(8,128)(2,1)}, u32[]{:S(2)}, u32[]{:S(2)}) async-start(bf16[4,256,1024]{2,1,0:T(8,128)(2,1)} %core_sum.4), calls=%async_computation.4 | async-start | bytes 4194304 | tf_op jit(solution)/shard_map/all_to_all | solution.py:63
  219.8 116.7 %reduce-scatter.6.cloned.1.call-start = ((), (), s32[]{:S(2)}) async-start(), calls=%async_computation.12 | async-start | bytes 3932160 | tf_op jit(solution)/shard_map/reduce_scatter | solution.py:1028
  245.4 23.1 %collective-permute-start.26 = (bf16[4,256,1024]{2,1,0:T(8,128)(2,1)}, bf16[4,256,1024]{2,1,0:T(8,128)(2,1)}, u32[]{:S(2)}, u32[]{:S(2)}) collective-permute-start(bf16[4,256,1024]{2,1,0:T(8,128)(2,1)} %bitcast.129), channel_id=1, source_target_pairs={{0,4},{4,0},{1,5},{5,1},{2,6},{6,2},{3,7},{7,3},{8,12},{12,8},{9,1... | collective-permute-start | bytes 6291464 | tf_op jit(solution)/shard_map/ppermute | solution.py:40
  272.1 2.4 collective-permute-start.27
  278.9 11.9 %collective-permute-start.28 = (bf16[512,128]{1,0:T(8,128)(2,1)}, bf16[512,128]{1,0:T(8,128)(2,1)S(1)}, u32[]{:S(2)}, u32[]{:S(2)}) collective-permute-start(bf16[512,128]{1,0:T(8,128)(2,1)} %get-tuple-element.283), channel_id=1, source_target_pairs={{0,8},{8,0},{16,24},{24,16},{1,9},{9,1},{17,25},{25,17},{2,10},{10... | collective-permute-start | bytes 393224 | tf_op jit(solution)/shard_map/ppermute | solution.py:45
  280.4 10.5 %collective-permute-start.29 = (bf16[512,128]{1,0:T(8,128)(2,1)}, bf16[512,128]{1,0:T(8,128)(2,1)S(1)}, u32[]{:S(2)}, u32[]{:S(2)}) collective-permute-start(bf16[512,128]{1,0:T(8,128)(2,1)} %get-tuple-element.284), channel_id=1, source_target_pairs={{0,16},{8,24},{16,0},{24,8},{1,17},{9,25},{17,1},{25,9},{2,18},{10... | collective-permute-start | bytes 393224 | tf_op jit(solution)/shard_map/ppermute | solution.py:45
  280.9 9.9 %collective-permute-start.30 = (bf16[512,128]{1,0:T(8,128)(2,1)}, bf16[512,128]{1,0:T(8,128)(2,1)S(1)}, u32[]{:S(2)}, u32[]{:S(2)}) collective-permute-start(bf16[512,128]{1,0:T(8,128)(2,1)} %get-tuple-element.285), channel_id=1, source_target_pairs={{0,24},{8,16},{16,8},{24,0},{1,25},{9,17},{17,9},{25,1},{2,26},{10... | collective-permute-start | bytes 393224 | tf_op jit(solution)/shard_map/ppermute | solution.py:45
  285.9 29.8 %all-to-all-start.4 = ((bf16[4,256,1024]{2,1,0:T(8,128)(2,1)}), bf16[4,256,1024]{2,1,0:T(8,128)(2,1)}, u32[]{:S(2)}, u32[]{:S(2)}) async-start(bf16[4,256,1024]{2,1,0:T(8,128)(2,1)} %core_sum.5), calls=%async_computation.5 | async-start | bytes 4194304 | tf_op jit(solution)/shard_map/all_to_all | solution.py:63
  290.3 109.9 %all-gather.11.cloned.1.call-start = ((), (), s32[]{:S(2)}) async-start(), calls=%async_computation.16 | async-start | bytes 7077888 | tf_op jit(solution)/shard_map/all_gather | solution.py:1091
  315.6 13.9 %collective-permute-start.35 = (bf16[4,256,1024]{2,1,0:T(8,128)(2,1)}, bf16[4,256,1024]{2,1,0:T(8,128)(2,1)}, u32[]{:S(2)}, u32[]{:S(2)}) collective-permute-start(bf16[4,256,1024]{2,1,0:T(8,128)(2,1)} %bitcast.124), channel_id=1, source_target_pairs={{0,4},{4,0},{1,5},{5,1},{2,6},{6,2},{3,7},{7,3},{8,12},{12,8},{9,1... | collective-permute-start | bytes 6291464 | tf_op jit(solution)/shard_map/ppermute | solution.py:40
  318.9 2.0 collective-permute-start.31
  326.1 6.9 %collective-permute-start.32 = (bf16[512,128]{1,0:T(8,128)(2,1)}, bf16[512,128]{1,0:T(8,128)(2,1)S(1)}, u32[]{:S(2)}, u32[]{:S(2)}) collective-permute-start(bf16[512,128]{1,0:T(8,128)(2,1)} %get-tuple-element.300), channel_id=1, source_target_pairs={{0,8},{8,0},{16,24},{24,16},{1,9},{9,1},{17,25},{25,17},{2,10},{10... | collective-permute-start | bytes 393224 | tf_op jit(solution)/shard_map/ppermute | solution.py:45
  328.0 8.6 %collective-permute-start.33 = (bf16[512,128]{1,0:T(8,128)(2,1)}, bf16[512,128]{1,0:T(8,128)(2,1)S(1)}, u32[]{:S(2)}, u32[]{:S(2)}) collective-permute-start(bf16[512,128]{1,0:T(8,128)(2,1)} %get-tuple-element.301), channel_id=1, source_target_pairs={{0,16},{8,24},{16,0},{24,8},{1,17},{9,25},{17,1},{25,9},{2,18},{10... | collective-permute-start | bytes 393224 | tf_op jit(solution)/shard_map/ppermute | solution.py:45
  329.5 7.1 %collective-permute-start.34 = (bf16[512,128]{1,0:T(8,128)(2,1)}, bf16[512,128]{1,0:T(8,128)(2,1)}, u32[]{:S(2)}, u32[]{:S(2)}) collective-permute-start(bf16[512,128]{1,0:T(8,128)(2,1)} %get-tuple-element.302), channel_id=1, source_target_pairs={{0,24},{8,16},{16,8},{24,0},{1,25},{9,17},{17,9},{25,1},{2,26},{10... | collective-permute-start | bytes 393224 | tf_op jit(solution)/shard_map/ppermute | solution.py:45
  341.1 39.3 %collective-permute-start.38 = (bf16[128,1024]{1,0:T(8,128)(2,1)}, bf16[128,1024]{1,0:T(8,128)(2,1)S(1)}, u32[]{:S(2)}, u32[]{:S(2)}) collective-permute-start(bf16[128,1024]{1,0:T(8,128)(2,1)} %get-tuple-element.413), channel_id=1, source_target_pairs={{0,3},{1,2},{2,1},{3,0},{4,7},{5,6},{6,5},{7,4},{8,11},{9,10},{10,... | collective-permute-start | bytes 786440 | tf_op jit(solution)/shard_map/ppermute | solution.py:50
  344.6 35.8 %collective-permute-start.37 = (bf16[128,1024]{1,0:T(8,128)(2,1)}, bf16[128,1024]{1,0:T(8,128)(2,1)}, u32[]{:S(2)}, u32[]{:S(2)}) collective-permute-start(bf16[128,1024]{1,0:T(8,128)(2,1)} %get-tuple-element.414), channel_id=1, source_target_pairs={{0,2},{1,3},{2,0},{3,1},{4,6},{5,7},{6,4},{7,5},{8,10},{9,11},{10,... | collective-permute-start | bytes 786440 | tf_op jit(solution)/shard_map/ppermute | solution.py:50
  344.6 35.8 %collective-permute-start.36 = (bf16[128,1024]{1,0:T(8,128)(2,1)}, bf16[128,1024]{1,0:T(8,128)(2,1)}, u32[]{:S(2)}, u32[]{:S(2)}) collective-permute-start(bf16[128,1024]{1,0:T(8,128)(2,1)} %get-tuple-element.415), channel_id=1, source_target_pairs={{0,1},{1,0},{2,3},{3,2},{4,5},{5,4},{6,7},{7,6},{8,9},{9,8},{10,11... | collective-permute-start | bytes 786440 | tf_op jit(solution)/shard_map/ppermute | solution.py:50
  345.5 34.9 %all-to-all-start.5 = ((bf16[4,256,1024]{2,1,0:T(8,128)(2,1)}), bf16[4,256,1024]{2,1,0:T(8,128)(2,1)}, u32[]{:S(2)}, u32[]{:S(2)}) async-start(bf16[4,256,1024]{2,1,0:T(8,128)(2,1)} %core_sum.6), calls=%async_computation.7 | async-start | bytes 4194304 | tf_op jit(solution)/shard_map/all_to_all | solution.py:63
  380.4 7.4 %collective-permute-start.39 = (bf16[4,256,1024]{2,1,0:T(8,128)(2,1)}, bf16[4,256,1024]{2,1,0:T(8,128)(2,1)}, u32[]{:S(2)}, u32[]{:S(2)}) collective-permute-start(bf16[4,256,1024]{2,1,0:T(8,128)(2,1)} %bitcast.127), channel_id=1, source_target_pairs={{0,4},{4,0},{1,5},{5,1},{2,6},{6,2},{3,7},{7,3},{8,12},{12,8},{9,1... | collective-permute-start | bytes 6291464 | tf_op jit(solution)/shard_map/ppermute | solution.py:40
  391.3 30.8 %all-to-all-start.6 = ((bf16[4,256,1024]{2,1,0:T(8,128)(2,1)}), bf16[4,256,1024]{2,1,0:T(8,128)(2,1)}, u32[]{:S(2)}, u32[]{:S(2)}) async-start(bf16[4,256,1024]{2,1,0:T(8,128)(2,1)} %core_sum.7), calls=%async_computation.8 | async-start | bytes 4194304 | tf_op jit(solution)/shard_map/all_to_all | solution.py:63
  395.7 86.4 %reduce-scatter.8.cloned.1.call-start = ((), (), s32[]{:S(2)}) async-start(), calls=%async_computation.13 | async-start | bytes 4718592 | tf_op jit(solution)/shard_map/reduce_scatter | solution.py:1034
  395.7 26.3 %collective-permute-start.40 = (bf16[256,384]{1,0:T(8,128)(2,1)}, bf16[256,384]{1,0:T(8,128)(2,1)}, u32[]{:S(2)}, u32[]{:S(2)}) collective-permute-start(bf16[256,384]{1,0:T(8,128)(2,1)} %get-tuple-element.321), channel_id=1, source_target_pairs={{0,1},{1,0},{2,3},{3,2},{4,5},{5,4},{6,7},{7,6},{8,9},{9,8},{10,11... | collective-permute-start | bytes 589832 | tf_op jit(solution)/shard_map/ppermute | solution.py:50
  397.0 25.0 %collective-permute-start.41 = (bf16[256,384]{1,0:T(8,128)(2,1)}, bf16[256,384]{1,0:T(8,128)(2,1)}, u32[]{:S(2)}, u32[]{:S(2)}) collective-permute-start(bf16[256,384]{1,0:T(8,128)(2,1)} %get-tuple-element.322), channel_id=1, source_target_pairs={{0,2},{1,3},{2,0},{3,1},{4,6},{5,7},{6,4},{7,5},{8,10},{9,11},{10,... | collective-permute-start | bytes 589832 | tf_op jit(solution)/shard_map/ppermute | solution.py:50
  399.9 22.2 %collective-permute-start.42 = (bf16[256,384]{1,0:T(8,128)(2,1)}, bf16[256,384]{1,0:T(8,128)(2,1)}, u32[]{:S(2)}, u32[]{:S(2)}) collective-permute-start(bf16[256,384]{1,0:T(8,128)(2,1)} %get-tuple-element.323), channel_id=1, source_target_pairs={{0,3},{1,2},{2,1},{3,0},{4,7},{5,6},{6,5},{7,4},{8,11},{9,10},{10,... | collective-permute-start | bytes 589832 | tf_op jit(solution)/shard_map/ppermute | solution.py:50
  427.9 36.8 %all-to-all-start.7 = ((bf16[4,256,896]{2,1,0:T(8,128)(2,1)}), bf16[4,256,896]{2,1,0:T(8,128)(2,1)}, u32[]{:S(2)}, u32[]{:S(2)}) async-start(bf16[4,256,896]{2,1,0:T(8,128)(2,1)} %broadcast_in_dim.55), calls=%async_computation.10 | async-start | bytes 3670016 | tf_op jit(solution)/shard_map/all_to_all | solution.py:63
  468.9 4.8 collective-permute-start.44
  470.2 4.6 collective-permute-start.43
  (59 other events, 331.2 us)
Sparse Core Ops, SparseCore 0:
  86.7 64.1 all-gather.6
  168.4 50.6 all-gather.8
  222.4 51.3 reduce-scatter.3
  276.1 60.2 reduce-scatter.5
  338.3 61.7 all-gather.10
  422.2 59.9 reduce-scatter.7

commit v6 on v5

--- a/solution.py
+++ b/solution.py
@@ -1112,14 +1112,20 @@
     )
     g_down = g_down.reshape(-1, feats)
     sent_qkv = send_pieces(grad_qkv)
-    sums_one, g_gate_up, g_gain_two, g_down = hold((sums_one, g_gate_up, g_gain_two, g_down))
     share_qkv = add_pieces(grad_qkv[0], sent_qkv)
-    out_sum_one = collect_out(hold(out_one[0], g_down, sent_qkv))
     share_out = add_pieces(out_rel[0], out_sent)
     spare = share_out.size // rows
-    if share_qkv.shape[0] == rows and spare % 128 == 0:
+    together = share_qkv.shape[0] == rows and spare % 128 == 0
+    beside = share_qkv
+    if together:
         beside = jnp.concatenate([share_qkv, share_out.reshape(rows, spare)], axis=1)
-        mixed = spread(hold(beside, sums_one))
+        beside = jnp.broadcast_to(beside, (chips,) + beside.shape)
+    sums_one, g_gate_up, g_gain_two, g_down, beside = hold(
+        (sums_one, g_gate_up, g_gain_two, g_down, beside)
+    )
+    out_sum_one = collect_out(hold(out_one[0], g_down, sent_qkv))
+    if together:
+        mixed = exchange(beside)
         near_qkv = mixed[:, :, : 3 * width]
         own_sum = last_sum(mixed[:, :, 3 * width :]).reshape(-1, width, feats)
         other_sum = swap_core(own_sum)

time: 504 us -> 508 us (level)
    all_to_all x8, waiting for transfers between devices: 43.9 us -> 22.9 us  [exchange(): return lax.all_to_all(value, 'chip', 0, 0)]
    reduce_scatter x2, waiting for transfers between devices: 0.35 us -> 12.1 us  [collect_out(): return lax.psum_scatter(flat_part, PLANE, scatter_dimension=0, tiled=True)]
    ppermute x12, waiting for transfers between devices: 2.19 us -> 13.4 us  [swap_shard(): return lax.ppermute(value, 'fsdp', [(i, i ^ mask) for i in range(count)])]
  transfers between devices with their start and end apart: 59 -> 59, of which waited for: 16 -> 17; matrix products, arithmetic and copies ran while one was open for 14% -> 14% of each run, Pallas kernels for 44% -> 44%
where the time goes in v6:
time: 508 us; the launch traced here: 499 us
  Pallas kernels  220 us (43%)
  waiting for transfers between devices  89.8 us (18%)
  starting transfers between devices  80.5 us (16%)
  local copies, waits for them, and re-layouts  49.3 us (10%)
  other arithmetic  44.1 us (9%)
  between operations  15.5 us (3%)
    pallas_call x2, Pallas kernels, attend_backward(): pl.pallas_call(backward_kernel, out_shape=(shape((seq_len // 2, feats), b...  48 us
    pallas_call x2, Pallas kernels, attend_forward(): pl.pallas_call(forward_kernel, out_shape=[narrow, narrow, narrow, shape((...  43.8 us
    pallas_call x2, Pallas kernels, feed_forward(): pl.pallas_call(functools.partial(ffn_kernel, split=split, sides=len(cot))...  42.5 us
    all_to_all x8, starting transfers between devices, exchange(): return lax.all_to_all(value, 'chip', 0, 0)  36.4 us
    ppermute x18, waiting for transfers between devices, swap_chip(): return lax.ppermute(value, 'chip', [(i, i ^ mask) for i in range(count)])  33.5 us
    pallas_call x1, Pallas kernels, weight_sums(): pl.pallas_call(functools.partial(weight_kernel, counts=[len(v) for v in s...  23.1 us
    all_to_all x8, waiting for transfers between devices, exchange(): return lax.all_to_all(value, 'chip', 0, 0)  22.9 us
    ppermute x18, starting transfers between devices, swap_chip(): return lax.ppermute(value, 'chip', [(i, i ^ mask) for i in range(count)])  21 us
  transfers between devices with their start and end apart: 59, of which 17 were waited for; matrix products, arithmetic and copies ran while one was open for 14% of the time, Pallas kernels for 44%

profile of v6, /device:TPU:0, one launch (start us, length us, event | category | flops | bytes accessed | tf_op | source)
XLA Modules:
  0.0 499.1 jit_solution(5756335773479671956)
XLA Ops:
  7.2 4.2 fusion.29
  13.7 5.3 %all-to-all-start = ((bf16[4,256,1024]{2,1,0:T(8,128)(2,1)}), bf16[4,256,1024]{2,1,0:T(8,128)(2,1)}, u32[]{:S(2)}, u32[]{:S(2)}) async-start(bf16[4,256,1024]{2,1,0:T(8,128)(2,1)} %broadcast_in_dim.46), calls=%async_computation | async-start | bytes 4194304 | tf_op jit(solution)/shard_map/all_to_all | solution.py:63
  21.2 4.4 collective-permute-start.2
  26.8 4.0 convert_reduce_fusion
  45.9 2.2 collective-permute-done.1
  49.6 2.5 collective-permute-start.6
  52.1 1.9 collective-permute-start.4
  54.0 4.4 all-to-all-start.1
  63.9 21.9 %attend_forward.2 = (bf16[2048,128]{1,0:T(8,128)(2,1)}, bf16[2048,128]{1,0:T(8,128)(2,1)}, bf16[2048,128]{1,0:T(8,128)(2,1)}, bf16[2,1024,1024]{2,1,0:T(8,128)(2...) custom-call(s32[16]{0:T(128)} %get-tuple-element.189.rel, ...), custom_call_target="tpu_custom_call" | custom-call | flops 31000000512 | bytes 1048576 | tf_op jit(solution)/shard_map/attend_forward/pallas_call | solution.py:582
  87.9 1.9 collective-permute-start.7
  93.0 4.1 all-to-all-start.2
  97.3 21.9 %attend_forward.3 = (bf16[2048,128]{1,0:T(8,128)(2,1)}, bf16[2048,128]{1,0:T(8,128)(2,1)}, bf16[2048,128]{1,0:T(8,128)(2,1)}, bf16[2,1024,1024]{2,1,0:T(8,128)(2...) custom-call(s32[16]{0:T(128)} %get-tuple-element.189.rel, ...), custom_call_target="tpu_custom_call" | custom-call | flops 31000000512 | bytes 1048576 | tf_op jit(solution)/shard_map/attend_forward/pallas_call | solution.py:582
  119.3 2.6 all-to-all-done.2
  123.2 3.5 mix.2
  133.8 3.6 collective-permute-done.13.refs_2_
  141.6 12.3 %collective-permute-done.17.refs_3_ = bf16[256,1024]{1,0:T(8,128)(2,1)S(1)} collective-permute-done((bf16[256,1024]{1,0:T(8,128)(2,1)S(1)}, bf16[256,1024]{1,0:T(8,128)(2,1)S(1)}, u32[]{:S(2)}, u32[]{:S(2)}) %collective-permute-start.17) | collective-permute-done | bytes 524320 | tf_op jit(solution)/shard_map/ppermute | solution.py:45
  153.9 9.7 %collective-permute-done.16.refs_2_ = bf16[256,1024]{1,0:T(8,128)(2,1)S(1)} collective-permute-done((bf16[256,1024]{1,0:T(8,128)(2,1)S(1)}, bf16[256,1024]{1,0:T(8,128)(2,1)S(1)}, u32[]{:S(2)}, u32[]{:S(2)}) %collective-permute-start.16) | collective-permute-done | bytes 524320 | tf_op jit(solution)/shard_map/ppermute | solution.py:45
  165.2 3.1 arrange.2
  169.1 3.4 mix.3
  172.6 4.9 collective-permute-done.20
  182.8 21.4 %feed_forward.2 = (bf16[4,2,256,1024]{3,2,1,0:T(8,128)(2,1)}, bf16[1024,1024]{1,0:T(8,128)(2,1)}, bf16[1024,1024]{1,0:T(8,128)(2,1)}, bf16[2048,512]{1,0:T(8,128)(2,1)}, bf16[2048,1024]{1,0:T(8,128)(2,1)}) custom-call(s32[3]{0:T(128)} %pad_add_fusion.ids.refs_0_, bf16[1024,1024]{1,0:T(8,128)(2,1)} %bitcast.122, bf16[1024,1024]{1,0:T(8,128)(2,1)} %bitcast.30.x_far.refs_1_, ...), custom_call_target="tpu_custom_call" | custom-call | flops 20000000000 | bytes 1048576 | tf_op jit(solution)/shard_map/feed_forward/pallas_call | solution.py:703
  204.2 3.1 collective-permute-done.22.refs_2_
  207.3 3.0 arrange.3
  211.9 3.5 core_sum.4
  215.4 4.5 all-to-all-start.3
  220.2 21.1 %feed_forward.3 = (bf16[4,2,256,1024]{3,2,1,0:T(8,128)(2,1)}, bf16[1024,1024]{1,0:T(8,128)(2,1)}, bf16[1024,1024]{1,0:T(8,128)(2,1)}, bf16[2048,512]{1,0:T(8,128)(2,1)}, bf16[2048,1024]{1,0:T(8,128)(2,1)}) custom-call(s32[3]{0:T(128)} %pad_add_fusion.ids.refs_0_, bf16[1024,1024]{1,0:T(8,128)(2,1)} %bitcast.125, bf16[1024,1024]{1,0:T(8,128)(2,1)} %bitcast.39.x_far.refs_7_, ...), custom_call_target="tpu_custom_call" | custom-call | flops 20000000000 | bytes 1048576 | tf_op jit(solution)/shard_map/feed_forward/pallas_call | solution.py:703
  241.3 4.1 all-to-all-done.3
  245.4 23.1 %weight_sums.1 = bf16[4,384,1024]{2,1,0:T(8,128)(2,1)} custom-call(s32[3]{0:T(128)} %pad_add_fusion.ids.refs_0_, bf16[1024,1024]{1,0:T(8,128)(2,1)} %bitcast.123, bf16[1024,1024]{1,0:T(8,128)(2,1)} %bitcast.30.x_far.refs_1_, bf16[2048,512]{1,0:T(8,128)(2,1)} %get-tuple-element.254.refs_2_, bf16[2048,1024]{1,0:T(8,128)(2,1)} %get-tuple-element.277.refs_3_, ...), custom_call_target="tpu_custom_call" | custom-call | flops 23000000512 | bytes 1048576 | tf_op jit(solution)/shard_map/weight_sums/pallas_call | solution.py:764
  268.5 2.1 convert_reduce_fusion.4
  274.5 4.4 unmix.2
  282.4 3.4 core_sum.5
  285.8 4.4 all-to-all-start.4
  291.6 24.0 %attend_backward.2 = (bf16[1024,1024]{1,0:T(8,128)(2,1)}, bf16[1024,1024]{1,0:T(8,128)(2,1)}, bf16[2,1024,384]{2,1,0:T(8,128)(2,1)}) custom-call(s32[16]{0:T(128)} %get-tuple-element.189.rel, s32[16]{0:T(128)} %get-tuple-element.190.send, s32[4]{0:T(128)} %get-tuple-element.430.first, s32[4]{0:T(128)} %get-tuple-element.428.full, ...), custom_call_target="tpu_custom_call" | custom-call | flops 31000000512 | bytes 1048576 | tf_op jit(solution)/shard_map/attend_backward/pallas_call | solution.py:616
  315.7 2.2 convert_reduce_fusion.3
  321.7 4.3 unmix.3
  326.1 1.9 collective-permute-start.32
  329.6 3.4 core_sum.6
  333.0 3.6 collective-permute-done.33.refs_2_
  336.6 2.5 add_convert_fusion
  341.1 3.5 collective-permute-start.38
  345.5 4.6 all-to-all-start.5
  350.1 24.0 %attend_backward.3 = (bf16[1024,1024]{1,0:T(8,128)(2,1)}, bf16[1024,1024]{1,0:T(8,128)(2,1)}, bf16[2,1024,384]{2,1,0:T(8,128)(2,1)}) custom-call(s32[16]{0:T(128)} %get-tuple-element.189.rel, s32[16]{0:T(128)} %get-tuple-element.190.send, s32[4]{0:T(128)} %get-tuple-element.431.first, s32[4]{0:T(128)} %get-tuple-element.429.full, ...), custom_call_target="tpu_custom_call" | custom-call | flops 31000000512 | bytes 1048576 | tf_op jit(solution)/shard_map/attend_backward/pallas_call | solution.py:616
  374.1 6.3 %qkv_first.1.refs_2_ = f32[1024,384]{1,0:T(8,128)} custom-call(bf16[2048,1024]{1,0:T(8,128)(2,1)} %bitcast.131, bf16[2048,384]{1,0:T(8,128)(2,1)} %bitcast.137), custom_call_target="tpu_custom_call" | custom-call | flops 6000000000 | bytes 1048576 | tf_op jit(solution)/shard_map/qkv_first/pallas_call | solution.py:791
  380.5 7.3 %qkv_sums.1 = (bf16[256,384]{1,0:T(8,128)(2,1)}, bf16[256,384]{1,0:T(8,128)(2,1)}, bf16[256,384]{1,0:T(8,128)(2,1)}, bf16[256,384]{1,0:T(8,128)(2,1)}) custom-call(s32[3]{0:T(128)} %pad_add_fusion.ids.refs_0_, bf16[2048,1024]{1,0:T(8,128)(2,1)} %bitcast.130, bf16[2048,384]{1,0:T(8,128)(2,1)} %bitcast.136, f32[1024,384]{1,0:T(8,128)} %qkv_first.1.refs_2_), custom_call_target="tpu_custom_call" | custom-call | flops 6000000000 | bytes 1048576 | tf_op jit(solution)/shard_map/qkv_sums/pallas_call | solution.py:810
  387.8 3.4 core_sum.7
  391.3 4.4 all-to-all-start.6
  397.1 2.8 collective-permute-start.41
  400.2 2.0 add_convert_fusion.3
  403.2 4.0 collective-permute-done.40
  407.3 7.2 %collective-permute-done.41 = bf16[256,384]{1,0:T(8,128)(2,1)} collective-permute-done((bf16[256,384]{1,0:T(8,128)(2,1)}, bf16[256,384]{1,0:T(8,128)(2,1)}, u32[]{:S(2)}, u32[]{:S(2)}) %collective-permute-start.41) | collective-permute-done | bytes 196640 | tf_op jit(solution)/shard_map/ppermute | solution.py:50
  416.6 9.0 %assemble.2 = (f32[256,4096]{1,0:T(8,128)}, f32[256,4096]{1,0:T(8,128)}, f32[256,1]{1,0:T(8,128)}, f32[8,128,1024]{2,1,0:T(8,128)}) custom-call(bf16[8,384,1024]{2,1,0:T(8,128)(2,1)} %bitcast.103, bf16[256,1]{1,0:T(8,128)(2,1)} %copy-done.26, bf16[256,4096]{1,0:T(8,128)(2,1)} %refs_2_, bf16[256,4096]{1,0:T(8,128)(2,1)} %refs_3_, bf16[8,384,1024]{2,1,0:T(8,128)(2,1)} %bitcast.104), custom_call_target="tpu_custom_call" | custom-call | flops 2000000000 | bytes 1048576 | tf_op jit(solution)/shard_map/assemble/pallas_call | solution.py:856
  427.1 2.4 broadcast_in_dim.55
  429.6 4.6 all-to-all-start.7
  434.2 2.1 convert_reduce_fusion.2
  436.4 2.6 convert_reduce_fusion.1
  439.9 16.3 %all-to-all-done.7 = bf16[4,256,896]{2,1,0:T(8,128)(2,1)} async-done(((bf16[4,256,896]{2,1,0:T(8,128)(2,1)}), bf16[4,256,896]{2,1,0:T(8,128)(2,1)}, u32[]{:S(2)}, u32[]{:S(2)}) %all-to-all-start.7) | async-done | bytes 1835040 | tf_op jit(solution)/shard_map/all_to_all | solution.py:63
  456.2 2.2 convert_reduce_fusion.5
  458.4 2.0 reshape.363
  462.3 2.9 fusion.20
  467.3 4.6 assemble.3
  473.5 12.1 %reduce-scatter.8.cloned.1.call-done = bf16[256,1024]{1,0:T(8,128)(2,1)} async-done(((bf16[2048,1024]{1,0:T(8,128)(2,1)}), bf16[256,1024]{1,0:T(8,128)(2,1)}) %reduce-scatter.8.cloned.1.call-update) | async-done | bytes 524304 | tf_op jit(solution)/shard_map/reduce_scatter | solution.py:1034
  485.6 2.0 fusion.21
  487.8 2.0 copy.78
  489.9 2.0 copy.77
  (310 shorter events, 85.2 us)
Async XLA Ops:
  12.1 118.9 %copy-start.4 = (bf16[256,1024]{1,0:T(8,128)(2,1)}, bf16[256,1024]{1,0:T(8,128)(2,1)S(1)}, u32[]{:S(2)}) copy-start(bf16[256,1024]{1,0:T(8,128)(2,1)S(1)} %get-tuple-element.402) | copy-start | bytes 1572868
  13.7 34.3 %all-to-all-start = ((bf16[4,256,1024]{2,1,0:T(8,128)(2,1)}), bf16[4,256,1024]{2,1,0:T(8,128)(2,1)}, u32[]{:S(2)}, u32[]{:S(2)}) async-start(bf16[4,256,1024]{2,1,0:T(8,128)(2,1)} %broadcast_in_dim.46), calls=%async_computation | async-start | bytes 4194304 | tf_op jit(solution)/shard_map/all_to_all | solution.py:63
  21.2 24.7 %collective-permute-start.2 = (bf16[256,512]{1,0:T(8,128)(2,1)S(1)}, bf16[256,512]{1,0:T(8,128)(2,1)}, u32[]{:S(2)}, u32[]{:S(2)}) collective-permute-start(bf16[256,512]{1,0:T(8,128)(2,1)S(1)} %concatenate.15), channel_id=1, source_target_pairs={{0,3},{1,2},{2,1},{3,0},{4,7},{5,6},{6,5},{7,4},{8,11},{9,10},{10,... | collective-permute-start | bytes 786440 | tf_op jit(solution)/shard_map/ppermute | solution.py:50
  25.6 22.4 %collective-permute-start.1 = (bf16[256,512]{1,0:T(8,128)(2,1)S(1)}, bf16[256,512]{1,0:T(8,128)(2,1)}, u32[]{:S(2)}, u32[]{:S(2)}) collective-permute-start(bf16[256,512]{1,0:T(8,128)(2,1)S(1)} %concatenate.15), channel_id=1, source_target_pairs={{0,2},{1,3},{2,0},{3,1},{4,6},{5,7},{6,4},{7,5},{8,10},{9,11},{10,... | collective-permute-start | bytes 786440 | tf_op jit(solution)/shard_map/ppermute | solution.py:50
  25.6 22.4 %collective-permute-start = (bf16[256,512]{1,0:T(8,128)(2,1)S(1)}, bf16[256,512]{1,0:T(8,128)(2,1)}, u32[]{:S(2)}, u32[]{:S(2)}) collective-permute-start(bf16[256,512]{1,0:T(8,128)(2,1)S(1)} %concatenate.15), channel_id=1, source_target_pairs={{0,1},{1,0},{2,3},{3,2},{4,5},{5,4},{6,7},{7,6},{8,9},{9,8},{10,11... | collective-permute-start | bytes 786440 | tf_op jit(solution)/shard_map/ppermute | solution.py:50
  44.3 47.1 %copy-start.14 = (bf16[256,1024]{1,0:T(8,128)(2,1)}, bf16[256,1024]{1,0:T(8,128)(2,1)S(1)}, u32[]{:S(2)}) copy-start(bf16[256,1024]{1,0:T(8,128)(2,1)S(1)} %get-tuple-element.215) | copy-start | bytes 1572868
  45.9 131.6 %copy-start.6 = (bf16[256,1024]{1,0:T(8,128)(2,1)}, bf16[256,1024]{1,0:T(8,128)(2,1)S(1)}, u32[]{:S(2)}) copy-start(bf16[256,1024]{1,0:T(8,128)(2,1)S(1)} %get-tuple-element.400) | copy-start | bytes 1572868
  49.6 14.3 %collective-permute-start.3 = (bf16[4,256,1024]{2,1,0:T(8,128)(2,1)}, bf16[4,256,1024]{2,1,0:T(8,128)(2,1)}, u32[]{:S(2)}, u32[]{:S(2)}) collective-permute-start(bf16[4,256,1024]{2,1,0:T(8,128)(2,1)} %all-to-all-done), channel_id=1, source_target_pairs={{0,4},{4,0},{1,5},{5,1},{2,6},{6,2},{3,7},{7,3},{8,12},{12,8},{9,1... | collective-permute-start | bytes 6291464 | tf_op jit(solution)/shard_map/ppermute | solution.py:40
  49.6 36.2 %collective-permute-start.6 = (bf16[128,1024]{1,0:T(8,128)(2,1)}, bf16[128,1024]{1,0:T(8,128)(2,1)}, u32[]{:S(2)}, u32[]{:S(2)}) collective-permute-start(bf16[128,1024]{1,0:T(8,128)(2,1)} %dynamic-slice_bitcast_fusion.4.refs_4_.refs_0_), channel_id=1, source_target_pairs={{0,3},{1,2},{2,1},{3,0},{4,7},{5,6},{6,5},{7,4},{8,11},{9,10},{10,... | collective-permute-start | bytes 786440 | tf_op jit(solution)/shard_map/ppermute | solution.py:50
  52.1 33.7 %collective-permute-start.5 = (bf16[128,1024]{1,0:T(8,128)(2,1)}, bf16[128,1024]{1,0:T(8,128)(2,1)}, u32[]{:S(2)}, u32[]{:S(2)}) collective-permute-start(bf16[128,1024]{1,0:T(8,128)(2,1)} %dynamic-slice_bitcast_fusion.4.refs_4_.refs_0_), channel_id=1, source_target_pairs={{0,2},{1,3},{2,0},{3,1},{4,6},{5,7},{6,4},{7,5},{8,10},{9,11},{10,... | collective-permute-start | bytes 786440 | tf_op jit(solution)/shard_map/ppermute | solution.py:50
  52.1 33.7 %collective-permute-start.4 = (bf16[128,1024]{1,0:T(8,128)(2,1)}, bf16[128,1024]{1,0:T(8,128)(2,1)}, u32[]{:S(2)}, u32[]{:S(2)}) collective-permute-start(bf16[128,1024]{1,0:T(8,128)(2,1)} %dynamic-slice_bitcast_fusion.4.refs_4_.refs_0_), channel_id=1, source_target_pairs={{0,1},{1,0},{2,3},{3,2},{4,5},{5,4},{6,7},{7,6},{8,9},{9,8},{10,11... | collective-permute-start | bytes 786440 | tf_op jit(solution)/shard_map/ppermute | solution.py:50
  54.0 31.8 %all-to-all-start.1 = ((bf16[4,256,1024]{2,1,0:T(8,128)(2,1)}), bf16[4,256,1024]{2,1,0:T(8,128)(2,1)}, u32[]{:S(2)}, u32[]{:S(2)}) async-start(bf16[4,256,1024]{2,1,0:T(8,128)(2,1)} %broadcast_in_dim.53), calls=%async_computation.1 | async-start | bytes 4194304 | tf_op jit(solution)/shard_map/all_to_all | solution.py:63
  58.5 124.3 %all-gather.7.cloned.1.call-start = ((), (), s32[]{:S(2)}) async-start(), calls=%async_computation.14 | async-start | bytes 3932160 | tf_op jit(solution)/shard_map/all_gather | solution.py:991
  85.8 11.5 %collective-permute-start.10 = (bf16[4,256,1024]{2,1,0:T(8,128)(2,1)}, bf16[4,256,1024]{2,1,0:T(8,128)(2,1)}, u32[]{:S(2)}, u32[]{:S(2)}) collective-permute-start(bf16[4,256,1024]{2,1,0:T(8,128)(2,1)} %all-to-all-done.1), channel_id=1, source_target_pairs={{0,4},{4,0},{1,5},{5,1},{2,6},{6,2},{3,7},{7,3},{8,12},{12,8},{9,1... | collective-permute-start | bytes 6291464 | tf_op jit(solution)/shard_map/ppermute | solution.py:40
  87.9 31.3 %collective-permute-start.7 = (bf16[512,128]{1,0:T(8,128)(2,1)}, bf16[512,128]{1,0:T(8,128)(2,1)S(1)}, u32[]{:S(2)}, u32[]{:S(2)}) collective-permute-start(bf16[512,128]{1,0:T(8,128)(2,1)} %get-tuple-element.207), channel_id=1, source_target_pairs={{0,8},{8,0},{16,24},{24,16},{1,9},{9,1},{17,25},{25,17},{2,10},{10... | collective-permute-start | bytes 393224 | tf_op jit(solution)/shard_map/ppermute | solution.py:45
  89.9 29.4 %collective-permute-start.8 = (bf16[512,128]{1,0:T(8,128)(2,1)}, bf16[512,128]{1,0:T(8,128)(2,1)S(1)}, u32[]{:S(2)}, u32[]{:S(2)}) collective-permute-start(bf16[512,128]{1,0:T(8,128)(2,1)} %get-tuple-element.208), channel_id=1, source_target_pairs={{0,16},{8,24},{16,0},{24,8},{1,17},{9,25},{17,1},{25,9},{2,18},{10... | collective-permute-start | bytes 393224 | tf_op jit(solution)/shard_map/ppermute | solution.py:45
  91.4 27.9 %collective-permute-start.9 = (bf16[512,128]{1,0:T(8,128)(2,1)}, bf16[512,128]{1,0:T(8,128)(2,1)S(1)}, u32[]{:S(2)}, u32[]{:S(2)}) collective-permute-start(bf16[512,128]{1,0:T(8,128)(2,1)} %get-tuple-element.209), channel_id=1, source_target_pairs={{0,24},{8,16},{16,8},{24,0},{1,25},{9,17},{17,9},{25,1},{2,26},{10... | collective-permute-start | bytes 393224 | tf_op jit(solution)/shard_map/ppermute | solution.py:45
  93.0 28.8 %all-to-all-start.2 = ((bf16[4,256,1024]{2,1,0:T(8,128)(2,1)}), bf16[4,256,1024]{2,1,0:T(8,128)(2,1)S(1)}, u32[]{:S(2)}, u32[]{:S(2)}) async-start(bf16[4,256,1024]{2,1,0:T(8,128)(2,1)} %broadcast_in_dim.54), calls=%async_computation.2 | async-start | bytes 4194304 | tf_op jit(solution)/shard_map/all_to_all | solution.py:63
  97.1 123.0 %all-gather.9.cloned.1.call-start = ((), (), s32[]{:S(2)}) async-start(), calls=%async_computation.15 | async-start | bytes 4718592 | tf_op jit(solution)/shard_map/all_gather | solution.py:974
  126.7 4.3 collective-permute-start.11
  127.5 6.3 %collective-permute-start.12 = (bf16[512,128]{1,0:T(8,128)(2,1)S(1)}, bf16[512,128]{1,0:T(8,128)(2,1)S(1)}, u32[]{:S(2)}, u32[]{:S(2)}) collective-permute-start(bf16[512,128]{1,0:T(8,128)(2,1)S(1)} %copy-done.56), channel_id=1, source_target_pairs={{0,8},{8,0},{16,24},{24,16},{1,9},{9,1},{17,25},{25,17},{2,10},{10... | collective-permute-start | bytes 393224 | tf_op jit(solution)/shard_map/ppermute | solution.py:45
  129.0 8.4 %collective-permute-start.13 = (bf16[512,128]{1,0:T(8,128)(2,1)S(1)}, bf16[512,128]{1,0:T(8,128)(2,1)S(1)}, u32[]{:S(2)}, u32[]{:S(2)}) collective-permute-start(bf16[512,128]{1,0:T(8,128)(2,1)S(1)} %copy-done.54), channel_id=1, source_target_pairs={{0,16},{8,24},{16,0},{24,8},{1,17},{9,25},{17,1},{25,9},{2,18},{10... | collective-permute-start | bytes 393224 | tf_op jit(solution)/shard_map/ppermute | solution.py:45
  129.5 7.9 %collective-permute-start.14 = (bf16[512,128]{1,0:T(8,128)(2,1)S(1)}, bf16[512,128]{1,0:T(8,128)(2,1)S(1)}, u32[]{:S(2)}, u32[]{:S(2)}) collective-permute-start(bf16[512,128]{1,0:T(8,128)(2,1)S(1)} %copy-done.52), channel_id=1, source_target_pairs={{0,24},{8,16},{16,8},{24,0},{1,25},{9,17},{17,9},{25,1},{2,26},{10... | collective-permute-start | bytes 393224 | tf_op jit(solution)/shard_map/ppermute | solution.py:45
  133.8 35.3 %copy-start.51 = (bf16[512,128]{1,0:T(8,128)(2,1)}, bf16[512,128]{1,0:T(8,128)(2,1)S(1)}, u32[]{:S(2)}) copy-start(bf16[512,128]{1,0:T(8,128)(2,1)S(1)} %collective-permute-done.12.refs_1_) | copy-start | bytes 393220
  137.4 31.7 %copy-start.53 = (bf16[512,128]{1,0:T(8,128)(2,1)}, bf16[512,128]{1,0:T(8,128)(2,1)S(1)}, u32[]{:S(2)}) copy-start(bf16[512,128]{1,0:T(8,128)(2,1)S(1)} %collective-permute-done.13.refs_2_) | copy-start | bytes 393220
  138.1 15.8 %collective-permute-start.17 = (bf16[256,1024]{1,0:T(8,128)(2,1)S(1)}, bf16[256,1024]{1,0:T(8,128)(2,1)S(1)}, u32[]{:S(2)}, u32[]{:S(2)}) collective-permute-start(bf16[256,1024]{1,0:T(8,128)(2,1)S(1)} %multiply_convert_fusion.1.refs_0_), channel_id=1, source_target_pairs={{0,24},{8,16},{16,8},{24,0},{1,25},{9,17},{17,9},{25,1},{2,26},{10... | collective-permute-start | bytes 1572872 | tf_op jit(solution)/shard_map/ppermute | solution.py:45
  139.6 24.0 %collective-permute-start.16 = (bf16[256,1024]{1,0:T(8,128)(2,1)S(1)}, bf16[256,1024]{1,0:T(8,128)(2,1)S(1)}, u32[]{:S(2)}, u32[]{:S(2)}) collective-permute-start(bf16[256,1024]{1,0:T(8,128)(2,1)S(1)} %multiply_convert_fusion.1.refs_0_), channel_id=1, source_target_pairs={{0,16},{8,24},{16,0},{24,8},{1,17},{9,25},{17,1},{25,9},{2,18},{10... | collective-permute-start | bytes 1572872 | tf_op jit(solution)/shard_map/ppermute | solution.py:45
  140.2 23.5 %collective-permute-start.15 = (bf16[256,1024]{1,0:T(8,128)(2,1)S(1)}, bf16[256,1024]{1,0:T(8,128)(2,1)S(1)}, u32[]{:S(2)}, u32[]{:S(2)}) collective-permute-start(bf16[256,1024]{1,0:T(8,128)(2,1)S(1)} %multiply_convert_fusion.1.refs_0_), channel_id=1, source_target_pairs={{0,8},{8,0},{16,24},{24,16},{1,9},{9,1},{17,25},{25,17},{2,10},{10... | collective-permute-start | bytes 1572872 | tf_op jit(solution)/shard_map/ppermute | solution.py:45
  168.3 122.5 %reduce-scatter.4.cloned.1.call-start = ((), (), s32[]{:S(2)}) async-start(), calls=%async_computation.11 | async-start | bytes 4718592 | tf_op jit(solution)/shard_map/reduce_scatter | solution.py:1034
  168.6 14.2 %collective-permute-start.19 = (bf16[4,256,1024]{2,1,0:T(8,128)(2,1)}, bf16[4,256,1024]{2,1,0:T(8,128)(2,1)}, u32[]{:S(2)}, u32[]{:S(2)}) collective-permute-start(bf16[4,256,1024]{2,1,0:T(8,128)(2,1)} %copy-done.22), channel_id=1, source_target_pairs={{0,4},{4,0},{1,5},{5,1},{2,6},{6,2},{3,7},{7,3},{8,12},{12,8},{9,1... | collective-permute-start | bytes 6291464 | tf_op jit(solution)/shard_map/ppermute | solution.py:40
  168.6 14.1 %collective-permute-start.18 = (bf16[4,256,1024]{2,1,0:T(8,128)(2,1)}, bf16[4,256,1024]{2,1,0:T(8,128)(2,1)}, u32[]{:S(2)}, u32[]{:S(2)}) collective-permute-start(bf16[4,256,1024]{2,1,0:T(8,128)(2,1)} %arrange.2), channel_id=1, source_target_pairs={{0,4},{4,0},{1,5},{5,1},{2,6},{6,2},{3,7},{7,3},{8,12},{12,8},{9,1... | collective-permute-start | bytes 6291464 | tf_op jit(solution)/shard_map/ppermute | solution.py:40
  172.5 5.0 collective-permute-start.20
  179.2 25.0 %collective-permute-start.23 = (bf16[256,1024]{1,0:T(8,128)(2,1)S(1)}, bf16[256,1024]{1,0:T(8,128)(2,1)S(1)}, u32[]{:S(2)}, u32[]{:S(2)}) collective-permute-start(bf16[256,1024]{1,0:T(8,128)(2,1)S(1)} %multiply_convert_fusion.refs_0_), channel_id=1, source_target_pairs={{0,24},{8,16},{16,8},{24,0},{1,25},{9,17},{17,9},{25,1},{2,26},{10... | collective-permute-start | bytes 1572872 | tf_op jit(solution)/shard_map/ppermute | solution.py:45
  180.7 26.6 %collective-permute-start.22 = (bf16[256,1024]{1,0:T(8,128)(2,1)S(1)}, bf16[256,1024]{1,0:T(8,128)(2,1)}, u32[]{:S(2)}, u32[]{:S(2)}) collective-permute-start(bf16[256,1024]{1,0:T(8,128)(2,1)S(1)} %multiply_convert_fusion.refs_0_), channel_id=1, source_target_pairs={{0,16},{8,24},{16,0},{24,8},{1,17},{9,25},{17,1},{25,9},{2,18},{10... | collective-permute-start | bytes 1572872 | tf_op jit(solution)/shard_map/ppermute | solution.py:45
  181.0 26.3 %collective-permute-start.21 = (bf16[256,1024]{1,0:T(8,128)(2,1)S(1)}, bf16[256,1024]{1,0:T(8,128)(2,1)}, u32[]{:S(2)}, u32[]{:S(2)}) collective-permute-start(bf16[256,1024]{1,0:T(8,128)(2,1)S(1)} %multiply_convert_fusion.refs_0_), channel_id=1, source_target_pairs={{0,8},{8,0},{16,24},{24,16},{1,9},{9,1},{17,25},{25,17},{2,10},{10... | collective-permute-start | bytes 1572872 | tf_op jit(solution)/shard_map/ppermute | solution.py:45
  207.3 4.6 collective-permute-start.25
  210.3 9.8 %collective-permute-start.24 = (bf16[4,256,1024]{2,1,0:T(8,128)(2,1)}, bf16[4,256,1024]{2,1,0:T(8,128)(2,1)}, u32[]{:S(2)}, u32[]{:S(2)}) collective-permute-start(bf16[4,256,1024]{2,1,0:T(8,128)(2,1)} %arrange.3), channel_id=1, source_target_pairs={{0,4},{4,0},{1,5},{5,1},{2,6},{6,2},{3,7},{7,3},{8,12},{12,8},{9,1... | collective-permute-start | bytes 6291464 | tf_op jit(solution)/shard_map/ppermute | solution.py:40
  215.4 30.0 %all-to-all-start.3 = ((bf16[4,256,1024]{2,1,0:T(8,128)(2,1)}), bf16[4,256,1024]{2,1,0:T(8,128)(2,1)}, u32[]{:S(2)}, u32[]{:S(2)}) async-start(bf16[4,256,1024]{2,1,0:T(8,128)(2,1)} %core_sum.4), calls=%async_computation.4 | async-start | bytes 4194304 | tf_op jit(solution)/shard_map/all_to_all | solution.py:63
  219.9 116.7 %reduce-scatter.6.cloned.1.call-start = ((), (), s32[]{:S(2)}) async-start(), calls=%async_computation.12 | async-start | bytes 3932160 | tf_op jit(solution)/shard_map/reduce_scatter | solution.py:1028
  245.4 23.1 %collective-permute-start.26 = (bf16[4,256,1024]{2,1,0:T(8,128)(2,1)}, bf16[4,256,1024]{2,1,0:T(8,128)(2,1)}, u32[]{:S(2)}, u32[]{:S(2)}) collective-permute-start(bf16[4,256,1024]{2,1,0:T(8,128)(2,1)} %bitcast.129), channel_id=1, source_target_pairs={{0,4},{4,0},{1,5},{5,1},{2,6},{6,2},{3,7},{7,3},{8,12},{12,8},{9,1... | collective-permute-start | bytes 6291464 | tf_op jit(solution)/shard_map/ppermute | solution.py:40
  272.1 2.4 collective-permute-start.27
  278.9 11.9 %collective-permute-start.28 = (bf16[512,128]{1,0:T(8,128)(2,1)}, bf16[512,128]{1,0:T(8,128)(2,1)S(1)}, u32[]{:S(2)}, u32[]{:S(2)}) collective-permute-start(bf16[512,128]{1,0:T(8,128)(2,1)} %get-tuple-element.283), channel_id=1, source_target_pairs={{0,8},{8,0},{16,24},{24,16},{1,9},{9,1},{17,25},{25,17},{2,10},{10... | collective-permute-start | bytes 393224 | tf_op jit(solution)/shard_map/ppermute | solution.py:45
  280.4 10.5 %collective-permute-start.29 = (bf16[512,128]{1,0:T(8,128)(2,1)}, bf16[512,128]{1,0:T(8,128)(2,1)S(1)}, u32[]{:S(2)}, u32[]{:S(2)}) collective-permute-start(bf16[512,128]{1,0:T(8,128)(2,1)} %get-tuple-element.284), channel_id=1, source_target_pairs={{0,16},{8,24},{16,0},{24,8},{1,17},{9,25},{17,1},{25,9},{2,18},{10... | collective-permute-start | bytes 393224 | tf_op jit(solution)/shard_map/ppermute | solution.py:45
  280.9 9.9 %collective-permute-start.30 = (bf16[512,128]{1,0:T(8,128)(2,1)}, bf16[512,128]{1,0:T(8,128)(2,1)S(1)}, u32[]{:S(2)}, u32[]{:S(2)}) collective-permute-start(bf16[512,128]{1,0:T(8,128)(2,1)} %get-tuple-element.285), channel_id=1, source_target_pairs={{0,24},{8,16},{16,8},{24,0},{1,25},{9,17},{17,9},{25,1},{2,26},{10... | collective-permute-start | bytes 393224 | tf_op jit(solution)/shard_map/ppermute | solution.py:45
  285.8 29.8 %all-to-all-start.4 = ((bf16[4,256,1024]{2,1,0:T(8,128)(2,1)}), bf16[4,256,1024]{2,1,0:T(8,128)(2,1)}, u32[]{:S(2)}, u32[]{:S(2)}) async-start(bf16[4,256,1024]{2,1,0:T(8,128)(2,1)} %core_sum.5), calls=%async_computation.5 | async-start | bytes 4194304 | tf_op jit(solution)/shard_map/all_to_all | solution.py:63
  290.3 126.3 %all-gather.11.cloned.1.call-start = ((), (), s32[]{:S(2)}) async-start(), calls=%async_computation.16 | async-start | bytes 7077888 | tf_op jit(solution)/shard_map/all_gather | solution.py:1091
  315.6 13.9 %collective-permute-start.35 = (bf16[4,256,1024]{2,1,0:T(8,128)(2,1)}, bf16[4,256,1024]{2,1,0:T(8,128)(2,1)}, u32[]{:S(2)}, u32[]{:S(2)}) collective-permute-start(bf16[4,256,1024]{2,1,0:T(8,128)(2,1)} %bitcast.124), channel_id=1, source_target_pairs={{0,4},{4,0},{1,5},{5,1},{2,6},{6,2},{3,7},{7,3},{8,12},{12,8},{9,1... | collective-permute-start | bytes 6291464 | tf_op jit(solution)/shard_map/ppermute | solution.py:40
  318.9 2.0 collective-permute-start.31
  326.1 6.9 %collective-permute-start.32 = (bf16[512,128]{1,0:T(8,128)(2,1)}, bf16[512,128]{1,0:T(8,128)(2,1)S(1)}, u32[]{:S(2)}, u32[]{:S(2)}) collective-permute-start(bf16[512,128]{1,0:T(8,128)(2,1)} %get-tuple-element.300), channel_id=1, source_target_pairs={{0,8},{8,0},{16,24},{24,16},{1,9},{9,1},{17,25},{25,17},{2,10},{10... | collective-permute-start | bytes 393224 | tf_op jit(solution)/shard_map/ppermute | solution.py:45
  328.0 8.6 %collective-permute-start.33 = (bf16[512,128]{1,0:T(8,128)(2,1)}, bf16[512,128]{1,0:T(8,128)(2,1)S(1)}, u32[]{:S(2)}, u32[]{:S(2)}) collective-permute-start(bf16[512,128]{1,0:T(8,128)(2,1)} %get-tuple-element.301), channel_id=1, source_target_pairs={{0,16},{8,24},{16,0},{24,8},{1,17},{9,25},{17,1},{25,9},{2,18},{10... | collective-permute-start | bytes 393224 | tf_op jit(solution)/shard_map/ppermute | solution.py:45
  329.5 7.1 %collective-permute-start.34 = (bf16[512,128]{1,0:T(8,128)(2,1)}, bf16[512,128]{1,0:T(8,128)(2,1)}, u32[]{:S(2)}, u32[]{:S(2)}) collective-permute-start(bf16[512,128]{1,0:T(8,128)(2,1)} %get-tuple-element.302), channel_id=1, source_target_pairs={{0,24},{8,16},{16,8},{24,0},{1,25},{9,17},{17,9},{25,1},{2,26},{10... | collective-permute-start | bytes 393224 | tf_op jit(solution)/shard_map/ppermute | solution.py:45
  341.1 39.3 %collective-permute-start.38 = (bf16[128,1024]{1,0:T(8,128)(2,1)}, bf16[128,1024]{1,0:T(8,128)(2,1)S(1)}, u32[]{:S(2)}, u32[]{:S(2)}) collective-permute-start(bf16[128,1024]{1,0:T(8,128)(2,1)} %get-tuple-element.413), channel_id=1, source_target_pairs={{0,3},{1,2},{2,1},{3,0},{4,7},{5,6},{6,5},{7,4},{8,11},{9,10},{10,... | collective-permute-start | bytes 786440 | tf_op jit(solution)/shard_map/ppermute | solution.py:50
  344.6 35.8 %collective-permute-start.37 = (bf16[128,1024]{1,0:T(8,128)(2,1)}, bf16[128,1024]{1,0:T(8,128)(2,1)}, u32[]{:S(2)}, u32[]{:S(2)}) collective-permute-start(bf16[128,1024]{1,0:T(8,128)(2,1)} %get-tuple-element.414), channel_id=1, source_target_pairs={{0,2},{1,3},{2,0},{3,1},{4,6},{5,7},{6,4},{7,5},{8,10},{9,11},{10,... | collective-permute-start | bytes 786440 | tf_op jit(solution)/shard_map/ppermute | solution.py:50
  344.6 35.8 %collective-permute-start.36 = (bf16[128,1024]{1,0:T(8,128)(2,1)}, bf16[128,1024]{1,0:T(8,128)(2,1)}, u32[]{:S(2)}, u32[]{:S(2)}) collective-permute-start(bf16[128,1024]{1,0:T(8,128)(2,1)} %get-tuple-element.415), channel_id=1, source_target_pairs={{0,1},{1,0},{2,3},{3,2},{4,5},{5,4},{6,7},{7,6},{8,9},{9,8},{10,11... | collective-permute-start | bytes 786440 | tf_op jit(solution)/shard_map/ppermute | solution.py:50
  345.5 35.0 %all-to-all-start.5 = ((bf16[4,256,1024]{2,1,0:T(8,128)(2,1)}), bf16[4,256,1024]{2,1,0:T(8,128)(2,1)}, u32[]{:S(2)}, u32[]{:S(2)}) async-start(bf16[4,256,1024]{2,1,0:T(8,128)(2,1)} %core_sum.6), calls=%async_computation.7 | async-start | bytes 4194304 | tf_op jit(solution)/shard_map/all_to_all | solution.py:63
  380.4 7.4 %collective-permute-start.39 = (bf16[4,256,1024]{2,1,0:T(8,128)(2,1)}, bf16[4,256,1024]{2,1,0:T(8,128)(2,1)}, u32[]{:S(2)}, u32[]{:S(2)}) collective-permute-start(bf16[4,256,1024]{2,1,0:T(8,128)(2,1)} %bitcast.127), channel_id=1, source_target_pairs={{0,4},{4,0},{1,5},{5,1},{2,6},{6,2},{3,7},{7,3},{8,12},{12,8},{9,1... | collective-permute-start | bytes 6291464 | tf_op jit(solution)/shard_map/ppermute | solution.py:40
  391.3 35.9 %all-to-all-start.6 = ((bf16[4,256,1024]{2,1,0:T(8,128)(2,1)}), bf16[4,256,1024]{2,1,0:T(8,128)(2,1)}, u32[]{:S(2)}, u32[]{:S(2)}) async-start(bf16[4,256,1024]{2,1,0:T(8,128)(2,1)} %core_sum.7), calls=%async_computation.8 | async-start | bytes 4194304 | tf_op jit(solution)/shard_map/all_to_all | solution.py:63
  395.7 89.9 %reduce-scatter.8.cloned.1.call-start = ((), (), s32[]{:S(2)}) async-start(), calls=%async_computation.13 | async-start | bytes 4718592 | tf_op jit(solution)/shard_map/reduce_scatter | solution.py:1034
  395.7 11.5 %collective-permute-start.40 = (bf16[256,384]{1,0:T(8,128)(2,1)}, bf16[256,384]{1,0:T(8,128)(2,1)}, u32[]{:S(2)}, u32[]{:S(2)}) collective-permute-start(bf16[256,384]{1,0:T(8,128)(2,1)} %get-tuple-element.321), channel_id=1, source_target_pairs={{0,1},{1,0},{2,3},{3,2},{4,5},{5,4},{6,7},{7,6},{8,9},{9,8},{10,11... | collective-permute-start | bytes 589832 | tf_op jit(solution)/shard_map/ppermute | solution.py:50
  397.1 17.4 %collective-permute-start.41 = (bf16[256,384]{1,0:T(8,128)(2,1)}, bf16[256,384]{1,0:T(8,128)(2,1)}, u32[]{:S(2)}, u32[]{:S(2)}) collective-permute-start(bf16[256,384]{1,0:T(8,128)(2,1)} %get-tuple-element.322), channel_id=1, source_target_pairs={{0,2},{1,3},{2,0},{3,1},{4,6},{5,7},{6,4},{7,5},{8,10},{9,11},{10,... | collective-permute-start | bytes 589832 | tf_op jit(solution)/shard_map/ppermute | solution.py:50
  399.9 14.6 %collective-permute-start.42 = (bf16[256,384]{1,0:T(8,128)(2,1)}, bf16[256,384]{1,0:T(8,128)(2,1)}, u32[]{:S(2)}, u32[]{:S(2)}) collective-permute-start(bf16[256,384]{1,0:T(8,128)(2,1)} %get-tuple-element.323), channel_id=1, source_target_pairs={{0,3},{1,2},{2,1},{3,0},{4,7},{5,6},{6,5},{7,4},{8,11},{9,10},{10,... | collective-permute-start | bytes 589832 | tf_op jit(solution)/shard_map/ppermute | solution.py:50
  429.6 26.6 %all-to-all-start.7 = ((bf16[4,256,896]{2,1,0:T(8,128)(2,1)}), bf16[4,256,896]{2,1,0:T(8,128)(2,1)}, u32[]{:S(2)}, u32[]{:S(2)}) async-start(bf16[4,256,896]{2,1,0:T(8,128)(2,1)} %broadcast_in_dim.55), calls=%async_computation.10 | async-start | bytes 3670016 | tf_op jit(solution)/shard_map/all_to_all | solution.py:63
  460.4 4.8 collective-permute-start.44
  461.7 4.7 collective-permute-start.43
  (59 other events, 366.3 us)
Sparse Core Ops, SparseCore 0:
  86.7 64.1 all-gather.6
  168.4 50.6 all-gather.8
  222.4 51.3 reduce-scatter.3
  276.1 60.2 reduce-scatter.5
  338.3 61.7 all-gather.10
  429.7 55.9 reduce-scatter.7
